TPU v7x, 128 devices: a whole 4x4x4 slice. The times are simulated.
128 devices in a mesh: head: 4 (over z_lo, core), tok: 32 (over x, z_hi, y).
Axes of the slice: x: 4, y: 4, z: 4 (z_hi: 2, z_lo: 2; z = z_hi * 2 + z_lo), core: 2. Of those that a mesh axis runs over, the one named last changes fastest.
Arguments:
- hidden_in: bfloat16 [8192, 2048], P('tok'), may hold values from -6 to 6
- queries: bfloat16 [8192, 2048], P('tok', 'head'), may hold values from -4.5 to 4.5
- keys: bfloat16 [8192, 2048], P('tok', 'head'), may hold values from -4.5 to 4.5
- values: bfloat16 [8192, 2048], P('tok', 'head'), may hold values from -6 to 6
- request_ids: int32 [8192], replicated, may hold values from 0 to 63, never falling along the last dimension, each value on 1 to 1024 neighbouring positions
- out_proj: bfloat16 [2048, 2048], P('head'), may hold values from -0.125 to 0.125
- norm_gain: float32 [2048], replicated, may hold values from 0.1 to 1.9
- expert_gate_up: bfloat16 [32, 2048, 2, 1408], P('tok', None, None, 'head'), may hold values from -0.125 to 0.125
- expert_down: bfloat16 [32, 1408, 2048], P('tok', 'head'), may hold values from -0.15625 to 0.15625
- shared_gate_up: bfloat16 [2048, 2, 2816], P(None, None, 'head'), may hold values from -0.125 to 0.125
- shared_down: bfloat16 [2816, 2048], P('head'), may hold values from -0.109375 to 0.109375
- shared_gate: bfloat16 [2048], replicated, may hold values from -0.125 to 0.125
- routes: int32 [8192, 4], P('tok'), may hold values from 0 to 31, all different within a row; in each aligned block of 256 rows (0 to 255, 256 to 511, ...) at most 48 rows name the same one
- route_weights: float32 [8192, 4], P('tok'), may hold values from 0.05 to 0.5
- page_slots: int32 [1024], replicated, may hold values from 0 to 1023, as said below
Outputs:
- layer_out: bfloat16 [8192, 2048], P('tok', 'head')
- decode_cache: bfloat16 [1024, 8, 4096], P('tok', 'head')
Inputs may be any that keep to these rules, and one draw needn't show every extreme that they name: `request_ids`: ids never fall along the tokens; each request holds 1 to 1024 consecutive tokens, and one holds exactly 1024. `routes`: each row names 4 different experts; among the rows of one device no expert is named more than 48 times, a bound that some block reaches. `page_slots`: a permutation; for any two aligned blocks, one of 32 pages and one of 32 cache rows, the number of pages of the first that go to rows of the second is exactly 1.
All inputs are finite; a program needn't handle non-finite values.
Results may differ from a plain program's by a relative error of at most 0.0065.
Values may be sent and summed in bfloat16 or wider, within the bound.
No kernel may reach another device: no remote copies, remote signals or barrier semaphores. Data moves between devices by JAX's collectives and lax.ppermute only.
A program may use at most 128 MiB of HBM per device.

v0:
```python
import math

import jax
import jax.numpy as jnp
from jax import lax
from jax.sharding import PartitionSpec as P

HD = 128
TOP = 4
EXPERTS = 32
PAGE = 8
REACH = 4
CAP = 48


def from_behind(value, axis, steps):
    count = lax.axis_size(axis)
    leading, last = (max(0, -steps), min(count, count - steps))
    return lax.ppermute(value, axis, [(source, source + steps) for source in range(leading, last)])


def run_experts(slots, gate_up, down):
    both = jnp.einsum("secd,edgf->secgf", slots, gate_up, preferred_element_type=jnp.float32)
    active = (jax.nn.silu(both[..., 0, :]) * both[..., 1, :]).astype(jnp.bfloat16)
    return jnp.einsum("secf,efd->secd", active, down, preferred_element_type=jnp.float32)


def per_device(
    hidden_in,
    queries,
    keys,
    values,
    request_ids,
    out_proj,
    norm_gain,
    expert_gate_up,
    expert_down,
    shared_gate_up,
    shared_down,
    shared_gate,
    routes,
    route_weights,
    page_slots,
):
    tok_rows = hidden_in.shape[0]
    model_width = hidden_in.shape[1]
    head_width = queries.shape[1]
    heads_here = head_width // HD
    tok_count = lax.axis_size("tok")
    head_count = lax.axis_size("head")
    tok_index = lax.axis_index("tok")
    head_index = lax.axis_index("head")
    column_width = model_width // head_count
    key_list = [keys]
    value_list = [values]
    for step in range(1, REACH + 1):
        far_keys, far_values = from_behind((keys, values), "tok", step)
        key_list.insert(0, far_keys)
        value_list.insert(0, far_values)
    span = REACH * tok_rows
    window_keys = jnp.concatenate(key_list, 0).reshape(span + tok_rows, heads_here, HD)
    window_values = jnp.concatenate(value_list, 0).reshape(span + tok_rows, heads_here, HD)
    padded_ids = jnp.concatenate([jnp.full((span,), -1, jnp.int32), request_ids], 0)
    base = tok_index * tok_rows
    key_ids = lax.dynamic_slice_in_dim(padded_ids, base, span + tok_rows, 0)
    query_ids = lax.dynamic_slice_in_dim(request_ids, base, tok_rows, 0)
    query_pos = jnp.arange(tok_rows, dtype=jnp.int32) + span
    key_pos = jnp.arange(span + tok_rows, dtype=jnp.int32)
    allowed = (query_ids[:, None] == key_ids[None, :]) & (key_pos[None, :] <= query_pos[:, None])
    scores = jnp.einsum(
        "qhd,khd->hqk",
        queries.reshape(tok_rows, heads_here, HD),
        window_keys,
        preferred_element_type=jnp.float32,
    ) * (1.0 / math.sqrt(HD))
    scores = jnp.where(allowed[None], scores, -1e30)
    top = jnp.max(scores, axis=-1, keepdims=True)
    weights = jnp.exp(scores - top)
    probs = (weights / jnp.sum(weights, axis=-1, keepdims=True)).astype(jnp.bfloat16)
    attended = (
        jnp.einsum("hqk,khd->qhd", probs, window_values, preferred_element_type=jnp.float32)
        .astype(jnp.bfloat16)
        .reshape(tok_rows, head_width)
    )
    projected = jnp.dot(attended, out_proj, preferred_element_type=jnp.float32)
    total = lax.psum(projected, "head")
    resid = hidden_in.astype(jnp.float32) + total
    mean_square = jnp.mean(resid * resid, axis=-1, keepdims=True)
    normed = (resid * lax.rsqrt(mean_square + 1e-06) * norm_gain).astype(jnp.bfloat16)
    resid_cols = lax.dynamic_slice_in_dim(resid, head_index * column_width, column_width, 1)
    shared_both = jnp.einsum(
        "td,dgf->tgf", normed, shared_gate_up, preferred_element_type=jnp.float32
    )
    shared_act = (jax.nn.silu(shared_both[:, 0, :]) * shared_both[:, 1, :]).astype(jnp.bfloat16)
    shared_scale = jax.nn.sigmoid(jnp.dot(normed, shared_gate, preferred_element_type=jnp.float32))
    shared_term = shared_scale[:, None] * jnp.dot(
        shared_act, shared_down, preferred_element_type=jnp.float32
    )
    flat_routes = routes.reshape(-1)
    assign = tok_rows * TOP
    expert_ids = jnp.arange(EXPERTS, dtype=jnp.int32)
    onehot = (flat_routes[:, None] == expert_ids[None, :]).astype(jnp.int32)
    before = jnp.cumsum(onehot, 0) - onehot
    rank = jnp.sum(before * onehot, 1)
    slot = flat_routes * CAP + rank
    source_row = (
        jnp.zeros((EXPERTS * CAP,), jnp.int32)
        .at[slot]
        .set(jnp.arange(assign, dtype=jnp.int32) // TOP)
    )
    filled = jnp.zeros((EXPERTS * CAP,), jnp.bool_).at[slot].set(True)
    outgoing = jnp.where(filled[:, None], normed[source_row], jnp.zeros((), jnp.bfloat16))
    local_experts = EXPERTS // tok_count
    outgoing = outgoing.reshape(tok_count, local_experts, CAP, model_width)
    partial_value = run_experts(
        lax.all_to_all(outgoing, "tok", split_axis=0, concat_axis=0, tiled=True),
        expert_gate_up,
        expert_down,
    )
    flat_weights = route_weights.reshape(tok_rows, TOP, 1)
    slot_cols, shared_cols = (
        lax.psum_scatter(
            partial_value.reshape(EXPERTS * CAP, model_width),
            "head",
            scatter_dimension=1,
            tiled=True,
        ),
        lax.psum_scatter(shared_term, "head", scatter_dimension=1, tiled=True),
    )
    returned = lax.all_to_all(
        slot_cols.reshape(tok_count, local_experts * CAP, column_width).astype(jnp.bfloat16),
        "tok",
        split_axis=0,
        concat_axis=0,
        tiled=True,
    ).astype(jnp.float32)
    picked = returned.reshape(EXPERTS * CAP, column_width)[slot].reshape(
        tok_rows, TOP, column_width
    )
    moe_cols = jnp.sum(picked * flat_weights, 1)
    layer_cols = resid_cols + shared_cols + moe_cols
    layer_out = layer_cols.astype(jnp.bfloat16)
    pages_here = tok_rows // PAGE
    pair = pages_here // tok_count
    quarter_page = PAGE // head_count
    slots_all = page_slots.reshape(tok_count, pages_here)
    owner_all = slots_all // pages_here
    same_owner = owner_all[:, :, None] == owner_all[:, None, :]
    earlier = slots_all[:, None, :] < slots_all[:, :, None]
    rank_all = jnp.sum((same_owner & earlier).astype(jnp.int32), 2)
    send_pos = owner_all * pair + rank_all
    mine_pos = lax.dynamic_index_in_dim(send_pos, tok_index, 0, keepdims=False)
    page_ids = jnp.arange(pages_here, dtype=jnp.int32)
    send_order = jnp.zeros((pages_here,), jnp.int32).at[mine_pos].set(page_ids)
    sources = jnp.arange(tok_count, dtype=jnp.int32)[:, None]
    target = jnp.where(owner_all == tok_index, sources * pair + rank_all, pages_here)
    arrival_slot = (
        jnp.zeros((pages_here + 1,), jnp.int32)
        .at[target.reshape(-1)]
        .set((slots_all % pages_here).reshape(-1))[:pages_here]
    )
    place_order = jnp.zeros((pages_here,), jnp.int32).at[arrival_slot].set(page_ids)
    kv_pages = jnp.stack([keys, values], 1).reshape(
        pages_here, head_count, quarter_page, 2, heads_here, HD
    )[send_order]
    row_width = 2 * head_count * heads_here * HD
    spread = kv_pages.reshape(
        tok_count, pair, head_count, quarter_page, 2, heads_here, HD
    ).transpose(2, 0, 1, 3, 4, 5, 6)
    spread = spread.reshape(head_count * tok_count, pair, quarter_page, 2, heads_here, HD)
    landed = lax.all_to_all(spread, ("head", "tok"), split_axis=0, concat_axis=0, tiled=True)
    landed = landed.reshape(head_count, tok_count, pair, quarter_page, 2, heads_here, HD).transpose(
        1, 2, 3, 4, 0, 5, 6
    )
    landed = landed.reshape(pages_here, quarter_page, row_width)
    decode_cache = landed[place_order]
    return (layer_out, decode_cache)


def solution(mesh):
    in_specs = (
        P("tok", None),
        P("tok", "head"),
        P("tok", "head"),
        P("tok", "head"),
        P(),
        P("head", None),
        P(),
        P("tok", None, None, "head"),
        P("tok", "head", None),
        P(None, None, "head"),
        P("head", None),
        P(),
        P("tok", None),
        P("tok", None),
        P(),
    )
    out_specs = (P("tok", "head"), P("tok", "head", None))
    return jax.shard_map(
        per_device, mesh=mesh, in_specs=in_specs, out_specs=out_specs, check_vma=False
    )
```

profile of v0, /device:TPU:0, one launch (start us, length us, event | category | flops | bytes accessed | tf_op | source)
XLA Modules:
  0.0 430.4 jit_solution(11822778492569103594)
XLA Ops:
  8.5 5.9 %collective-permute-start.4 = (bf16[256,512]{0,1:T(8,128)(2,1)S(1)}, bf16[256,512]{0,1:T(8,128)(2,1)S(1)}, u32[]{:S(2)}, u32[]{:S(2)}) collective-permute-start(bf16[256,512]{0,1:T(8,128)(2,1)S(1)} %copy.77), channel_id=1, source_target_pairs={{0,4},{1,5},{2,6},{3,7},{4,8},{5,9},{6,10},{7,11},{8,12},{9,13},{1... | collective-permute-start | bytes 786440 | tf_op jit(solution)/shard_map/ppermute | solution.py:19
  14.4 5.6 %collective-permute-start.5 = (bf16[256,512]{0,1:T(8,128)(2,1)S(1)}, bf16[256,512]{0,1:T(8,128)(2,1)}, u32[]{:S(2)}, u32[]{:S(2)}) collective-permute-start(bf16[256,512]{0,1:T(8,128)(2,1)S(1)} %copy.77), channel_id=1, source_target_pairs={{0,3},{1,4},{2,5},{3,6},{4,7},{5,8},{6,9},{7,10},{8,11},{9,12},{10... | collective-permute-start | bytes 786440 | tf_op jit(solution)/shard_map/ppermute | solution.py:19
  26.1 5.1 %collective-permute-start = (bf16[256,512]{1,0:T(8,128)(2,1)}, bf16[256,512]{1,0:T(8,128)(2,1)}, u32[]{:S(2)}, u32[]{:S(2)}) collective-permute-start(bf16[256,512]{1,0:T(8,128)(2,1)} %param.18), channel_id=1, source_target_pairs={{0,4},{1,5},{2,6},{3,7},{4,8},{5,9},{6,10},{7,11},{8,12},{9,13},{1... | collective-permute-start | bytes 786440 | tf_op jit(solution)/shard_map/ppermute | solution.py:19
  33.8 4.1 collective-permute-done.4
  39.2 4.0 collective-permute-start.2
  44.2 5.4 %collective-permute-start.3 = (bf16[256,512]{1,0:T(8,128)(2,1)}, bf16[256,512]{1,0:T(8,128)(2,1)S(1)}, u32[]{:S(2)}, u32[]{:S(2)}) collective-permute-start(bf16[256,512]{1,0:T(8,128)(2,1)} %param.18), channel_id=1, source_target_pairs={{0,1},{1,2},{2,3},{3,4},{4,5},{5,6},{6,7},{7,8},{8,9},{9,10},{10,1... | collective-permute-start | bytes 786440 | tf_op jit(solution)/shard_map/ppermute | solution.py:19
  58.9 3.5 exponential_reduce_fusion
  62.4 4.5 %fusion.15 = bf16[4,128,256]{2,1,0:T(8,128)(2,1)S(1)} fusion(bf16[1280,4,128]{0,2,1:T(8,128)(2,1)} %bitcast.151, f32[4,256]{1,0:T(4,128)S(1)} %exponential_reduce_fusion, bf16[1280,4,128]{0,2,1:T(8,128)(2,1)} %bitcast.155, pred[256,1280]{0,1:T(8,128)(4,1)} %fusion.14, bf16[256,512]{1,0:T(8,128)(2,1)} %param.16), kind=kOutput, calls=%fused_computation.32 | convolution fusion | flops 677775616 | bytes 3477504 | tf_op jit(solution)/shard_map/hqk,khd->qhd/dot_general | solution.py:81
  66.9 3.6 fusion.75
  71.6 9.0 %reduce-window.6 = s32[32,8,128]{2,1,0:T(8,128)S(1)} reduce-window(s32[32,8,128]{2,1,0:T(8,128)S(1)} %fusion.42, s32[]{:T(128)} %constant.46.clone.1), window={size=1x1x128 pad=0_0x0_0x127_0}, to_apply=%region_5.6 | reduce-window | flops 4161536 | bytes 262148 | tf_op jit(solution)/shard_map/reduce-window
  81.4 4.5 %scatter_custom_fusion.1 = s32[1536]{0:T(1024)S(1)} fusion(s32[1024]{0:T(1024)S(1)} %bitcast.158, s32[1024]{0:T(1024)S(1)} %add_select_fusion.3, s32[]{:T(128)} %constant.46.clone.1), kind=kCustom, calls=%fused_computation.98 | custom fusion | bytes 6148 | tf_op jit(solution)/shard_map/scatter | solution.py:109
  85.9 4.3 %scatter_custom_fusion = pred[1536]{0:T(1024)(128)(4,1)S(1)} fusion(s32[1024]{0:T(1024)S(1)} %bitcast.159, pred[1024]{0:T(1024)(128)(4,1)S(1)} %broadcast.250, pred[]{:T(512)} %constant.99.clone.1), kind=kCustom, calls=%fused_computation.102 | custom fusion | bytes 1537 | tf_op jit(solution)/shard_map/scatter | solution.py:111
  90.4 47.3 %all-reduce.3.cloned.1.call-done = f32[256,2048]{1,0:T(8,128)} async-done(((f32[256,2048]{1,0:T(8,128)}), f32[256,2048]{1,0:T(8,128)}) %all-reduce.3.cloned.1.call-update) | async-done | bytes 2097168 | tf_op jit(solution)/shard_map/psum | solution.py:86
  142.5 14.1 %gather_fusion = bf16[1536,2048]{1,0:T(8,128)(2,1)} fusion(bf16[256,2048]{1,0:T(8,128)(2,1)} %multiply_convert_fusion, s32[2048]{0:T(1024)S(1)} %pad_clamp_fusion), kind=kCustom, calls=%fused_computation | custom fusion | bytes 12589056 | tf_op jit(solution)/shard_map/gather | solution.py:112
  159.9 83.3 %all_to_all.15 = bf16[32,1,48,2048]{3,2,1,0:T(8,128)(2,1)S(1)} all-to-all(bf16[32,1,48,2048]{3,2,1,0:T(8,128)(2,1)S(1)} %broadcast_select_fusion), channel_id=1, replica_groups=mesh['head'=4,'tok'=32] {'tok'}, dimensions={0} | all-to-all | bytes 12582912 | tf_op jit(solution)/shard_map/all_to_all | solution.py:116
  243.2 5.2 %fusion.7 = f32[32,1,48,2,352]{4,2,3,0,1:T(8,128)S(1)} fusion(bf16[1,2048,2,352]{1,3,2,0:T(8,128)(2,1)S(1)} %copy-done, bf16[32,1,48,2048]{3,2,1,0:T(8,128)(2,1)S(1)} %all_to_all.15), kind=kOutput, calls=%fused_computation.22 | convolution fusion | flops 4429185024 | bytes 13500416 | tf_op jit(solution)/shard_map/secd,edgf->secgf/dot_general | solution.py:23
  248.5 6.4 %fusion.12 = f32[32,48,2048]{2,1,0:T(8,128)} fusion(bf16[1,352,2048]{2,1,0:T(8,128)(2,1)S(1)} %copy-done.13, f32[32,1,48,2,352]{4,2,3,0,1:T(8,128)S(1)} %fusion.7), kind=kOutput, calls=%fused_computation.28 | convolution fusion | flops 2217836544 | bytes 18350080 | tf_op jit(solution)/shard_map/secf,efd->secd/dot_general | solution.py:25
  256.5 4.5 %fusion.18 = f32[256,2,704]{0,2,1:T(8,128)S(1)} fusion(bf16[2048,2,704]{0,2,1:T(8,128)(2,1)} %param.24, bf16[256,2048]{1,0:T(8,128)(2,1)S(1)} %copy-done.2), kind=kOutput, calls=%fused_computation.34 | convolution fusion | flops 1476395008 | bytes 8257536 | tf_op jit(solution)/shard_map/td,dgf->tgf/dot_general | solution.py:91
  265.4 4.3 scatter_custom_fusion.3
  273.6 5.1 %all-to-all-start.2 = ((bf16[128,1,2,2,4,128]{5,4,3,2,1,0:T(4,128)(2,1)}), bf16[128,1,2,2,4,128]{5,4,3,2,1,0:T(4,128)(2,1)S(1)}, u32[]{:S(2)}, u32[]{:S(2)}) async-start(bf16[128,1,2,2,4,128]{5,4,3,2,1,0:T(4,128)(2,1)} %copy.93), calls=%async_computation.4 | async-start | bytes 1048576 | tf_op jit(solution)/shard_map/all_to_all | solution.py:171
  278.7 91.5 %reduce-scatter.5.cloned.1.call-done = f32[1536,512]{1,0:T(8,128)} async-done(((f32[1536,2048]{1,0:T(8,128)}), f32[1536,512]{1,0:T(8,128)}) %reduce-scatter.5.cloned.1.call-update) | async-done | bytes 3145744 | tf_op jit(solution)/shard_map/reduce_scatter | solution.py:122
  373.4 9.5 %all-to-all-start.1 = ((bf16[32,48,512]{2,1,0:T(8,128)(2,1)}), bf16[32,48,512]{2,1,0:T(8,128)(2,1)S(1)}, u32[]{:S(2)}, u32[]{:S(2)}) async-start(bf16[32,48,512]{2,1,0:T(8,128)(2,1)} %bitcast.32), calls=%async_computation.3 | async-start | bytes 3145728 | tf_op jit(solution)/shard_map/all_to_all | solution.py:130
  386.6 19.7 %all-to-all-done.1 = bf16[32,48,512]{2,1,0:T(8,128)(2,1)S(1)} async-done(((bf16[32,48,512]{2,1,0:T(8,128)(2,1)}), bf16[32,48,512]{2,1,0:T(8,128)(2,1)S(1)}, u32[]{:S(2)}, u32[]{:S(2)}) %all-to-all-start.1) | async-done | bytes 1572896 | tf_op jit(solution)/shard_map/all_to_all | solution.py:130
  408.6 7.2 %gather_fusion.1 = f32[1024,512]{1,0:T(8,128)} fusion(f32[1536,512]{1,0:T(8,128)} %bitcast_convert_fusion, s32[1024]{0:T(1024)S(1)} %broadcast_clamp_fusion), kind=kCustom, calls=%fused_computation.1 | custom fusion | bytes 4198400 | tf_op jit(solution)/shard_map/gather | solution.py:137
  (124 shorter events, 58.3 us)
Async XLA Ops:
  7.2 236.1 %copy-start = (bf16[1,2048,2,352]{1,3,2,0:T(8,128)(2,1)S(1)}, bf16[1,2048,2,352]{1,3,2,0:T(8,128)(2,1)}, u32[]{:S(2)}) copy-start(bf16[1,2048,2,352]{1,3,2,0:T(8,128)(2,1)} %param.22) | copy-start | bytes 8650756
  7.2 130.5 %all-reduce.3.cloned.1.call-start = ((), (), s32[]{:S(2)}) async-start(), calls=%async_computation.5 | async-start | bytes 4194304 | tf_op jit(solution)/shard_map/psum | solution.py:86
  8.5 29.4 %collective-permute-start.4 = (bf16[256,512]{0,1:T(8,128)(2,1)S(1)}, bf16[256,512]{0,1:T(8,128)(2,1)S(1)}, u32[]{:S(2)}, u32[]{:S(2)}) collective-permute-start(bf16[256,512]{0,1:T(8,128)(2,1)S(1)} %copy.77), channel_id=1, source_target_pairs={{0,4},{1,5},{2,6},{3,7},{4,8},{5,9},{6,10},{7,11},{8,12},{9,13},{1... | collective-permute-start | bytes 786440 | tf_op jit(solution)/shard_map/ppermute | solution.py:19
  14.4 24.9 %collective-permute-start.5 = (bf16[256,512]{0,1:T(8,128)(2,1)S(1)}, bf16[256,512]{0,1:T(8,128)(2,1)}, u32[]{:S(2)}, u32[]{:S(2)}) collective-permute-start(bf16[256,512]{0,1:T(8,128)(2,1)S(1)} %copy.77), channel_id=1, source_target_pairs={{0,3},{1,4},{2,5},{3,6},{4,7},{5,8},{6,9},{7,10},{8,11},{9,12},{10... | collective-permute-start | bytes 786440 | tf_op jit(solution)/shard_map/ppermute | solution.py:19
  20.0 24.3 %collective-permute-start.6 = (bf16[256,512]{0,1:T(8,128)(2,1)S(1)}, bf16[256,512]{0,1:T(8,128)(2,1)}, u32[]{:S(2)}, u32[]{:S(2)}) collective-permute-start(bf16[256,512]{0,1:T(8,128)(2,1)S(1)} %copy.77), channel_id=1, source_target_pairs={{0,2},{1,3},{2,4},{3,5},{4,6},{5,7},{6,8},{7,9},{8,10},{9,11},{10,... | collective-permute-start | bytes 786440 | tf_op jit(solution)/shard_map/ppermute | solution.py:19
  23.2 27.4 %collective-permute-start.7 = (bf16[256,512]{0,1:T(8,128)(2,1)S(1)}, bf16[256,512]{0,1:T(8,128)(2,1)}, u32[]{:S(2)}, u32[]{:S(2)}) collective-permute-start(bf16[256,512]{0,1:T(8,128)(2,1)S(1)} %copy.77), channel_id=1, source_target_pairs={{0,1},{1,2},{2,3},{3,4},{4,5},{5,6},{6,7},{7,8},{8,9},{9,10},{10,1... | collective-permute-start | bytes 786440 | tf_op jit(solution)/shard_map/ppermute | solution.py:19
  26.1 25.5 %collective-permute-start = (bf16[256,512]{1,0:T(8,128)(2,1)}, bf16[256,512]{1,0:T(8,128)(2,1)}, u32[]{:S(2)}, u32[]{:S(2)}) collective-permute-start(bf16[256,512]{1,0:T(8,128)(2,1)} %param.18), channel_id=1, source_target_pairs={{0,4},{1,5},{2,6},{3,7},{4,8},{5,9},{6,10},{7,11},{8,12},{9,13},{1... | collective-permute-start | bytes 786440 | tf_op jit(solution)/shard_map/ppermute | solution.py:19
  37.9 15.7 %collective-permute-start.1 = (bf16[256,512]{1,0:T(8,128)(2,1)}, bf16[256,512]{1,0:T(8,128)(2,1)S(1)}, u32[]{:S(2)}, u32[]{:S(2)}) collective-permute-start(bf16[256,512]{1,0:T(8,128)(2,1)} %param.18), channel_id=1, source_target_pairs={{0,3},{1,4},{2,5},{3,6},{4,7},{5,8},{6,9},{7,10},{8,11},{9,12},{10... | collective-permute-start | bytes 786440 | tf_op jit(solution)/shard_map/ppermute | solution.py:19
  39.2 16.6 %copy-start.4 = (bf16[256,512]{1,0:T(8,128)(2,1)S(1)}, bf16[256,512]{1,0:T(8,128)(2,1)}, u32[]{:S(2)}) copy-start(bf16[256,512]{1,0:T(8,128)(2,1)} %param.18) | copy-start | bytes 786436
  39.2 15.1 %collective-permute-start.2 = (bf16[256,512]{1,0:T(8,128)(2,1)}, bf16[256,512]{1,0:T(8,128)(2,1)S(1)}, u32[]{:S(2)}, u32[]{:S(2)}) collective-permute-start(bf16[256,512]{1,0:T(8,128)(2,1)} %param.18), channel_id=1, source_target_pairs={{0,2},{1,3},{2,4},{3,5},{4,6},{5,7},{6,8},{7,9},{8,10},{9,11},{10,... | collective-permute-start | bytes 786440 | tf_op jit(solution)/shard_map/ppermute | solution.py:19
  44.2 10.8 %collective-permute-start.3 = (bf16[256,512]{1,0:T(8,128)(2,1)}, bf16[256,512]{1,0:T(8,128)(2,1)S(1)}, u32[]{:S(2)}, u32[]{:S(2)}) collective-permute-start(bf16[256,512]{1,0:T(8,128)(2,1)} %param.18), channel_id=1, source_target_pairs={{0,1},{1,2},{2,3},{3,4},{4,5},{5,6},{6,7},{7,8},{8,9},{9,10},{10,1... | collective-permute-start | bytes 786440 | tf_op jit(solution)/shard_map/ppermute | solution.py:19
  51.6 4.1 copy-start.6
  54.3 4.6 %copy-start.14 = (bf16[256,512]{1,0:T(8,128)(2,1)S(1)}, bf16[256,512]{1,0:T(8,128)(2,1)}, u32[]{:S(2)}) copy-start(bf16[256,512]{1,0:T(8,128)(2,1)} %param.16) | copy-start | bytes 786436
  70.5 299.7 %reduce-scatter.5.cloned.1.call-start = ((), (), s32[]{:S(2)}) async-start(), calls=%async_computation.7 | async-start | bytes 15728640 | tf_op jit(solution)/shard_map/reduce_scatter | solution.py:122
  90.4 50.9 %copy-start.9 = (f32[2048]{0:T(1024)S(1)}, f32[2048]{0:T(1024)}, u32[]{:S(2)}) copy-start(f32[2048]{0:T(1024)} %param.21) | copy-start | bytes 24580
  139.9 1.3 copy-start.3
  243.2 5.2 %copy-start.13 = (bf16[1,352,2048]{2,1,0:T(8,128)(2,1)S(1)}, bf16[1,352,2048]{2,1,0:T(8,128)(2,1)}, u32[]{:S(2)}) copy-start(bf16[1,352,2048]{2,1,0:T(8,128)(2,1)} %param.23) | copy-start | bytes 4325380
  254.9 1.3 copy-start.2
  254.9 166.9 %reduce-scatter.3.cloned.1.call-start = ((), (), s32[]{:S(2)}) async-start(), calls=%async_computation.6 | async-start | bytes 2621440 | tf_op jit(solution)/shard_map/reduce_scatter | solution.py:128
  256.5 4.5 %copy-start.12 = (bf16[704,2048]{1,0:T(8,128)(2,1)S(1)}, bf16[704,2048]{1,0:T(8,128)(2,1)}, u32[]{:S(2)}) copy-start(bf16[704,2048]{1,0:T(8,128)(2,1)} %param.25) | copy-start | bytes 8650756
  273.6 99.8 %all-to-all-start.2 = ((bf16[128,1,2,2,4,128]{5,4,3,2,1,0:T(4,128)(2,1)}), bf16[128,1,2,2,4,128]{5,4,3,2,1,0:T(4,128)(2,1)S(1)}, u32[]{:S(2)}, u32[]{:S(2)}) async-start(bf16[128,1,2,2,4,128]{5,4,3,2,1,0:T(4,128)(2,1)} %copy.93), calls=%async_computation.4 | async-start | bytes 1048576 | tf_op jit(solution)/shard_map/all_to_all | solution.py:171
  373.4 9.6 %copy-start.11 = (f32[256,4]{0,1:T(4,128)S(1)}, f32[256,4]{0,1:T(4,128)}, u32[]{:S(2)}) copy-start(f32[256,4]{0,1:T(4,128)} %param.28) | copy-start | bytes 12292
  373.4 33.0 %all-to-all-start.1 = ((bf16[32,48,512]{2,1,0:T(8,128)(2,1)}), bf16[32,48,512]{2,1,0:T(8,128)(2,1)S(1)}, u32[]{:S(2)}, u32[]{:S(2)}) async-start(bf16[32,48,512]{2,1,0:T(8,128)(2,1)} %bitcast.32), calls=%async_computation.3 | async-start | bytes 3145728 | tf_op jit(solution)/shard_map/all_to_all | solution.py:130
  415.8 8.1 %copy-start.1 = (bf16[1,2048,2,352]{1,3,2,0:T(8,128)(2,1)S(1)}, bf16[1,2048,2,352]{1,3,2,0:T(8,128)(2,1)}, u32[]{:S(2)}) copy-start(bf16[1,2048,2,352]{1,3,2,0:T(8,128)(2,1)} %param.22) | copy-start | bytes 8650756
  (4 other events, 3.1 us)
Sparse Core Ops, SparseCore 0:
  70.6 67.0 all-reduce.2
  255.0 115.0 reduce-scatter.4
  372.7 45.8 reduce-scatter.2
where the time goes:
time: 432 us; the launch traced here: 430 us
  waiting for transfers between devices  163 us (38%)
  blocking collectives  83.3 us (19%)
  local copies, waits for them, and re-layouts  62.6 us (14%)
  starting transfers between devices  48.2 us (11%)
  matrix products  30.5 us (7%)
  other arithmetic  28.8 us (7%)
  between operations  14.3 us (3%)
    reduce_scatter x1, waiting for transfers between devices, per_device(): lax.psum_scatter(partial_value.reshape(EXPERTS * CAP, model_width), 'head...  91.5 us
    all_to_all x1, blocking collectives, per_device(): lax.all_to_all(outgoing, 'tok', split_axis=0, concat_axis=0, tiled=True)  83.3 us
    psum x1, waiting for transfers between devices, per_device(): total = lax.psum(projected, 'head')  47.3 us
    ppermute x8, starting transfers between devices, from_behind(): lax.ppermute(value, axis, [(source, source + steps) for source in range(l...  33.5 us
    all_to_all x1, waiting for transfers between devices, per_device(): lax.all_to_all(slot_cols.reshape(tok_count, local_experts * CAP, column_w...  19.7 us
    gather x1, local copies, waits for them, and re-layouts, per_device(): normed[source_row]  14.1 us
    unnamed x42, local copies, waits for them, and re-layouts  11.6 us
    all_to_all x1, starting transfers between devices, per_device(): lax.all_to_all(slot_cols.reshape(tok_count, local_experts * CAP, column_w...  9.54 us
  transfers between devices with their start and end apart: 13, of which 4 were waited for; matrix products, arithmetic and copies ran while one was open for 16% of the time, Pallas kernels for 0%

commit v1 on v0

v1 whole, which is shorter than its diff:
```python
import math

import jax
import jax.numpy as jnp
from jax import lax
from jax.experimental import pallas as pl
from jax.experimental.pallas import tpu as pltpu
from jax.sharding import PartitionSpec as P

HD = 128
TOP = 4
EXPERTS = 32
PAGE = 8
CAP = 48
ROW = 4
CORES = 2
CHIPS = 2
BF = jnp.bfloat16
F32 = jnp.float32
BOTH = ("head", "tok")
INTRA = [(0, 1), (1, 0), (2, 3), (3, 2)]
CROSS = [(0, 2), (2, 0), (1, 3), (3, 1)]


def attention_kernel(ids_col, ids_row, own, past, out):
    block = out.shape[2] * 2
    scale = 1.0 / math.sqrt(HD)
    span = ROW * block
    row_pos = lax.broadcasted_iota(jnp.int32, (block, block), 0)
    col_pos = lax.broadcasted_iota(jnp.int32, (block, block), 1)
    causal = col_pos <= row_pos
    for y in range(ROW):
        query = own[y, :, 0:HD]
        query_ids = ids_col[pl.ds(y * block, block), 0:1]
        pieces = []
        for b in range(y, ROW):
            key = past[b, :, 0:HD]
            key_ids = ids_row[0:1, pl.ds(b * block, block)]
            score = lax.dot_general(
                query, key, (((1,), (1,)), ((), ())), preferred_element_type=F32
            )
            pieces.append(jnp.where(query_ids == key_ids, score * scale, -1e30))
        for b in range(y + 1):
            key = own[b, :, HD : 2 * HD]
            key_ids = ids_row[0:1, pl.ds(span + b * block, block)]
            score = lax.dot_general(
                query, key, (((1,), (1,)), ((), ())), preferred_element_type=F32
            )
            allowed = query_ids == key_ids
            if b == y:
                allowed = allowed & causal
            pieces.append(jnp.where(allowed, score * scale, -1e30))
        top = pieces[0].max(-1, keepdims=True)
        for piece in pieces[1:]:
            top = jnp.maximum(top, piece.max(-1, keepdims=True))
        weights = [jnp.exp(piece - top) for piece in pieces]
        total = weights[0].sum(-1, keepdims=True)
        for weight in weights[1:]:
            total = total + weight.sum(-1, keepdims=True)
        inverse = 1.0 / total
        mixed = jnp.zeros((block, HD), F32)
        index = 0
        for b in range(y, ROW):
            prob = (weights[index] * inverse).astype(BF)
            mixed += jnp.dot(prob, past[b, :, HD : 2 * HD], preferred_element_type=F32)
            index += 1
        for b in range(y + 1):
            prob = (weights[index] * inverse).astype(BF)
            mixed += jnp.dot(prob, own[b, :, 2 * HD : 3 * HD], preferred_element_type=F32)
            index += 1
        half = block // 2
        out[0, y] = mixed[:half].astype(BF)
        out[1, y] = mixed[half:].astype(BF)


def attention(ids_col, ids_row, own, past):
    block = own.shape[1]
    return pl.pallas_call(
        attention_kernel,
        out_shape=jax.ShapeDtypeStruct((2, ROW, block // 2, HD), BF),
        in_specs=[pl.BlockSpec(memory_space=pltpu.VMEM)] * 4,
        out_specs=pl.BlockSpec(memory_space=pltpu.VMEM),
        compiler_params=pltpu.CompilerParams(vmem_limit_bytes=48 << 20),
        cost_estimate=pl.CostEstimate(
            flops=4 * 5 * ROW * block * block * HD,
            bytes_accessed=6 << 20,
            transcendentals=5 * ROW * block * block,
        ),
        name="row_attention",
    )(ids_col, ids_row, own, past)


def page_copy(keys, values, page_slots, tok_rows, tok_count, head_count, tok_index, heads_here):
    pages_here = tok_rows // PAGE
    quarter_page = PAGE // head_count
    width = heads_here * HD
    slots_all = page_slots.reshape(tok_count, pages_here)
    owner_all = slots_all // pages_here
    mine = lax.dynamic_index_in_dim(owner_all, tok_index, 0, keepdims=False)
    pick = (jnp.arange(tok_count, dtype=jnp.int32)[:, None] == mine[None, :]).astype(BF)
    kv = jnp.stack(
        [
            keys.reshape(pages_here, head_count, quarter_page, width),
            values.reshape(pages_here, head_count, quarter_page, width),
        ],
        3,
    )
    spread = jnp.einsum("op,phqsw->hoqsw", pick, kv, preferred_element_type=F32).astype(BF)
    spread = spread.reshape(head_count * tok_count, quarter_page * 2, width)
    landed = lax.all_to_all(spread, BOTH, split_axis=0, concat_axis=0, tiled=True)
    arrival = jnp.sum(jnp.where(owner_all == tok_index, slots_all % pages_here, 0), 1)
    place = (jnp.arange(pages_here, dtype=jnp.int32)[:, None] == arrival[None, :]).astype(BF)
    landed = landed.reshape(head_count, tok_count, quarter_page, 2, width)
    cache = jnp.einsum("ro,hoqsw->rqshw", place, landed, preferred_element_type=F32).astype(BF)
    return cache.reshape(pages_here, quarter_page, 2 * head_count * width)


def per_device(
    hidden_in,
    queries,
    keys,
    values,
    request_ids,
    out_proj,
    norm_gain,
    expert_gate_up,
    expert_down,
    shared_gate_up,
    shared_down,
    shared_gate,
    routes,
    route_weights,
    page_slots,
):
    tok_rows, model_width = hidden_in.shape
    head_width = queries.shape[1]
    heads_here = head_width // HD
    tok_count = lax.axis_size("tok")
    head_count = lax.axis_size("head")
    tok_index = lax.axis_index("tok")
    head_index = lax.axis_index("head")
    core = head_index % CORES
    column_width = model_width // head_count
    rows_of_blocks = tok_count // ROW
    half = tok_rows // 2
    slots_core = CAP // CORES

    gate_up_own = jnp.transpose(expert_gate_up[0], (1, 2, 0))
    down_own = expert_down[0]
    out_peer = lax.ppermute(out_proj, "head", INTRA)
    gate_up_peer = lax.ppermute(gate_up_own, "head", INTRA)
    down_peer = lax.ppermute(down_own, "head", INTRA)

    packed = jnp.stack(
        [
            jnp.concatenate(
                [part[:, i * HD : (i + 1) * HD] for part in (queries, keys, values)], 1
            )
            for i in range(heads_here)
        ],
        0,
    )
    row_groups = [[r * ROW + y for y in range(ROW)] for r in range(rows_of_blocks)]
    own = lax.all_to_all(
        packed, "tok", split_axis=0, concat_axis=0, tiled=True, axis_index_groups=row_groups
    )
    past = lax.ppermute(
        own[:, :, HD:], "tok", [(s, s + ROW) for s in range(tok_count - ROW)]
    )
    span = ROW * tok_rows
    base = (tok_index // ROW) * span
    padded_ids = jnp.concatenate([jnp.full((span,), -1, jnp.int32), request_ids], 0)
    window_ids = lax.dynamic_slice_in_dim(padded_ids, base, 2 * span, 0)
    ids_row = window_ids[None, :]
    ids_col = jnp.broadcast_to(window_ids[span:, None], (span, HD))
    attended = attention(ids_col, ids_row, own, past)

    core_groups = [
        [
            (chip * CORES + c) * tok_count + r * ROW + y
            for c in range(CORES)
            for y in range(ROW)
        ]
        for chip in range(CHIPS)
        for r in range(rows_of_blocks)
    ]
    gathered = lax.all_to_all(
        attended.reshape(CORES * ROW, half, HD),
        BOTH,
        split_axis=0,
        concat_axis=0,
        tiled=True,
        axis_index_groups=core_groups,
    ).reshape(CORES, ROW, half, HD)
    att_own = lax.dynamic_index_in_dim(gathered, core, 0, keepdims=False)
    att_peer = lax.dynamic_index_in_dim(gathered, 1 - core, 0, keepdims=False)
    att = jnp.concatenate([att_own[y] for y in range(ROW)] + [att_peer[y] for y in range(ROW)], 1)
    projected = jnp.dot(att[:, :head_width], out_proj, preferred_element_type=F32) + jnp.dot(
        att[:, head_width:], out_peer, preferred_element_type=F32
    )
    projected_far = lax.ppermute(projected.astype(BF), "head", CROSS)
    hidden_half = lax.dynamic_slice_in_dim(hidden_in, core * half, half, 0)
    resid = hidden_half.astype(F32) + (projected + projected_far.astype(F32))
    mean_square = jnp.mean(resid * resid, axis=-1, keepdims=True)
    normed_own = (resid * lax.rsqrt(mean_square + 1e-06) * norm_gain).astype(BF)
    normed_peer = lax.ppermute(normed_own, "head", INTRA)

    expert_ids = jnp.arange(EXPERTS, dtype=jnp.int32)
    named = routes[:, :, None] == expert_ids[None, None, :]
    onehot = jnp.sum(named.astype(F32), 1)
    weight_of = jnp.sum(jnp.where(named, route_weights[:, :, None], 0.0), 1)
    earlier = (
        jnp.arange(tok_rows, dtype=jnp.int32)[None, :] < jnp.arange(tok_rows, dtype=jnp.int32)[:, None]
    ).astype(BF)
    rank = jnp.dot(earlier, onehot.astype(BF), preferred_element_type=F32).astype(jnp.int32)
    rank_t = jnp.where(onehot > 0, rank, -1).T
    weight_t = weight_of.T
    rank_rel = jnp.where(core == 0, rank_t, jnp.roll(rank_t, half, 1))
    place = jnp.arange(slots_core, dtype=jnp.int32) * CORES
    select = (rank_rel[:, None, :] == (place + core)[None, :, None]).astype(BF)
    select = select.reshape(EXPERTS * slots_core, tok_rows)
    normed_rel = jnp.concatenate([normed_own, normed_peer], 0)
    outgoing = jnp.dot(select, normed_rel, preferred_element_type=F32).astype(BF)
    arrived = lax.all_to_all(
        outgoing.reshape(tok_count, slots_core, model_width),
        "tok",
        split_axis=0,
        concat_axis=0,
        tiled=True,
    ).reshape(tok_count * slots_core, model_width)

    normed_abs = jnp.where(
        core == 0, normed_rel, jnp.concatenate([normed_peer, normed_own], 0)
    )
    shared_both = jnp.einsum("td,dgf->tgf", normed_abs, shared_gate_up, preferred_element_type=F32)
    shared_act = (jax.nn.silu(shared_both[:, 0, :]) * shared_both[:, 1, :]).astype(BF)
    shared_scale = jax.nn.sigmoid(jnp.dot(normed_abs, shared_gate, preferred_element_type=F32))
    shared_term = shared_scale[:, None] * jnp.dot(
        shared_act, shared_down, preferred_element_type=F32
    )
    shared_cols = lax.psum_scatter(
        shared_term.astype(BF), "head", scatter_dimension=1, tiled=True
    ).astype(F32)

    def expert(gate_up, down):
        gate = lax.dot_general(
            arrived, gate_up[0], (((1,), (1,)), ((), ())), preferred_element_type=F32
        )
        up = lax.dot_general(
            arrived, gate_up[1], (((1,), (1,)), ((), ())), preferred_element_type=F32
        )
        active = (jax.nn.silu(gate) * up).astype(BF)
        return jnp.dot(active, down, preferred_element_type=F32)

    partial = (expert(gate_up_own, down_own) + expert(gate_up_peer, down_peer)).astype(BF)
    partial = partial.reshape(tok_count, slots_core, head_count, column_width)
    partial = jnp.transpose(partial, (2, 0, 1, 3)).reshape(
        head_count * tok_count, slots_core, column_width
    )
    returned = lax.all_to_all(partial, BOTH, split_axis=0, concat_axis=0, tiled=True)
    returned = returned.reshape(CHIPS, CORES * EXPERTS * slots_core, column_width)

    wanted = place[None, :] + jnp.arange(CORES, dtype=jnp.int32)[:, None]
    spread = jnp.where(
        rank_t[None, :, None, :] == wanted[:, None, :, None], weight_t[None, :, None, :], 0.0
    ).reshape(CORES * EXPERTS * slots_core, tok_rows)
    high = spread.astype(BF)
    low = (spread - high.astype(F32)).astype(BF)
    contract = (((0,), (0,)), ((), ()))
    moe_cols = sum(
        lax.dot_general(side, returned[chip], contract, preferred_element_type=F32)
        for chip in range(CHIPS)
        for side in (high, low)
    )

    own_cols = lax.dynamic_slice_in_dim(resid, head_index * column_width, column_width, 1)
    peer_cols = lax.dynamic_slice_in_dim(
        resid, (head_index + 1 - 2 * core) * column_width, column_width, 1
    )
    from_peer = lax.ppermute(peer_cols, "head", INTRA)
    resid_cols = jnp.where(
        core == 0,
        jnp.concatenate([own_cols, from_peer], 0),
        jnp.concatenate([from_peer, own_cols], 0),
    )
    layer_out = (resid_cols + shared_cols + moe_cols).astype(BF)
    decode_cache = page_copy(
        keys, values, page_slots, tok_rows, tok_count, head_count, tok_index, heads_here
    )
    return (layer_out, decode_cache)


def solution(mesh):
    in_specs = (
        P("tok", None),
        P("tok", "head"),
        P("tok", "head"),
        P("tok", "head"),
        P(),
        P("head", None),
        P(),
        P("tok", None, None, "head"),
        P("tok", "head", None),
        P(None, None, "head"),
        P("head", None),
        P(),
        P("tok", None),
        P("tok", None),
        P(),
    )
    out_specs = (P("tok", "head"), P("tok", "head", None))
    return jax.shard_map(
        per_device, mesh=mesh, in_specs=in_specs, out_specs=out_specs, check_vma=False
    )
```

time: 432 us -> 259 us (0.60)
  waiting for transfers between devices: 163 us -> 90.4 us
  blocking collectives: 83.3 us -> 17.2 us
  local copies, waits for them, and re-layouts: 62.6 us -> 33.5 us
  other arithmetic: 28.8 us -> 4.97 us
  matrix products: 30.5 us -> 53.1 us
  starting transfers between devices: 48.2 us -> 39.6 us
    reduce_scatter x2 -> x1, waiting for transfers between devices: 91.5 us -> 0.02 us  [per_device(): lax.psum_scatter(shared_term.astype(BF), 'head', scatter_dimension=1, til...]
    all_to_all x1, blocking collectives: 83.3 us -> 17.2 us  [per_device(): lax.all_to_all(packed, 'tok', split_axis=0, concat_axis=0, tiled=True, ax...]
    psum x1 -> x0, waiting for transfers between devices: 47.3 us -> none  [per_device(): total = lax.psum(projected, 'head')]
    all_to_all x2 -> x4, waiting for transfers between devices: 19.7 us -> 64.9 us  [the longest x1 32.5 us: per_device(): lax.all_to_all(outgoing.reshape(tok_count, slots_core, model_width), 'tok...]
    dot_general x7 -> x17, matrix products: 27 us -> 53.1 us  [the longest x2 19.8 us: expert(): return jnp.dot(active, down, preferred_element_type=F32)]
    ppermute x8 -> x7, starting transfers between devices: 33.5 us -> 7.58 us  [the longest x1 5.8 us: per_device(): lax.ppermute(own[:, :, HD:], 'tok', [(s, s + ROW) for s in range(tok_coun...]
    gather x4 -> x0, local copies, waits for them, and re-layouts: 24.7 us -> none  [the longest x1 14.1 us: per_device(): normed[source_row]]
    ppermute x8 -> x7, waiting for transfers between devices: 4.11 us -> 25.5 us  [the longest x1 12.9 us: per_device(): projected_far = lax.ppermute(projected.astype(BF), 'head', CROSS)]
  transfers between devices with their start and end apart: 13 -> 12, of which waited for: 4 -> 6; matrix products, arithmetic and copies ran while one was open for 16% -> 29% of each run, Pallas kernels for 0% -> 2%
where the time goes in v1:
time: 259 us; the launch traced here: 257 us
  waiting for transfers between devices  90.4 us (35%)
  matrix products  53.1 us (21%)
  starting transfers between devices  39.6 us (15%)
  local copies, waits for them, and re-layouts  33.5 us (13%)
  blocking collectives  17.2 us (7%)
  between operations  14.6 us (6%)
  other arithmetic  4.97 us (2%)
  Pallas kernels  3.93 us (2%)
    all_to_all x1, waiting for transfers between devices, per_device(): lax.all_to_all(outgoing.reshape(tok_count, slots_core, model_width), 'tok...  32.5 us
    all_to_all x1, waiting for transfers between devices, per_device(): lax.all_to_all(partial, BOTH, split_axis=0, concat_axis=0, tiled=True)  25.6 us
    dot_general x2, matrix products, expert(): return jnp.dot(active, down, preferred_element_type=F32)  19.8 us
    all_to_all x1, blocking collectives, per_device(): lax.all_to_all(packed, 'tok', split_axis=0, concat_axis=0, tiled=True, ax...  17.2 us
    ppermute x1, waiting for transfers between devices, per_device(): projected_far = lax.ppermute(projected.astype(BF), 'head', CROSS)  12.9 us
    ppermute x1, waiting for transfers between devices, per_device(): lax.ppermute(own[:, :, HD:], 'tok', [(s, s + ROW) for s in range(tok_coun...  10.9 us
    reshape x2, local copies, waits for them, and re-layouts, per_device(): partial = partial.reshape(tok_count, slots_core, head_count, column_width)  10.3 us
    all_to_all x1, starting transfers between devices, per_device(): lax.all_to_all(partial, BOTH, split_axis=0, concat_axis=0, tiled=True)  9.99 us
  transfers between devices with their start and end apart: 12, of which 6 were waited for; matrix products, arithmetic and copies ran while one was open for 29% of the time, Pallas kernels for 2%

profile of v1, /device:TPU:0, one launch (start us, length us, event | category | flops | bytes accessed | tf_op | source)
XLA Modules:
  0.0 257.2 jit_solution(2477463728016718470)
XLA Ops:
  10.6 17.2 %all_to_all.25.own = bf16[4,256,384]{2,1,0:T(8,128)(2,1)S(1)} all-to-all(bf16[4,256,384]{2,1,0:T(8,128)(2,1)S(1)} %pad_maximum_fusion.1), channel_id=1, replica_groups={{0,1,2,3},{4,5,6,7},{8,9,10,11},{12,13,14,15},{16,17,18,19},{20,21,22,2..., dimensions={0} | all-to-all | bytes 1572864 | tf_op jit(solution)/shard_map/all_to_all | solution.py:164
  29.5 5.8 %collective-permute-start = (bf16[4,256,256]{2,1,0:T(8,128)(2,1)}, bf16[4,256,256]{2,1,0:T(8,128)(2,1)S(1)}, u32[]{:S(2)}, u32[]{:S(2)}) collective-permute-start(bf16[4,256,256]{2,1,0:T(8,128)(2,1)} %slice.146), channel_id=1, source_target_pairs={{0,4},{1,5},{2,6},{3,7},{4,8},{5,9},{6,10},{7,11},{8,12},{9,13},{1... | collective-permute-start | bytes 1572872 | tf_op jit(solution)/shard_map/ppermute | solution.py:167
  35.4 10.9 %collective-permute-done.past = bf16[4,256,256]{2,1,0:T(8,128)(2,1)S(1)} collective-permute-done((bf16[4,256,256]{2,1,0:T(8,128)(2,1)}, bf16[4,256,256]{2,1,0:T(8,128)(2,1)S(1)}, u32[]{:S(2)}, u32[]{:S(2)}) %collective-permute-start) | collective-permute-done | bytes 524320 | tf_op jit(solution)/shard_map/ppermute | solution.py:167
  47.6 3.9 %row_attention.1 = bf16[2,4,128,128]{3,2,1,0:T(8,128)(2,1)} custom-call(s32[1024,128]{1,0:T(8,128)S(1)} %broadcast_in_dim.29.ids_col, s32[1,2048]{1,0:T(1,128)S(1)} %bitcast.122, bf16[4,256,384]{2,1,0:T(8,128)(2,1)S(1)} %copy-done.2, bf16[4,256,256]{2,1,0:T(8,128)(2,1)S(1)} %collective-permute-done.past), custom_call_target="tpu_custom_call" | custom-call | flops 671088640 | bytes 6291456 | tf_op jit(solution)/shard_map/row_attention/pallas_call | solution.py:78
  51.6 3.4 %all-to-all-start.1 = ((bf16[8,128,128]{2,1,0:T(8,128)(2,1)}), bf16[8,128,128]{2,1,0:T(8,128)(2,1)S(1)}, u32[]{:S(2)}, u32[]{:S(2)}) async-start(bf16[8,128,128]{2,1,0:T(8,128)(2,1)} %bitcast.5), calls=%async_computation.1 | async-start | bytes 524288 | tf_op jit(solution)/shard_map/all_to_all | solution.py:187
  55.0 6.8 %all-to-all-done.1 = bf16[8,128,128]{2,1,0:T(8,128)(2,1)S(1)} async-done(((bf16[8,128,128]{2,1,0:T(8,128)(2,1)}), bf16[8,128,128]{2,1,0:T(8,128)(2,1)S(1)}, u32[]{:S(2)}, u32[]{:S(2)}) %all-to-all-start.1) | async-done | bytes 262176 | tf_op jit(solution)/shard_map/all_to_all | solution.py:187
  63.9 3.0 %fusion.75 = (bf16[128,2048]{1,0:T(8,128)(2,1)S(1)}, f32[128,2048]{1,0:T(8,128)}) fusion(f32[128,2048]{1,0:T(8,128)S(1)} %fusion.33, bf16[512,2048]{1,0:T(8,128)(2,1)} %collective-permute-done.1, bf16[128,128]{1,0:T(8,128)(2,1)S(1)} %get-tuple-element.22, bf16[128,128]{1,0:T(8,128)(2,1)S(1)} %get-tuple-element.17, ...), kind=kOutput, calls=%fused_computation.134 | convolution fusion | flops 269484032 | bytes 4849664 | tf_op jit(solution)/shard_map/dot_general | solution.py:198
  68.2 12.9 %collective-permute-done.2 = bf16[128,2048]{1,0:T(8,128)(2,1)} collective-permute-done((bf16[128,2048]{1,0:T(8,128)(2,1)S(1)}, bf16[128,2048]{1,0:T(8,128)(2,1)}, u32[]{:S(2)}, u32[]{:S(2)}) %collective-permute-start.2) | collective-permute-done | bytes 524320 | tf_op jit(solution)/shard_map/ppermute | solution.py:201
  86.1 3.7 %convolution_convert_fusion = bf16[768,2048]{1,0:T(8,128)(2,1)} fusion(pred[768,256]{1,0:T(32,128)(4,1)S(1)} %bitcast_compare_fusion, bf16[128,2048]{1,0:T(8,128)(2,1)} %collective-permute-done.4, bf16[128,2048]{1,0:T(8,128)(2,1)S(1)} %multiply_convert_fusion.1), kind=kOutput, calls=%fused_computation.1 | convolution fusion | flops 808976384 | bytes 4390912 | tf_op jit(solution)/shard_map/dot_general | solution.py:223
  89.8 8.6 %all-to-all-start.2 = ((bf16[32,24,2048]{2,1,0:T(8,128)(2,1)}), bf16[32,24,2048]{2,1,0:T(8,128)(2,1)}, u32[]{:S(2)}, u32[]{:S(2)}) async-start(bf16[32,24,2048]{2,1,0:T(8,128)(2,1)} %bitcast.123), calls=%async_computation.3 | async-start | bytes 6291456 | tf_op jit(solution)/shard_map/all_to_all | solution.py:224
  108.8 32.5 %all-to-all-done.2 = bf16[32,24,2048]{2,1,0:T(8,128)(2,1)} async-done(((bf16[32,24,2048]{2,1,0:T(8,128)(2,1)}), bf16[32,24,2048]{2,1,0:T(8,128)(2,1)}, u32[]{:S(2)}, u32[]{:S(2)}) %all-to-all-start.2) | async-done | bytes 3145760 | tf_op jit(solution)/shard_map/all_to_all | solution.py:224
  141.3 9.7 %all-to-all-start.4 = ((bf16[128,4,512]{2,1,0:T(4,128)(2,1)}), bf16[128,4,512]{2,1,0:T(4,128)(2,1)}, u32[]{:S(2)}, u32[]{:S(2)}) async-start(bf16[128,4,512]{2,1,0:T(4,128)(2,1)} %copy.43), calls=%async_computation.5 | async-start | bytes 1048576 | tf_op jit(solution)/shard_map/all_to_all | solution.py:110
  151.0 4.6 %fusion.5 = f32[768,352]{0,1:T(8,128)} fusion(bf16[768,2048]{1,0:T(8,128)(2,1)} %bitcast.24, bf16[2,352,2048]{2,1,0:T(8,128)(2,1)} %bitcast.140), kind=kOutput, calls=%fused_computation.15 | convolution fusion | flops 1107296256 | bytes 5668864 | tf_op jit(solution)/shard_map/dot_general | solution.py:246
  155.7 4.6 %fusion.2 = f32[768,352]{0,1:T(8,128)} fusion(bf16[768,2048]{1,0:T(8,128)(2,1)} %bitcast.24, bf16[2,352,2048]{2,1,0:T(8,128)(2,1)} %collective-permute-done.5), kind=kOutput, calls=%fused_computation.9 | convolution fusion | flops 1107296256 | bytes 5668864 | tf_op jit(solution)/shard_map/dot_general | solution.py:249
  160.3 9.4 %fusion.10 = f32[768,2048]{1,0:T(8,128)} fusion(bf16[768,2048]{1,0:T(8,128)(2,1)} %bitcast.24, bf16[2,352,2048]{2,1,0:T(8,128)(2,1)} %bitcast.141, f32[768,352]{0,1:T(8,128)} %fusion.5, bf16[1,352,2048]{2,1,0:T(8,128)(2,1)} %param.23), kind=kOutput, calls=%fused_computation.25 | convolution fusion | flops 2216214528 | bytes 13402112 | tf_op jit(solution)/shard_map/dot_general | solution.py:253
  169.7 10.3 %add_convert_fusion = bf16[768,2048]{1,0:T(8,128)(2,1)} fusion(f32[768,2048]{1,0:T(8,128)} %fusion.10, bf16[352,2048]{1,0:T(8,128)(2,1)} %collective-permute-done.6, f32[768,352]{0,1:T(8,128)} %fusion.2, bf16[768,2048]{1,0:T(8,128)(2,1)} %bitcast.24, bf16[2,352,2048]{2,1,0:T(8,128)(2,1)} %collective-permute-done.5), kind=kOutput, calls=%fused_computation | convolution fusion | flops 2219360256 | bytes 16547840 | tf_op jit(solution)/shard_map/dot_general | solution.py:253
  180.1 6.2 %reshape.224 = bf16[32,24,4,512]{3,2,1,0:T(4,128)(2,1)} reshape(bf16[768,2048]{1,0:T(8,128)(2,1)} %add_convert_fusion) | data formatting | bytes 6291456 | tf_op jit(solution)/shard_map/reshape | solution.py:256
  186.2 4.1 %copy.39 = bf16[32,24,4,512]{3,1,0,2:T(8,128)(2,1)} copy(bf16[32,24,4,512]{3,2,1,0:T(4,128)(2,1)} %reshape.224) | data formatting | bytes 6291456 | tf_op jit(solution)/shard_map/reshape | solution.py:256
  190.4 10.0 %all-to-all-start.3 = ((bf16[128,24,512]{2,1,0:T(8,128)(2,1)}), bf16[128,24,512]{2,1,0:T(8,128)(2,1)}, u32[]{:S(2)}, u32[]{:S(2)}) async-start(bf16[128,24,512]{2,1,0:T(8,128)(2,1)} %bitcast.128), calls=%async_computation.4 | async-start | bytes 6291456 | tf_op jit(solution)/shard_map/all_to_all | solution.py:260
  202.4 4.8 %fusion.17 = f32[256,2,704]{0,2,1:T(8,128)S(1)} fusion(bf16[2048,2,704]{0,2,1:T(8,128)(2,1)} %param.24, bf16[128,2048]{1,0:T(8,128)(2,1)S(1)} %multiply_convert_fusion.1, bf16[128,2048]{1,0:T(8,128)(2,1)} %collective-permute-done.4, pred[]{:T(512)S(6)} %eq.112), kind=kOutput, calls=%fused_computation.36 | convolution fusion | flops 1481113600 | bytes 8257537 | tf_op jit(solution)/shard_map/td,dgf->tgf/dot_general | solution.py:235
  207.2 2.0 fusion
  216.3 25.6 %all-to-all-done.3 = bf16[128,24,512]{2,1,0:T(8,128)(2,1)} async-done(((bf16[128,24,512]{2,1,0:T(8,128)(2,1)}), bf16[128,24,512]{2,1,0:T(8,128)(2,1)}, u32[]{:S(2)}, u32[]{:S(2)}) %all-to-all-start.3) | async-done | bytes 3145760 | tf_op jit(solution)/shard_map/all_to_all | solution.py:260
  241.9 2.2 fusion.70
  247.1 3.3 %fusion.25 = bf16[256,512]{1,0:T(8,128)(2,1)} fusion(f32[128,512]{1,0:T(8,128)} %collective-permute-done.3, f32[128,512]{1,0:T(8,128)} %get-tuple-element.14, bf16[256,512]{1,0:T(8,128)(2,1)} %reduce-scatter.2.cloned.1.call-done, pred[]{:T(512)S(6)} %eq.112, f32[256,512]{1,0:T(8,128)S(1)} %convolution_add_fusion.2, bf16[1536,256]{1,0:T(8,128)(2,1)} %bitcast.129, ...), kind=kOutput, calls=%fused_computation.52 | convolution fusion | flops 403701760 | bytes 3932161 | tf_op jit(solution)/shard_map/dot_general | solution.py:271
  (89 shorter events, 36.9 us)
Async XLA Ops:
  7.2 200.0 %copy-start = (bf16[704,2048]{1,0:T(8,128)(2,1)S(1)}, bf16[704,2048]{1,0:T(8,128)(2,1)}, u32[]{:S(2)}) copy-start(bf16[704,2048]{1,0:T(8,128)(2,1)} %param.25) | copy-start | bytes 8650756
  7.2 56.7 %collective-permute-start.1 = (bf16[512,2048]{1,0:T(8,128)(2,1)}, bf16[512,2048]{1,0:T(8,128)(2,1)}, u32[]{:S(2)}, u32[]{:S(2)}) collective-permute-start(bf16[512,2048]{1,0:T(8,128)(2,1)} %param.20), channel_id=1, source_target_pairs={{0,32},{32,0},{64,96},{96,64},{1,33},{33,1},{65,97},{97,65},{2,34}... | collective-permute-start | bytes 6291464 | tf_op jit(solution)/shard_map/ppermute | solution.py:150
  10.5 24.9 %copy-start.7 = (s32[8192]{0:T(1024)S(1)}, s32[8192]{0:T(1024)}, u32[]{:S(2)}) copy-start(s32[8192]{0:T(1024)} %param.19) | copy-start | bytes 98308
  29.5 16.8 %collective-permute-start = (bf16[4,256,256]{2,1,0:T(8,128)(2,1)}, bf16[4,256,256]{2,1,0:T(8,128)(2,1)S(1)}, u32[]{:S(2)}, u32[]{:S(2)}) collective-permute-start(bf16[4,256,256]{2,1,0:T(8,128)(2,1)} %slice.146), channel_id=1, source_target_pairs={{0,4},{1,5},{2,6},{3,7},{4,8},{5,9},{6,10},{7,11},{8,12},{9,13},{1... | collective-permute-start | bytes 1572872 | tf_op jit(solution)/shard_map/ppermute | solution.py:167
  46.5 1.1 copy-start.2
  51.6 10.3 %all-to-all-start.1 = ((bf16[8,128,128]{2,1,0:T(8,128)(2,1)}), bf16[8,128,128]{2,1,0:T(8,128)(2,1)S(1)}, u32[]{:S(2)}, u32[]{:S(2)}) async-start(bf16[8,128,128]{2,1,0:T(8,128)(2,1)} %bitcast.5), calls=%async_computation.1 | async-start | bytes 524288 | tf_op jit(solution)/shard_map/all_to_all | solution.py:187
  63.9 4.1 %copy-start.9 = (s32[256,4]{0,1:T(4,128)S(1)}, s32[256,4]{0,1:T(4,128)}, u32[]{:S(2)}) copy-start(s32[256,4]{0,1:T(4,128)} %param.27) | copy-start | bytes 12292
  63.9 4.1 %copy-start.10 = (f32[256,4]{0,1:T(4,128)S(1)}, f32[256,4]{0,1:T(4,128)}, u32[]{:S(2)}) copy-start(f32[256,4]{0,1:T(4,128)} %param.28) | copy-start | bytes 12292
  67.0 16.9 %copy-start.8 = (f32[2048]{0:T(1024)S(1)}, f32[2048]{0:T(1024)}, u32[]{:S(2)}) copy-start(f32[2048]{0:T(1024)} %param.21) | copy-start | bytes 24580
  67.0 14.1 %collective-permute-start.2 = (bf16[128,2048]{1,0:T(8,128)(2,1)S(1)}, bf16[128,2048]{1,0:T(8,128)(2,1)}, u32[]{:S(2)}, u32[]{:S(2)}) collective-permute-start(bf16[128,2048]{1,0:T(8,128)(2,1)S(1)} %get-tuple-element.40), channel_id=1, source_target_pairs={{0,64},{64,0},{32,96},{96,32},{1,65},{65,1},{33,97},{97,33},{2,66}... | collective-permute-start | bytes 1572872 | tf_op jit(solution)/shard_map/ppermute | solution.py:201
  82.9 1.0 copy-start.6
  84.0 2.1 collective-permute-start.4
  89.8 51.5 %all-to-all-start.2 = ((bf16[32,24,2048]{2,1,0:T(8,128)(2,1)}), bf16[32,24,2048]{2,1,0:T(8,128)(2,1)}, u32[]{:S(2)}, u32[]{:S(2)}) async-start(bf16[32,24,2048]{2,1,0:T(8,128)(2,1)} %bitcast.123), calls=%async_computation.3 | async-start | bytes 6291456 | tf_op jit(solution)/shard_map/all_to_all | solution.py:224
  98.5 7.6 %copy-start.11 = (s32[1024]{0:T(1024)S(1)}, s32[1024]{0:T(1024)}, u32[]{:S(2)}) copy-start(s32[1024]{0:T(1024)} %param.29) | copy-start | bytes 12292
  98.5 57.2 %collective-permute-start.5 = (bf16[2,352,2048]{2,1,0:T(8,128)(2,1)}, bf16[2,352,2048]{2,1,0:T(8,128)(2,1)}, u32[]{:S(2)}, u32[]{:S(2)}) collective-permute-start(bf16[2,352,2048]{2,1,0:T(8,128)(2,1)} %bitcast.139), channel_id=1, source_target_pairs={{0,32},{32,0},{64,96},{96,64},{1,33},{33,1},{65,97},{97,65},{2,34}... | collective-permute-start | bytes 8650760 | tf_op jit(solution)/shard_map/ppermute | solution.py:151
  98.6 71.2 %collective-permute-start.6 = (bf16[352,2048]{1,0:T(8,128)(2,1)}, bf16[352,2048]{1,0:T(8,128)(2,1)}, u32[]{:S(2)}, u32[]{:S(2)}) collective-permute-start(bf16[352,2048]{1,0:T(8,128)(2,1)} %bitcast.142), channel_id=1, source_target_pairs={{0,32},{32,0},{64,96},{96,64},{1,33},{33,1},{65,97},{97,65},{2,34}... | collective-permute-start | bytes 4325384 | tf_op jit(solution)/shard_map/ppermute | solution.py:152
  141.3 49.1 %all-to-all-start.4 = ((bf16[128,4,512]{2,1,0:T(4,128)(2,1)}), bf16[128,4,512]{2,1,0:T(4,128)(2,1)}, u32[]{:S(2)}, u32[]{:S(2)}) async-start(bf16[128,4,512]{2,1,0:T(4,128)(2,1)} %copy.43), calls=%async_computation.5 | async-start | bytes 1048576 | tf_op jit(solution)/shard_map/all_to_all | solution.py:110
  190.4 10.3 %copy-start.12 = (bf16[2048]{0:T(1024)(128)(2,1)S(1)}, bf16[2048]{0:T(1024)(128)(2,1)}, u32[]{:S(2)}) copy-start(bf16[2048]{0:T(1024)(128)(2,1)} %param.26) | copy-start | bytes 12292
  190.4 51.6 %all-to-all-start.3 = ((bf16[128,24,512]{2,1,0:T(8,128)(2,1)}), bf16[128,24,512]{2,1,0:T(8,128)(2,1)}, u32[]{:S(2)}, u32[]{:S(2)}) async-start(bf16[128,24,512]{2,1,0:T(8,128)(2,1)} %bitcast.128), calls=%async_computation.4 | async-start | bytes 6291456 | tf_op jit(solution)/shard_map/all_to_all | solution.py:260
  200.4 46.7 %reduce-scatter.2.cloned.1.call-start = ((), (), s32[]{:S(2)}) async-start(), calls=%async_computation.6 | async-start | bytes 1310720 | tf_op jit(solution)/shard_map/reduce_scatter | solution.py:241
  216.3 30.7 %collective-permute-start.3 = (f32[128,512]{1,0:T(8,128)}, f32[128,512]{1,0:T(8,128)}, u32[]{:S(2)}, u32[]{:S(2)}) collective-permute-start(f32[128,512]{1,0:T(8,128)} %get-tuple-element.15), channel_id=1, source_target_pairs={{0,32},{32,0},{64,96},{96,64},{1,33},{33,1},{65,97},{97,65},{2,34}... | collective-permute-start | bytes 786440 | tf_op jit(solution)/shard_map/ppermute | solution.py:280
  241.9 2.2 copy-start.5
  244.1 2.3 copy-start.3
  244.1 1.7 copy-start.4
  (1 other events, 0.9 us)
Sparse Core Ops, SparseCore 0:
  209.4 37.1 reduce-scatter.1

commit v2 on v1

--- a/solution.py
+++ b/solution.py
@@ -80,7 +80,7 @@
         out_shape=jax.ShapeDtypeStruct((2, ROW, block // 2, HD), BF),
         in_specs=[pl.BlockSpec(memory_space=pltpu.VMEM)] * 4,
         out_specs=pl.BlockSpec(memory_space=pltpu.VMEM),
-        compiler_params=pltpu.CompilerParams(vmem_limit_bytes=48 << 20),
+        compiler_params=pltpu.CompilerParams(vmem_limit_bytes=24 << 20),
         cost_estimate=pl.CostEstimate(
             flops=4 * 5 * ROW * block * block * HD,
             bytes_accessed=6 << 20,
@@ -90,28 +90,227 @@
     )(ids_col, ids_row, own, past)
 
 
-def page_copy(keys, values, page_slots, tok_rows, tok_count, head_count, tok_index, heads_here):
-    pages_here = tok_rows // PAGE
+def project_kernel(core, att, out_own, out_peer, total, total_low):
+    c = core[0]
+    left = jnp.concatenate([att[c, y] for y in range(ROW)], 1)
+    right = jnp.concatenate([att[1 - c, y] for y in range(ROW)], 1)
+    width = total.shape[1]
+    step = width // 4
+    for i in range(4):
+        cols = pl.ds(i * step, step)
+        part = jnp.dot(left, out_own[:, cols], preferred_element_type=F32) + jnp.dot(
+            right, out_peer[:, cols], preferred_element_type=F32
+        )
+        total[:, cols] = part
+        total_low[:, cols] = part.astype(BF)
+
+
+def project(core, att, out_own, out_peer):
+    rows = att.shape[2]
+    depth, width = out_own.shape
+    vmem = pl.BlockSpec(memory_space=pltpu.VMEM)
+    return pl.pallas_call(
+        project_kernel,
+        out_shape=(
+            jax.ShapeDtypeStruct((rows, width), F32),
+            jax.ShapeDtypeStruct((rows, width), BF),
+        ),
+        in_specs=[pl.BlockSpec(memory_space=pltpu.SMEM), vmem, vmem, vmem],
+        out_specs=(vmem, vmem),
+        compiler_params=pltpu.CompilerParams(vmem_limit_bytes=24 << 20),
+        cost_estimate=pl.CostEstimate(
+            flops=4 * rows * depth * width, bytes_accessed=6 << 20, transcendentals=0
+        ),
+        name="project",
+    )(core, att, out_own, out_peer)
+
+
+def norm_kernel(core, hidden, near, far, gain, resid, normed):
+    rows = near.shape[0]
+    start = pl.multiple_of(core[0] * rows, rows)
+    block = rows // 4
+    for i in range(4):
+        here = pl.ds(i * block, block)
+        value = hidden[pl.ds(start + i * block, block), :].astype(F32) + (
+            near[here, :] + far[here, :].astype(F32)
+        )
+        resid[here, :] = value
+        mean_square = jnp.mean(value * value, axis=-1, keepdims=True)
+        normed[here, :] = (value * lax.rsqrt(mean_square + 1e-06) * gain[...]).astype(BF)
+
+
+def add_and_norm(core, hidden, near, far, gain):
+    rows, width = near.shape
+    vmem = pl.BlockSpec(memory_space=pltpu.VMEM)
+    return pl.pallas_call(
+        norm_kernel,
+        out_shape=(
+            jax.ShapeDtypeStruct((rows, width), F32),
+            jax.ShapeDtypeStruct((rows, width), BF),
+        ),
+        in_specs=[pl.BlockSpec(memory_space=pltpu.SMEM), vmem, vmem, vmem, vmem],
+        out_specs=(vmem, vmem),
+        compiler_params=pltpu.CompilerParams(vmem_limit_bytes=16 << 20),
+        cost_estimate=pl.CostEstimate(
+            flops=8 * rows * width, bytes_accessed=4 << 20, transcendentals=rows
+        ),
+        name="add_and_norm",
+    )(core, hidden, near, far, gain)
+
+
+def expert_kernel(
+    x_hbm, both_own, both_peer, down_own, down_peer, out_hbm, x, gate, up, down, act, out, sems, out_sems
+):
+    hidden = both_own.shape[1]
+    rows = x.shape[0]
+    groups, _, width = out.shape
+    block = rows // 2
+    first = pl.ds(0, hidden)
+    second = pl.ds(hidden, hidden)
+    copies = [
+        pltpu.make_async_copy(x_hbm, x, sems.at[0]),
+        pltpu.make_async_copy(both_own.at[0], gate.at[first], sems.at[1]),
+        pltpu.make_async_copy(both_peer.at[0], gate.at[second], sems.at[2]),
+        pltpu.make_async_copy(both_own.at[1], up.at[first], sems.at[3]),
+        pltpu.make_async_copy(both_peer.at[1], up.at[second], sems.at[4]),
+        pltpu.make_async_copy(down_own, down.at[first], sems.at[5]),
+        pltpu.make_async_copy(down_peer, down.at[second], sems.at[6]),
+    ]
+    for copy in copies:
+        copy.start()
+    for copy in copies[:5]:
+        copy.wait()
+
+    @pl.loop(0, 2)
+    def _(m):
+        here = pl.ds(pl.multiple_of(m * block, block), block)
+        left = x[here, :]
+        contract = (((1,), (1,)), ((), ()))
+        g = lax.dot_general(left, gate[...], contract, preferred_element_type=F32)
+        u = lax.dot_general(left, up[...], contract, preferred_element_type=F32)
+        act[here, :] = (g / (1.0 + jnp.exp(-g)) * u).astype(BF)
+
+    for copy in copies[5:]:
+        copy.wait()
+
+    @pl.loop(0, 2)
+    def _(m):
+        here = pl.ds(pl.multiple_of(m * block, block), block)
+        left = act[here, :]
+        for i in range(groups):
+            result = jnp.dot(
+                left, down[:, i * width : (i + 1) * width], preferred_element_type=F32
+            )
+            out[i, here, :] = result.astype(BF)
+            pltpu.make_async_copy(
+                out.at[i, here], out_hbm.at[i, here], out_sems.at[m, i]
+            ).start()
+
+    for m in range(2):
+        here = pl.ds(m * block, block)
+        for i in range(groups):
+            pltpu.make_async_copy(
+                out.at[i, here], out_hbm.at[i, here], out_sems.at[m, i]
+            ).wait()
+
+
+def experts(x, both_own, both_peer, down_own, down_peer, groups):
+    rows, depth = x.shape
+    hidden, width = down_own.shape
+    column_width = width // groups
+    anywhere = pl.BlockSpec(memory_space=pltpu.HBM)
+    return pl.pallas_call(
+        expert_kernel,
+        out_shape=jax.ShapeDtypeStruct((groups, rows, column_width), BF),
+        in_specs=[anywhere] * 5,
+        out_specs=anywhere,
+        scratch_shapes=[
+            pltpu.VMEM((rows, depth), BF),
+            pltpu.VMEM((2 * hidden, depth), BF),
+            pltpu.VMEM((2 * hidden, depth), BF),
+            pltpu.VMEM((2 * hidden, width), BF),
+            pltpu.VMEM((rows, 2 * hidden), BF),
+            pltpu.VMEM((groups, rows, column_width), BF),
+            pltpu.SemaphoreType.DMA((7,)),
+            pltpu.SemaphoreType.DMA((2, groups)),
+        ],
+        compiler_params=pltpu.CompilerParams(vmem_limit_bytes=28 << 20),
+        cost_estimate=pl.CostEstimate(
+            flops=12 * rows * depth * hidden,
+            bytes_accessed=15 << 20,
+            transcendentals=2 * rows * hidden,
+        ),
+        name="experts",
+    )(x, both_own, both_peer, down_own, down_peer)
+
+
+def combine_kernel(core, high, low, returned, mine, peers, shared, out):
+    rows = mine.shape[0]
+    sides = (high, low)
+    total = shared[...]
+    for chip in range(returned.shape[0]):
+        for side in sides:
+            total += jnp.dot(side[...], returned[chip], preferred_element_type=F32)
+    first = core[0] == 0
+    low_half = jnp.where(first, mine[...], peers[...])
+    high_half = jnp.where(first, peers[...], mine[...])
+    out[0:rows, :] = (total[0:rows] + low_half).astype(BF)
+    out[rows : 2 * rows, :] = (total[rows:] + high_half).astype(BF)
+
+
+def combine(core, high, low, returned, mine, peers, shared):
+    vmem = pl.BlockSpec(memory_space=pltpu.VMEM)
+    rows, width = shared.shape
+    return pl.pallas_call(
+        combine_kernel,
+        out_shape=jax.ShapeDtypeStruct((rows, width), BF),
+        in_specs=[pl.BlockSpec(memory_space=pltpu.SMEM)] + [vmem] * 6,
+        out_specs=vmem,
+        compiler_params=pltpu.CompilerParams(vmem_limit_bytes=24 << 20),
+        cost_estimate=pl.CostEstimate(
+            flops=8 * rows * width * high.shape[1], bytes_accessed=7 << 20, transcendentals=0
+        ),
+        name="combine",
+    )(core, high, low, returned, mine, peers, shared)
+
+
+def page_pieces(keys, values, owner_all, tok_count, head_count, tok_index):
+    pages_here = owner_all.shape[1]
+    tok_rows = keys.shape[0]
     quarter_page = PAGE // head_count
-    width = heads_here * HD
-    slots_all = page_slots.reshape(tok_count, pages_here)
-    owner_all = slots_all // pages_here
     mine = lax.dynamic_index_in_dim(owner_all, tok_index, 0, keepdims=False)
-    pick = (jnp.arange(tok_count, dtype=jnp.int32)[:, None] == mine[None, :]).astype(BF)
-    kv = jnp.stack(
-        [
-            keys.reshape(pages_here, head_count, quarter_page, width),
-            values.reshape(pages_here, head_count, quarter_page, width),
-        ],
-        3,
-    )
-    spread = jnp.einsum("op,phqsw->hoqsw", pick, kv, preferred_element_type=F32).astype(BF)
-    spread = spread.reshape(head_count * tok_count, quarter_page * 2, width)
-    landed = lax.all_to_all(spread, BOTH, split_axis=0, concat_axis=0, tiled=True)
+    row = jnp.arange(tok_rows, dtype=jnp.int32)
+    quarter = row // (tok_count * quarter_page)
+    owner = row // quarter_page % tok_count
+    line = quarter * quarter_page + row % quarter_page
+    token_owner = jnp.repeat(mine, PAGE)
+    token_line = jnp.arange(tok_rows, dtype=jnp.int32) % PAGE
+    pick = (
+        (owner[:, None] == token_owner[None, :]) & (line[:, None] == token_line[None, :])
+    ).astype(BF)
+    parts = [
+        jnp.dot(pick, part, preferred_element_type=F32).astype(BF) for part in (keys, values)
+    ]
+    return jnp.concatenate(parts, 1).reshape(head_count * tok_count, quarter_page, -1)
+
+
+def place_pages(landed, slots_all, owner_all, tok_count, head_count, tok_index):
+    pages_here = owner_all.shape[1]
+    quarter_page = PAGE // head_count
+    rows = pages_here * quarter_page
     arrival = jnp.sum(jnp.where(owner_all == tok_index, slots_all % pages_here, 0), 1)
-    place = (jnp.arange(pages_here, dtype=jnp.int32)[:, None] == arrival[None, :]).astype(BF)
-    landed = landed.reshape(head_count, tok_count, quarter_page, 2, width)
-    cache = jnp.einsum("ro,hoqsw->rqshw", place, landed, preferred_element_type=F32).astype(BF)
+    row = jnp.arange(rows, dtype=jnp.int32)
+    target = jnp.repeat(arrival, quarter_page) * quarter_page + row % quarter_page
+    place = (row[:, None] == target[None, :]).astype(BF)
+    landed = landed.reshape(head_count, rows, -1)
+    width = landed.shape[2] // 2
+    placed = [
+        jnp.dot(place, landed[h], preferred_element_type=F32).astype(BF)
+        for h in range(head_count)
+    ]
+    cache = jnp.concatenate(
+        [p[:, :width] for p in placed] + [p[:, width:] for p in placed], 1
+    )
     return cache.reshape(pages_here, quarter_page, 2 * head_count * width)
 
 
@@ -164,6 +363,11 @@
     own = lax.all_to_all(
         packed, "tok", split_axis=0, concat_axis=0, tiled=True, axis_index_groups=row_groups
     )
+    slots_all = page_slots.reshape(tok_count, tok_rows // PAGE)
+    owner_all = slots_all // (tok_rows // PAGE)
+    pieces = page_pieces(keys, values, owner_all, tok_count, head_count, tok_index)
+    pieces, own = lax.optimization_barrier((pieces, own))
+    landed = lax.all_to_all(pieces, BOTH, split_axis=0, concat_axis=0, tiled=True)
     past = lax.ppermute(
         own[:, :, HD:], "tok", [(s, s + ROW) for s in range(tok_count - ROW)]
     )
@@ -173,6 +377,7 @@
     window_ids = lax.dynamic_slice_in_dim(padded_ids, base, 2 * span, 0)
     ids_row = window_ids[None, :]
     ids_col = jnp.broadcast_to(window_ids[span:, None], (span, HD))
+    past, landed = lax.optimization_barrier((past, landed))
     attended = attention(ids_col, ids_row, own, past)
 
     core_groups = [
@@ -192,17 +397,12 @@
         tiled=True,
         axis_index_groups=core_groups,
     ).reshape(CORES, ROW, half, HD)
-    att_own = lax.dynamic_index_in_dim(gathered, core, 0, keepdims=False)
-    att_peer = lax.dynamic_index_in_dim(gathered, 1 - core, 0, keepdims=False)
-    att = jnp.concatenate([att_own[y] for y in range(ROW)] + [att_peer[y] for y in range(ROW)], 1)
-    projected = jnp.dot(att[:, :head_width], out_proj, preferred_element_type=F32) + jnp.dot(
-        att[:, head_width:], out_peer, preferred_element_type=F32
-    )
-    projected_far = lax.ppermute(projected.astype(BF), "head", CROSS)
-    hidden_half = lax.dynamic_slice_in_dim(hidden_in, core * half, half, 0)
-    resid = hidden_half.astype(F32) + (projected + projected_far.astype(F32))
-    mean_square = jnp.mean(resid * resid, axis=-1, keepdims=True)
-    normed_own = (resid * lax.rsqrt(mean_square + 1e-06) * norm_gain).astype(BF)
+    core_ref = core.reshape(1)
+    projected, projected_low = project(core_ref, gathered, out_proj, out_peer)
+    projected_far = lax.ppermute(projected_low, "head", CROSS)
+    resid, normed_own = add_and_norm(
+        core_ref, hidden_in, projected, projected_far, norm_gain[None, :]
+    )
     normed_peer = lax.ppermute(normed_own, "head", INTRA)
 
     expert_ids = jnp.arange(EXPERTS, dtype=jnp.int32)
@@ -238,25 +438,19 @@
     shared_term = shared_scale[:, None] * jnp.dot(
         shared_act, shared_down, preferred_element_type=F32
     )
-    shared_cols = lax.psum_scatter(
-        shared_term.astype(BF), "head", scatter_dimension=1, tiled=True
-    ).astype(F32)
-
-    def expert(gate_up, down):
-        gate = lax.dot_general(
-            arrived, gate_up[0], (((1,), (1,)), ((), ())), preferred_element_type=F32
-        )
-        up = lax.dot_general(
-            arrived, gate_up[1], (((1,), (1,)), ((), ())), preferred_element_type=F32
-        )
-        active = (jax.nn.silu(gate) * up).astype(BF)
-        return jnp.dot(active, down, preferred_element_type=F32)
-
-    partial = (expert(gate_up_own, down_own) + expert(gate_up_peer, down_peer)).astype(BF)
-    partial = partial.reshape(tok_count, slots_core, head_count, column_width)
-    partial = jnp.transpose(partial, (2, 0, 1, 3)).reshape(
-        head_count * tok_count, slots_core, column_width
-    )
+    chip = head_index // CORES
+    chip_width = CORES * column_width
+    shared_near = lax.dynamic_slice_in_dim(shared_term, chip * chip_width, chip_width, 1)
+    shared_send = lax.dynamic_slice_in_dim(
+        shared_term, (1 - chip) * chip_width, chip_width, 1
+    ).astype(BF)
+    shared_near, shared_send, arrived = lax.optimization_barrier(
+        (shared_near, shared_send, arrived)
+    )
+    shared_far = lax.ppermute(shared_send, "head", CROSS)
+
+    partial = experts(arrived, gate_up_own, gate_up_peer, down_own, down_peer, head_count)
+    partial = partial.reshape(head_count * tok_count, slots_core, column_width)
     returned = lax.all_to_all(partial, BOTH, split_axis=0, concat_axis=0, tiled=True)
     returned = returned.reshape(CHIPS, CORES * EXPERTS * slots_core, column_width)
 
@@ -265,28 +459,21 @@
         rank_t[None, :, None, :] == wanted[:, None, :, None], weight_t[None, :, None, :], 0.0
     ).reshape(CORES * EXPERTS * slots_core, tok_rows)
     high = spread.astype(BF)
-    low = (spread - high.astype(F32)).astype(BF)
-    contract = (((0,), (0,)), ((), ()))
-    moe_cols = sum(
-        lax.dot_general(side, returned[chip], contract, preferred_element_type=F32)
-        for chip in range(CHIPS)
-        for side in (high, low)
-    )
-
+    low = (spread - high.astype(F32)).astype(BF).T
+    high = high.T
+    shared_chip = shared_near + shared_far.astype(F32)
+    shared_own = lax.dynamic_slice_in_dim(shared_chip, core * column_width, column_width, 1)
+    shared_peer = lax.dynamic_slice_in_dim(
+        shared_chip, (1 - core) * column_width, column_width, 1
+    ).astype(BF)
+    shared_cols = shared_own + lax.ppermute(shared_peer, "head", INTRA).astype(F32)
     own_cols = lax.dynamic_slice_in_dim(resid, head_index * column_width, column_width, 1)
     peer_cols = lax.dynamic_slice_in_dim(
         resid, (head_index + 1 - 2 * core) * column_width, column_width, 1
     )
     from_peer = lax.ppermute(peer_cols, "head", INTRA)
-    resid_cols = jnp.where(
-        core == 0,
-        jnp.concatenate([own_cols, from_peer], 0),
-        jnp.concatenate([from_peer, own_cols], 0),
-    )
-    layer_out = (resid_cols + shared_cols + moe_cols).astype(BF)
-    decode_cache = page_copy(
-        keys, values, page_slots, tok_rows, tok_count, head_count, tok_index, heads_here
-    )
+    layer_out = combine(core_ref, high, low, returned, own_cols, from_peer, shared_cols)
+    decode_cache = place_pages(landed, slots_all, owner_all, tok_count, head_count, tok_index)
     return (layer_out, decode_cache)
 
 

time: 259 us -> 233 us (0.90)
  matrix products: 53.1 us -> 16 us
  Pallas kernels: 3.93 us -> 25.9 us
  blocking collectives: 17.2 us -> 0 us
  between operations: 14.6 us -> 1.29 us
  waiting for transfers between devices: 90.4 us -> 98.7 us
  local copies, waits for them, and re-layouts: 33.5 us -> 39.7 us
  other arithmetic: 4.97 us -> 8.12 us
    ppermute x1 -> x3, waiting for transfers between devices: 12.9 us -> 49.9 us  [the longest x1 37.8 us: per_device(): shared_far = lax.ppermute(shared_send, 'head', CROSS)]
    dot_general x12 -> x6, matrix products: 40.8 us -> 5.8 us  [the longest x4 4.54 us: place_pages(): jnp.dot(place, landed[h], preferred_element_type=F32).astype(BF)]
    all_to_all x1, waiting for transfers between devices: 25.6 us -> 0.01 us  [per_device(): lax.all_to_all(partial, BOTH, split_axis=0, concat_axis=0, tiled=True)]
    all_to_all x1 -> x2, waiting for transfers between devices: 0.01 us -> 21.5 us  [the longest x1 13.3 us: per_device(): lax.all_to_all(pieces, BOTH, split_axis=0, concat_axis=0, tiled=True)]
    pallas_call x0 -> x4, Pallas kernels: none -> 20.8 us  [the longest x1 13.5 us: experts(): pl.pallas_call(expert_kernel, out_shape=jax.ShapeDtypeStruct((groups, row...]
    all_to_all x1 -> x0, blocking collectives: 17.2 us -> none  [per_device(): lax.all_to_all(packed, 'tok', split_axis=0, concat_axis=0, tiled=True, ax...]
    ppermute x1, waiting for transfers between devices: 10.9 us -> 0.01 us  [per_device(): lax.ppermute(own[:, :, HD:], 'tok', [(s, s + ROW) for s in range(tok_coun...]
    reshape x4 -> x3, local copies, waits for them, and re-layouts: 11.6 us -> 2.19 us  [the longest x1 1.14 us: place_pages(): return cache.reshape(pages_here, quarter_page, 2 * head_count * width)]
  transfers between devices with their start and end apart: 12 -> 14, of which waited for: 6 -> 6; matrix products, arithmetic and copies ran while one was open for 29% -> 21% of each run, Pallas kernels for 2% -> 3%
where the time goes in v2:
time: 233 us; the launch traced here: 230 us
  waiting for transfers between devices  98.7 us (42%)
  starting transfers between devices  40.4 us (17%)
  local copies, waits for them, and re-layouts  39.7 us (17%)
  Pallas kernels  25.9 us (11%)
  matrix products  16 us (7%)
  other arithmetic  8.12 us (3%)
    ppermute x1, waiting for transfers between devices, per_device(): shared_far = lax.ppermute(shared_send, 'head', CROSS)  37.8 us
    all_to_all x1, waiting for transfers between devices, per_device(): lax.all_to_all(outgoing.reshape(tok_count, slots_core, model_width), 'tok...  25.6 us
    pallas_call x1, Pallas kernels, experts(): pl.pallas_call(expert_kernel, out_shape=jax.ShapeDtypeStruct((groups, row...  13.5 us
    all_to_all x1, waiting for transfers between devices, per_device(): lax.all_to_all(pieces, BOTH, split_axis=0, concat_axis=0, tiled=True)  13.3 us
    ppermute x1, waiting for transfers between devices, per_device(): projected_far = lax.ppermute(projected_low, 'head', CROSS)  12 us
    unnamed x59, local copies, waits for them, and re-layouts  10.8 us
    all_to_all x1, starting transfers between devices, per_device(): lax.all_to_all(partial, BOTH, split_axis=0, concat_axis=0, tiled=True)  9.8 us
    all_to_all x1, waiting for transfers between devices, per_device(): lax.all_to_all(packed, 'tok', split_axis=0, concat_axis=0, tiled=True, ax...  8.16 us
  transfers between devices with their start and end apart: 14, of which 6 were waited for; matrix products, arithmetic and copies ran while one was open for 21% of the time, Pallas kernels for 3%

profile of v2, /device:TPU:0, one launch (start us, length us, event | category | flops | bytes accessed | tf_op | source)
XLA Modules:
  0.0 230.0 jit_solution(14087636514930802341)
XLA Ops:
  4.9 4.7 %all-to-all-start = ((bf16[4,256,384]{2,1,0:T(8,128)(2,1)}), bf16[4,256,384]{2,1,0:T(8,128)(2,1)}, u32[]{:S(2)}, u32[]{:S(2)}) async-start(bf16[4,256,384]{2,1,0:T(8,128)(2,1)} %pad_maximum_fusion), calls=%async_computation | async-start | bytes 1572864 | tf_op jit(solution)/shard_map/all_to_all | solution.py:363
  13.8 8.2 %all-to-all-done.own = bf16[4,256,384]{2,1,0:T(8,128)(2,1)} async-done(((bf16[4,256,384]{2,1,0:T(8,128)(2,1)}), bf16[4,256,384]{2,1,0:T(8,128)(2,1)}, u32[]{:S(2)}, u32[]{:S(2)}) %all-to-all-start) | async-done | bytes 786464 | tf_op jit(solution)/shard_map/all_to_all | solution.py:363
  21.9 1.9 slice.109
  23.8 5.8 %collective-permute-start = (bf16[4,256,256]{2,1,0:T(8,128)(2,1)}, bf16[4,256,256]{2,1,0:T(8,128)(2,1)S(1)}, u32[]{:S(2)}, u32[]{:S(2)}) collective-permute-start(bf16[4,256,256]{2,1,0:T(8,128)(2,1)} %slice.109), channel_id=1, source_target_pairs={{0,4},{1,5},{2,6},{3,7},{4,8},{5,9},{6,10},{7,11},{8,12},{9,13},{1... | collective-permute-start | bytes 1572872 | tf_op jit(solution)/shard_map/ppermute | solution.py:371
  29.6 6.9 %all-to-all-start.1 = ((bf16[128,2,1024]{2,1,0:T(2,128)(2,1)}), bf16[128,2,1024]{2,1,0:T(2,128)(2,1)}, u32[]{:S(2)}, u32[]{:S(2)}) async-start(bf16[128,2,1024]{2,1,0:T(2,128)(2,1)} %reshape.158), calls=%async_computation.1 | async-start | bytes 1048576 | tf_op jit(solution)/shard_map/all_to_all | solution.py:370
  36.7 13.3 %all-to-all-done.1 = bf16[128,2,1024]{2,1,0:T(2,128)(2,1)} async-done(((bf16[128,2,1024]{2,1,0:T(2,128)(2,1)}), bf16[128,2,1024]{2,1,0:T(2,128)(2,1)}, u32[]{:S(2)}, u32[]{:S(2)}) %all-to-all-start.1) | async-done | bytes 524320 | tf_op jit(solution)/shard_map/all_to_all | solution.py:370
  50.3 5.1 %row_attention.1 = bf16[2,4,128,128]{3,2,1,0:T(8,128)(2,1)} custom-call(s32[1024,128]{1,0:T(8,128)S(1)} %broadcast_in_dim.75.ids_col, s32[1,2048]{1,0:T(1,128)S(1)} %bitcast.64, bf16[4,256,384]{2,1,0:T(8,128)(2,1)} %all-to-all-done.own, bf16[4,256,256]{2,1,0:T(8,128)(2,1)S(1)} %collective-permute-done.past), custom_call_target="tpu_custom_call" | custom-call | flops 671088640 | bytes 6291456 | tf_op jit(solution)/shard_map/row_attention/pallas_call | solution.py:78
  55.3 3.4 %all-to-all-start.2 = ((bf16[8,128,128]{2,1,0:T(8,128)(2,1)}), bf16[8,128,128]{2,1,0:T(8,128)(2,1)S(1)}, u32[]{:S(2)}, u32[]{:S(2)}) async-start(bf16[8,128,128]{2,1,0:T(8,128)(2,1)} %bitcast.13), calls=%async_computation.2 | async-start | bytes 524288 | tf_op jit(solution)/shard_map/all_to_all | solution.py:392
  60.1 3.0 %copy.24 = s32[1536,256]{0,1:T(8,128)} copy(s32[1536,256]{1,0:T(8,128)} %bitcast.71) | data formatting | bytes 3145728 | tf_op jit(solution)/shard_map/eq | solution.py:459
  64.4 3.1 %copy.25 = f32[1536,256]{0,1:T(8,128)} copy(f32[1536,256]{1,0:T(8,128)} %bitcast.70) | data formatting | bytes 3145728 | tf_op jit(solution)/shard_map/jit(_where)/broadcast_in_dim | solution.py:458
  69.2 2.5 %project.1 = (f32[128,2048]{1,0:T(8,128)S(1)}, bf16[128,2048]{1,0:T(8,128)(2,1)S(1)}) custom-call(s32[1]{0:T(128)} %bitcast.core, bf16[2,4,128,128]{3,2,1,0:T(8,128)(2,1)S(1)} %bitcast.62, bf16[512,2048]{1,0:T(8,128)(2,1)S(1)} %copy-done.4, bf16[512,2048]{1,0:T(8,128)(2,1)} %collective-permute-done.1.out_peer), custom_call_target="tpu_custom_call" | custom-call | flops 536870912 | bytes 6291456 | tf_op jit(solution)/shard_map/project/pallas_call | solution.py:112
  74.0 12.0 %collective-permute-done.2.far = bf16[128,2048]{1,0:T(8,128)(2,1)S(1)} collective-permute-done((bf16[128,2048]{1,0:T(8,128)(2,1)S(1)}, bf16[128,2048]{1,0:T(8,128)(2,1)S(1)}, u32[]{:S(2)}, u32[]{:S(2)}) %collective-permute-start.2) | collective-permute-done | bytes 524320 | tf_op jit(solution)/shard_map/ppermute | solution.py:402
  90.5 2.7 %convolution_convert_fusion = bf16[768,2048]{1,0:T(8,128)(2,1)} fusion(pred[768,256]{1,0:T(32,128)(4,1)S(1)} %bitcast_compare_fusion, bf16[256,2048]{1,0:T(8,128)(2,1)S(1)} %constant_dynamic-update-slice_fusion), kind=kOutput, calls=%fused_computation | convolution fusion | flops 806879232 | bytes 4390912 | tf_op jit(solution)/shard_map/dot_general | solution.py:423
  93.2 6.6 %all-to-all-start.3 = ((bf16[32,24,2048]{2,1,0:T(8,128)(2,1)}), bf16[32,24,2048]{2,1,0:T(8,128)(2,1)}, u32[]{:S(2)}, u32[]{:S(2)}) async-start(bf16[32,24,2048]{2,1,0:T(8,128)(2,1)} %bitcast.69), calls=%async_computation.3 | async-start | bytes 6291456 | tf_op jit(solution)/shard_map/all_to_all | solution.py:424
  100.1 3.0 %fusion.7.high = bf16[256,1536]{1,0:T(8,128)(2,1)} fusion(f32[1536,256]{0,1:T(8,128)} %copy.25, s32[1536,256]{0,1:T(8,128)} %copy.24, s32[1536]{0:T(1024)S(1)} %eq.120), kind=kLoop, calls=%fused_computation.25 | loop fusion | flops 786432 | bytes 3938304 | tf_op jit(solution)/shard_map/transpose | solution.py:463
  103.1 2.2 fusion.39
  107.2 1.8 fusion.18
  109.0 4.6 %fusion.1 = f32[256,2,704]{0,2,1:T(8,128)S(1)} fusion(bf16[2048,2,704]{0,2,1:T(8,128)(2,1)} %param.24, bf16[256,2048]{1,0:T(8,128)(2,1)S(1)} %copy-done.17, bf16[128,2048]{1,0:T(8,128)(2,1)S(1)} %get-tuple-element.18, bf16[128,2048]{1,0:T(8,128)(2,1)} %collective-permute-done.3, pred[]{:T(512)S(6)} %eq.123), kind=kOutput, calls=%fused_computation.13 | convolution fusion | flops 1479016448 | bytes 9306113 | tf_op jit(solution)/shard_map/td,dgf->tgf/dot_general | solution.py:435
  116.6 25.6 %all-to-all-done.3 = bf16[32,24,2048]{2,1,0:T(8,128)(2,1)} async-done(((bf16[32,24,2048]{2,1,0:T(8,128)(2,1)}), bf16[32,24,2048]{2,1,0:T(8,128)(2,1)}, u32[]{:S(2)}, u32[]{:S(2)}) %all-to-all-start.3) | async-done | bytes 3145760 | tf_op jit(solution)/shard_map/all_to_all | solution.py:424
  142.2 1.8 copy-done.10
  145.4 13.5 %experts.1 = bf16[4,768,512]{2,1,0:T(8,128)(2,1)S(1)} custom-call(bf16[768,2048]{1,0:T(8,128)(2,1)} %bitcast.22.x_hbm, bf16[2,352,2048]{2,1,0:T(8,128)(2,1)S(1)} %bitcast.66, bf16[2,352,2048]{2,1,0:T(8,128)(2,1)} %collective-permute-done.4.both_peer, bf16[352,2048]{1,0:T(8,128)(2,1)S(1)} %bitcast.68, bf16[352,2048]{1,0:T(8,128)(2,1)} %collective-permute-done.5.down_peer), custom_call_target="tpu_custom_call" | custom-call | flops 6643777536 | bytes 15728640 | tf_op jit(solution)/shard_map/experts/pallas_call | solution.py:222
  160.6 9.8 %all-to-all-start.4 = ((bf16[128,24,512]{2,1,0:T(8,128)(2,1)}), bf16[128,24,512]{2,1,0:T(8,128)(2,1)}, u32[]{:S(2)}, u32[]{:S(2)}) async-start(bf16[128,24,512]{2,1,0:T(8,128)(2,1)} %bitcast.61), calls=%async_computation.4 | async-start | bytes 6291456 | tf_op jit(solution)/shard_map/all_to_all | solution.py:454
  179.8 37.8 %collective-permute-done.7 = bf16[256,1024]{1,0:T(8,128)(2,1)S(1)} collective-permute-done((bf16[256,1024]{1,0:T(8,128)(2,1)}, bf16[256,1024]{1,0:T(8,128)(2,1)S(1)}, u32[]{:S(2)}, u32[]{:S(2)}) %collective-permute-start.7) | collective-permute-done | bytes 524320 | tf_op jit(solution)/shard_map/ppermute | solution.py:450
  225.6 4.4 %combine.1 = bf16[256,512]{1,0:T(8,128)(2,1)} custom-call(s32[1]{0:T(128)} %bitcast.core, bf16[256,1536]{1,0:T(8,128)(2,1)S(1)} %copy-done.3, bf16[256,1536]{1,0:T(8,128)(2,1)S(1)} %copy-done.2, bf16[2,1536,512]{2,1,0:T(8,128)(2,1)} %bitcast.28.returned, f32[128,512]{1,0:T(8,128)S(1)} %copy-done.5, f32[128,512]{1,0:T(8,128)} %collective-permute-done.6.peers, ...), custom_call_target="tpu_custom_call" | custom-call | flops 1610612736 | bytes 7340032 | tf_op jit(solution)/shard_map/combine/pallas_call | solution.py:264
  (134 shorter events, 45.2 us)
Async XLA Ops:
  0.6 112.9 %copy-start = (bf16[704,2048]{1,0:T(8,128)(2,1)S(1)}, bf16[704,2048]{1,0:T(8,128)(2,1)}, u32[]{:S(2)}) copy-start(bf16[704,2048]{1,0:T(8,128)(2,1)} %param.25) | copy-start | bytes 8650756
  3.8 7.6 %copy-start.19 = (bf16[256,512]{1,0:T(8,128)(2,1)S(1)}, bf16[256,512]{1,0:T(8,128)(2,1)}, u32[]{:S(2)}) copy-start(bf16[256,512]{1,0:T(8,128)(2,1)} %param.17) | copy-start | bytes 786436
  4.9 8.9 %copy-start.20 = (s32[8192]{0:T(1024)S(1)}, s32[8192]{0:T(1024)}, u32[]{:S(2)}) copy-start(s32[8192]{0:T(1024)} %param.19) | copy-start | bytes 98308
  4.9 17.1 %all-to-all-start = ((bf16[4,256,384]{2,1,0:T(8,128)(2,1)}), bf16[4,256,384]{2,1,0:T(8,128)(2,1)}, u32[]{:S(2)}, u32[]{:S(2)}) async-start(bf16[4,256,384]{2,1,0:T(8,128)(2,1)} %pad_maximum_fusion), calls=%async_computation | async-start | bytes 1572864 | tf_op jit(solution)/shard_map/all_to_all | solution.py:363
  9.6 58.0 %collective-permute-start.1 = (bf16[512,2048]{1,0:T(8,128)(2,1)}, bf16[512,2048]{1,0:T(8,128)(2,1)}, u32[]{:S(2)}, u32[]{:S(2)}) collective-permute-start(bf16[512,2048]{1,0:T(8,128)(2,1)} %out_own.1), channel_id=1, source_target_pairs={{0,32},{32,0},{64,96},{96,64},{1,33},{33,1},{65,97},{97,65},{2,34}... | collective-permute-start | bytes 6291464 | tf_op jit(solution)/shard_map/ppermute | solution.py:349
  9.6 132.6 %collective-permute-start.4 = (bf16[2,352,2048]{2,1,0:T(8,128)(2,1)}, bf16[2,352,2048]{2,1,0:T(8,128)(2,1)}, u32[]{:S(2)}, u32[]{:S(2)}) collective-permute-start(bf16[2,352,2048]{2,1,0:T(8,128)(2,1)} %bitcast.65), channel_id=1, source_target_pairs={{0,32},{32,0},{64,96},{96,64},{1,33},{33,1},{65,97},{97,65},{2,34}... | collective-permute-start | bytes 8650760 | tf_op jit(solution)/shard_map/ppermute | solution.py:350
  10.1 132.1 %collective-permute-start.5 = (bf16[352,2048]{1,0:T(8,128)(2,1)}, bf16[352,2048]{1,0:T(8,128)(2,1)}, u32[]{:S(2)}, u32[]{:S(2)}) collective-permute-start(bf16[352,2048]{1,0:T(8,128)(2,1)} %bitcast.67), channel_id=1, source_target_pairs={{0,32},{32,0},{64,96},{96,64},{1,33},{33,1},{65,97},{97,65},{2,34}... | collective-permute-start | bytes 4325384 | tf_op jit(solution)/shard_map/ppermute | solution.py:351
  11.7 24.8 %copy-start.22 = (s32[256,4]{0,1:T(4,128)S(1)}, s32[256,4]{0,1:T(4,128)}, u32[]{:S(2)}) copy-start(s32[256,4]{0,1:T(4,128)} %param.27) | copy-start | bytes 12292
  11.8 24.8 %copy-start.23 = (f32[256,4]{0,1:T(4,128)S(1)}, f32[256,4]{0,1:T(4,128)}, u32[]{:S(2)}) copy-start(f32[256,4]{0,1:T(4,128)} %param.28) | copy-start | bytes 12292
  23.8 26.2 %collective-permute-start = (bf16[4,256,256]{2,1,0:T(8,128)(2,1)}, bf16[4,256,256]{2,1,0:T(8,128)(2,1)S(1)}, u32[]{:S(2)}, u32[]{:S(2)}) collective-permute-start(bf16[4,256,256]{2,1,0:T(8,128)(2,1)} %slice.109), channel_id=1, source_target_pairs={{0,4},{1,5},{2,6},{3,7},{4,8},{5,9},{6,10},{7,11},{8,12},{9,13},{1... | collective-permute-start | bytes 1572872 | tf_op jit(solution)/shard_map/ppermute | solution.py:371
  29.6 20.4 %all-to-all-start.1 = ((bf16[128,2,1024]{2,1,0:T(2,128)(2,1)}), bf16[128,2,1024]{2,1,0:T(2,128)(2,1)}, u32[]{:S(2)}, u32[]{:S(2)}) async-start(bf16[128,2,1024]{2,1,0:T(2,128)(2,1)} %reshape.158), calls=%async_computation.1 | async-start | bytes 1048576 | tf_op jit(solution)/shard_map/all_to_all | solution.py:370
  55.3 12.2 %all-to-all-start.2 = ((bf16[8,128,128]{2,1,0:T(8,128)(2,1)}), bf16[8,128,128]{2,1,0:T(8,128)(2,1)S(1)}, u32[]{:S(2)}, u32[]{:S(2)}) async-start(bf16[8,128,128]{2,1,0:T(8,128)(2,1)} %bitcast.13), calls=%async_computation.2 | async-start | bytes 524288 | tf_op jit(solution)/shard_map/all_to_all | solution.py:392
  71.6 14.4 %copy-start.6 = (bf16[256,2048]{1,0:T(8,128)(2,1)S(1)}, bf16[256,2048]{1,0:T(8,128)(2,1)}, u32[]{:S(2)}) copy-start(bf16[256,2048]{1,0:T(8,128)(2,1)} %hidden.1) | copy-start | bytes 3145732
  71.7 14.4 %copy-start.9 = (f32[2048]{0:T(1024)S(1)}, f32[2048]{0:T(1024)}, u32[]{:S(2)}) copy-start(f32[2048]{0:T(1024)} %param.21) | copy-start | bytes 24580
  71.7 14.3 %collective-permute-start.2 = (bf16[128,2048]{1,0:T(8,128)(2,1)S(1)}, bf16[128,2048]{1,0:T(8,128)(2,1)S(1)}, u32[]{:S(2)}, u32[]{:S(2)}) collective-permute-start(bf16[128,2048]{1,0:T(8,128)(2,1)S(1)} %get-tuple-element.17), channel_id=1, source_target_pairs={{0,64},{64,0},{32,96},{96,32},{1,65},{65,1},{33,97},{97,33},{2,66}... | collective-permute-start | bytes 1572872 | tf_op jit(solution)/shard_map/ppermute | solution.py:402
  87.4 2.0 collective-permute-start.3
  93.2 6.9 %copy-start.24 = (bf16[2048]{0:T(1024)(128)(2,1)S(1)}, bf16[2048]{0:T(1024)(128)(2,1)}, u32[]{:S(2)}) copy-start(bf16[2048]{0:T(1024)(128)(2,1)} %param.26) | copy-start | bytes 12292
  93.2 49.0 %all-to-all-start.3 = ((bf16[32,24,2048]{2,1,0:T(8,128)(2,1)}), bf16[32,24,2048]{2,1,0:T(8,128)(2,1)}, u32[]{:S(2)}, u32[]{:S(2)}) async-start(bf16[32,24,2048]{2,1,0:T(8,128)(2,1)} %bitcast.69), calls=%async_computation.3 | async-start | bytes 6291456 | tf_op jit(solution)/shard_map/all_to_all | solution.py:424
  160.6 61.8 %all-to-all-start.4 = ((bf16[128,24,512]{2,1,0:T(8,128)(2,1)}), bf16[128,24,512]{2,1,0:T(8,128)(2,1)}, u32[]{:S(2)}, u32[]{:S(2)}) async-start(bf16[128,24,512]{2,1,0:T(8,128)(2,1)} %bitcast.61), calls=%async_computation.4 | async-start | bytes 6291456 | tf_op jit(solution)/shard_map/all_to_all | solution.py:454
  175.2 42.4 %copy-start.14 = (f32[256,1024]{1,0:T(8,128)S(1)}, f32[256,1024]{1,0:T(8,128)}, u32[]{:S(2)}) copy-start(f32[256,1024]{1,0:T(8,128)} %constant_dynamic-slice_fusion.2) | copy-start | bytes 3145732
  177.5 41.2 %copy-start.8 = (f32[128,2048]{1,0:T(8,128)S(1)}, f32[128,2048]{1,0:T(8,128)}, u32[]{:S(2)}) copy-start(f32[128,2048]{1,0:T(8,128)} %copy-done.7) | copy-start | bytes 3145732
  178.7 38.9 %collective-permute-start.7 = (bf16[256,1024]{1,0:T(8,128)(2,1)}, bf16[256,1024]{1,0:T(8,128)(2,1)S(1)}, u32[]{:S(2)}, u32[]{:S(2)}) collective-permute-start(bf16[256,1024]{1,0:T(8,128)(2,1)} %dynamic-slice_convert_fusion), channel_id=1, source_target_pairs={{0,64},{64,0},{32,96},{96,32},{1,65},{65,1},{33,97},{97,33},{2,66}... | collective-permute-start | bytes 1572872 | tf_op jit(solution)/shard_map/ppermute | solution.py:450
  218.7 2.5 %collective-permute-start.8 = (bf16[256,512]{1,0:T(8,128)(2,1)}, bf16[256,512]{1,0:T(8,128)(2,1)}, u32[]{:S(2)}, u32[]{:S(2)}) collective-permute-start(bf16[256,512]{1,0:T(8,128)(2,1)} %dynamic-slice_convert_fusion.1), channel_id=1, source_target_pairs={{0,32},{32,0},{64,96},{96,64},{1,33},{33,1},{65,97},{97,65},{2,34}... | collective-permute-start | bytes 786440 | tf_op jit(solution)/shard_map/ppermute | solution.py:469
  219.5 2.9 %collective-permute-start.6 = (f32[128,512]{1,0:T(8,128)}, f32[128,512]{1,0:T(8,128)}, u32[]{:S(2)}, u32[]{:S(2)}) collective-permute-start(f32[128,512]{1,0:T(8,128)} %get-tuple-element.26), channel_id=1, source_target_pairs={{0,32},{32,0},{64,96},{96,64},{1,33},{33,1},{65,97},{97,65},{2,34}... | collective-permute-start | bytes 786440 | tf_op jit(solution)/shard_map/ppermute | solution.py:474
  (15 other events, 38.1 us)

commit v3 on v2

--- a/solution.py
+++ b/solution.py
@@ -22,15 +22,34 @@
 CROSS = [(0, 2), (2, 0), (1, 3), (3, 1)]
 
 
-def attention_kernel(ids_col, ids_row, own, past, out):
+def attention_kernel(
+    place, ids_col_hbm, ids_row_hbm, query_hbm, own_hbm, past_hbm, out_hbm,
+    ids_col, ids_row, query_parts, own, past, out, sems, out_sems,
+):
     block = out.shape[2] * 2
+    pairs = (
+        (query_hbm, query_parts),
+        (own_hbm, own),
+        (past_hbm, past),
+        (ids_col_hbm, ids_col),
+        (ids_row_hbm, ids_row),
+    )
+    copies = [
+        pltpu.make_async_copy(source, target, sems.at[i])
+        for i, (source, target) in enumerate(pairs)
+    ]
+    for copy in copies:
+        copy.start()
+    for copy in copies:
+        copy.wait()
+    stores = []
     scale = 1.0 / math.sqrt(HD)
     span = ROW * block
     row_pos = lax.broadcasted_iota(jnp.int32, (block, block), 0)
     col_pos = lax.broadcasted_iota(jnp.int32, (block, block), 1)
     causal = col_pos <= row_pos
     for y in range(ROW):
-        query = own[y, :, 0:HD]
+        query = query_parts[lax.rem(place[0] + (ROW - y), ROW)]
         query_ids = ids_col[pl.ds(y * block, block), 0:1]
         pieces = []
         for b in range(y, ROW):
@@ -41,7 +60,7 @@
             )
             pieces.append(jnp.where(query_ids == key_ids, score * scale, -1e30))
         for b in range(y + 1):
-            key = own[b, :, HD : 2 * HD]
+            key = own[b, :, 0:HD]
             key_ids = ids_row[0:1, pl.ds(span + b * block, block)]
             score = lax.dot_general(
                 query, key, (((1,), (1,)), ((), ())), preferred_element_type=F32
@@ -66,58 +85,112 @@
             index += 1
         for b in range(y + 1):
             prob = (weights[index] * inverse).astype(BF)
-            mixed += jnp.dot(prob, own[b, :, 2 * HD : 3 * HD], preferred_element_type=F32)
+            mixed += jnp.dot(prob, own[b, :, HD : 2 * HD], preferred_element_type=F32)
             index += 1
         half = block // 2
         out[0, y] = mixed[:half].astype(BF)
         out[1, y] = mixed[half:].astype(BF)
-
-
-def attention(ids_col, ids_row, own, past):
+        for c in range(2):
+            store = pltpu.make_async_copy(out.at[c, y], out_hbm.at[c, y], out_sems.at[c, y])
+            store.start()
+            stores.append(store)
+    for store in stores:
+        store.wait()
+
+
+def attention(place, ids_col, ids_row, query_parts, own, past):
     block = own.shape[1]
+    hbm = pl.BlockSpec(memory_space=pltpu.HBM)
+    operands = (ids_col, ids_row, query_parts, own, past)
+    result = jax.ShapeDtypeStruct((2, ROW, block // 2, HD), BF)
     return pl.pallas_call(
         attention_kernel,
-        out_shape=jax.ShapeDtypeStruct((2, ROW, block // 2, HD), BF),
-        in_specs=[pl.BlockSpec(memory_space=pltpu.VMEM)] * 4,
-        out_specs=pl.BlockSpec(memory_space=pltpu.VMEM),
-        compiler_params=pltpu.CompilerParams(vmem_limit_bytes=24 << 20),
+        out_shape=result,
+        in_specs=[pl.BlockSpec(memory_space=pltpu.SMEM)] + [hbm] * 5,
+        out_specs=hbm,
+        scratch_shapes=[pltpu.VMEM(o.shape, o.dtype) for o in operands]
+        + [
+            pltpu.VMEM(result.shape, BF),
+            pltpu.SemaphoreType.DMA((5,)),
+            pltpu.SemaphoreType.DMA((2, ROW)),
+        ],
+        compiler_params=pltpu.CompilerParams(vmem_limit_bytes=58 << 20),
         cost_estimate=pl.CostEstimate(
             flops=4 * 5 * ROW * block * block * HD,
-            bytes_accessed=6 << 20,
+            bytes_accessed=3 << 20,
             transcendentals=5 * ROW * block * block,
         ),
         name="row_attention",
-    )(ids_col, ids_row, own, past)
-
-
-def project_kernel(core, att, out_own, out_peer, total, total_low):
+    )(place, *operands)
+
+
+def project_kernel(
+    core, att_hbm, own_hbm, peer_hbm, total_hbm, low_hbm,
+    att, own, peer, total, total_low, att_sem, sems, out_sems,
+):
+    width = total.shape[1]
+    step = width // 4
+    att_copy = pltpu.make_async_copy(att_hbm, att, att_sem)
+    att_copy.start()
+    copies = []
+    for i in range(4):
+        cols = pl.ds(i * step, step)
+        copies.append(
+            (
+                pltpu.make_async_copy(own_hbm.at[:, cols], own.at[:, cols], sems.at[0, i]),
+                pltpu.make_async_copy(peer_hbm.at[:, cols], peer.at[:, cols], sems.at[1, i]),
+            )
+        )
+    for pair in copies:
+        for copy in pair:
+            copy.start()
+    att_copy.wait()
     c = core[0]
+    stores = []
     left = jnp.concatenate([att[c, y] for y in range(ROW)], 1)
     right = jnp.concatenate([att[1 - c, y] for y in range(ROW)], 1)
-    width = total.shape[1]
-    step = width // 4
     for i in range(4):
         cols = pl.ds(i * step, step)
-        part = jnp.dot(left, out_own[:, cols], preferred_element_type=F32) + jnp.dot(
-            right, out_peer[:, cols], preferred_element_type=F32
+        for copy in copies[i]:
+            copy.wait()
+        part = jnp.dot(left, own[:, cols], preferred_element_type=F32) + jnp.dot(
+            right, peer[:, cols], preferred_element_type=F32
         )
+        total_low[:, cols] = part.astype(BF)
         total[:, cols] = part
-        total_low[:, cols] = part.astype(BF)
+        for j, (source, target) in enumerate(((total_low, low_hbm), (total, total_hbm))):
+            store = pltpu.make_async_copy(
+                source.at[:, cols], target.at[:, cols], out_sems.at[j, i]
+            )
+            store.start()
+            stores.append(store)
+    for store in stores:
+        store.wait()
 
 
 def project(core, att, out_own, out_peer):
     rows = att.shape[2]
     depth, width = out_own.shape
-    vmem = pl.BlockSpec(memory_space=pltpu.VMEM)
+    hbm = pl.BlockSpec(memory_space=pltpu.HBM)
     return pl.pallas_call(
         project_kernel,
         out_shape=(
             jax.ShapeDtypeStruct((rows, width), F32),
             jax.ShapeDtypeStruct((rows, width), BF),
         ),
-        in_specs=[pl.BlockSpec(memory_space=pltpu.SMEM), vmem, vmem, vmem],
-        out_specs=(vmem, vmem),
-        compiler_params=pltpu.CompilerParams(vmem_limit_bytes=24 << 20),
+        in_specs=[pl.BlockSpec(memory_space=pltpu.SMEM), hbm, hbm, hbm],
+        out_specs=(hbm, hbm),
+        scratch_shapes=[
+            pltpu.VMEM(att.shape, BF),
+            pltpu.VMEM((depth, width), BF),
+            pltpu.VMEM((depth, width), BF),
+            pltpu.VMEM((rows, width), F32),
+            pltpu.VMEM((rows, width), BF),
+            pltpu.SemaphoreType.DMA,
+            pltpu.SemaphoreType.DMA((2, 4)),
+            pltpu.SemaphoreType.DMA((2, 4)),
+        ],
+        compiler_params=pltpu.CompilerParams(vmem_limit_bytes=58 << 20),
         cost_estimate=pl.CostEstimate(
             flops=4 * rows * depth * width, bytes_accessed=6 << 20, transcendentals=0
         ),
@@ -125,37 +198,161 @@
     )(core, att, out_own, out_peer)
 
 
-def norm_kernel(core, hidden, near, far, gain, resid, normed):
+def norm_kernel(
+    core, hidden_hbm, near_hbm, far_hbm, gain_hbm, resid_hbm, normed_hbm,
+    hidden, near, far, gain, normed, sems, out_sems,
+):
     rows = near.shape[0]
+    parts = 2
+    block = rows // parts
     start = pl.multiple_of(core[0] * rows, rows)
-    block = rows // 4
-    for i in range(4):
+    gain_copy = pltpu.make_async_copy(gain_hbm, gain, sems.at[3, 0])
+    gain_copy.start()
+    copies = []
+    for i in range(parts):
         here = pl.ds(i * block, block)
-        value = hidden[pl.ds(start + i * block, block), :].astype(F32) + (
-            near[here, :] + far[here, :].astype(F32)
+        copies.append(
+            [
+                pltpu.make_async_copy(near_hbm.at[here], near.at[here], sems.at[0, i]),
+                pltpu.make_async_copy(far_hbm.at[here], far.at[here], sems.at[1, i]),
+                pltpu.make_async_copy(
+                    hidden_hbm.at[pl.ds(start + i * block, block)], hidden.at[here], sems.at[2, i]
+                ),
+            ]
         )
-        resid[here, :] = value
+        for copy in copies[i]:
+            copy.start()
+    gain_copy.wait()
+    stores = []
+    for i in range(parts):
+        here = pl.ds(i * block, block)
+        for copy in copies[i]:
+            copy.wait()
+        value = hidden[here, :].astype(F32) + (near[here, :] + far[here, :].astype(F32))
         mean_square = jnp.mean(value * value, axis=-1, keepdims=True)
         normed[here, :] = (value * lax.rsqrt(mean_square + 1e-06) * gain[...]).astype(BF)
+        near[here, :] = value
+        for j, (source, target) in enumerate(((normed, normed_hbm), (near, resid_hbm))):
+            store = pltpu.make_async_copy(source.at[here], target.at[here], out_sems.at[j, i])
+            store.start()
+            stores.append(store)
+    for store in stores:
+        store.wait()
 
 
 def add_and_norm(core, hidden, near, far, gain):
     rows, width = near.shape
-    vmem = pl.BlockSpec(memory_space=pltpu.VMEM)
+    hbm = pl.BlockSpec(memory_space=pltpu.HBM)
     return pl.pallas_call(
         norm_kernel,
         out_shape=(
             jax.ShapeDtypeStruct((rows, width), F32),
             jax.ShapeDtypeStruct((rows, width), BF),
         ),
-        in_specs=[pl.BlockSpec(memory_space=pltpu.SMEM), vmem, vmem, vmem, vmem],
+        in_specs=[pl.BlockSpec(memory_space=pltpu.SMEM), hbm, hbm, hbm, hbm],
+        out_specs=(hbm, hbm),
+        scratch_shapes=[
+            pltpu.VMEM((rows, width), BF),
+            pltpu.VMEM((rows, width), F32),
+            pltpu.VMEM((rows, width), BF),
+            pltpu.VMEM((1, width), F32),
+            pltpu.VMEM((rows, width), BF),
+            pltpu.SemaphoreType.DMA((4, 2)),
+            pltpu.SemaphoreType.DMA((2, 2)),
+        ],
+        compiler_params=pltpu.CompilerParams(vmem_limit_bytes=58 << 20),
+        cost_estimate=pl.CostEstimate(
+            flops=8 * rows * width, bytes_accessed=4 << 20, transcendentals=rows
+        ),
+        name="add_and_norm",
+    )(core, hidden, near, far, gain)
+
+
+def gather_kernel(
+    select_hbm, own_hbm, peer_hbm, out_hbm, select, rows, out, sems, out_sems
+):
+    half = rows.shape[0] // 2
+    total, block = out.shape[0], out.shape[0] // 3
+    copies = [
+        pltpu.make_async_copy(own_hbm, rows.at[pl.ds(0, half)], sems.at[0]),
+        pltpu.make_async_copy(peer_hbm, rows.at[pl.ds(half, half)], sems.at[1]),
+        pltpu.make_async_copy(select_hbm, select, sems.at[2]),
+    ]
+    for copy in copies:
+        copy.start()
+    for copy in copies:
+        copy.wait()
+    stores = []
+    for i in range(total // block):
+        here = pl.ds(i * block, block)
+        out[here, :] = jnp.dot(
+            select[here, :], rows[...], preferred_element_type=F32
+        ).astype(BF)
+        store = pltpu.make_async_copy(out.at[here], out_hbm.at[here], out_sems.at[i])
+        store.start()
+        stores.append(store)
+    for store in stores:
+        store.wait()
+
+
+def gather_rows(select, own, peer):
+    slots, rows = select.shape
+    width = own.shape[1]
+    hbm = pl.BlockSpec(memory_space=pltpu.HBM)
+    return pl.pallas_call(
+        gather_kernel,
+        out_shape=jax.ShapeDtypeStruct((slots, width), BF),
+        in_specs=[hbm, hbm, hbm],
+        out_specs=hbm,
+        scratch_shapes=[
+            pltpu.VMEM((slots, rows), BF),
+            pltpu.VMEM((rows, width), BF),
+            pltpu.VMEM((slots, width), BF),
+            pltpu.SemaphoreType.DMA((3,)),
+            pltpu.SemaphoreType.DMA((3,)),
+        ],
+        compiler_params=pltpu.CompilerParams(vmem_limit_bytes=58 << 20),
+        cost_estimate=pl.CostEstimate(
+            flops=2 * slots * rows * width, bytes_accessed=5 << 20, transcendentals=0
+        ),
+        name="gather_rows",
+    )(select, own, peer)
+
+
+def slot_weight_kernel(rank, weight, high, low):
+    slots = high.shape[1]
+    per_core = CAP // CORES
+    experts_here = rank.shape[1]
+    lane = lax.broadcasted_iota(jnp.int32, (1, slots), 1)
+    expert_of = lax.rem(lax.div(lane, per_core), experts_here)
+    wanted = lax.rem(lane, per_core) * CORES + lax.div(lane, per_core * experts_here)
+    expand = (
+        lax.broadcasted_iota(jnp.int32, (experts_here, slots), 0) == expert_of
+    ).astype(BF)
+    ranks = jnp.dot(rank[...].astype(BF), expand, preferred_element_type=F32)
+    hit = ranks.astype(jnp.int32) == wanted
+    top = weight[...].astype(BF)
+    rest = (weight[...] - top.astype(F32)).astype(BF)
+    for side, out in ((top, high), (rest, low)):
+        spread = jnp.dot(side, expand, preferred_element_type=F32)
+        out[...] = jnp.where(hit, spread, 0.0).astype(BF)
+
+
+def slot_weights(rank, weight, slots):
+    rows = rank.shape[0]
+    vmem = pl.BlockSpec(memory_space=pltpu.VMEM)
+    shape = jax.ShapeDtypeStruct((rows, slots), BF)
+    return pl.pallas_call(
+        slot_weight_kernel,
+        out_shape=(shape, shape),
+        in_specs=[vmem, vmem],
         out_specs=(vmem, vmem),
         compiler_params=pltpu.CompilerParams(vmem_limit_bytes=16 << 20),
         cost_estimate=pl.CostEstimate(
-            flops=8 * rows * width, bytes_accessed=4 << 20, transcendentals=rows
-        ),
-        name="add_and_norm",
-    )(core, hidden, near, far, gain)
+            flops=6 * rows * slots * 32, bytes_accessed=2 << 20, transcendentals=0
+        ),
+        name="slot_weights",
+    )(rank, weight)
 
 
 def expert_kernel(
@@ -167,30 +364,35 @@
     block = rows // 2
     first = pl.ds(0, hidden)
     second = pl.ds(hidden, hidden)
+    top_rows, low_rows = pl.ds(0, block), pl.ds(block, block)
     copies = [
-        pltpu.make_async_copy(x_hbm, x, sems.at[0]),
+        pltpu.make_async_copy(x_hbm.at[top_rows], x.at[top_rows], sems.at[0]),
         pltpu.make_async_copy(both_own.at[0], gate.at[first], sems.at[1]),
         pltpu.make_async_copy(both_peer.at[0], gate.at[second], sems.at[2]),
         pltpu.make_async_copy(both_own.at[1], up.at[first], sems.at[3]),
         pltpu.make_async_copy(both_peer.at[1], up.at[second], sems.at[4]),
-        pltpu.make_async_copy(down_own, down.at[first], sems.at[5]),
-        pltpu.make_async_copy(down_peer, down.at[second], sems.at[6]),
+        pltpu.make_async_copy(x_hbm.at[low_rows], x.at[low_rows], sems.at[5]),
+        pltpu.make_async_copy(down_own, down.at[first], sems.at[6]),
+        pltpu.make_async_copy(down_peer, down.at[second], sems.at[7]),
     ]
     for copy in copies:
         copy.start()
-    for copy in copies[:5]:
+    contract = (((1,), (1,)), ((), ()))
+    for copy in copies[:3]:
         copy.wait()
-
-    @pl.loop(0, 2)
-    def _(m):
-        here = pl.ds(pl.multiple_of(m * block, block), block)
+    for m in range(2):
+        here = pl.ds(m * block, block)
+        if m == 1:
+            copies[5].wait()
         left = x[here, :]
-        contract = (((1,), (1,)), ((), ()))
         g = lax.dot_general(left, gate[...], contract, preferred_element_type=F32)
+        if m == 0:
+            copies[3].wait()
+            copies[4].wait()
         u = lax.dot_general(left, up[...], contract, preferred_element_type=F32)
         act[here, :] = (g / (1.0 + jnp.exp(-g)) * u).astype(BF)
 
-    for copy in copies[5:]:
+    for copy in copies[6:]:
         copy.wait()
 
     @pl.loop(0, 2)
@@ -231,10 +433,10 @@
             pltpu.VMEM((2 * hidden, width), BF),
             pltpu.VMEM((rows, 2 * hidden), BF),
             pltpu.VMEM((groups, rows, column_width), BF),
-            pltpu.SemaphoreType.DMA((7,)),
+            pltpu.SemaphoreType.DMA((8,)),
             pltpu.SemaphoreType.DMA((2, groups)),
         ],
-        compiler_params=pltpu.CompilerParams(vmem_limit_bytes=28 << 20),
+        compiler_params=pltpu.CompilerParams(vmem_limit_bytes=60 << 20),
         cost_estimate=pl.CostEstimate(
             flops=12 * rows * depth * hidden,
             bytes_accessed=15 << 20,
@@ -244,13 +446,37 @@
     )(x, both_own, both_peer, down_own, down_peer)
 
 
-def combine_kernel(core, high, low, returned, mine, peers, shared, out):
+def combine_kernel(
+    core, high_hbm, low_hbm, back_hbm, mine_hbm, peers_hbm, shared_hbm, out,
+    high, low, back, mine, peers, shared, sems,
+):
     rows = mine.shape[0]
-    sides = (high, low)
-    total = shared[...]
-    for chip in range(returned.shape[0]):
-        for side in sides:
-            total += jnp.dot(side[...], returned[chip], preferred_element_type=F32)
+    pairs = (
+        (high_hbm, high),
+        (back_hbm.at[0], back.at[0]),
+        (low_hbm, low),
+        (back_hbm.at[1], back.at[1]),
+        (shared_hbm, shared),
+        (mine_hbm, mine),
+        (peers_hbm, peers),
+    )
+    copies = [
+        pltpu.make_async_copy(source, target, sems.at[i])
+        for i, (source, target) in enumerate(pairs)
+    ]
+    for copy in copies:
+        copy.start()
+    copies[0].wait()
+    copies[1].wait()
+    total = jnp.dot(high[...], back[0], preferred_element_type=F32)
+    copies[2].wait()
+    total += jnp.dot(low[...], back[0], preferred_element_type=F32)
+    copies[3].wait()
+    total += jnp.dot(high[...], back[1], preferred_element_type=F32)
+    total += jnp.dot(low[...], back[1], preferred_element_type=F32)
+    for copy in copies[4:]:
+        copy.wait()
+    total += shared[...]
     first = core[0] == 0
     low_half = jnp.where(first, mine[...], peers[...])
     high_half = jnp.where(first, peers[...], mine[...])
@@ -259,19 +485,22 @@
 
 
 def combine(core, high, low, returned, mine, peers, shared):
-    vmem = pl.BlockSpec(memory_space=pltpu.VMEM)
+    hbm = pl.BlockSpec(memory_space=pltpu.HBM)
     rows, width = shared.shape
+    operands = (high, low, returned, mine, peers, shared)
     return pl.pallas_call(
         combine_kernel,
         out_shape=jax.ShapeDtypeStruct((rows, width), BF),
-        in_specs=[pl.BlockSpec(memory_space=pltpu.SMEM)] + [vmem] * 6,
-        out_specs=vmem,
-        compiler_params=pltpu.CompilerParams(vmem_limit_bytes=24 << 20),
+        in_specs=[pl.BlockSpec(memory_space=pltpu.SMEM)] + [hbm] * 6,
+        out_specs=pl.BlockSpec(memory_space=pltpu.VMEM),
+        scratch_shapes=[pltpu.VMEM(o.shape, o.dtype) for o in operands]
+        + [pltpu.SemaphoreType.DMA((7,))],
+        compiler_params=pltpu.CompilerParams(vmem_limit_bytes=60 << 20),
         cost_estimate=pl.CostEstimate(
             flops=8 * rows * width * high.shape[1], bytes_accessed=7 << 20, transcendentals=0
         ),
         name="combine",
-    )(core, high, low, returned, mine, peers, shared)
+    )(core, *operands)
 
 
 def page_pieces(keys, values, owner_all, tok_count, head_count, tok_index):
@@ -352,9 +581,7 @@
 
     packed = jnp.stack(
         [
-            jnp.concatenate(
-                [part[:, i * HD : (i + 1) * HD] for part in (queries, keys, values)], 1
-            )
+            jnp.concatenate([part[:, i * HD : (i + 1) * HD] for part in (keys, values)], 1)
             for i in range(heads_here)
         ],
         0,
@@ -363,13 +590,30 @@
     own = lax.all_to_all(
         packed, "tok", split_axis=0, concat_axis=0, tiled=True, axis_index_groups=row_groups
     )
+    queries, own = lax.optimization_barrier((queries, own))
+    place_in_row = tok_index % ROW
+    query_parts = []
+    for step in range(ROW):
+        target = (place_in_row + step) % ROW
+        part = lax.dynamic_slice_in_dim(queries, target * HD, HD, 1)
+        if step:
+            part = lax.ppermute(
+                part,
+                "tok",
+                [
+                    (r * ROW + y, r * ROW + (y + step) % ROW)
+                    for r in range(rows_of_blocks)
+                    for y in range(ROW)
+                ],
+            )
+        query_parts.append(part)
     slots_all = page_slots.reshape(tok_count, tok_rows // PAGE)
     owner_all = slots_all // (tok_rows // PAGE)
     pieces = page_pieces(keys, values, owner_all, tok_count, head_count, tok_index)
     pieces, own = lax.optimization_barrier((pieces, own))
     landed = lax.all_to_all(pieces, BOTH, split_axis=0, concat_axis=0, tiled=True)
     past = lax.ppermute(
-        own[:, :, HD:], "tok", [(s, s + ROW) for s in range(tok_count - ROW)]
+        own, "tok", [(s, s + ROW) for s in range(tok_count - ROW)]
     )
     span = ROW * tok_rows
     base = (tok_index // ROW) * span
@@ -378,7 +622,9 @@
     ids_row = window_ids[None, :]
     ids_col = jnp.broadcast_to(window_ids[span:, None], (span, HD))
     past, landed = lax.optimization_barrier((past, landed))
-    attended = attention(ids_col, ids_row, own, past)
+    attended = attention(
+        place_in_row.reshape(1), ids_col, ids_row, jnp.stack(query_parts, 0), own, past
+    )
 
     core_groups = [
         [
@@ -413,14 +659,21 @@
         jnp.arange(tok_rows, dtype=jnp.int32)[None, :] < jnp.arange(tok_rows, dtype=jnp.int32)[:, None]
     ).astype(BF)
     rank = jnp.dot(earlier, onehot.astype(BF), preferred_element_type=F32).astype(jnp.int32)
-    rank_t = jnp.where(onehot > 0, rank, -1).T
-    weight_t = weight_of.T
+    rank = jnp.where(onehot > 0, rank, -1)
+    rank_t = rank.T
     rank_rel = jnp.where(core == 0, rank_t, jnp.roll(rank_t, half, 1))
     place = jnp.arange(slots_core, dtype=jnp.int32) * CORES
     select = (rank_rel[:, None, :] == (place + core)[None, :, None]).astype(BF)
     select = select.reshape(EXPERTS * slots_core, tok_rows)
-    normed_rel = jnp.concatenate([normed_own, normed_peer], 0)
-    outgoing = jnp.dot(select, normed_rel, preferred_element_type=F32).astype(BF)
+    outgoing = gather_rows(select, normed_own, normed_peer)
+    rank, weight_of, outgoing = lax.optimization_barrier((rank, weight_of, outgoing))
+    high, low = slot_weights(rank, weight_of, CORES * EXPERTS * slots_core)
+    normed_abs = jnp.where(
+        core == 0,
+        jnp.concatenate([normed_own, normed_peer], 0),
+        jnp.concatenate([normed_peer, normed_own], 0),
+    )
+    normed_abs, outgoing = lax.optimization_barrier((normed_abs, outgoing))
     arrived = lax.all_to_all(
         outgoing.reshape(tok_count, slots_core, model_width),
         "tok",
@@ -428,10 +681,6 @@
         concat_axis=0,
         tiled=True,
     ).reshape(tok_count * slots_core, model_width)
-
-    normed_abs = jnp.where(
-        core == 0, normed_rel, jnp.concatenate([normed_peer, normed_own], 0)
-    )
     shared_both = jnp.einsum("td,dgf->tgf", normed_abs, shared_gate_up, preferred_element_type=F32)
     shared_act = (jax.nn.silu(shared_both[:, 0, :]) * shared_both[:, 1, :]).astype(BF)
     shared_scale = jax.nn.sigmoid(jnp.dot(normed_abs, shared_gate, preferred_element_type=F32))
@@ -451,16 +700,10 @@
 
     partial = experts(arrived, gate_up_own, gate_up_peer, down_own, down_peer, head_count)
     partial = partial.reshape(head_count * tok_count, slots_core, column_width)
+    partial, shared_far = lax.optimization_barrier((partial, shared_far))
     returned = lax.all_to_all(partial, BOTH, split_axis=0, concat_axis=0, tiled=True)
     returned = returned.reshape(CHIPS, CORES * EXPERTS * slots_core, column_width)
 
-    wanted = place[None, :] + jnp.arange(CORES, dtype=jnp.int32)[:, None]
-    spread = jnp.where(
-        rank_t[None, :, None, :] == wanted[:, None, :, None], weight_t[None, :, None, :], 0.0
-    ).reshape(CORES * EXPERTS * slots_core, tok_rows)
-    high = spread.astype(BF)
-    low = (spread - high.astype(F32)).astype(BF).T
-    high = high.T
     shared_chip = shared_near + shared_far.astype(F32)
     shared_own = lax.dynamic_slice_in_dim(shared_chip, core * column_width, column_width, 1)
     shared_peer = lax.dynamic_slice_in_dim(

time: 233 us -> 216 us (0.927)
  waiting for transfers between devices: 98.7 us -> 84.9 us
  local copies, waits for them, and re-layouts: 39.7 us -> 26.9 us
  Pallas kernels: 25.9 us -> 33.5 us
  other arithmetic: 8.12 us -> 12 us
  matrix products: 16 us -> 12.3 us
  starting transfers between devices: 40.4 us -> 43.5 us
    ppermute x1, waiting for transfers between devices: 37.8 us -> 0.01 us  [per_device(): shared_far = lax.ppermute(shared_send, 'head', CROSS)]
    all_to_all x1, waiting for transfers between devices: 0.01 us -> 20.5 us  [per_device(): lax.all_to_all(partial, BOTH, split_axis=0, concat_axis=0, tiled=True)]
    all_to_all x1, waiting for transfers between devices: 13.3 us -> 2.12 us  [per_device(): lax.all_to_all(pieces, BOTH, split_axis=0, concat_axis=0, tiled=True)]
    all_to_all x1, waiting for transfers between devices: 0.01 us -> 6.91 us  [per_device(): lax.all_to_all(attended.reshape(CORES * ROW, half, HD), BOTH, split_axis=...]
    ppermute x1 -> x4, starting transfers between devices: 5.8 us -> 11.8 us  [the longest x1 6.59 us: per_device(): lax.ppermute(own, 'tok', [(s, s + ROW) for s in range(tok_count - ROW)])]
    ppermute x1 -> x4, waiting for transfers between devices: 0.01 us -> 5.13 us  [the longest x3 5.13 us: per_device(): lax.ppermute(part, 'tok', [(r * ROW + y, r * ROW + (y + step) % ROW) for...]
    all_to_all x1, waiting for transfers between devices: 25.6 us -> 30.4 us  [per_device(): lax.all_to_all(outgoing.reshape(tok_count, slots_core, model_width), 'tok...]
    pallas_call x1 -> x3, Pallas kernels: 5.07 us -> 9.7 us  [the longest x1 5.45 us: attention(): pl.pallas_call(attention_kernel, out_shape=result, in_specs=[pl.BlockSpec...]
  transfers between devices with their start and end apart: 14 -> 17, of which waited for: 6 -> 8; matrix products, arithmetic and copies ran while one was open for 21% -> 21% of each run, Pallas kernels for 3% -> 9%
where the time goes in v3:
time: 216 us; the launch traced here: 214 us
  waiting for transfers between devices  84.9 us (39%)
  starting transfers between devices  43.5 us (20%)
  Pallas kernels  33.5 us (16%)
  local copies, waits for them, and re-layouts  26.9 us (12%)
  matrix products  12.3 us (6%)
  other arithmetic  12 us (6%)
    all_to_all x1, waiting for transfers between devices, per_device(): lax.all_to_all(outgoing.reshape(tok_count, slots_core, model_width), 'tok...  30.4 us
    all_to_all x1, waiting for transfers between devices, per_device(): lax.all_to_all(partial, BOTH, split_axis=0, concat_axis=0, tiled=True)  20.5 us
    ppermute x1, waiting for transfers between devices, per_device(): projected_far = lax.ppermute(projected_low, 'head', CROSS)  12.3 us
    pallas_call x1, Pallas kernels, experts(): pl.pallas_call(expert_kernel, out_shape=jax.ShapeDtypeStruct((groups, row...  12.2 us
    all_to_all x1, starting transfers between devices, per_device(): lax.all_to_all(partial, BOTH, split_axis=0, concat_axis=0, tiled=True)  8.73 us
    all_to_all x1, waiting for transfers between devices, per_device(): lax.all_to_all(packed, 'tok', split_axis=0, concat_axis=0, tiled=True, ax...  7.56 us
    all_to_all x1, waiting for transfers between devices, per_device(): lax.all_to_all(attended.reshape(CORES * ROW, half, HD), BOTH, split_axis=...  6.91 us
    ppermute x1, starting transfers between devices, per_device(): lax.ppermute(own, 'tok', [(s, s + ROW) for s in range(tok_count - ROW)])  6.59 us
  transfers between devices with their start and end apart: 17, of which 8 were waited for; matrix products, arithmetic and copies ran while one was open for 21% of the time, Pallas kernels for 9%

profile of v3, /device:TPU:0, one launch (start us, length us, event | category | flops | bytes accessed | tf_op | source)
XLA Modules:
  0.0 214.4 jit_solution(13404040015890682762)
XLA Ops:
  3.8 4.5 %all-to-all-start = ((bf16[4,256,256]{2,1,0:T(8,128)(2,1)}), bf16[4,256,256]{2,1,0:T(8,128)(2,1)}, u32[]{:S(2)}, u32[]{:S(2)}) async-start(bf16[4,256,256]{2,1,0:T(8,128)(2,1)} %pad_maximum_fusion), calls=%async_computation | async-start | bytes 1048576 | tf_op jit(solution)/shard_map/all_to_all | solution.py:590
  11.0 7.6 %all-to-all-done.own_hbm = bf16[4,256,256]{2,1,0:T(8,128)(2,1)} async-done(((bf16[4,256,256]{2,1,0:T(8,128)(2,1)}), bf16[4,256,256]{2,1,0:T(8,128)(2,1)}, u32[]{:S(2)}, u32[]{:S(2)}) %all-to-all-start) | async-done | bytes 524320 | tf_op jit(solution)/shard_map/all_to_all | solution.py:590
  18.6 6.6 %collective-permute-start.3 = (bf16[4,256,256]{2,1,0:T(8,128)(2,1)}, bf16[4,256,256]{2,1,0:T(8,128)(2,1)}, u32[]{:S(2)}, u32[]{:S(2)}) collective-permute-start(bf16[4,256,256]{2,1,0:T(8,128)(2,1)} %all-to-all-done.own_hbm), channel_id=1, source_target_pairs={{0,4},{1,5},{2,6},{3,7},{4,8},{5,9},{6,10},{7,11},{8,12},{9,13},{1... | collective-permute-start | bytes 1572872 | tf_op jit(solution)/shard_map/ppermute | solution.py:615
  25.2 5.5 %all-to-all-start.1 = ((bf16[128,2,1024]{2,1,0:T(2,128)(2,1)}), bf16[128,2,1024]{2,1,0:T(2,128)(2,1)S(1)}, u32[]{:S(2)}, u32[]{:S(2)}) async-start(bf16[128,2,1024]{2,1,0:T(2,128)(2,1)} %reshape.134), calls=%async_computation.1 | async-start | bytes 1048576 | tf_op jit(solution)/shard_map/all_to_all | solution.py:614
  33.4 2.7 %collective-permute-start.1 = (bf16[256,128]{1,0:T(8,128)(2,1)S(1)}, bf16[256,128]{1,0:T(8,128)(2,1)S(1)}, u32[]{:S(2)}, u32[]{:S(2)}) collective-permute-start(bf16[256,128]{1,0:T(8,128)(2,1)S(1)} %get-tuple-element.56), channel_id=1, source_target_pairs={{0,2},{1,3},{2,0},{3,1},{4,6},{5,7},{6,4},{7,5},{8,10},{9,11},{10,... | collective-permute-start | bytes 196616 | tf_op jit(solution)/shard_map/ppermute | solution.py:600
  37.6 3.2 %collective-permute-done = bf16[256,128]{1,0:T(8,128)(2,1)S(1)} collective-permute-done((bf16[256,128]{1,0:T(8,128)(2,1)S(1)}, bf16[256,128]{1,0:T(8,128)(2,1)S(1)}, u32[]{:S(2)}, u32[]{:S(2)}) %collective-permute-start) | collective-permute-done | bytes 65568 | tf_op jit(solution)/shard_map/ppermute | solution.py:600
  40.8 1.9 collective-permute-done.1
  43.5 2.1 all-to-all-done.1
  46.6 5.5 %row_attention.1 = bf16[2,4,128,128]{3,2,1,0:T(8,128)(2,1)} custom-call(s32[1]{0:T(128)} %bitcast.3.place, s32[1024,128]{1,0:T(8,128)} %broadcast_in_dim.31.ids_col_hbm, s32[1,2048]{1,0:T(1,128)} %bitcast.69, bf16[4,256,128]{2,1,0:T(8,128)(2,1)} %pad_maximum_fusion.2.query_hbm, bf16[4,256,256]{2,1,0:T(8,128)(2,1)} %all-to-all-done.own_hbm, ...), custom_call_target="tpu_custom_call" | custom-call | flops 671088640 | bytes 3145728 | tf_op jit(solution)/shard_map/row_attention/pallas_call | solution.py:106
  52.0 4.1 %all-to-all-start.2 = ((bf16[8,128,128]{2,1,0:T(8,128)(2,1)}), bf16[8,128,128]{2,1,0:T(8,128)(2,1)}, u32[]{:S(2)}, u32[]{:S(2)}) async-start(bf16[8,128,128]{2,1,0:T(8,128)(2,1)} %bitcast.64), calls=%async_computation.2 | async-start | bytes 524288 | tf_op jit(solution)/shard_map/all_to_all | solution.py:638
  56.1 6.9 %all-to-all-done.2 = bf16[8,128,128]{2,1,0:T(8,128)(2,1)} async-done(((bf16[8,128,128]{2,1,0:T(8,128)(2,1)}), bf16[8,128,128]{2,1,0:T(8,128)(2,1)}, u32[]{:S(2)}, u32[]{:S(2)}) %all-to-all-start.2) | async-done | bytes 262176 | tf_op jit(solution)/shard_map/all_to_all | solution.py:638
  63.0 4.3 %project.1 = (f32[128,2048]{1,0:T(8,128)}, bf16[128,2048]{1,0:T(8,128)(2,1)}) custom-call(s32[1]{0:T(128)} %bitcast.core, bf16[2,4,128,128]{3,2,1,0:T(8,128)(2,1)} %bitcast.15.att_hbm, bf16[512,2048]{1,0:T(8,128)(2,1)} %own_hbm.1, bf16[512,2048]{1,0:T(8,128)(2,1)} %collective-permute-done.4.peer_hbm), custom_call_target="tpu_custom_call" | custom-call | flops 536870912 | bytes 6291456 | tf_op jit(solution)/shard_map/project/pallas_call | solution.py:175
  69.4 12.3 %collective-permute-done.5.far_hbm = bf16[128,2048]{1,0:T(8,128)(2,1)} collective-permute-done((bf16[128,2048]{1,0:T(8,128)(2,1)}, bf16[128,2048]{1,0:T(8,128)(2,1)}, u32[]{:S(2)}, u32[]{:S(2)}) %collective-permute-start.5) | collective-permute-done | bytes 524320 | tf_op jit(solution)/shard_map/ppermute | solution.py:648
  81.7 2.7 %add_and_norm.1 = (f32[128,2048]{1,0:T(8,128)}, bf16[128,2048]{1,0:T(8,128)(2,1)}) custom-call(s32[1]{0:T(128)} %bitcast.core, bf16[256,2048]{1,0:T(8,128)(2,1)} %hidden_hbm.1, f32[128,2048]{1,0:T(8,128)} %get-tuple-element.29.near_hbm, bf16[128,2048]{1,0:T(8,128)(2,1)} %collective-permute-done.5.far_hbm, f32[1,2048]{1,0:T(1,128)} %bitcast.68), custom_call_target="tpu_custom_call" | custom-call | flops 2097152 | bytes 4194304 | tf_op jit(solution)/shard_map/add_and_norm/pallas_call | solution.py:246
  90.0 3.4 %gather_rows.1 = bf16[768,2048]{1,0:T(8,128)(2,1)} custom-call(bf16[768,256]{1,0:T(8,128)(2,1)} %fusion.3.select_hbm, bf16[128,2048]{1,0:T(8,128)(2,1)} %get-tuple-element.31.own_hbm, bf16[128,2048]{1,0:T(8,128)(2,1)} %copy-done.6), custom_call_target="tpu_custom_call" | custom-call | flops 805306368 | bytes 5242880 | tf_op jit(solution)/shard_map/gather_rows/pallas_call | solution.py:302
  93.5 2.6 %maximum_select_fusion = bf16[256,2048]{1,0:T(8,128)(2,1)} fusion(bf16[128,2048]{1,0:T(8,128)(2,1)} %copy-done.6, bf16[128,2048]{1,0:T(8,128)(2,1)S(1)} %copy-done.5, pred[]{:T(512)S(6)} %eq.102), kind=kLoop, calls=%fused_computation.9 | loop fusion | flops 4718592 | bytes 2097153 | tf_op jit(solution)/shard_map/jit(_where)/select_n | solution.py:671
  96.1 5.5 %all-to-all-start.3 = ((bf16[32,24,2048]{2,1,0:T(8,128)(2,1)}), bf16[32,24,2048]{2,1,0:T(8,128)(2,1)}, u32[]{:S(2)}, u32[]{:S(2)}) async-start(bf16[32,24,2048]{2,1,0:T(8,128)(2,1)} %bitcast.62), calls=%async_computation.3 | async-start | bytes 6291456 | tf_op jit(solution)/shard_map/all_to_all | solution.py:677
  108.7 4.7 %fusion.1 = f32[256,2,704]{0,2,1:T(8,128)S(1)} fusion(bf16[2048,2,704]{0,2,1:T(8,128)(2,1)} %param.24, bf16[256,2048]{1,0:T(8,128)(2,1)} %maximum_select_fusion), kind=kOutput, calls=%fused_computation.10 | convolution fusion | flops 1476395008 | bytes 8257536 | tf_op jit(solution)/shard_map/td,dgf->tgf/dot_general | solution.py:684
  115.8 30.4 %all-to-all-done.3 = bf16[32,24,2048]{2,1,0:T(8,128)(2,1)} async-done(((bf16[32,24,2048]{2,1,0:T(8,128)(2,1)}), bf16[32,24,2048]{2,1,0:T(8,128)(2,1)}, u32[]{:S(2)}, u32[]{:S(2)}) %all-to-all-start.3) | async-done | bytes 3145760 | tf_op jit(solution)/shard_map/all_to_all | solution.py:677
  147.1 12.2 %experts.1 = bf16[4,768,512]{2,1,0:T(8,128)(2,1)} custom-call(bf16[768,2048]{1,0:T(8,128)(2,1)} %bitcast.22.x_hbm, bf16[2,352,2048]{2,1,0:T(8,128)(2,1)} %bitcast.72, bf16[2,352,2048]{2,1,0:T(8,128)(2,1)} %collective-permute-done.7.both_peer, bf16[352,2048]{1,0:T(8,128)(2,1)} %bitcast.74, bf16[352,2048]{1,0:T(8,128)(2,1)} %collective-permute-done.8.down_peer), custom_call_target="tpu_custom_call" | custom-call | flops 6643777536 | bytes 15728640 | tf_op jit(solution)/shard_map/experts/pallas_call | solution.py:424
  159.4 8.7 %all-to-all-start.4 = ((bf16[128,24,512]{2,1,0:T(8,128)(2,1)}), bf16[128,24,512]{2,1,0:T(8,128)(2,1)}, u32[]{:S(2)}, u32[]{:S(2)}) async-start(bf16[128,24,512]{2,1,0:T(8,128)(2,1)} %bitcast.63), calls=%async_computation.4 | async-start | bytes 6291456 | tf_op jit(solution)/shard_map/all_to_all | solution.py:704
  187.2 2.0 convert_add_fusion.1.shared_hbm
  189.2 20.5 %all-to-all-done.4 = bf16[128,24,512]{2,1,0:T(8,128)(2,1)} async-done(((bf16[128,24,512]{2,1,0:T(8,128)(2,1)}), bf16[128,24,512]{2,1,0:T(8,128)(2,1)}, u32[]{:S(2)}, u32[]{:S(2)}) %all-to-all-start.4) | async-done | bytes 3145760 | tf_op jit(solution)/shard_map/all_to_all | solution.py:704
  209.7 4.5 %combine.1 = bf16[256,512]{1,0:T(8,128)(2,1)} custom-call(s32[1]{0:T(128)} %bitcast.core, bf16[256,1536]{1,0:T(8,128)(2,1)} %copy-done.1, bf16[256,1536]{1,0:T(8,128)(2,1)} %copy-done.2, bf16[2,1536,512]{2,1,0:T(8,128)(2,1)} %bitcast.28.back_hbm, f32[128,512]{1,0:T(8,128)} %get-tuple-element.49.mine_hbm, f32[128,512]{1,0:T(8,128)} %collective-permute-done.10.peers_hbm, ...), custom_call_target="tpu_custom_call" | custom-call | flops 1610612736 | bytes 7340032 | tf_op jit(solution)/shard_map/combine/pallas_call | solution.py:491
  (117 shorter events, 48.4 us)
Async XLA Ops:
  0.6 112.8 %copy-start = (bf16[704,2048]{1,0:T(8,128)(2,1)S(1)}, bf16[704,2048]{1,0:T(8,128)(2,1)}, u32[]{:S(2)}) copy-start(bf16[704,2048]{1,0:T(8,128)(2,1)} %param.25) | copy-start | bytes 8650756
  0.6 8.7 %copy-start.9 = (bf16[256,512]{1,0:T(8,128)(2,1)S(1)}, bf16[256,512]{1,0:T(8,128)(2,1)}, u32[]{:S(2)}) copy-start(bf16[256,512]{1,0:T(8,128)(2,1)} %param.18) | copy-start | bytes 786436
  0.7 7.7 %copy-start.13 = (s32[1024]{0:T(1024)S(1)}, s32[1024]{0:T(1024)}, u32[]{:S(2)}) copy-start(s32[1024]{0:T(1024)} %param.29) | copy-start | bytes 12292
  0.7 62.4 %collective-permute-start.4 = (bf16[512,2048]{1,0:T(8,128)(2,1)}, bf16[512,2048]{1,0:T(8,128)(2,1)}, u32[]{:S(2)}, u32[]{:S(2)}) collective-permute-start(bf16[512,2048]{1,0:T(8,128)(2,1)} %own_hbm.1), channel_id=1, source_target_pairs={{0,32},{32,0},{64,96},{96,64},{1,33},{33,1},{65,97},{97,65},{2,34}... | collective-permute-start | bytes 6291464 | tf_op jit(solution)/shard_map/ppermute | solution.py:578
  1.9 7.8 %copy-start.10 = (bf16[256,512]{1,0:T(8,128)(2,1)S(1)}, bf16[256,512]{1,0:T(8,128)(2,1)}, u32[]{:S(2)}) copy-start(bf16[256,512]{1,0:T(8,128)(2,1)} %param.17) | copy-start | bytes 786436
  3.8 14.8 %all-to-all-start = ((bf16[4,256,256]{2,1,0:T(8,128)(2,1)}), bf16[4,256,256]{2,1,0:T(8,128)(2,1)}, u32[]{:S(2)}, u32[]{:S(2)}) async-start(bf16[4,256,256]{2,1,0:T(8,128)(2,1)} %pad_maximum_fusion), calls=%async_computation | async-start | bytes 1048576 | tf_op jit(solution)/shard_map/all_to_all | solution.py:590
  9.4 21.5 %copy-start.12 = (s32[8192]{0:T(1024)S(1)}, s32[8192]{0:T(1024)}, u32[]{:S(2)}) copy-start(s32[8192]{0:T(1024)} %param.19) | copy-start | bytes 98308
  18.6 27.0 %collective-permute-start.3 = (bf16[4,256,256]{2,1,0:T(8,128)(2,1)}, bf16[4,256,256]{2,1,0:T(8,128)(2,1)}, u32[]{:S(2)}, u32[]{:S(2)}) collective-permute-start(bf16[4,256,256]{2,1,0:T(8,128)(2,1)} %all-to-all-done.own_hbm), channel_id=1, source_target_pairs={{0,4},{1,5},{2,6},{3,7},{4,8},{5,9},{6,10},{7,11},{8,12},{9,13},{1... | collective-permute-start | bytes 1572872 | tf_op jit(solution)/shard_map/ppermute | solution.py:615
  25.2 20.4 %all-to-all-start.1 = ((bf16[128,2,1024]{2,1,0:T(2,128)(2,1)}), bf16[128,2,1024]{2,1,0:T(2,128)(2,1)S(1)}, u32[]{:S(2)}, u32[]{:S(2)}) async-start(bf16[128,2,1024]{2,1,0:T(2,128)(2,1)} %reshape.134), calls=%async_computation.1 | async-start | bytes 1048576 | tf_op jit(solution)/shard_map/all_to_all | solution.py:614
  32.4 8.4 %collective-permute-start = (bf16[256,128]{1,0:T(8,128)(2,1)S(1)}, bf16[256,128]{1,0:T(8,128)(2,1)S(1)}, u32[]{:S(2)}, u32[]{:S(2)}) collective-permute-start(bf16[256,128]{1,0:T(8,128)(2,1)S(1)} %get-tuple-element.57), channel_id=1, source_target_pairs={{0,1},{1,2},{2,3},{3,0},{4,5},{5,6},{6,7},{7,4},{8,9},{9,10},{10,1... | collective-permute-start | bytes 196616 | tf_op jit(solution)/shard_map/ppermute | solution.py:600
  33.4 9.3 %collective-permute-start.1 = (bf16[256,128]{1,0:T(8,128)(2,1)S(1)}, bf16[256,128]{1,0:T(8,128)(2,1)S(1)}, u32[]{:S(2)}, u32[]{:S(2)}) collective-permute-start(bf16[256,128]{1,0:T(8,128)(2,1)S(1)} %get-tuple-element.56), channel_id=1, source_target_pairs={{0,2},{1,3},{2,0},{3,1},{4,6},{5,7},{6,4},{7,5},{8,10},{9,11},{10,... | collective-permute-start | bytes 196616 | tf_op jit(solution)/shard_map/ppermute | solution.py:600
  36.2 6.6 %collective-permute-start.2 = (bf16[256,128]{1,0:T(8,128)(2,1)S(1)}, bf16[256,128]{1,0:T(8,128)(2,1)S(1)}, u32[]{:S(2)}, u32[]{:S(2)}) collective-permute-start(bf16[256,128]{1,0:T(8,128)(2,1)S(1)} %get-tuple-element.55), channel_id=1, source_target_pairs={{0,3},{1,0},{2,1},{3,2},{4,7},{5,4},{6,5},{7,6},{8,11},{9,8},{10,9... | collective-permute-start | bytes 196616 | tf_op jit(solution)/shard_map/ppermute | solution.py:600
  45.6 21.8 %copy-start.7 = (bf16[128,2,1024]{2,1,0:T(2,128)(2,1)}, bf16[128,2,1024]{2,1,0:T(2,128)(2,1)S(1)}, u32[]{:S(2)}) copy-start(bf16[128,2,1024]{2,1,0:T(2,128)(2,1)S(1)} %all-to-all-done.1) | copy-start | bytes 1572868
  52.0 11.0 %all-to-all-start.2 = ((bf16[8,128,128]{2,1,0:T(8,128)(2,1)}), bf16[8,128,128]{2,1,0:T(8,128)(2,1)}, u32[]{:S(2)}, u32[]{:S(2)}) async-start(bf16[8,128,128]{2,1,0:T(8,128)(2,1)} %bitcast.64), calls=%async_computation.2 | async-start | bytes 524288 | tf_op jit(solution)/shard_map/all_to_all | solution.py:638
  67.4 14.4 %collective-permute-start.5 = (bf16[128,2048]{1,0:T(8,128)(2,1)}, bf16[128,2048]{1,0:T(8,128)(2,1)}, u32[]{:S(2)}, u32[]{:S(2)}) collective-permute-start(bf16[128,2048]{1,0:T(8,128)(2,1)} %get-tuple-element.30), channel_id=1, source_target_pairs={{0,64},{64,0},{32,96},{96,32},{1,65},{65,1},{33,97},{97,33},{2,66}... | collective-permute-start | bytes 1572872 | tf_op jit(solution)/shard_map/ppermute | solution.py:648
  84.5 4.8 %collective-permute-start.6 = (bf16[128,2048]{1,0:T(8,128)(2,1)}, bf16[128,2048]{1,0:T(8,128)(2,1)S(1)}, u32[]{:S(2)}, u32[]{:S(2)}) collective-permute-start(bf16[128,2048]{1,0:T(8,128)(2,1)} %get-tuple-element.31.own_hbm), channel_id=1, source_target_pairs={{0,32},{32,0},{64,96},{96,64},{1,33},{33,1},{65,97},{97,65},{2,34}... | collective-permute-start | bytes 1572872 | tf_op jit(solution)/shard_map/ppermute | solution.py:652
  96.1 8.1 %copy-start.8 = (bf16[128,2,1024]{2,1,0:T(2,128)(2,1)S(1)}, bf16[128,2,1024]{2,1,0:T(2,128)(2,1)}, u32[]{:S(2)}) copy-start(bf16[128,2,1024]{2,1,0:T(2,128)(2,1)} %copy-done.7) | copy-start | bytes 1572868
  96.1 50.1 %all-to-all-start.3 = ((bf16[32,24,2048]{2,1,0:T(8,128)(2,1)}), bf16[32,24,2048]{2,1,0:T(8,128)(2,1)}, u32[]{:S(2)}, u32[]{:S(2)}) async-start(bf16[32,24,2048]{2,1,0:T(8,128)(2,1)} %bitcast.62), calls=%async_computation.3 | async-start | bytes 6291456 | tf_op jit(solution)/shard_map/all_to_all | solution.py:677
  101.6 45.5 %collective-permute-start.7 = (bf16[2,352,2048]{2,1,0:T(8,128)(2,1)}, bf16[2,352,2048]{2,1,0:T(8,128)(2,1)}, u32[]{:S(2)}, u32[]{:S(2)}) collective-permute-start(bf16[2,352,2048]{2,1,0:T(8,128)(2,1)} %bitcast.71), channel_id=1, source_target_pairs={{0,32},{32,0},{64,96},{96,64},{1,33},{33,1},{65,97},{97,65},{2,34}... | collective-permute-start | bytes 8650760 | tf_op jit(solution)/shard_map/ppermute | solution.py:579
  101.9 45.3 %collective-permute-start.8 = (bf16[352,2048]{1,0:T(8,128)(2,1)}, bf16[352,2048]{1,0:T(8,128)(2,1)}, u32[]{:S(2)}, u32[]{:S(2)}) collective-permute-start(bf16[352,2048]{1,0:T(8,128)(2,1)} %bitcast.73), channel_id=1, source_target_pairs={{0,32},{32,0},{64,96},{96,64},{1,33},{33,1},{65,97},{97,65},{2,34}... | collective-permute-start | bytes 4325384 | tf_op jit(solution)/shard_map/ppermute | solution.py:580
  146.2 13.2 %collective-permute-start.9 = (bf16[256,1024]{1,0:T(8,128)(2,1)S(1)}, bf16[256,1024]{1,0:T(8,128)(2,1)}, u32[]{:S(2)}, u32[]{:S(2)}) collective-permute-start(bf16[256,1024]{1,0:T(8,128)(2,1)S(1)} %dynamic-slice_convert_fusion), channel_id=1, source_target_pairs={{0,64},{64,0},{32,96},{96,32},{1,65},{65,1},{33,97},{97,33},{2,66}... | collective-permute-start | bytes 1572872 | tf_op jit(solution)/shard_map/ppermute | solution.py:699
  159.4 50.3 %all-to-all-start.4 = ((bf16[128,24,512]{2,1,0:T(8,128)(2,1)}), bf16[128,24,512]{2,1,0:T(8,128)(2,1)}, u32[]{:S(2)}, u32[]{:S(2)}) async-start(bf16[128,24,512]{2,1,0:T(8,128)(2,1)} %bitcast.63), calls=%async_computation.4 | async-start | bytes 6291456 | tf_op jit(solution)/shard_map/all_to_all | solution.py:704
  181.1 6.1 %collective-permute-start.11 = (bf16[256,512]{1,0:T(8,128)(2,1)}, bf16[256,512]{1,0:T(8,128)(2,1)}, u32[]{:S(2)}, u32[]{:S(2)}) collective-permute-start(bf16[256,512]{1,0:T(8,128)(2,1)} %dynamic-slice_convert_fusion.1), channel_id=1, source_target_pairs={{0,32},{32,0},{64,96},{96,64},{1,33},{33,1},{65,97},{97,65},{2,34}... | collective-permute-start | bytes 786440 | tf_op jit(solution)/shard_map/ppermute | solution.py:712
  181.9 7.3 %collective-permute-start.10 = (f32[128,512]{1,0:T(8,128)}, f32[128,512]{1,0:T(8,128)}, u32[]{:S(2)}, u32[]{:S(2)}) collective-permute-start(f32[128,512]{1,0:T(8,128)} %get-tuple-element.48), channel_id=1, source_target_pairs={{0,32},{32,0},{64,96},{96,64},{1,33},{33,1},{65,97},{97,65},{2,34}... | collective-permute-start | bytes 786440 | tf_op jit(solution)/shard_map/ppermute | solution.py:717
  (10 other events, 34.3 us)

commit v4 on v3

--- a/solution.py
+++ b/solution.py
@@ -356,76 +356,95 @@
 
 
 def expert_kernel(
-    x_hbm, both_own, both_peer, down_own, down_peer, out_hbm, x, gate, up, down, act, out, sems, out_sems
+    x_hbm, both_own, both_peer, down_own, down_peer, out_hbm,
+    x, gate, up, down, act, out, x_sems, sems, down_sems, out_sems,
 ):
     hidden = both_own.shape[1]
     rows = x.shape[0]
     groups, _, width = out.shape
-    block = rows // 2
-    first = pl.ds(0, hidden)
-    second = pl.ds(hidden, hidden)
-    top_rows, low_rows = pl.ds(0, block), pl.ds(block, block)
-    copies = [
-        pltpu.make_async_copy(x_hbm.at[top_rows], x.at[top_rows], sems.at[0]),
-        pltpu.make_async_copy(both_own.at[0], gate.at[first], sems.at[1]),
-        pltpu.make_async_copy(both_peer.at[0], gate.at[second], sems.at[2]),
-        pltpu.make_async_copy(both_own.at[1], up.at[first], sems.at[3]),
-        pltpu.make_async_copy(both_peer.at[1], up.at[second], sems.at[4]),
-        pltpu.make_async_copy(x_hbm.at[low_rows], x.at[low_rows], sems.at[5]),
-        pltpu.make_async_copy(down_own, down.at[first], sems.at[6]),
-        pltpu.make_async_copy(down_peer, down.at[second], sems.at[7]),
-    ]
-    for copy in copies:
+    parts = 3
+    block = rows // parts
+    step = 256
+    bounds = [(lo, min(lo + step, 2 * hidden)) for lo in range(0, 2 * hidden, step)]
+    x_copies = [
+        pltpu.make_async_copy(
+            x_hbm.at[pl.ds(m * block, block)], x.at[pl.ds(m * block, block)], x_sems.at[m]
+        )
+        for m in range(parts)
+    ]
+    chunks = []
+    for n, (lo, hi) in enumerate(bounds):
+        copies = []
+        for j, (source, start, stop) in enumerate(
+            (
+                (both_own, lo, min(hi, hidden)),
+                (both_peer, max(lo, hidden) - hidden, hi - hidden),
+            )
+        ):
+            if stop <= start:
+                continue
+            shift = hidden * j
+            for k, target in enumerate((gate, up)):
+                copies.append(
+                    pltpu.make_async_copy(
+                        source.at[k, pl.ds(start, stop - start)],
+                        target.at[pl.ds(start + shift, stop - start)],
+                        sems.at[n, j, k],
+                    )
+                )
+        chunks.append(copies)
+    down_copies = [
+        pltpu.make_async_copy(source, down.at[pl.ds(j * hidden, hidden)], down_sems.at[j])
+        for j, source in enumerate((down_own, down_peer))
+    ]
+    for copy in [x_copies[0]] + chunks[0] + x_copies[1:]:
+        copy.start()
+    for copies in chunks[1:]:
+        for copy in copies:
+            copy.start()
+    for copy in down_copies:
         copy.start()
     contract = (((1,), (1,)), ((), ()))
-    for copy in copies[:3]:
+    for n, (lo, hi) in enumerate(bounds):
+        for copy in chunks[n]:
+            copy.wait()
+        for m in range(parts):
+            here = pl.ds(m * block, block)
+            if n == 0:
+                x_copies[m].wait()
+            left = x[here, :]
+            g = lax.dot_general(left, gate[lo:hi, :], contract, preferred_element_type=F32)
+            u = lax.dot_general(left, up[lo:hi, :], contract, preferred_element_type=F32)
+            act[here, lo:hi] = (g / (1.0 + jnp.exp(-g)) * u).astype(BF)
+    for copy in down_copies:
         copy.wait()
-    for m in range(2):
-        here = pl.ds(m * block, block)
-        if m == 1:
-            copies[5].wait()
-        left = x[here, :]
-        g = lax.dot_general(left, gate[...], contract, preferred_element_type=F32)
-        if m == 0:
-            copies[3].wait()
-            copies[4].wait()
-        u = lax.dot_general(left, up[...], contract, preferred_element_type=F32)
-        act[here, :] = (g / (1.0 + jnp.exp(-g)) * u).astype(BF)
-
-    for copy in copies[6:]:
-        copy.wait()
-
-    @pl.loop(0, 2)
-    def _(m):
-        here = pl.ds(pl.multiple_of(m * block, block), block)
-        left = act[here, :]
-        for i in range(groups):
+    stores = []
+    for i in range(groups):
+        for m in range(parts):
+            here = pl.ds(m * block, block)
             result = jnp.dot(
-                left, down[:, i * width : (i + 1) * width], preferred_element_type=F32
+                act[here, :], down[:, i * width : (i + 1) * width], preferred_element_type=F32
             )
             out[i, here, :] = result.astype(BF)
-            pltpu.make_async_copy(
+            store = pltpu.make_async_copy(
                 out.at[i, here], out_hbm.at[i, here], out_sems.at[m, i]
-            ).start()
-
-    for m in range(2):
-        here = pl.ds(m * block, block)
-        for i in range(groups):
-            pltpu.make_async_copy(
-                out.at[i, here], out_hbm.at[i, here], out_sems.at[m, i]
-            ).wait()
+            )
+            store.start()
+            stores.append(store)
+    for store in stores:
+        store.wait()
 
 
 def experts(x, both_own, both_peer, down_own, down_peer, groups):
     rows, depth = x.shape
     hidden, width = down_own.shape
     column_width = width // groups
-    anywhere = pl.BlockSpec(memory_space=pltpu.HBM)
+    hbm = pl.BlockSpec(memory_space=pltpu.HBM)
     return pl.pallas_call(
         expert_kernel,
         out_shape=jax.ShapeDtypeStruct((groups, rows, column_width), BF),
-        in_specs=[anywhere] * 5,
-        out_specs=anywhere,
+        in_specs=[hbm] * 5,
+        out_specs=hbm,
         scratch_shapes=[
             pltpu.VMEM((rows, depth), BF),
             pltpu.VMEM((2 * hidden, depth), BF),
@@ -433,8 +452,10 @@
             pltpu.VMEM((2 * hidden, width), BF),
             pltpu.VMEM((rows, 2 * hidden), BF),
             pltpu.VMEM((groups, rows, column_width), BF),
-            pltpu.SemaphoreType.DMA((8,)),
-            pltpu.SemaphoreType.DMA((2, groups)),
+            pltpu.SemaphoreType.DMA((3,)),
+            pltpu.SemaphoreType.DMA((pl.cdiv(2 * hidden, 256), 2, 2)),
+            pltpu.SemaphoreType.DMA((2,)),
+            pltpu.SemaphoreType.DMA((3, groups)),
         ],
         compiler_params=pltpu.CompilerParams(vmem_limit_bytes=60 << 20),
         cost_estimate=pl.CostEstimate(
@@ -451,30 +472,38 @@
     high, low, back, mine, peers, shared, sems,
 ):
     rows = mine.shape[0]
-    pairs = (
-        (high_hbm, high),
-        (back_hbm.at[0], back.at[0]),
-        (low_hbm, low),
-        (back_hbm.at[1], back.at[1]),
-        (shared_hbm, shared),
-        (mine_hbm, mine),
-        (peers_hbm, peers),
-    )
+    chips, depth = back.shape[0], back.shape[1]
+    block = depth // CORES
+    pieces = [(chip, pl.ds(c * block, block)) for chip in range(chips) for c in range(CORES)]
     copies = [
-        pltpu.make_async_copy(source, target, sems.at[i])
-        for i, (source, target) in enumerate(pairs)
-    ]
-    for copy in copies:
+        pltpu.make_async_copy(back_hbm.at[chip, here], back.at[chip, here], sems.at[i])
+        for i, (chip, here) in enumerate(pieces)
+    ]
+    rest = [
+        pltpu.make_async_copy(source, target, sems.at[len(pieces) + i])
+        for i, (source, target) in enumerate(
+            (
+                (high_hbm, high),
+                (low_hbm, low),
+                (shared_hbm, shared),
+                (mine_hbm, mine),
+                (peers_hbm, peers),
+            )
+        )
+    ]
+    for copy in [rest[0], copies[0], rest[1]] + copies[1:] + rest[2:]:
         copy.start()
-    copies[0].wait()
-    copies[1].wait()
-    total = jnp.dot(high[...], back[0], preferred_element_type=F32)
-    copies[2].wait()
-    total += jnp.dot(low[...], back[0], preferred_element_type=F32)
-    copies[3].wait()
-    total += jnp.dot(high[...], back[1], preferred_element_type=F32)
-    total += jnp.dot(low[...], back[1], preferred_element_type=F32)
-    for copy in copies[4:]:
+    total = None
+    for i, (copy, (chip, here)) in enumerate(zip(copies, pieces)):
+        if i == 0:
+            rest[0].wait()
+        copy.wait()
+        for side in (high, low):
+            if i == 0 and side is low:
+                rest[1].wait()
+            part = jnp.dot(side[:, here], back[chip, here], preferred_element_type=F32)
+            total = part if total is None else total + part
+    for copy in rest[2:]:
         copy.wait()
     total += shared[...]
     first = core[0] == 0
@@ -486,15 +515,16 @@
 
 def combine(core, high, low, returned, mine, peers, shared):
     hbm = pl.BlockSpec(memory_space=pltpu.HBM)
+    vmem = pl.BlockSpec(memory_space=pltpu.VMEM)
     rows, width = shared.shape
     operands = (high, low, returned, mine, peers, shared)
     return pl.pallas_call(
         combine_kernel,
         out_shape=jax.ShapeDtypeStruct((rows, width), BF),
         in_specs=[pl.BlockSpec(memory_space=pltpu.SMEM)] + [hbm] * 6,
-        out_specs=pl.BlockSpec(memory_space=pltpu.VMEM),
+        out_specs=vmem,
         scratch_shapes=[pltpu.VMEM(o.shape, o.dtype) for o in operands]
-        + [pltpu.SemaphoreType.DMA((7,))],
+        + [pltpu.SemaphoreType.DMA((9,))],
         compiler_params=pltpu.CompilerParams(vmem_limit_bytes=60 << 20),
         cost_estimate=pl.CostEstimate(
             flops=8 * rows * width * high.shape[1], bytes_accessed=7 << 20, transcendentals=0
@@ -590,7 +620,15 @@
     own = lax.all_to_all(
         packed, "tok", split_axis=0, concat_axis=0, tiled=True, axis_index_groups=row_groups
     )
-    queries, own = lax.optimization_barrier((queries, own))
+    span = ROW * tok_rows
+    base = (tok_index // ROW) * span
+    padded_ids = jnp.concatenate([jnp.full((span,), -1, jnp.int32), request_ids], 0)
+    window_ids = lax.dynamic_slice_in_dim(padded_ids, base, 2 * span, 0)
+    ids_row = window_ids[None, :]
+    ids_col = jnp.broadcast_to(window_ids[span:, None], (span, HD))
+    queries, own, ids_row, ids_col = lax.optimization_barrier(
+        (queries, own, ids_row, ids_col)
+    )
     place_in_row = tok_index % ROW
     query_parts = []
     for step in range(ROW):
@@ -610,18 +648,9 @@
     slots_all = page_slots.reshape(tok_count, tok_rows // PAGE)
     owner_all = slots_all // (tok_rows // PAGE)
     pieces = page_pieces(keys, values, owner_all, tok_count, head_count, tok_index)
-    pieces, own = lax.optimization_barrier((pieces, own))
-    landed = lax.all_to_all(pieces, BOTH, split_axis=0, concat_axis=0, tiled=True)
     past = lax.ppermute(
         own, "tok", [(s, s + ROW) for s in range(tok_count - ROW)]
     )
-    span = ROW * tok_rows
-    base = (tok_index // ROW) * span
-    padded_ids = jnp.concatenate([jnp.full((span,), -1, jnp.int32), request_ids], 0)
-    window_ids = lax.dynamic_slice_in_dim(padded_ids, base, 2 * span, 0)
-    ids_row = window_ids[None, :]
-    ids_col = jnp.broadcast_to(window_ids[span:, None], (span, HD))
-    past, landed = lax.optimization_barrier((past, landed))
     attended = attention(
         place_in_row.reshape(1), ids_col, ids_row, jnp.stack(query_parts, 0), own, past
     )
@@ -643,14 +672,6 @@
         tiled=True,
         axis_index_groups=core_groups,
     ).reshape(CORES, ROW, half, HD)
-    core_ref = core.reshape(1)
-    projected, projected_low = project(core_ref, gathered, out_proj, out_peer)
-    projected_far = lax.ppermute(projected_low, "head", CROSS)
-    resid, normed_own = add_and_norm(
-        core_ref, hidden_in, projected, projected_far, norm_gain[None, :]
-    )
-    normed_peer = lax.ppermute(normed_own, "head", INTRA)
-
     expert_ids = jnp.arange(EXPERTS, dtype=jnp.int32)
     named = routes[:, :, None] == expert_ids[None, None, :]
     onehot = jnp.sum(named.astype(F32), 1)
@@ -665,15 +686,26 @@
     place = jnp.arange(slots_core, dtype=jnp.int32) * CORES
     select = (rank_rel[:, None, :] == (place + core)[None, :, None]).astype(BF)
     select = select.reshape(EXPERTS * slots_core, tok_rows)
+    core_ref = core.reshape(1)
+    projected, projected_low = project(core_ref, gathered, out_proj, out_peer)
+    projected_far = lax.ppermute(projected_low, "head", CROSS)
+    pieces, _ = lax.optimization_barrier((pieces, projected_low))
+    landed = lax.all_to_all(pieces, BOTH, split_axis=0, concat_axis=0, tiled=True)
+    projected_far, select, landed = lax.optimization_barrier((projected_far, select, landed))
+    resid, normed_own = add_and_norm(
+        core_ref, hidden_in, projected, projected_far, norm_gain[None, :]
+    )
+    normed_peer = lax.ppermute(normed_own, "head", INTRA)
+
     outgoing = gather_rows(select, normed_own, normed_peer)
-    rank, weight_of, outgoing = lax.optimization_barrier((rank, weight_of, outgoing))
+    rank, weight_of, _ = lax.optimization_barrier((rank, weight_of, outgoing))
     high, low = slot_weights(rank, weight_of, CORES * EXPERTS * slots_core)
+    late_own, late_peer, _ = lax.optimization_barrier((normed_own, normed_peer, outgoing))
     normed_abs = jnp.where(
         core == 0,
-        jnp.concatenate([normed_own, normed_peer], 0),
-        jnp.concatenate([normed_peer, normed_own], 0),
-    )
-    normed_abs, outgoing = lax.optimization_barrier((normed_abs, outgoing))
+        jnp.concatenate([late_own, late_peer], 0),
+        jnp.concatenate([late_peer, late_own], 0),
+    )
     arrived = lax.all_to_all(
         outgoing.reshape(tok_count, slots_core, model_width),
         "tok",

time: 216 us -> 210 us (0.972)
  waiting for transfers between devices: 84.9 us -> 76.3 us
  local copies, waits for them, and re-layouts: 26.9 us -> 29.6 us
  matrix products: 12.3 us -> 14.5 us
    ppermute x1, waiting for transfers between devices: 12.3 us -> 0.01 us  [per_device(): projected_far = lax.ppermute(projected_low, 'head', CROSS)]
    all_to_all x1, waiting for transfers between devices: 2.12 us -> 9.05 us  [per_device(): lax.all_to_all(pieces, BOTH, split_axis=0, concat_axis=0, tiled=True)]
    all_to_all x1, waiting for transfers between devices: 7.56 us -> 4.18 us  [per_device(): lax.all_to_all(packed, 'tok', split_axis=0, concat_axis=0, tiled=True, ax...]
    select_n x1 -> x0, other arithmetic: 2.63 us -> none  [per_device(): jnp.where(core == 0, jnp.concatenate([normed_own, normed_peer], 0), jnp.c...]
    ppermute x3, starting transfers between devices: 5.17 us -> 2.64 us  [per_device(): lax.ppermute(part, 'tok', [(r * ROW + y, r * ROW + (y + step) % ROW) for...]
    unnamed x42 -> x46, local copies, waits for them, and re-layouts: 6.2 us -> 6.81 us
  transfers between devices with their start and end apart: 17 -> 17, of which waited for: 8 -> 9; matrix products, arithmetic and copies ran while one was open for 21% -> 25% of each run, Pallas kernels for 9% -> 9%
where the time goes in v4:
time: 210 us; the launch traced here: 209 us
  waiting for transfers between devices  76.3 us (36%)
  starting transfers between devices  42.4 us (20%)
  Pallas kernels  32.9 us (16%)
  local copies, waits for them, and re-layouts  29.6 us (14%)
  matrix products  14.5 us (7%)
  other arithmetic  11.8 us (6%)
    all_to_all x1, waiting for transfers between devices, per_device(): lax.all_to_all(outgoing.reshape(tok_count, slots_core, model_width), 'tok...  29.9 us
    all_to_all x1, waiting for transfers between devices, per_device(): lax.all_to_all(partial, BOTH, split_axis=0, concat_axis=0, tiled=True)  20.5 us
    pallas_call x1, Pallas kernels, experts(): pl.pallas_call(expert_kernel, out_shape=jax.ShapeDtypeStruct((groups, row...  11.8 us
    all_to_all x1, starting transfers between devices, per_device(): lax.all_to_all(partial, BOTH, split_axis=0, concat_axis=0, tiled=True)  9.85 us
    all_to_all x1, waiting for transfers between devices, per_device(): lax.all_to_all(pieces, BOTH, split_axis=0, concat_axis=0, tiled=True)  9.05 us
    all_to_all x1, starting transfers between devices, per_device(): lax.all_to_all(pieces, BOTH, split_axis=0, concat_axis=0, tiled=True)  7.65 us
    unnamed x46, local copies, waits for them, and re-layouts  6.81 us
    all_to_all x1, waiting for transfers between devices, per_device(): lax.all_to_all(attended.reshape(CORES * ROW, half, HD), BOTH, split_axis=...  6.66 us
  transfers between devices with their start and end apart: 17, of which 9 were waited for; matrix products, arithmetic and copies ran while one was open for 25% of the time, Pallas kernels for 9%

profile of v4, /device:TPU:0, one launch (start us, length us, event | category | flops | bytes accessed | tf_op | source)
XLA Modules:
  0.0 208.8 jit_solution(2558760379351280919)
XLA Ops:
  3.9 4.5 %all-to-all-start = ((bf16[4,256,256]{2,1,0:T(8,128)(2,1)}), bf16[4,256,256]{2,1,0:T(8,128)(2,1)}, u32[]{:S(2)}, u32[]{:S(2)}) async-start(bf16[4,256,256]{2,1,0:T(8,128)(2,1)} %pad_maximum_fusion), calls=%async_computation | async-start | bytes 1048576 | tf_op jit(solution)/shard_map/all_to_all | solution.py:620
  14.5 4.2 %all-to-all-done.own_hbm = bf16[4,256,256]{2,1,0:T(8,128)(2,1)} async-done(((bf16[4,256,256]{2,1,0:T(8,128)(2,1)}), bf16[4,256,256]{2,1,0:T(8,128)(2,1)}, u32[]{:S(2)}, u32[]{:S(2)}) %all-to-all-start) | async-done | bytes 524320 | tf_op jit(solution)/shard_map/all_to_all | solution.py:620
  19.6 6.6 %collective-permute-start.3 = (bf16[4,256,256]{2,1,0:T(8,128)(2,1)}, bf16[4,256,256]{2,1,0:T(8,128)(2,1)}, u32[]{:S(2)}, u32[]{:S(2)}) collective-permute-start(bf16[4,256,256]{2,1,0:T(8,128)(2,1)} %all-to-all-done.own_hbm), channel_id=1, source_target_pairs={{0,4},{1,5},{2,6},{3,7},{4,8},{5,9},{6,10},{7,11},{8,12},{9,13},{1... | collective-permute-start | bytes 1572872 | tf_op jit(solution)/shard_map/ppermute | solution.py:651
  27.2 1.7 dynamic-slice_bitcast_fusion
  33.5 2.6 %collective-permute-done.1 = bf16[256,128]{1,0:T(8,128)(2,1)} collective-permute-done((bf16[256,128]{1,0:T(8,128)(2,1)}, bf16[256,128]{1,0:T(8,128)(2,1)}, u32[]{:S(2)}, u32[]{:S(2)}) %collective-permute-start.1) | collective-permute-done | bytes 65568 | tf_op jit(solution)/shard_map/ppermute | solution.py:638
  38.9 5.4 %row_attention.1 = bf16[2,4,128,128]{3,2,1,0:T(8,128)(2,1)} custom-call(s32[1]{0:T(128)} %bitcast.1.place, s32[1024,128]{1,0:T(8,128)} %broadcast_in_dim.32.ids_col_hbm, s32[1,2048]{1,0:T(1,128)} %bitcast.66, bf16[4,256,128]{2,1,0:T(8,128)(2,1)} %pad_maximum_fusion.2.query_hbm, bf16[4,256,256]{2,1,0:T(8,128)(2,1)} %all-to-all-done.own_hbm, ...), custom_call_target="tpu_custom_call" | custom-call | flops 671088640 | bytes 3145728 | tf_op jit(solution)/shard_map/row_attention/pallas_call | solution.py:106
  44.4 3.4 %all-to-all-start.1 = ((bf16[8,128,128]{2,1,0:T(8,128)(2,1)}), bf16[8,128,128]{2,1,0:T(8,128)(2,1)S(1)}, u32[]{:S(2)}, u32[]{:S(2)}) async-start(bf16[8,128,128]{2,1,0:T(8,128)(2,1)} %bitcast.64), calls=%async_computation.1 | async-start | bytes 524288 | tf_op jit(solution)/shard_map/all_to_all | solution.py:667
  48.0 6.7 %all-to-all-done.1 = bf16[8,128,128]{2,1,0:T(8,128)(2,1)S(1)} async-done(((bf16[8,128,128]{2,1,0:T(8,128)(2,1)}), bf16[8,128,128]{2,1,0:T(8,128)(2,1)S(1)}, u32[]{:S(2)}, u32[]{:S(2)}) %all-to-all-start.1) | async-done | bytes 262176 | tf_op jit(solution)/shard_map/all_to_all | solution.py:667
  55.4 4.3 %project.1 = (f32[128,2048]{1,0:T(8,128)}, bf16[128,2048]{1,0:T(8,128)(2,1)}) custom-call(s32[1]{0:T(128)} %bitcast.core, bf16[2,4,128,128]{3,2,1,0:T(8,128)(2,1)} %bitcast.63, bf16[512,2048]{1,0:T(8,128)(2,1)} %own_hbm.1, bf16[512,2048]{1,0:T(8,128)(2,1)} %collective-permute-done.4.peer_hbm), custom_call_target="tpu_custom_call" | custom-call | flops 536870912 | bytes 6291456 | tf_op jit(solution)/shard_map/project/pallas_call | solution.py:175
  60.7 7.7 %all-to-all-start.2 = ((bf16[128,2,1024]{2,1,0:T(2,128)(2,1)}), bf16[128,2,1024]{2,1,0:T(2,128)(2,1)S(1)}, u32[]{:S(2)}, u32[]{:S(2)}) async-start(bf16[128,2,1024]{2,1,0:T(2,128)(2,1)} %reshape.136), calls=%async_computation.2 | async-start | bytes 1048576 | tf_op jit(solution)/shard_map/all_to_all | solution.py:693
  71.4 1.7 fusion.3.select_hbm
  73.1 9.0 %all-to-all-done.2 = bf16[128,2,1024]{2,1,0:T(2,128)(2,1)S(1)} async-done(((bf16[128,2,1024]{2,1,0:T(2,128)(2,1)}), bf16[128,2,1024]{2,1,0:T(2,128)(2,1)S(1)}, u32[]{:S(2)}, u32[]{:S(2)}) %all-to-all-start.2) | async-done | bytes 524320 | tf_op jit(solution)/shard_map/all_to_all | solution.py:693
  82.1 2.7 %add_and_norm.1 = (f32[128,2048]{1,0:T(8,128)}, bf16[128,2048]{1,0:T(8,128)(2,1)}) custom-call(s32[1]{0:T(128)} %bitcast.core, bf16[256,2048]{1,0:T(8,128)(2,1)} %hidden_hbm.1, f32[128,2048]{1,0:T(8,128)} %get-tuple-element.32.near_hbm, bf16[128,2048]{1,0:T(8,128)(2,1)} %collective-permute-done.5.far_hbm, f32[1,2048]{1,0:T(1,128)} %bitcast.65), custom_call_target="tpu_custom_call" | custom-call | flops 2097152 | bytes 4194304 | tf_op jit(solution)/shard_map/add_and_norm/pallas_call | solution.py:246
  84.9 2.1 %collective-permute-done.6.peer_hbm = bf16[128,2048]{1,0:T(8,128)(2,1)S(1)} collective-permute-done((bf16[128,2048]{1,0:T(8,128)(2,1)}, bf16[128,2048]{1,0:T(8,128)(2,1)S(1)}, u32[]{:S(2)}, u32[]{:S(2)}) %collective-permute-start.6) | collective-permute-done | bytes 524320 | tf_op jit(solution)/shard_map/ppermute | solution.py:698
  87.9 3.4 %gather_rows.1 = bf16[768,2048]{1,0:T(8,128)(2,1)} custom-call(bf16[768,256]{1,0:T(8,128)(2,1)} %fusion.3.select_hbm, bf16[128,2048]{1,0:T(8,128)(2,1)} %get-tuple-element.39.own_hbm, bf16[128,2048]{1,0:T(8,128)(2,1)} %copy-done.9), custom_call_target="tpu_custom_call" | custom-call | flops 805306368 | bytes 5242880 | tf_op jit(solution)/shard_map/gather_rows/pallas_call | solution.py:302
  91.4 4.8 %all-to-all-start.3 = ((bf16[32,24,2048]{2,1,0:T(8,128)(2,1)}), bf16[32,24,2048]{2,1,0:T(8,128)(2,1)}, u32[]{:S(2)}, u32[]{:S(2)}) async-start(bf16[32,24,2048]{2,1,0:T(8,128)(2,1)} %bitcast.61), calls=%async_computation.3 | async-start | bytes 6291456 | tf_op jit(solution)/shard_map/all_to_all | solution.py:709
  101.6 2.0 fusion.8
  103.7 4.4 %fusion.1 = f32[256,2,704]{0,2,1:T(8,128)S(1)} fusion(bf16[2048,2,704]{0,2,1:T(8,128)(2,1)} %param.24, bf16[128,2048]{1,0:T(8,128)(2,1)S(1)} %copy-done.10, bf16[128,2048]{1,0:T(8,128)(2,1)S(1)} %copy-done.8, pred[]{:T(512)S(6)} %eq.102), kind=kOutput, calls=%fused_computation.10 | convolution fusion | flops 1481113600 | bytes 8257537 | tf_op jit(solution)/shard_map/td,dgf->tgf/dot_general | solution.py:716
  110.5 29.9 %all-to-all-done.3 = bf16[32,24,2048]{2,1,0:T(8,128)(2,1)} async-done(((bf16[32,24,2048]{2,1,0:T(8,128)(2,1)}), bf16[32,24,2048]{2,1,0:T(8,128)(2,1)}, u32[]{:S(2)}, u32[]{:S(2)}) %all-to-all-start.3) | async-done | bytes 3145760 | tf_op jit(solution)/shard_map/all_to_all | solution.py:709
  140.9 11.8 %experts.1 = bf16[4,768,512]{2,1,0:T(8,128)(2,1)} custom-call(bf16[768,2048]{1,0:T(8,128)(2,1)} %bitcast.22.x_hbm, bf16[2,352,2048]{2,1,0:T(8,128)(2,1)} %bitcast.69, bf16[2,352,2048]{2,1,0:T(8,128)(2,1)} %collective-permute-done.7.both_peer, bf16[352,2048]{1,0:T(8,128)(2,1)} %bitcast.71, bf16[352,2048]{1,0:T(8,128)(2,1)} %collective-permute-done.8.down_peer), custom_call_target="tpu_custom_call" | custom-call | flops 6643777536 | bytes 15728640 | tf_op jit(solution)/shard_map/experts/pallas_call | solution.py:443
  152.8 9.8 %all-to-all-start.4 = ((bf16[128,24,512]{2,1,0:T(8,128)(2,1)}), bf16[128,24,512]{2,1,0:T(8,128)(2,1)}, u32[]{:S(2)}, u32[]{:S(2)}) async-start(bf16[128,24,512]{2,1,0:T(8,128)(2,1)} %bitcast.62), calls=%async_computation.4 | async-start | bytes 6291456 | tf_op jit(solution)/shard_map/all_to_all | solution.py:736
  181.7 2.0 convert_add_fusion.1.shared_hbm
  183.7 20.5 %all-to-all-done.4 = bf16[128,24,512]{2,1,0:T(8,128)(2,1)} async-done(((bf16[128,24,512]{2,1,0:T(8,128)(2,1)}), bf16[128,24,512]{2,1,0:T(8,128)(2,1)}, u32[]{:S(2)}, u32[]{:S(2)}) %all-to-all-start.4) | async-done | bytes 3145760 | tf_op jit(solution)/shard_map/all_to_all | solution.py:736
  204.2 4.4 %combine.1 = bf16[256,512]{1,0:T(8,128)(2,1)} custom-call(s32[1]{0:T(128)} %bitcast.core, bf16[256,1536]{1,0:T(8,128)(2,1)} %copy-done.1, bf16[256,1536]{1,0:T(8,128)(2,1)} %copy-done.2, bf16[2,1536,512]{2,1,0:T(8,128)(2,1)} %bitcast.28.back_hbm, f32[128,512]{1,0:T(8,128)} %get-tuple-element.51.mine_hbm, f32[128,512]{1,0:T(8,128)} %collective-permute-done.10.peers_hbm, ...), custom_call_target="tpu_custom_call" | custom-call | flops 1610612736 | bytes 7340032 | tf_op jit(solution)/shard_map/combine/pallas_call | solution.py:521
  (120 shorter events, 51.7 us)
Async XLA Ops:
  0.6 107.5 %copy-start = (bf16[704,2048]{1,0:T(8,128)(2,1)S(1)}, bf16[704,2048]{1,0:T(8,128)(2,1)}, u32[]{:S(2)}) copy-start(bf16[704,2048]{1,0:T(8,128)(2,1)} %param.25) | copy-start | bytes 8650756
  0.7 8.4 %copy-start.13 = (s32[8192]{0:T(1024)S(1)}, s32[8192]{0:T(1024)}, u32[]{:S(2)}) copy-start(s32[8192]{0:T(1024)} %param.19) | copy-start | bytes 98308
  0.7 8.4 %copy-start.15 = (f32[256,4]{0,1:T(4,128)S(1)}, f32[256,4]{0,1:T(4,128)}, u32[]{:S(2)}) copy-start(f32[256,4]{0,1:T(4,128)} %param.28) | copy-start | bytes 12292
  0.7 8.4 %copy-start.16 = (s32[256,4]{0,1:T(4,128)S(1)}, s32[256,4]{0,1:T(4,128)}, u32[]{:S(2)}) copy-start(s32[256,4]{0,1:T(4,128)} %param.27) | copy-start | bytes 12292
  0.7 54.0 %collective-permute-start.4 = (bf16[512,2048]{1,0:T(8,128)(2,1)}, bf16[512,2048]{1,0:T(8,128)(2,1)}, u32[]{:S(2)}, u32[]{:S(2)}) collective-permute-start(bf16[512,2048]{1,0:T(8,128)(2,1)} %own_hbm.1), channel_id=1, source_target_pairs={{0,32},{32,0},{64,96},{96,64},{1,33},{33,1},{65,97},{97,65},{2,34}... | collective-permute-start | bytes 6291464 | tf_op jit(solution)/shard_map/ppermute | solution.py:608
  1.9 10.9 %copy-start.6 = (bf16[256,512]{1,0:T(8,128)(2,1)S(1)}, bf16[256,512]{1,0:T(8,128)(2,1)}, u32[]{:S(2)}) copy-start(bf16[256,512]{1,0:T(8,128)(2,1)} %param.18) | copy-start | bytes 786436
  3.0 23.3 %copy-start.7 = (bf16[256,512]{1,0:T(8,128)(2,1)S(1)}, bf16[256,512]{1,0:T(8,128)(2,1)}, u32[]{:S(2)}) copy-start(bf16[256,512]{1,0:T(8,128)(2,1)} %param.17) | copy-start | bytes 786436
  3.9 14.8 %all-to-all-start = ((bf16[4,256,256]{2,1,0:T(8,128)(2,1)}), bf16[4,256,256]{2,1,0:T(8,128)(2,1)}, u32[]{:S(2)}, u32[]{:S(2)}) async-start(bf16[4,256,256]{2,1,0:T(8,128)(2,1)} %pad_maximum_fusion), calls=%async_computation | async-start | bytes 1048576 | tf_op jit(solution)/shard_map/all_to_all | solution.py:620
  19.6 19.3 %collective-permute-start.3 = (bf16[4,256,256]{2,1,0:T(8,128)(2,1)}, bf16[4,256,256]{2,1,0:T(8,128)(2,1)}, u32[]{:S(2)}, u32[]{:S(2)}) collective-permute-start(bf16[4,256,256]{2,1,0:T(8,128)(2,1)} %all-to-all-done.own_hbm), channel_id=1, source_target_pairs={{0,4},{1,5},{2,6},{3,7},{4,8},{5,9},{6,10},{7,11},{8,12},{9,13},{1... | collective-permute-start | bytes 1572872 | tf_op jit(solution)/shard_map/ppermute | solution.py:651
  28.8 4.6 %collective-permute-start.2 = (bf16[256,128]{1,0:T(8,128)(2,1)}, bf16[256,128]{1,0:T(8,128)(2,1)}, u32[]{:S(2)}, u32[]{:S(2)}) collective-permute-start(bf16[256,128]{1,0:T(8,128)(2,1)} %get-tuple-element.57), channel_id=1, source_target_pairs={{0,3},{1,0},{2,1},{3,2},{4,7},{5,4},{6,5},{7,6},{8,11},{9,8},{10,9... | collective-permute-start | bytes 196616 | tf_op jit(solution)/shard_map/ppermute | solution.py:638
  30.0 6.1 %collective-permute-start.1 = (bf16[256,128]{1,0:T(8,128)(2,1)}, bf16[256,128]{1,0:T(8,128)(2,1)}, u32[]{:S(2)}, u32[]{:S(2)}) collective-permute-start(bf16[256,128]{1,0:T(8,128)(2,1)} %get-tuple-element.58), channel_id=1, source_target_pairs={{0,2},{1,3},{2,0},{3,1},{4,6},{5,7},{6,4},{7,5},{8,10},{9,11},{10,... | collective-permute-start | bytes 196616 | tf_op jit(solution)/shard_map/ppermute | solution.py:638
  31.5 5.8 %collective-permute-start = (bf16[256,128]{1,0:T(8,128)(2,1)}, bf16[256,128]{1,0:T(8,128)(2,1)}, u32[]{:S(2)}, u32[]{:S(2)}) collective-permute-start(bf16[256,128]{1,0:T(8,128)(2,1)} %get-tuple-element.59), channel_id=1, source_target_pairs={{0,1},{1,2},{2,3},{3,0},{4,5},{5,6},{6,7},{7,4},{8,9},{9,10},{10,1... | collective-permute-start | bytes 196616 | tf_op jit(solution)/shard_map/ppermute | solution.py:638
  33.5 14.4 %copy-start.11 = (f32[256,32]{0,1:T(8,128)S(1)}, f32[256,32]{0,1:T(8,128)}, u32[]{:S(2)}) copy-start(f32[256,32]{0,1:T(8,128)} %get-tuple-element.49) | copy-start | bytes 98308
  44.4 10.3 %all-to-all-start.1 = ((bf16[8,128,128]{2,1,0:T(8,128)(2,1)}), bf16[8,128,128]{2,1,0:T(8,128)(2,1)S(1)}, u32[]{:S(2)}, u32[]{:S(2)}) async-start(bf16[8,128,128]{2,1,0:T(8,128)(2,1)} %bitcast.64), calls=%async_computation.1 | async-start | bytes 524288 | tf_op jit(solution)/shard_map/all_to_all | solution.py:667
  59.6 22.5 %collective-permute-start.5 = (bf16[128,2048]{1,0:T(8,128)(2,1)}, bf16[128,2048]{1,0:T(8,128)(2,1)}, u32[]{:S(2)}, u32[]{:S(2)}) collective-permute-start(bf16[128,2048]{1,0:T(8,128)(2,1)} %get-tuple-element.29), channel_id=1, source_target_pairs={{0,64},{64,0},{32,96},{96,32},{1,65},{65,1},{33,97},{97,33},{2,66}... | collective-permute-start | bytes 1572872 | tf_op jit(solution)/shard_map/ppermute | solution.py:691
  60.7 21.4 %all-to-all-start.2 = ((bf16[128,2,1024]{2,1,0:T(2,128)(2,1)}), bf16[128,2,1024]{2,1,0:T(2,128)(2,1)S(1)}, u32[]{:S(2)}, u32[]{:S(2)}) async-start(bf16[128,2,1024]{2,1,0:T(2,128)(2,1)} %reshape.136), calls=%async_computation.2 | async-start | bytes 1048576 | tf_op jit(solution)/shard_map/all_to_all | solution.py:693
  84.8 2.2 %collective-permute-start.6 = (bf16[128,2048]{1,0:T(8,128)(2,1)}, bf16[128,2048]{1,0:T(8,128)(2,1)S(1)}, u32[]{:S(2)}, u32[]{:S(2)}) collective-permute-start(bf16[128,2048]{1,0:T(8,128)(2,1)} %get-tuple-element.39.own_hbm), channel_id=1, source_target_pairs={{0,32},{32,0},{64,96},{96,64},{1,33},{33,1},{65,97},{97,65},{2,34}... | collective-permute-start | bytes 1572872 | tf_op jit(solution)/shard_map/ppermute | solution.py:698
  91.4 49.0 %all-to-all-start.3 = ((bf16[32,24,2048]{2,1,0:T(8,128)(2,1)}), bf16[32,24,2048]{2,1,0:T(8,128)(2,1)}, u32[]{:S(2)}, u32[]{:S(2)}) async-start(bf16[32,24,2048]{2,1,0:T(8,128)(2,1)} %bitcast.61), calls=%async_computation.3 | async-start | bytes 6291456 | tf_op jit(solution)/shard_map/all_to_all | solution.py:709
  96.2 44.7 %collective-permute-start.7 = (bf16[2,352,2048]{2,1,0:T(8,128)(2,1)}, bf16[2,352,2048]{2,1,0:T(8,128)(2,1)}, u32[]{:S(2)}, u32[]{:S(2)}) collective-permute-start(bf16[2,352,2048]{2,1,0:T(8,128)(2,1)} %bitcast.68), channel_id=1, source_target_pairs={{0,32},{32,0},{64,96},{96,64},{1,33},{33,1},{65,97},{97,65},{2,34}... | collective-permute-start | bytes 8650760 | tf_op jit(solution)/shard_map/ppermute | solution.py:609
  96.4 44.4 %collective-permute-start.8 = (bf16[352,2048]{1,0:T(8,128)(2,1)}, bf16[352,2048]{1,0:T(8,128)(2,1)}, u32[]{:S(2)}, u32[]{:S(2)}) collective-permute-start(bf16[352,2048]{1,0:T(8,128)(2,1)} %bitcast.70), channel_id=1, source_target_pairs={{0,32},{32,0},{64,96},{96,64},{1,33},{33,1},{65,97},{97,65},{2,34}... | collective-permute-start | bytes 4325384 | tf_op jit(solution)/shard_map/ppermute | solution.py:610
  140.3 12.4 %collective-permute-start.9 = (bf16[256,1024]{1,0:T(8,128)(2,1)S(1)}, bf16[256,1024]{1,0:T(8,128)(2,1)}, u32[]{:S(2)}, u32[]{:S(2)}) collective-permute-start(bf16[256,1024]{1,0:T(8,128)(2,1)S(1)} %dynamic-slice_convert_fusion), channel_id=1, source_target_pairs={{0,64},{64,0},{32,96},{96,32},{1,65},{65,1},{33,97},{97,33},{2,66}... | collective-permute-start | bytes 1572872 | tf_op jit(solution)/shard_map/ppermute | solution.py:731
  152.8 51.4 %all-to-all-start.4 = ((bf16[128,24,512]{2,1,0:T(8,128)(2,1)}), bf16[128,24,512]{2,1,0:T(8,128)(2,1)}, u32[]{:S(2)}, u32[]{:S(2)}) async-start(bf16[128,24,512]{2,1,0:T(8,128)(2,1)} %bitcast.62), calls=%async_computation.4 | async-start | bytes 6291456 | tf_op jit(solution)/shard_map/all_to_all | solution.py:736
  175.6 6.1 %collective-permute-start.11 = (bf16[256,512]{1,0:T(8,128)(2,1)}, bf16[256,512]{1,0:T(8,128)(2,1)}, u32[]{:S(2)}, u32[]{:S(2)}) collective-permute-start(bf16[256,512]{1,0:T(8,128)(2,1)} %dynamic-slice_convert_fusion.1), channel_id=1, source_target_pairs={{0,32},{32,0},{64,96},{96,64},{1,33},{33,1},{65,97},{97,65},{2,34}... | collective-permute-start | bytes 786440 | tf_op jit(solution)/shard_map/ppermute | solution.py:744
  176.4 7.3 %collective-permute-start.10 = (f32[128,512]{1,0:T(8,128)}, f32[128,512]{1,0:T(8,128)}, u32[]{:S(2)}, u32[]{:S(2)}) collective-permute-start(f32[128,512]{1,0:T(8,128)} %get-tuple-element.50), channel_id=1, source_target_pairs={{0,32},{32,0},{64,96},{96,64},{1,33},{33,1},{65,97},{97,65},{2,34}... | collective-permute-start | bytes 786440 | tf_op jit(solution)/shard_map/ppermute | solution.py:749
  (12 other events, 37.2 us)

commit v5 on v4

--- a/solution.py
+++ b/solution.py
@@ -22,16 +22,44 @@
 CROSS = [(0, 2), (2, 0), (1, 3), (3, 1)]
 
 
+def pack_kernel(keys, values, out, sems):
+    copies = []
+    for i in range(out.shape[0]):
+        for j, part in enumerate((keys, values)):
+            copy = pltpu.make_async_copy(
+                part.at[:, pl.ds(i * HD, HD)], out.at[i, :, pl.ds(j * HD, HD)], sems.at[i, j]
+            )
+            copy.start()
+            copies.append(copy)
+    for copy in copies:
+        copy.wait()
+
+
+def pack_heads(keys, values):
+    rows, width = keys.shape
+    hbm = pl.BlockSpec(memory_space=pltpu.HBM)
+    heads = width // HD
+    return pl.pallas_call(
+        pack_kernel,
+        out_shape=jax.ShapeDtypeStruct((heads, rows, 2 * HD), BF),
+        in_specs=[hbm, hbm],
+        out_specs=hbm,
+        scratch_shapes=[pltpu.SemaphoreType.DMA((heads, 2))],
+        compiler_params=pltpu.CompilerParams(vmem_limit_bytes=60 << 20),
+        cost_estimate=pl.CostEstimate(flops=0, bytes_accessed=1 << 20, transcendentals=0),
+        name="pack_heads",
+    )(keys, values)
+
+
 def attention_kernel(
-    place, ids_col_hbm, ids_row_hbm, query_hbm, own_hbm, past_hbm, out_hbm,
-    ids_col, ids_row, query_parts, own, past, out, sems, out_sems,
+    place, ids_row_hbm, query_hbm, own_hbm, past_hbm, out_hbm,
+    ids_row, query_parts, own, past, out, sems, out_sems,
 ):
     block = out.shape[2] * 2
     pairs = (
         (query_hbm, query_parts),
         (own_hbm, own),
         (past_hbm, past),
-        (ids_col_hbm, ids_col),
         (ids_row_hbm, ids_row),
     )
     copies = [
@@ -48,9 +76,11 @@
     row_pos = lax.broadcasted_iota(jnp.int32, (block, block), 0)
     col_pos = lax.broadcasted_iota(jnp.int32, (block, block), 1)
     causal = col_pos <= row_pos
+    same = col_pos == row_pos
     for y in range(ROW):
         query = query_parts[lax.rem(place[0] + (ROW - y), ROW)]
-        query_ids = ids_col[pl.ds(y * block, block), 0:1]
+        row_ids = ids_row[0:1, pl.ds(span + y * block, block)]
+        query_ids = jnp.sum(jnp.where(same, row_ids, 0), axis=1, keepdims=True)
         pieces = []
         for b in range(y, ROW):
             key = past[b, :, 0:HD]
@@ -98,20 +128,20 @@
         store.wait()
 
 
-def attention(place, ids_col, ids_row, query_parts, own, past):
+def attention(place, ids_row, query_parts, own, past):
     block = own.shape[1]
     hbm = pl.BlockSpec(memory_space=pltpu.HBM)
-    operands = (ids_col, ids_row, query_parts, own, past)
+    operands = (ids_row, query_parts, own, past)
     result = jax.ShapeDtypeStruct((2, ROW, block // 2, HD), BF)
     return pl.pallas_call(
         attention_kernel,
         out_shape=result,
-        in_specs=[pl.BlockSpec(memory_space=pltpu.SMEM)] + [hbm] * 5,
+        in_specs=[pl.BlockSpec(memory_space=pltpu.SMEM)] + [hbm] * 4,
         out_specs=hbm,
         scratch_shapes=[pltpu.VMEM(o.shape, o.dtype) for o in operands]
         + [
             pltpu.VMEM(result.shape, BF),
-            pltpu.SemaphoreType.DMA((5,)),
+            pltpu.SemaphoreType.DMA((4,)),
             pltpu.SemaphoreType.DMA((2, ROW)),
         ],
         compiler_params=pltpu.CompilerParams(vmem_limit_bytes=58 << 20),
@@ -319,7 +349,7 @@
     )(select, own, peer)
 
 
-def slot_weight_kernel(rank, weight, high, low):
+def slot_weight_kernel(rank, weight, high):
     slots = high.shape[1]
     per_core = CAP // CORES
     experts_here = rank.shape[1]
@@ -331,11 +361,8 @@
     ).astype(BF)
     ranks = jnp.dot(rank[...].astype(BF), expand, preferred_element_type=F32)
     hit = ranks.astype(jnp.int32) == wanted
-    top = weight[...].astype(BF)
-    rest = (weight[...] - top.astype(F32)).astype(BF)
-    for side, out in ((top, high), (rest, low)):
-        spread = jnp.dot(side, expand, preferred_element_type=F32)
-        out[...] = jnp.where(hit, spread, 0.0).astype(BF)
+    spread = jnp.dot(weight[...].astype(BF), expand, preferred_element_type=F32)
+    high[...] = jnp.where(hit, spread, 0.0).astype(BF)
 
 
 def slot_weights(rank, weight, slots):
@@ -344,9 +371,9 @@
     shape = jax.ShapeDtypeStruct((rows, slots), BF)
     return pl.pallas_call(
         slot_weight_kernel,
-        out_shape=(shape, shape),
+        out_shape=shape,
         in_specs=[vmem, vmem],
-        out_specs=(vmem, vmem),
+        out_specs=vmem,
         compiler_params=pltpu.CompilerParams(vmem_limit_bytes=16 << 20),
         cost_estimate=pl.CostEstimate(
             flops=6 * rows * slots * 32, bytes_accessed=2 << 20, transcendentals=0
@@ -397,27 +424,40 @@
         pltpu.make_async_copy(source, down.at[pl.ds(j * hidden, hidden)], down_sems.at[j])
         for j, source in enumerate((down_own, down_peer))
     ]
-    for copy in [x_copies[0]] + chunks[0] + x_copies[1:]:
-        copy.start()
-    for copies in chunks[1:]:
+    def begin(copies):
         for copy in copies:
             copy.start()
-    for copy in down_copies:
-        copy.start()
+
+    def finish(copies):
+        for copy in copies:
+            copy.wait()
+
+    def halves(n, m):
+        lo, hi = bounds[n]
+        here = pl.ds(m * block, block)
+        left = x[here, :]
+        g = lax.dot_general(left, gate[lo:hi, :], contract, preferred_element_type=F32)
+        u = lax.dot_general(left, up[lo:hi, :], contract, preferred_element_type=F32)
+        act[here, lo:hi] = (g / (1.0 + jnp.exp(-g)) * u).astype(BF)
+
     contract = (((1,), (1,)), ((), ()))
-    for n, (lo, hi) in enumerate(bounds):
-        for copy in chunks[n]:
-            copy.wait()
-        for m in range(parts):
-            here = pl.ds(m * block, block)
-            if n == 0:
-                x_copies[m].wait()
-            left = x[here, :]
-            g = lax.dot_general(left, gate[lo:hi, :], contract, preferred_element_type=F32)
-            u = lax.dot_general(left, up[lo:hi, :], contract, preferred_element_type=F32)
-            act[here, lo:hi] = (g / (1.0 + jnp.exp(-g)) * u).astype(BF)
-    for copy in down_copies:
-        copy.wait()
+    begin([x_copies[0]] + chunks[0])
+    begin(x_copies[1:])
+    finish([x_copies[0]] + chunks[0])
+    begin(chunks[1])
+    halves(0, 0)
+    finish(x_copies[1:])
+    begin(chunks[2])
+    for m in range(1, parts):
+        halves(0, m)
+    finish(chunks[1])
+    begin(down_copies)
+    for m in range(parts):
+        halves(1, m)
+    finish(chunks[2])
+    for m in range(parts):
+        halves(2, m)
+    finish(down_copies)
     stores = []
     for i in range(groups):
         for m in range(parts):
@@ -468,8 +508,8 @@
 
 
 def combine_kernel(
-    core, high_hbm, low_hbm, back_hbm, mine_hbm, peers_hbm, shared_hbm, out,
-    high, low, back, mine, peers, shared, sems,
+    core, high_hbm, back_hbm, mine_hbm, peers_hbm, shared_hbm, out,
+    high, back, mine, peers, shared, sems,
 ):
     rows = mine.shape[0]
     chips, depth = back.shape[0], back.shape[1]
@@ -484,26 +524,22 @@
         for i, (source, target) in enumerate(
             (
                 (high_hbm, high),
-                (low_hbm, low),
                 (shared_hbm, shared),
                 (mine_hbm, mine),
                 (peers_hbm, peers),
             )
         )
     ]
-    for copy in [rest[0], copies[0], rest[1]] + copies[1:] + rest[2:]:
+    for copy in [rest[0]] + copies + rest[1:]:
         copy.start()
     total = None
     for i, (copy, (chip, here)) in enumerate(zip(copies, pieces)):
         if i == 0:
             rest[0].wait()
         copy.wait()
-        for side in (high, low):
-            if i == 0 and side is low:
-                rest[1].wait()
-            part = jnp.dot(side[:, here], back[chip, here], preferred_element_type=F32)
-            total = part if total is None else total + part
-    for copy in rest[2:]:
+        part = jnp.dot(high[:, here], back[chip, here], preferred_element_type=F32)
+        total = part if total is None else total + part
+    for copy in rest[1:]:
         copy.wait()
     total += shared[...]
     first = core[0] == 0
@@ -513,18 +549,18 @@
     out[rows : 2 * rows, :] = (total[rows:] + high_half).astype(BF)
 
 
-def combine(core, high, low, returned, mine, peers, shared):
+def combine(core, high, returned, mine, peers, shared):
     hbm = pl.BlockSpec(memory_space=pltpu.HBM)
     vmem = pl.BlockSpec(memory_space=pltpu.VMEM)
     rows, width = shared.shape
-    operands = (high, low, returned, mine, peers, shared)
+    operands = (high, returned, mine, peers, shared)
     return pl.pallas_call(
         combine_kernel,
         out_shape=jax.ShapeDtypeStruct((rows, width), BF),
-        in_specs=[pl.BlockSpec(memory_space=pltpu.SMEM)] + [hbm] * 6,
+        in_specs=[pl.BlockSpec(memory_space=pltpu.SMEM)] + [hbm] * 5,
         out_specs=vmem,
         scratch_shapes=[pltpu.VMEM(o.shape, o.dtype) for o in operands]
-        + [pltpu.SemaphoreType.DMA((9,))],
+        + [pltpu.SemaphoreType.DMA((8,))],
         compiler_params=pltpu.CompilerParams(vmem_limit_bytes=60 << 20),
         cost_estimate=pl.CostEstimate(
             flops=8 * rows * width * high.shape[1], bytes_accessed=7 << 20, transcendentals=0
@@ -550,10 +586,10 @@
     parts = [
         jnp.dot(pick, part, preferred_element_type=F32).astype(BF) for part in (keys, values)
     ]
-    return jnp.concatenate(parts, 1).reshape(head_count * tok_count, quarter_page, -1)
-
-
-def place_pages(landed, slots_all, owner_all, tok_count, head_count, tok_index):
+    return jnp.concatenate(parts, 1).reshape(head_count, tok_count * quarter_page, -1)
+
+
+def place_pages(landed, slots_all, owner_all, head_count, head_index, tok_index):
     pages_here = owner_all.shape[1]
     quarter_page = PAGE // head_count
     rows = pages_here * quarter_page
@@ -561,14 +597,17 @@
     row = jnp.arange(rows, dtype=jnp.int32)
     target = jnp.repeat(arrival, quarter_page) * quarter_page + row % quarter_page
     place = (row[:, None] == target[None, :]).astype(BF)
-    landed = landed.reshape(head_count, rows, -1)
-    width = landed.shape[2] // 2
-    placed = [
-        jnp.dot(place, landed[h], preferred_element_type=F32).astype(BF)
-        for h in range(head_count)
+    placed = jnp.dot(
+        place, landed.reshape(rows, -1), preferred_element_type=F32
+    ).astype(BF)
+    chip_width = placed.shape[1] // head_count
+    width = chip_width // 2
+    ordered = [
+        lax.dynamic_slice_in_dim(placed, (g ^ head_index) * chip_width, chip_width, 1)
+        for g in range(head_count)
     ]
     cache = jnp.concatenate(
-        [p[:, :width] for p in placed] + [p[:, width:] for p in placed], 1
+        [p[:, :width] for p in ordered] + [p[:, width:] for p in ordered], 1
     )
     return cache.reshape(pages_here, quarter_page, 2 * head_count * width)
 
@@ -609,13 +648,7 @@
     gate_up_peer = lax.ppermute(gate_up_own, "head", INTRA)
     down_peer = lax.ppermute(down_own, "head", INTRA)
 
-    packed = jnp.stack(
-        [
-            jnp.concatenate([part[:, i * HD : (i + 1) * HD] for part in (keys, values)], 1)
-            for i in range(heads_here)
-        ],
-        0,
-    )
+    packed = pack_heads(keys, values)
     row_groups = [[r * ROW + y for y in range(ROW)] for r in range(rows_of_blocks)]
     own = lax.all_to_all(
         packed, "tok", split_axis=0, concat_axis=0, tiled=True, axis_index_groups=row_groups
@@ -625,10 +658,7 @@
     padded_ids = jnp.concatenate([jnp.full((span,), -1, jnp.int32), request_ids], 0)
     window_ids = lax.dynamic_slice_in_dim(padded_ids, base, 2 * span, 0)
     ids_row = window_ids[None, :]
-    ids_col = jnp.broadcast_to(window_ids[span:, None], (span, HD))
-    queries, own, ids_row, ids_col = lax.optimization_barrier(
-        (queries, own, ids_row, ids_col)
-    )
+    queries, own = lax.optimization_barrier((queries, own))
     place_in_row = tok_index % ROW
     query_parts = []
     for step in range(ROW):
@@ -652,7 +682,7 @@
         own, "tok", [(s, s + ROW) for s in range(tok_count - ROW)]
     )
     attended = attention(
-        place_in_row.reshape(1), ids_col, ids_row, jnp.stack(query_parts, 0), own, past
+        place_in_row.reshape(1), ids_row, jnp.stack(query_parts, 0), own, past
     )
 
     core_groups = [
@@ -687,10 +717,19 @@
     select = (rank_rel[:, None, :] == (place + core)[None, :, None]).astype(BF)
     select = select.reshape(EXPERTS * slots_core, tok_rows)
     core_ref = core.reshape(1)
+    page_rows = [lax.dynamic_index_in_dim(pieces, head_index, 0, keepdims=False)]
+    for flip in range(1, head_count):
+        part = lax.dynamic_index_in_dim(pieces, head_index ^ flip, 0, keepdims=False)
+        part, _ = lax.optimization_barrier((part, attended))
+        page_rows.append(
+            lax.ppermute(part, "head", [(h, h ^ flip) for h in range(head_count)])
+        )
+    page_rows, gathered = lax.optimization_barrier((page_rows, gathered))
     projected, projected_low = project(core_ref, gathered, out_proj, out_peer)
     projected_far = lax.ppermute(projected_low, "head", CROSS)
-    pieces, _ = lax.optimization_barrier((pieces, projected_low))
-    landed = lax.all_to_all(pieces, BOTH, split_axis=0, concat_axis=0, tiled=True)
+    page_rows, _ = lax.optimization_barrier((page_rows, projected_low))
+    page_rows = jnp.concatenate(page_rows, 1).reshape(tok_count, -1, head_count * 2 * head_width)
+    landed = lax.all_to_all(page_rows, "tok", split_axis=0, concat_axis=0, tiled=True)
     projected_far, select, landed = lax.optimization_barrier((projected_far, select, landed))
     resid, normed_own = add_and_norm(
         core_ref, hidden_in, projected, projected_far, norm_gain[None, :]
@@ -699,7 +738,7 @@
 
     outgoing = gather_rows(select, normed_own, normed_peer)
     rank, weight_of, _ = lax.optimization_barrier((rank, weight_of, outgoing))
-    high, low = slot_weights(rank, weight_of, CORES * EXPERTS * slots_core)
+    high = slot_weights(rank, weight_of, CORES * EXPERTS * slots_core)
     late_own, late_peer, _ = lax.optimization_barrier((normed_own, normed_peer, outgoing))
     normed_abs = jnp.where(
         core == 0,
@@ -747,8 +786,8 @@
         resid, (head_index + 1 - 2 * core) * column_width, column_width, 1
     )
     from_peer = lax.ppermute(peer_cols, "head", INTRA)
-    layer_out = combine(core_ref, high, low, returned, own_cols, from_peer, shared_cols)
-    decode_cache = place_pages(landed, slots_all, owner_all, tok_count, head_count, tok_index)
+    layer_out = combine(core_ref, high, returned, own_cols, from_peer, shared_cols)
+    decode_cache = place_pages(landed, slots_all, owner_all, head_count, head_index, tok_index)
     return (layer_out, decode_cache)
 
 

time: 210 us -> 227 us (1.081)
  Pallas kernels: 32.9 us -> 48.4 us
  waiting for transfers between devices: 76.3 us -> 89.9 us
  local copies, waits for them, and re-layouts: 29.6 us -> 20.9 us
  matrix products: 14.5 us -> 9.54 us
  starting transfers between devices: 42.4 us -> 46 us
    pallas_call x1 -> x2, Pallas kernels: 0.8 us -> 17.6 us  [the longest x1 17.1 us: pack_heads(): pl.pallas_call(pack_kernel, out_shape=jax.ShapeDtypeStruct((heads, rows,...]
    all_to_all x1, waiting for transfers between devices: 6.66 us -> 0.01 us  [per_device(): lax.all_to_all(attended.reshape(CORES * ROW, half, HD), BOTH, split_axis=...]
    all_to_all x1, waiting for transfers between devices: 20.5 us -> 26.6 us  [per_device(): lax.all_to_all(partial, BOTH, split_axis=0, concat_axis=0, tiled=True)]
    ppermute x0 -> x3, waiting for transfers between devices: none -> 5.55 us  [per_device(): lax.ppermute(part, 'head', [(h, h ^ flip) for h in range(head_count)])]
    squeeze x4 -> x1, local copies, waits for them, and re-layouts: 5.77 us -> 0.83 us  [per_device(): lax.dynamic_index_in_dim(pieces, head_index ^ flip, 0, keepdims=False)]
    all_to_all x1, waiting for transfers between devices: 4.18 us -> 8.69 us  [per_device(): lax.all_to_all(packed, 'tok', split_axis=0, concat_axis=0, tiled=True, ax...]
    all_to_all x1, waiting for transfers between devices: 29.9 us -> 33.9 us  [per_device(): lax.all_to_all(outgoing.reshape(tok_count, slots_core, model_width), 'tok...]
    slice x4 -> x0, local copies, waits for them, and re-layouts: 3.22 us -> none  [the longest x2 2.12 us: per_device(): part[:, i * HD:(i + 1) * HD]]
  transfers between devices with their start and end apart: 17 -> 20, of which waited for: 9 -> 11; matrix products, arithmetic and copies ran while one was open for 25% -> 16% of each run, Pallas kernels for 9% -> 15%
where the time goes in v5:
time: 227 us; the launch traced here: 226 us
  waiting for transfers between devices  89.9 us (40%)
  Pallas kernels  48.4 us (21%)
  starting transfers between devices  46 us (20%)
  local copies, waits for them, and re-layouts  20.9 us (9%)
  other arithmetic  9.89 us (4%)
  matrix products  9.54 us (4%)
    all_to_all x1, waiting for transfers between devices, per_device(): lax.all_to_all(outgoing.reshape(tok_count, slots_core, model_width), 'tok...  33.9 us
    all_to_all x1, waiting for transfers between devices, per_device(): lax.all_to_all(partial, BOTH, split_axis=0, concat_axis=0, tiled=True)  26.6 us
    pallas_call x1, Pallas kernels, pack_heads(): pl.pallas_call(pack_kernel, out_shape=jax.ShapeDtypeStruct((heads, rows,...  17.1 us
    pallas_call x1, Pallas kernels, experts(): pl.pallas_call(expert_kernel, out_shape=jax.ShapeDtypeStruct((groups, row...  11.5 us
    all_to_all x1, starting transfers between devices, per_device(): lax.all_to_all(partial, BOTH, split_axis=0, concat_axis=0, tiled=True)  9.85 us
    all_to_all x1, starting transfers between devices, per_device(): lax.all_to_all(page_rows, 'tok', split_axis=0, concat_axis=0, tiled=True)  9.69 us
    all_to_all x1, waiting for transfers between devices, per_device(): lax.all_to_all(packed, 'tok', split_axis=0, concat_axis=0, tiled=True, ax...  8.69 us
    all_to_all x1, waiting for transfers between devices, per_device(): lax.all_to_all(page_rows, 'tok', split_axis=0, concat_axis=0, tiled=True)  7.68 us
  transfers between devices with their start and end apart: 20, of which 11 were waited for; matrix products, arithmetic and copies ran while one was open for 16% of the time, Pallas kernels for 15%

profile of v5, /device:TPU:0, one launch (start us, length us, event | category | flops | bytes accessed | tf_op | source)
XLA Modules:
  0.0 226.0 jit_solution(3626297200581511809)
XLA Ops:
  0.8 17.1 %pack_heads.1 = bf16[4,256,256]{2,1,0:T(8,128)(2,1)} custom-call(bf16[256,512]{1,0:T(8,128)(2,1)} %keys.1, bf16[256,512]{1,0:T(8,128)(2,1)} %values.1), custom_call_target="tpu_custom_call" | custom-call | bytes 1048576 | tf_op jit(solution)/shard_map/pack_heads/pallas_call | solution.py:42
  17.9 4.6 %all-to-all-start = ((bf16[4,256,256]{2,1,0:T(8,128)(2,1)}), bf16[4,256,256]{2,1,0:T(8,128)(2,1)}, u32[]{:S(2)}, u32[]{:S(2)}) async-start(bf16[4,256,256]{2,1,0:T(8,128)(2,1)} %pack_heads.1), calls=%async_computation | async-start | bytes 1048576 | tf_op jit(solution)/shard_map/all_to_all | solution.py:653
  24.0 8.7 %all-to-all-done.own_hbm = bf16[4,256,256]{2,1,0:T(8,128)(2,1)} async-done(((bf16[4,256,256]{2,1,0:T(8,128)(2,1)}), bf16[4,256,256]{2,1,0:T(8,128)(2,1)}, u32[]{:S(2)}, u32[]{:S(2)}) %all-to-all-start) | async-done | bytes 524320 | tf_op jit(solution)/shard_map/all_to_all | solution.py:653
  32.7 6.6 %collective-permute-start.3 = (bf16[4,256,256]{2,1,0:T(8,128)(2,1)}, bf16[4,256,256]{2,1,0:T(8,128)(2,1)}, u32[]{:S(2)}, u32[]{:S(2)}) collective-permute-start(bf16[4,256,256]{2,1,0:T(8,128)(2,1)} %all-to-all-done.own_hbm), channel_id=1, source_target_pairs={{0,4},{1,5},{2,6},{3,7},{4,8},{5,9},{6,10},{7,11},{8,12},{9,13},{1... | collective-permute-start | bytes 1572872 | tf_op jit(solution)/shard_map/ppermute | solution.py:681
  46.9 2.7 %collective-permute-done.1 = bf16[256,128]{1,0:T(8,128)(2,1)S(1)} collective-permute-done((bf16[256,128]{1,0:T(8,128)(2,1)S(1)}, bf16[256,128]{1,0:T(8,128)(2,1)S(1)}, u32[]{:S(2)}, u32[]{:S(2)}) %collective-permute-start.1) | collective-permute-done | bytes 65568 | tf_op jit(solution)/shard_map/ppermute | solution.py:668
  51.5 5.2 %row_attention.1 = bf16[2,4,128,128]{3,2,1,0:T(8,128)(2,1)} custom-call(s32[1]{0:T(128)} %bitcast.5.place, s32[1,2048]{1,0:T(1,128)} %bitcast.68, bf16[4,256,128]{2,1,0:T(8,128)(2,1)} %pad_maximum_fusion.2.query_hbm, bf16[4,256,256]{2,1,0:T(8,128)(2,1)} %all-to-all-done.own_hbm, bf16[4,256,256]{2,1,0:T(8,128)(2,1)} %collective-permute-done.3.past_hbm), custom_call_target="tpu_custom_call" | custom-call | flops 671088640 | bytes 3145728 | tf_op jit(solution)/shard_map/row_attention/pallas_call | solution.py:136
  56.7 3.4 %all-to-all-start.1 = ((bf16[8,128,128]{2,1,0:T(8,128)(2,1)}), bf16[8,128,128]{2,1,0:T(8,128)(2,1)S(1)}, u32[]{:S(2)}, u32[]{:S(2)}) async-start(bf16[8,128,128]{2,1,0:T(8,128)(2,1)} %bitcast.63), calls=%async_computation.1 | async-start | bytes 524288 | tf_op jit(solution)/shard_map/all_to_all | solution.py:697
  62.3 4.8 %collective-permute-done.5 = bf16[64,1024]{1,0:T(8,128)(2,1)S(1)} collective-permute-done((bf16[64,1024]{1,0:T(8,128)(2,1)}, bf16[64,1024]{1,0:T(8,128)(2,1)S(1)}, u32[]{:S(2)}, u32[]{:S(2)}) %collective-permute-start.5) | collective-permute-done | bytes 131104 | tf_op jit(solution)/shard_map/ppermute | solution.py:725
  69.2 4.3 %project.1 = (f32[128,2048]{1,0:T(8,128)}, bf16[128,2048]{1,0:T(8,128)(2,1)}) custom-call(s32[1]{0:T(128)} %bitcast.core, bf16[2,4,128,128]{3,2,1,0:T(8,128)(2,1)} %bitcast.62, bf16[512,2048]{1,0:T(8,128)(2,1)} %own_hbm.1, bf16[512,2048]{1,0:T(8,128)(2,1)} %collective-permute-done.7.peer_hbm), custom_call_target="tpu_custom_call" | custom-call | flops 536870912 | bytes 6291456 | tf_op jit(solution)/shard_map/project/pallas_call | solution.py:205
  76.8 9.7 %all-to-all-start.2 = ((bf16[32,2,4096]{2,1,0:T(2,128)(2,1)}), bf16[32,2,4096]{2,1,0:T(2,128)(2,1)S(1)}, u32[]{:S(2)}, u32[]{:S(2)}) async-start(bf16[32,2,4096]{2,1,0:T(2,128)(2,1)} %reshape.133), calls=%async_computation.2 | async-start | bytes 1048576 | tf_op jit(solution)/shard_map/all_to_all | solution.py:732
  92.3 7.7 %all-to-all-done.2 = bf16[32,2,4096]{2,1,0:T(2,128)(2,1)S(1)} async-done(((bf16[32,2,4096]{2,1,0:T(2,128)(2,1)}), bf16[32,2,4096]{2,1,0:T(2,128)(2,1)S(1)}, u32[]{:S(2)}, u32[]{:S(2)}) %all-to-all-start.2) | async-done | bytes 524320 | tf_op jit(solution)/shard_map/all_to_all | solution.py:732
  100.0 2.7 %add_and_norm.1 = (f32[128,2048]{1,0:T(8,128)}, bf16[128,2048]{1,0:T(8,128)(2,1)}) custom-call(s32[1]{0:T(128)} %bitcast.core, bf16[256,2048]{1,0:T(8,128)(2,1)} %hidden_hbm.1, f32[128,2048]{1,0:T(8,128)} %get-tuple-element.48.near_hbm, bf16[128,2048]{1,0:T(8,128)(2,1)} %collective-permute-done.8.far_hbm, f32[1,2048]{1,0:T(1,128)} %bitcast.67), custom_call_target="tpu_custom_call" | custom-call | flops 2097152 | bytes 4194304 | tf_op jit(solution)/shard_map/add_and_norm/pallas_call | solution.py:276
  102.8 2.1 collective-permute-done.9.peer_hbm
  105.7 3.4 %gather_rows.1 = bf16[768,2048]{1,0:T(8,128)(2,1)} custom-call(bf16[768,256]{1,0:T(8,128)(2,1)} %fusion.3.select_hbm, bf16[128,2048]{1,0:T(8,128)(2,1)} %get-tuple-element.53.own_hbm, bf16[128,2048]{1,0:T(8,128)(2,1)} %copy-done.8), custom_call_target="tpu_custom_call" | custom-call | flops 805306368 | bytes 5242880 | tf_op jit(solution)/shard_map/gather_rows/pallas_call | solution.py:332
  109.2 4.8 %all-to-all-start.3 = ((bf16[32,24,2048]{2,1,0:T(8,128)(2,1)}), bf16[32,24,2048]{2,1,0:T(8,128)(2,1)}, u32[]{:S(2)}, u32[]{:S(2)}) async-start(bf16[32,24,2048]{2,1,0:T(8,128)(2,1)} %bitcast.59), calls=%async_computation.3 | async-start | bytes 6291456 | tf_op jit(solution)/shard_map/all_to_all | solution.py:748
  114.7 2.0 fusion.8
  116.7 4.4 %fusion.1 = f32[256,2,704]{0,2,1:T(8,128)S(1)} fusion(bf16[2048,2,704]{0,2,1:T(8,128)(2,1)} %param.24, bf16[128,2048]{1,0:T(8,128)(2,1)S(1)} %copy-done.9, bf16[128,2048]{1,0:T(8,128)(2,1)S(1)} %copy-done.7, pred[]{:T(512)S(6)} %eq.109), kind=kOutput, calls=%fused_computation.7 | convolution fusion | flops 1481113600 | bytes 8257537 | tf_op jit(solution)/shard_map/td,dgf->tgf/dot_general | solution.py:755
  124.3 33.9 %all-to-all-done.3 = bf16[32,24,2048]{2,1,0:T(8,128)(2,1)} async-done(((bf16[32,24,2048]{2,1,0:T(8,128)(2,1)}), bf16[32,24,2048]{2,1,0:T(8,128)(2,1)}, u32[]{:S(2)}, u32[]{:S(2)}) %all-to-all-start.3) | async-done | bytes 3145760 | tf_op jit(solution)/shard_map/all_to_all | solution.py:748
  158.2 11.5 %experts.1 = bf16[4,768,512]{2,1,0:T(8,128)(2,1)} custom-call(bf16[768,2048]{1,0:T(8,128)(2,1)} %bitcast.23.x_hbm, bf16[2,352,2048]{2,1,0:T(8,128)(2,1)} %bitcast.71, bf16[2,352,2048]{2,1,0:T(8,128)(2,1)} %collective-permute-done.10.both_peer, bf16[352,2048]{1,0:T(8,128)(2,1)} %bitcast.73, bf16[352,2048]{1,0:T(8,128)(2,1)} %collective-permute-done.11.down_peer), custom_call_target="tpu_custom_call" | custom-call | flops 6643777536 | bytes 15728640 | tf_op jit(solution)/shard_map/experts/pallas_call | solution.py:483
  170.9 9.8 %all-to-all-start.4 = ((bf16[128,24,512]{2,1,0:T(8,128)(2,1)}), bf16[128,24,512]{2,1,0:T(8,128)(2,1)}, u32[]{:S(2)}, u32[]{:S(2)}) async-start(bf16[128,24,512]{2,1,0:T(8,128)(2,1)} %bitcast.60), calls=%async_computation.4 | async-start | bytes 6291456 | tf_op jit(solution)/shard_map/all_to_all | solution.py:775
  183.1 1.9 constant_dynamic-slice_fusion
  193.6 2.1 convert_add_fusion.1.shared_hbm
  195.6 26.6 %all-to-all-done.4 = bf16[128,24,512]{2,1,0:T(8,128)(2,1)} async-done(((bf16[128,24,512]{2,1,0:T(8,128)(2,1)}), bf16[128,24,512]{2,1,0:T(8,128)(2,1)}, u32[]{:S(2)}, u32[]{:S(2)}) %all-to-all-start.4) | async-done | bytes 3145760 | tf_op jit(solution)/shard_map/all_to_all | solution.py:775
  222.3 3.5 %combine.1 = bf16[256,512]{1,0:T(8,128)(2,1)} custom-call(s32[1]{0:T(128)} %bitcast.core, bf16[256,1536]{1,0:T(8,128)(2,1)} %copy-done.1, bf16[2,1536,512]{2,1,0:T(8,128)(2,1)} %bitcast.29.back_hbm, f32[128,512]{1,0:T(8,128)} %get-tuple-element.65.mine_hbm, f32[128,512]{1,0:T(8,128)} %collective-permute-done.13.peers_hbm, ...), custom_call_target="tpu_custom_call" | custom-call | flops 1610612736 | bytes 7340032 | tf_op jit(solution)/shard_map/combine/pallas_call | solution.py:557
  (119 shorter events, 40.9 us)
Async XLA Ops:
  0.6 120.5 %copy-start = (bf16[704,2048]{1,0:T(8,128)(2,1)S(1)}, bf16[704,2048]{1,0:T(8,128)(2,1)}, u32[]{:S(2)}) copy-start(bf16[704,2048]{1,0:T(8,128)(2,1)} %param.25) | copy-start | bytes 8650756
  0.7 22.9 %copy-start.6 = (bf16[256,512]{1,0:T(8,128)(2,1)S(1)}, bf16[256,512]{1,0:T(8,128)(2,1)}, u32[]{:S(2)}) copy-start(bf16[256,512]{1,0:T(8,128)(2,1)} %keys.1) | copy-start | bytes 786436
  0.7 38.6 %copy-start.17 = (f32[256,4]{0,1:T(4,128)S(1)}, f32[256,4]{0,1:T(4,128)}, u32[]{:S(2)}) copy-start(f32[256,4]{0,1:T(4,128)} %param.28) | copy-start | bytes 12292
  0.7 38.6 %copy-start.18 = (s32[256,4]{0,1:T(4,128)S(1)}, s32[256,4]{0,1:T(4,128)}, u32[]{:S(2)}) copy-start(s32[256,4]{0,1:T(4,128)} %param.27) | copy-start | bytes 12292
  0.7 67.8 %collective-permute-start.7 = (bf16[512,2048]{1,0:T(8,128)(2,1)}, bf16[512,2048]{1,0:T(8,128)(2,1)}, u32[]{:S(2)}, u32[]{:S(2)}) collective-permute-start(bf16[512,2048]{1,0:T(8,128)(2,1)} %own_hbm.1), channel_id=1, source_target_pairs={{0,32},{32,0},{64,96},{96,64},{1,33},{33,1},{65,97},{97,65},{2,34}... | collective-permute-start | bytes 6291464 | tf_op jit(solution)/shard_map/ppermute | solution.py:647
  17.9 14.8 %all-to-all-start = ((bf16[4,256,256]{2,1,0:T(8,128)(2,1)}), bf16[4,256,256]{2,1,0:T(8,128)(2,1)}, u32[]{:S(2)}, u32[]{:S(2)}) async-start(bf16[4,256,256]{2,1,0:T(8,128)(2,1)} %pack_heads.1), calls=%async_computation | async-start | bytes 1048576 | tf_op jit(solution)/shard_map/all_to_all | solution.py:653
  32.7 18.9 %collective-permute-start.3 = (bf16[4,256,256]{2,1,0:T(8,128)(2,1)}, bf16[4,256,256]{2,1,0:T(8,128)(2,1)}, u32[]{:S(2)}, u32[]{:S(2)}) collective-permute-start(bf16[4,256,256]{2,1,0:T(8,128)(2,1)} %all-to-all-done.own_hbm), channel_id=1, source_target_pairs={{0,4},{1,5},{2,6},{3,7},{4,8},{5,9},{6,10},{7,11},{8,12},{9,13},{1... | collective-permute-start | bytes 1572872 | tf_op jit(solution)/shard_map/ppermute | solution.py:681
  42.6 4.3 %collective-permute-start.2 = (bf16[256,128]{1,0:T(8,128)(2,1)S(1)}, bf16[256,128]{1,0:T(8,128)(2,1)S(1)}, u32[]{:S(2)}, u32[]{:S(2)}) collective-permute-start(bf16[256,128]{1,0:T(8,128)(2,1)S(1)} %get-tuple-element.71), channel_id=1, source_target_pairs={{0,3},{1,0},{2,1},{3,2},{4,7},{5,4},{6,5},{7,6},{8,11},{9,8},{10,9... | collective-permute-start | bytes 196616 | tf_op jit(solution)/shard_map/ppermute | solution.py:668
  43.8 5.8 %collective-permute-start.1 = (bf16[256,128]{1,0:T(8,128)(2,1)S(1)}, bf16[256,128]{1,0:T(8,128)(2,1)S(1)}, u32[]{:S(2)}, u32[]{:S(2)}) collective-permute-start(bf16[256,128]{1,0:T(8,128)(2,1)S(1)} %get-tuple-element.72), channel_id=1, source_target_pairs={{0,2},{1,3},{2,0},{3,1},{4,6},{5,7},{6,4},{7,5},{8,10},{9,11},{10,... | collective-permute-start | bytes 196616 | tf_op jit(solution)/shard_map/ppermute | solution.py:668
  45.3 5.5 %collective-permute-start = (bf16[256,128]{1,0:T(8,128)(2,1)S(1)}, bf16[256,128]{1,0:T(8,128)(2,1)S(1)}, u32[]{:S(2)}, u32[]{:S(2)}) collective-permute-start(bf16[256,128]{1,0:T(8,128)(2,1)S(1)} %get-tuple-element.73), channel_id=1, source_target_pairs={{0,1},{1,2},{2,3},{3,0},{4,5},{5,6},{6,7},{7,4},{8,9},{9,10},{10,1... | collective-permute-start | bytes 196616 | tf_op jit(solution)/shard_map/ppermute | solution.py:668
  56.7 11.8 %all-to-all-start.1 = ((bf16[8,128,128]{2,1,0:T(8,128)(2,1)}), bf16[8,128,128]{2,1,0:T(8,128)(2,1)S(1)}, u32[]{:S(2)}, u32[]{:S(2)}) async-start(bf16[8,128,128]{2,1,0:T(8,128)(2,1)} %bitcast.63), calls=%async_computation.1 | async-start | bytes 524288 | tf_op jit(solution)/shard_map/all_to_all | solution.py:697
  60.2 2.1 collective-permute-start.4
  60.6 6.6 %collective-permute-start.5 = (bf16[64,1024]{1,0:T(8,128)(2,1)}, bf16[64,1024]{1,0:T(8,128)(2,1)S(1)}, u32[]{:S(2)}, u32[]{:S(2)}) collective-permute-start(bf16[64,1024]{1,0:T(8,128)(2,1)} %get-tuple-element.35), channel_id=1, source_target_pairs={{0,64},{32,96},{64,0},{96,32},{1,65},{33,97},{65,1},{97,33},{2,66}... | collective-permute-start | bytes 393224 | tf_op jit(solution)/shard_map/ppermute | solution.py:725
  61.6 6.9 %collective-permute-start.6 = (bf16[64,1024]{1,0:T(8,128)(2,1)}, bf16[64,1024]{1,0:T(8,128)(2,1)}, u32[]{:S(2)}, u32[]{:S(2)}) collective-permute-start(bf16[64,1024]{1,0:T(8,128)(2,1)} %get-tuple-element.36), channel_id=1, source_target_pairs={{0,96},{32,64},{64,32},{96,0},{1,97},{33,65},{65,33},{97,1},{2,98}... | collective-permute-start | bytes 393224 | tf_op jit(solution)/shard_map/ppermute | solution.py:725
  73.6 26.4 %collective-permute-start.8 = (bf16[128,2048]{1,0:T(8,128)(2,1)}, bf16[128,2048]{1,0:T(8,128)(2,1)}, u32[]{:S(2)}, u32[]{:S(2)}) collective-permute-start(bf16[128,2048]{1,0:T(8,128)(2,1)} %get-tuple-element.38), channel_id=1, source_target_pairs={{0,64},{64,0},{32,96},{96,32},{1,65},{65,1},{33,97},{97,33},{2,66}... | collective-permute-start | bytes 1572872 | tf_op jit(solution)/shard_map/ppermute | solution.py:729
  76.8 23.2 %all-to-all-start.2 = ((bf16[32,2,4096]{2,1,0:T(2,128)(2,1)}), bf16[32,2,4096]{2,1,0:T(2,128)(2,1)S(1)}, u32[]{:S(2)}, u32[]{:S(2)}) async-start(bf16[32,2,4096]{2,1,0:T(2,128)(2,1)} %reshape.133), calls=%async_computation.2 | async-start | bytes 1048576 | tf_op jit(solution)/shard_map/all_to_all | solution.py:732
  102.7 2.2 collective-permute-start.9
  109.2 49.0 %all-to-all-start.3 = ((bf16[32,24,2048]{2,1,0:T(8,128)(2,1)}), bf16[32,24,2048]{2,1,0:T(8,128)(2,1)}, u32[]{:S(2)}, u32[]{:S(2)}) async-start(bf16[32,24,2048]{2,1,0:T(8,128)(2,1)} %bitcast.59), calls=%async_computation.3 | async-start | bytes 6291456 | tf_op jit(solution)/shard_map/all_to_all | solution.py:748
  114.1 44.2 %collective-permute-start.10 = (bf16[2,352,2048]{2,1,0:T(8,128)(2,1)}, bf16[2,352,2048]{2,1,0:T(8,128)(2,1)}, u32[]{:S(2)}, u32[]{:S(2)}) collective-permute-start(bf16[2,352,2048]{2,1,0:T(8,128)(2,1)} %bitcast.70), channel_id=1, source_target_pairs={{0,32},{32,0},{64,96},{96,64},{1,33},{33,1},{65,97},{97,65},{2,34}... | collective-permute-start | bytes 8650760 | tf_op jit(solution)/shard_map/ppermute | solution.py:648
  114.3 43.9 %collective-permute-start.11 = (bf16[352,2048]{1,0:T(8,128)(2,1)}, bf16[352,2048]{1,0:T(8,128)(2,1)}, u32[]{:S(2)}, u32[]{:S(2)}) collective-permute-start(bf16[352,2048]{1,0:T(8,128)(2,1)} %bitcast.72), channel_id=1, source_target_pairs={{0,32},{32,0},{64,96},{96,64},{1,33},{33,1},{65,97},{97,65},{2,34}... | collective-permute-start | bytes 4325384 | tf_op jit(solution)/shard_map/ppermute | solution.py:649
  158.2 12.7 %collective-permute-start.12 = (bf16[256,1024]{1,0:T(8,128)(2,1)}, bf16[256,1024]{1,0:T(8,128)(2,1)}, u32[]{:S(2)}, u32[]{:S(2)}) collective-permute-start(bf16[256,1024]{1,0:T(8,128)(2,1)} %dynamic-slice_convert_fusion), channel_id=1, source_target_pairs={{0,64},{64,0},{32,96},{96,32},{1,65},{65,1},{33,97},{97,33},{2,66}... | collective-permute-start | bytes 1572872 | tf_op jit(solution)/shard_map/ppermute | solution.py:770
  170.9 51.4 %all-to-all-start.4 = ((bf16[128,24,512]{2,1,0:T(8,128)(2,1)}), bf16[128,24,512]{2,1,0:T(8,128)(2,1)}, u32[]{:S(2)}, u32[]{:S(2)}) async-start(bf16[128,24,512]{2,1,0:T(8,128)(2,1)} %bitcast.60), calls=%async_computation.4 | async-start | bytes 6291456 | tf_op jit(solution)/shard_map/all_to_all | solution.py:775
  185.1 10.6 %collective-permute-start.13 = (f32[128,512]{1,0:T(8,128)}, f32[128,512]{1,0:T(8,128)}, u32[]{:S(2)}, u32[]{:S(2)}) collective-permute-start(f32[128,512]{1,0:T(8,128)} %get-tuple-element.64), channel_id=1, source_target_pairs={{0,32},{32,0},{64,96},{96,64},{1,33},{33,1},{65,97},{97,65},{2,34}... | collective-permute-start | bytes 786440 | tf_op jit(solution)/shard_map/ppermute | solution.py:788
  189.5 4.1 %collective-permute-start.14 = (bf16[256,512]{1,0:T(8,128)(2,1)}, bf16[256,512]{1,0:T(8,128)(2,1)}, u32[]{:S(2)}, u32[]{:S(2)}) collective-permute-start(bf16[256,512]{1,0:T(8,128)(2,1)} %dynamic-slice_convert_fusion.1), channel_id=1, source_target_pairs={{0,32},{32,0},{64,96},{96,64},{1,33},{33,1},{65,97},{97,65},{2,34}... | collective-permute-start | bytes 786440 | tf_op jit(solution)/shard_map/ppermute | solution.py:783
  (17 other events, 113.0 us)

commit v6 on v5

--- a/solution.py
+++ b/solution.py
@@ -22,29 +22,22 @@
 CROSS = [(0, 2), (2, 0), (1, 3), (3, 1)]
 
 
-def pack_kernel(keys, values, out, sems):
-    copies = []
+def pack_kernel(keys, values, out):
     for i in range(out.shape[0]):
-        for j, part in enumerate((keys, values)):
-            copy = pltpu.make_async_copy(
-                part.at[:, pl.ds(i * HD, HD)], out.at[i, :, pl.ds(j * HD, HD)], sems.at[i, j]
-            )
-            copy.start()
-            copies.append(copy)
-    for copy in copies:
-        copy.wait()
+        here = pl.ds(i * HD, HD)
+        out[i, :, 0:HD] = keys[:, here]
+        out[i, :, HD : 2 * HD] = values[:, here]
 
 
 def pack_heads(keys, values):
     rows, width = keys.shape
-    hbm = pl.BlockSpec(memory_space=pltpu.HBM)
+    vmem = pl.BlockSpec(memory_space=pltpu.VMEM)
     heads = width // HD
     return pl.pallas_call(
         pack_kernel,
         out_shape=jax.ShapeDtypeStruct((heads, rows, 2 * HD), BF),
-        in_specs=[hbm, hbm],
-        out_specs=hbm,
-        scratch_shapes=[pltpu.SemaphoreType.DMA((heads, 2))],
+        in_specs=[vmem, vmem],
+        out_specs=vmem,
         compiler_params=pltpu.CompilerParams(vmem_limit_bytes=60 << 20),
         cost_estimate=pl.CostEstimate(flops=0, bytes_accessed=1 << 20, transcendentals=0),
         name="pack_heads",
@@ -88,7 +81,7 @@
             score = lax.dot_general(
                 query, key, (((1,), (1,)), ((), ())), preferred_element_type=F32
             )
-            pieces.append(jnp.where(query_ids == key_ids, score * scale, -1e30))
+            pieces.append(jnp.where(query_ids == key_ids, score, -1e30))
         for b in range(y + 1):
             key = own[b, :, 0:HD]
             key_ids = ids_row[0:1, pl.ds(span + b * block, block)]
@@ -98,11 +91,11 @@
             allowed = query_ids == key_ids
             if b == y:
                 allowed = allowed & causal
-            pieces.append(jnp.where(allowed, score * scale, -1e30))
+            pieces.append(jnp.where(allowed, score, -1e30))
         top = pieces[0].max(-1, keepdims=True)
         for piece in pieces[1:]:
             top = jnp.maximum(top, piece.max(-1, keepdims=True))
-        weights = [jnp.exp(piece - top) for piece in pieces]
+        weights = [jnp.exp((piece - top) * scale) for piece in pieces]
         total = weights[0].sum(-1, keepdims=True)
         for weight in weights[1:]:
             total = total + weight.sum(-1, keepdims=True)
@@ -110,13 +103,14 @@
         mixed = jnp.zeros((block, HD), F32)
         index = 0
         for b in range(y, ROW):
-            prob = (weights[index] * inverse).astype(BF)
+            prob = weights[index].astype(BF)
             mixed += jnp.dot(prob, past[b, :, HD : 2 * HD], preferred_element_type=F32)
             index += 1
         for b in range(y + 1):
-            prob = (weights[index] * inverse).astype(BF)
+            prob = weights[index].astype(BF)
             mixed += jnp.dot(prob, own[b, :, HD : 2 * HD], preferred_element_type=F32)
             index += 1
+        mixed = mixed * inverse
         half = block // 2
         out[0, y] = mixed[:half].astype(BF)
         out[1, y] = mixed[half:].astype(BF)
@@ -586,10 +580,10 @@
     parts = [
         jnp.dot(pick, part, preferred_element_type=F32).astype(BF) for part in (keys, values)
     ]
-    return jnp.concatenate(parts, 1).reshape(head_count, tok_count * quarter_page, -1)
-
-
-def place_pages(landed, slots_all, owner_all, head_count, head_index, tok_index):
+    return jnp.concatenate(parts, 1).reshape(head_count * tok_count, quarter_page, -1)
+
+
+def place_pages(landed, slots_all, owner_all, tok_count, head_count, tok_index):
     pages_here = owner_all.shape[1]
     quarter_page = PAGE // head_count
     rows = pages_here * quarter_page
@@ -597,17 +591,14 @@
     row = jnp.arange(rows, dtype=jnp.int32)
     target = jnp.repeat(arrival, quarter_page) * quarter_page + row % quarter_page
     place = (row[:, None] == target[None, :]).astype(BF)
-    placed = jnp.dot(
-        place, landed.reshape(rows, -1), preferred_element_type=F32
-    ).astype(BF)
-    chip_width = placed.shape[1] // head_count
-    width = chip_width // 2
-    ordered = [
-        lax.dynamic_slice_in_dim(placed, (g ^ head_index) * chip_width, chip_width, 1)
-        for g in range(head_count)
+    landed = landed.reshape(head_count, rows, -1)
+    width = landed.shape[2] // 2
+    placed = [
+        jnp.dot(place, landed[h], preferred_element_type=F32).astype(BF)
+        for h in range(head_count)
     ]
     cache = jnp.concatenate(
-        [p[:, :width] for p in ordered] + [p[:, width:] for p in ordered], 1
+        [p[:, :width] for p in placed] + [p[:, width:] for p in placed], 1
     )
     return cache.reshape(pages_here, quarter_page, 2 * head_count * width)
 
@@ -717,20 +708,12 @@
     select = (rank_rel[:, None, :] == (place + core)[None, :, None]).astype(BF)
     select = select.reshape(EXPERTS * slots_core, tok_rows)
     core_ref = core.reshape(1)
-    page_rows = [lax.dynamic_index_in_dim(pieces, head_index, 0, keepdims=False)]
-    for flip in range(1, head_count):
-        part = lax.dynamic_index_in_dim(pieces, head_index ^ flip, 0, keepdims=False)
-        part, _ = lax.optimization_barrier((part, attended))
-        page_rows.append(
-            lax.ppermute(part, "head", [(h, h ^ flip) for h in range(head_count)])
-        )
-    page_rows, gathered = lax.optimization_barrier((page_rows, gathered))
+    gathered, select, pieces = lax.optimization_barrier((gathered, select, pieces))
     projected, projected_low = project(core_ref, gathered, out_proj, out_peer)
     projected_far = lax.ppermute(projected_low, "head", CROSS)
-    page_rows, _ = lax.optimization_barrier((page_rows, projected_low))
-    page_rows = jnp.concatenate(page_rows, 1).reshape(tok_count, -1, head_count * 2 * head_width)
-    landed = lax.all_to_all(page_rows, "tok", split_axis=0, concat_axis=0, tiled=True)
-    projected_far, select, landed = lax.optimization_barrier((projected_far, select, landed))
+    pieces, _ = lax.optimization_barrier((pieces, projected_low))
+    landed = lax.all_to_all(pieces, BOTH, split_axis=0, concat_axis=0, tiled=True)
+    projected_far, landed = lax.optimization_barrier((projected_far, landed))
     resid, normed_own = add_and_norm(
         core_ref, hidden_in, projected, projected_far, norm_gain[None, :]
     )
@@ -787,7 +770,7 @@
     )
     from_peer = lax.ppermute(peer_cols, "head", INTRA)
     layer_out = combine(core_ref, high, returned, own_cols, from_peer, shared_cols)
-    decode_cache = place_pages(landed, slots_all, owner_all, head_count, head_index, tok_index)
+    decode_cache = place_pages(landed, slots_all, owner_all, tok_count, head_count, tok_index)
     return (layer_out, decode_cache)
 
 

time: 227 us -> 206 us (0.907)
  waiting for transfers between devices: 89.9 us -> 64.8 us
  blocking collectives: 0 us -> 23.6 us
  Pallas kernels: 48.4 us -> 33 us
  starting transfers between devices: 46 us -> 34.2 us
  matrix products: 9.54 us -> 14.6 us
  local copies, waits for them, and re-layouts: 20.9 us -> 25.2 us
    all_to_all x0 -> x1, blocking collectives: none -> 23.6 us  [per_device(): lax.all_to_all(pieces, BOTH, split_axis=0, concat_axis=0, tiled=True)]
    pallas_call x1, Pallas kernels: 17.1 us -> 2.06 us  [pack_heads(): pl.pallas_call(pack_kernel, out_shape=jax.ShapeDtypeStruct((heads, rows,...]
    all_to_all x1, waiting for transfers between devices: 33.9 us -> 23.1 us  [per_device(): lax.all_to_all(outgoing.reshape(tok_count, slots_core, model_width), 'tok...]
    all_to_all x1 -> x0, starting transfers between devices: 9.69 us -> none  [per_device(): lax.all_to_all(page_rows, 'tok', split_axis=0, concat_axis=0, tiled=True)]
    all_to_all x1 -> x0, waiting for transfers between devices: 7.68 us -> none  [per_device(): lax.all_to_all(page_rows, 'tok', split_axis=0, concat_axis=0, tiled=True)]
    ppermute x3 -> x0, waiting for transfers between devices: 5.55 us -> none  [per_device(): lax.ppermute(part, 'head', [(h, h ^ flip) for h in range(head_count)])]
    squeeze x1 -> x4, local copies, waits for them, and re-layouts: 0.83 us -> 5.8 us  [place_pages(): landed[h]]
    all_to_all x1, waiting for transfers between devices: 8.69 us -> 4.68 us  [per_device(): lax.all_to_all(packed, 'tok', split_axis=0, concat_axis=0, tiled=True, ax...]
  transfers between devices with their start and end apart: 20 -> 16, of which waited for: 11 -> 9; matrix products, arithmetic and copies ran while one was open for 16% -> 21% of each run, Pallas kernels for 15% -> 8%
where the time goes in v6:
time: 206 us; the launch traced here: 205 us
  waiting for transfers between devices  64.8 us (31%)
  starting transfers between devices  34.2 us (17%)
  Pallas kernels  33 us (16%)
  local copies, waits for them, and re-layouts  25.2 us (12%)
  blocking collectives  23.6 us (11%)
  matrix products  14.6 us (7%)
  other arithmetic  8.26 us (4%)
    all_to_all x1, waiting for transfers between devices, per_device(): lax.all_to_all(partial, BOTH, split_axis=0, concat_axis=0, tiled=True)  27.9 us
    all_to_all x1, blocking collectives, per_device(): lax.all_to_all(pieces, BOTH, split_axis=0, concat_axis=0, tiled=True)  23.6 us
    all_to_all x1, waiting for transfers between devices, per_device(): lax.all_to_all(outgoing.reshape(tok_count, slots_core, model_width), 'tok...  23.1 us
    pallas_call x1, Pallas kernels, experts(): pl.pallas_call(expert_kernel, out_shape=jax.ShapeDtypeStruct((groups, row...  11.5 us
    all_to_all x1, starting transfers between devices, per_device(): lax.all_to_all(partial, BOTH, split_axis=0, concat_axis=0, tiled=True)  9.85 us
    unnamed x44, local copies, waits for them, and re-layouts  6.76 us
    ppermute x1, starting transfers between devices, per_device(): lax.ppermute(own, 'tok', [(s, s + ROW) for s in range(tok_count - ROW)])  5.8 us
    squeeze x4, local copies, waits for them, and re-layouts, place_pages(): landed[h]  5.8 us
  transfers between devices with their start and end apart: 16, of which 9 were waited for; matrix products, arithmetic and copies ran while one was open for 21% of the time, Pallas kernels for 8%

profile of v6, /device:TPU:0, one launch (start us, length us, event | category | flops | bytes accessed | tf_op | source)
XLA Modules:
  0.0 204.8 jit_solution(4682428380575690671)
XLA Ops:
  0.7 2.1 %pack_heads.1 = bf16[4,256,256]{2,1,0:T(8,128)(2,1)} custom-call(bf16[256,512]{1,0:T(8,128)(2,1)} %keys.1, bf16[256,512]{1,0:T(8,128)(2,1)} %values.1), custom_call_target="tpu_custom_call" | custom-call | bytes 1048576 | tf_op jit(solution)/shard_map/pack_heads/pallas_call | solution.py:36
  2.8 4.5 %all-to-all-start = ((bf16[4,256,256]{2,1,0:T(8,128)(2,1)}), bf16[4,256,256]{2,1,0:T(8,128)(2,1)}, u32[]{:S(2)}, u32[]{:S(2)}) async-start(bf16[4,256,256]{2,1,0:T(8,128)(2,1)} %pack_heads.1), calls=%async_computation | async-start | bytes 1048576 | tf_op jit(solution)/shard_map/all_to_all | solution.py:644
  12.2 4.7 %all-to-all-done.own_hbm = bf16[4,256,256]{2,1,0:T(8,128)(2,1)} async-done(((bf16[4,256,256]{2,1,0:T(8,128)(2,1)}), bf16[4,256,256]{2,1,0:T(8,128)(2,1)}, u32[]{:S(2)}, u32[]{:S(2)}) %all-to-all-start) | async-done | bytes 524320 | tf_op jit(solution)/shard_map/all_to_all | solution.py:644
  16.9 5.8 %collective-permute-start.3 = (bf16[4,256,256]{2,1,0:T(8,128)(2,1)}, bf16[4,256,256]{2,1,0:T(8,128)(2,1)S(1)}, u32[]{:S(2)}, u32[]{:S(2)}) collective-permute-start(bf16[4,256,256]{2,1,0:T(8,128)(2,1)} %all-to-all-done.own_hbm), channel_id=1, source_target_pairs={{0,4},{1,5},{2,6},{3,7},{4,8},{5,9},{6,10},{7,11},{8,12},{9,13},{1... | collective-permute-start | bytes 1572872 | tf_op jit(solution)/shard_map/ppermute | solution.py:672
  28.0 2.7 %collective-permute-done.1 = bf16[256,128]{1,0:T(8,128)(2,1)S(1)} collective-permute-done((bf16[256,128]{1,0:T(8,128)(2,1)S(1)}, bf16[256,128]{1,0:T(8,128)(2,1)S(1)}, u32[]{:S(2)}, u32[]{:S(2)}) %collective-permute-start.1) | collective-permute-done | bytes 65568 | tf_op jit(solution)/shard_map/ppermute | solution.py:659
  33.5 4.7 %row_attention.1 = bf16[2,4,128,128]{3,2,1,0:T(8,128)(2,1)} custom-call(s32[1]{0:T(128)} %bitcast.1.place, s32[1,2048]{1,0:T(1,128)} %bitcast.60, bf16[4,256,128]{2,1,0:T(8,128)(2,1)} %pad_maximum_fusion.1.query_hbm, bf16[4,256,256]{2,1,0:T(8,128)(2,1)} %all-to-all-done.own_hbm, bf16[4,256,256]{2,1,0:T(8,128)(2,1)} %copy-done.17), custom_call_target="tpu_custom_call" | custom-call | flops 671088640 | bytes 3145728 | tf_op jit(solution)/shard_map/row_attention/pallas_call | solution.py:130
  38.2 4.1 %all-to-all-start.1 = ((bf16[8,128,128]{2,1,0:T(8,128)(2,1)}), bf16[8,128,128]{2,1,0:T(8,128)(2,1)}, u32[]{:S(2)}, u32[]{:S(2)}) async-start(bf16[8,128,128]{2,1,0:T(8,128)(2,1)} %bitcast.55), calls=%async_computation.1 | async-start | bytes 524288 | tf_op jit(solution)/shard_map/all_to_all | solution.py:688
  45.1 1.7 fusion.3.select_hbm
  46.8 2.4 %all-to-all-done.1 = bf16[8,128,128]{2,1,0:T(8,128)(2,1)} async-done(((bf16[8,128,128]{2,1,0:T(8,128)(2,1)}), bf16[8,128,128]{2,1,0:T(8,128)(2,1)}, u32[]{:S(2)}, u32[]{:S(2)}) %all-to-all-start.1) | async-done | bytes 262176 | tf_op jit(solution)/shard_map/all_to_all | solution.py:688
  49.2 4.3 %project.1 = (f32[128,2048]{1,0:T(8,128)}, bf16[128,2048]{1,0:T(8,128)(2,1)}) custom-call(s32[1]{0:T(128)} %bitcast.core, bf16[2,4,128,128]{3,2,1,0:T(8,128)(2,1)} %bitcast.8.att_hbm, bf16[512,2048]{1,0:T(8,128)(2,1)} %own_hbm.1, bf16[512,2048]{1,0:T(8,128)(2,1)} %collective-permute-done.4.peer_hbm), custom_call_target="tpu_custom_call" | custom-call | flops 536870912 | bytes 6291456 | tf_op jit(solution)/shard_map/project/pallas_call | solution.py:199
  54.6 23.6 %all_to_all.25 = bf16[128,2,1024]{2,1,0:T(2,128)(2,1)S(1)} all-to-all(bf16[128,2,1024]{2,1,0:T(2,128)(2,1)S(1)} %copy-done.4), channel_id=1, replica_groups=mesh['head'=4,'tok'=32] {'head','tok'}, dimensions={0} | all-to-all | bytes 1048576 | tf_op jit(solution)/shard_map/all_to_all | solution.py:715
  79.0 2.7 %add_and_norm.1 = (f32[128,2048]{1,0:T(8,128)}, bf16[128,2048]{1,0:T(8,128)(2,1)}) custom-call(s32[1]{0:T(128)} %bitcast.core, bf16[256,2048]{1,0:T(8,128)(2,1)} %hidden_hbm.1, f32[128,2048]{1,0:T(8,128)} %get-tuple-element.27.near_hbm, bf16[128,2048]{1,0:T(8,128)(2,1)} %copy-done.10, f32[1,2048]{1,0:T(1,128)} %bitcast.59), custom_call_target="tpu_custom_call" | custom-call | flops 2097152 | bytes 4194304 | tf_op jit(solution)/shard_map/add_and_norm/pallas_call | solution.py:270
  81.9 2.1 %collective-permute-done.6.peer_hbm = bf16[128,2048]{1,0:T(8,128)(2,1)S(1)} collective-permute-done((bf16[128,2048]{1,0:T(8,128)(2,1)}, bf16[128,2048]{1,0:T(8,128)(2,1)S(1)}, u32[]{:S(2)}, u32[]{:S(2)}) %collective-permute-start.6) | collective-permute-done | bytes 524320 | tf_op jit(solution)/shard_map/ppermute | solution.py:720
  84.8 3.5 %gather_rows.1 = bf16[768,2048]{1,0:T(8,128)(2,1)} custom-call(bf16[768,256]{1,0:T(8,128)(2,1)} %fusion.3.select_hbm, bf16[128,2048]{1,0:T(8,128)(2,1)} %get-tuple-element.35.own_hbm, bf16[128,2048]{1,0:T(8,128)(2,1)} %copy-done.8), custom_call_target="tpu_custom_call" | custom-call | flops 805306368 | bytes 5242880 | tf_op jit(solution)/shard_map/gather_rows/pallas_call | solution.py:326
  88.3 4.8 %all-to-all-start.3 = ((bf16[32,24,2048]{2,1,0:T(8,128)(2,1)}), bf16[32,24,2048]{2,1,0:T(8,128)(2,1)}, u32[]{:S(2)}, u32[]{:S(2)}) async-start(bf16[32,24,2048]{2,1,0:T(8,128)(2,1)} %bitcast.53), calls=%async_computation.3 | async-start | bytes 6291456 | tf_op jit(solution)/shard_map/all_to_all | solution.py:731
  95.7 1.9 constant_dynamic-slice_fusion
  105.4 2.0 fusion.8
  107.5 4.4 %fusion.1 = f32[256,2,704]{0,2,1:T(8,128)S(1)} fusion(bf16[2048,2,704]{0,2,1:T(8,128)(2,1)} %param.24, bf16[128,2048]{1,0:T(8,128)(2,1)S(1)} %copy-done.9, bf16[128,2048]{1,0:T(8,128)(2,1)S(1)} %copy-done.7, pred[]{:T(512)S(6)} %eq.102), kind=kOutput, calls=%fused_computation.10 | convolution fusion | flops 1481113600 | bytes 8257537 | tf_op jit(solution)/shard_map/td,dgf->tgf/dot_general | solution.py:738
  114.2 23.1 %all-to-all-done.3 = bf16[32,24,2048]{2,1,0:T(8,128)(2,1)} async-done(((bf16[32,24,2048]{2,1,0:T(8,128)(2,1)}), bf16[32,24,2048]{2,1,0:T(8,128)(2,1)}, u32[]{:S(2)}, u32[]{:S(2)}) %all-to-all-start.3) | async-done | bytes 3145760 | tf_op jit(solution)/shard_map/all_to_all | solution.py:731
  137.8 11.5 %experts.1 = bf16[4,768,512]{2,1,0:T(8,128)(2,1)} custom-call(bf16[768,2048]{1,0:T(8,128)(2,1)} %bitcast.18.x_hbm, bf16[2,352,2048]{2,1,0:T(8,128)(2,1)} %bitcast.63, bf16[2,352,2048]{2,1,0:T(8,128)(2,1)} %collective-permute-done.7.both_peer, bf16[352,2048]{1,0:T(8,128)(2,1)} %bitcast.65, bf16[352,2048]{1,0:T(8,128)(2,1)} %collective-permute-done.8.down_peer), custom_call_target="tpu_custom_call" | custom-call | flops 6643777536 | bytes 15728640 | tf_op jit(solution)/shard_map/experts/pallas_call | solution.py:477
  149.7 9.8 %all-to-all-start.4 = ((bf16[128,24,512]{2,1,0:T(8,128)(2,1)}), bf16[128,24,512]{2,1,0:T(8,128)(2,1)}, u32[]{:S(2)}, u32[]{:S(2)}) async-start(bf16[128,24,512]{2,1,0:T(8,128)(2,1)} %bitcast.54), calls=%async_computation.4 | async-start | bytes 6291456 | tf_op jit(solution)/shard_map/all_to_all | solution.py:758
  171.2 2.1 %convert_add_fusion.1.shared_hbm = f32[256,512]{1,0:T(8,128)} fusion(bf16[256,512]{1,0:T(8,128)(2,1)} %collective-permute-done.11, f32[256,1024]{1,0:T(8,128)} %copy-done.3, s32[]{:T(128)S(6)} %select_n.197), kind=kLoop, calls=%fused_computation.21 | loop fusion | flops 262144 | bytes 1310724 | tf_op jit(solution)/shard_map/add | solution.py:766
  173.2 27.9 %all-to-all-done.4 = bf16[128,24,512]{2,1,0:T(8,128)(2,1)} async-done(((bf16[128,24,512]{2,1,0:T(8,128)(2,1)}), bf16[128,24,512]{2,1,0:T(8,128)(2,1)}, u32[]{:S(2)}, u32[]{:S(2)}) %all-to-all-start.4) | async-done | bytes 3145760 | tf_op jit(solution)/shard_map/all_to_all | solution.py:758
  201.1 3.5 %combine.1 = bf16[256,512]{1,0:T(8,128)(2,1)} custom-call(s32[1]{0:T(128)} %bitcast.core, bf16[256,1536]{1,0:T(8,128)(2,1)} %copy-done.1, bf16[2,1536,512]{2,1,0:T(8,128)(2,1)} %bitcast.24.back_hbm, f32[128,512]{1,0:T(8,128)} %get-tuple-element.47.mine_hbm, f32[128,512]{1,0:T(8,128)} %collective-permute-done.10.peers_hbm, ...), custom_call_target="tpu_custom_call" | custom-call | flops 1610612736 | bytes 7340032 | tf_op jit(solution)/shard_map/combine/pallas_call | solution.py:551
  (111 shorter events, 43.6 us)
Async XLA Ops:
  0.6 111.3 %copy-start = (bf16[704,2048]{1,0:T(8,128)(2,1)S(1)}, bf16[704,2048]{1,0:T(8,128)(2,1)}, u32[]{:S(2)}) copy-start(bf16[704,2048]{1,0:T(8,128)(2,1)} %param.25) | copy-start | bytes 8650756
  0.6 9.6 %copy-start.5 = (bf16[256,512]{1,0:T(8,128)(2,1)S(1)}, bf16[256,512]{1,0:T(8,128)(2,1)}, u32[]{:S(2)}) copy-start(bf16[256,512]{1,0:T(8,128)(2,1)} %values.1) | copy-start | bytes 786436
  0.7 10.6 %copy-start.6 = (bf16[256,512]{1,0:T(8,128)(2,1)S(1)}, bf16[256,512]{1,0:T(8,128)(2,1)}, u32[]{:S(2)}) copy-start(bf16[256,512]{1,0:T(8,128)(2,1)} %keys.1) | copy-start | bytes 786436
  0.7 6.6 %copy-start.13 = (s32[1024]{0:T(1024)S(1)}, s32[1024]{0:T(1024)}, u32[]{:S(2)}) copy-start(s32[1024]{0:T(1024)} %param.29) | copy-start | bytes 12292
  0.7 7.0 %copy-start.14 = (f32[256,4]{0,1:T(4,128)S(1)}, f32[256,4]{0,1:T(4,128)}, u32[]{:S(2)}) copy-start(f32[256,4]{0,1:T(4,128)} %param.28) | copy-start | bytes 12292
  0.7 7.0 %copy-start.15 = (s32[256,4]{0,1:T(4,128)S(1)}, s32[256,4]{0,1:T(4,128)}, u32[]{:S(2)}) copy-start(s32[256,4]{0,1:T(4,128)} %param.27) | copy-start | bytes 12292
  2.8 14.1 %all-to-all-start = ((bf16[4,256,256]{2,1,0:T(8,128)(2,1)}), bf16[4,256,256]{2,1,0:T(8,128)(2,1)}, u32[]{:S(2)}, u32[]{:S(2)}) async-start(bf16[4,256,256]{2,1,0:T(8,128)(2,1)} %pack_heads.1), calls=%async_computation | async-start | bytes 1048576 | tf_op jit(solution)/shard_map/all_to_all | solution.py:644
  7.3 41.9 %collective-permute-start.4 = (bf16[512,2048]{1,0:T(8,128)(2,1)}, bf16[512,2048]{1,0:T(8,128)(2,1)}, u32[]{:S(2)}, u32[]{:S(2)}) collective-permute-start(bf16[512,2048]{1,0:T(8,128)(2,1)} %own_hbm.1), channel_id=1, source_target_pairs={{0,32},{32,0},{64,96},{96,64},{1,33},{33,1},{65,97},{97,65},{2,34}... | collective-permute-start | bytes 6291464 | tf_op jit(solution)/shard_map/ppermute | solution.py:638
  16.9 15.8 %collective-permute-start.3 = (bf16[4,256,256]{2,1,0:T(8,128)(2,1)}, bf16[4,256,256]{2,1,0:T(8,128)(2,1)S(1)}, u32[]{:S(2)}, u32[]{:S(2)}) collective-permute-start(bf16[4,256,256]{2,1,0:T(8,128)(2,1)} %all-to-all-done.own_hbm), channel_id=1, source_target_pairs={{0,4},{1,5},{2,6},{3,7},{4,8},{5,9},{6,10},{7,11},{8,12},{9,13},{1... | collective-permute-start | bytes 1572872 | tf_op jit(solution)/shard_map/ppermute | solution.py:672
  23.7 4.3 %collective-permute-start.2 = (bf16[256,128]{1,0:T(8,128)(2,1)S(1)}, bf16[256,128]{1,0:T(8,128)(2,1)S(1)}, u32[]{:S(2)}, u32[]{:S(2)}) collective-permute-start(bf16[256,128]{1,0:T(8,128)(2,1)S(1)} %get-tuple-element.53), channel_id=1, source_target_pairs={{0,3},{1,0},{2,1},{3,2},{4,7},{5,4},{6,5},{7,6},{8,11},{9,8},{10,9... | collective-permute-start | bytes 196616 | tf_op jit(solution)/shard_map/ppermute | solution.py:659
  24.9 5.8 %collective-permute-start.1 = (bf16[256,128]{1,0:T(8,128)(2,1)S(1)}, bf16[256,128]{1,0:T(8,128)(2,1)S(1)}, u32[]{:S(2)}, u32[]{:S(2)}) collective-permute-start(bf16[256,128]{1,0:T(8,128)(2,1)S(1)} %get-tuple-element.54), channel_id=1, source_target_pairs={{0,2},{1,3},{2,0},{3,1},{4,6},{5,7},{6,4},{7,5},{8,10},{9,11},{10,... | collective-permute-start | bytes 196616 | tf_op jit(solution)/shard_map/ppermute | solution.py:659
  26.4 5.5 %collective-permute-start = (bf16[256,128]{1,0:T(8,128)(2,1)S(1)}, bf16[256,128]{1,0:T(8,128)(2,1)S(1)}, u32[]{:S(2)}, u32[]{:S(2)}) collective-permute-start(bf16[256,128]{1,0:T(8,128)(2,1)S(1)} %get-tuple-element.55), channel_id=1, source_target_pairs={{0,1},{1,2},{2,3},{3,0},{4,5},{5,6},{6,7},{7,4},{8,9},{9,10},{10,1... | collective-permute-start | bytes 196616 | tf_op jit(solution)/shard_map/ppermute | solution.py:659
  38.2 11.0 %all-to-all-start.1 = ((bf16[8,128,128]{2,1,0:T(8,128)(2,1)}), bf16[8,128,128]{2,1,0:T(8,128)(2,1)}, u32[]{:S(2)}, u32[]{:S(2)}) async-start(bf16[8,128,128]{2,1,0:T(8,128)(2,1)} %bitcast.55), calls=%async_computation.1 | async-start | bytes 524288 | tf_op jit(solution)/shard_map/all_to_all | solution.py:688
  49.2 5.4 %copy-start.4 = (bf16[128,2,1024]{2,1,0:T(2,128)(2,1)S(1)}, bf16[128,2,1024]{2,1,0:T(2,128)(2,1)}, u32[]{:S(2)}) copy-start(bf16[128,2,1024]{2,1,0:T(2,128)(2,1)} %reshape.135) | copy-start | bytes 1572868
  53.5 24.7 %collective-permute-start.5 = (bf16[128,2048]{1,0:T(8,128)(2,1)}, bf16[128,2048]{1,0:T(8,128)(2,1)S(1)}, u32[]{:S(2)}, u32[]{:S(2)}) collective-permute-start(bf16[128,2048]{1,0:T(8,128)(2,1)} %get-tuple-element.28), channel_id=1, source_target_pairs={{0,64},{64,0},{32,96},{96,32},{1,65},{65,1},{33,97},{97,33},{2,66}... | collective-permute-start | bytes 1572872 | tf_op jit(solution)/shard_map/ppermute | solution.py:713
  81.8 2.2 %collective-permute-start.6 = (bf16[128,2048]{1,0:T(8,128)(2,1)}, bf16[128,2048]{1,0:T(8,128)(2,1)S(1)}, u32[]{:S(2)}, u32[]{:S(2)}) collective-permute-start(bf16[128,2048]{1,0:T(8,128)(2,1)} %get-tuple-element.35.own_hbm), channel_id=1, source_target_pairs={{0,32},{32,0},{64,96},{96,64},{1,33},{33,1},{65,97},{97,65},{2,34}... | collective-permute-start | bytes 1572872 | tf_op jit(solution)/shard_map/ppermute | solution.py:720
  88.3 49.0 %all-to-all-start.3 = ((bf16[32,24,2048]{2,1,0:T(8,128)(2,1)}), bf16[32,24,2048]{2,1,0:T(8,128)(2,1)}, u32[]{:S(2)}, u32[]{:S(2)}) async-start(bf16[32,24,2048]{2,1,0:T(8,128)(2,1)} %bitcast.53), calls=%async_computation.3 | async-start | bytes 6291456 | tf_op jit(solution)/shard_map/all_to_all | solution.py:731
  93.1 44.7 %collective-permute-start.7 = (bf16[2,352,2048]{2,1,0:T(8,128)(2,1)}, bf16[2,352,2048]{2,1,0:T(8,128)(2,1)}, u32[]{:S(2)}, u32[]{:S(2)}) collective-permute-start(bf16[2,352,2048]{2,1,0:T(8,128)(2,1)} %bitcast.62), channel_id=1, source_target_pairs={{0,32},{32,0},{64,96},{96,64},{1,33},{33,1},{65,97},{97,65},{2,34}... | collective-permute-start | bytes 8650760 | tf_op jit(solution)/shard_map/ppermute | solution.py:639
  93.3 44.4 %collective-permute-start.8 = (bf16[352,2048]{1,0:T(8,128)(2,1)}, bf16[352,2048]{1,0:T(8,128)(2,1)}, u32[]{:S(2)}, u32[]{:S(2)}) collective-permute-start(bf16[352,2048]{1,0:T(8,128)(2,1)} %bitcast.64), channel_id=1, source_target_pairs={{0,32},{32,0},{64,96},{96,64},{1,33},{33,1},{65,97},{97,65},{2,34}... | collective-permute-start | bytes 4325384 | tf_op jit(solution)/shard_map/ppermute | solution.py:640
  95.0 10.4 %copy-start.12 = (bf16[2048,1]{0,1:T(2,128)(2,1)S(1)}, bf16[2048,1]{0,1:T(2,128)(2,1)}, u32[]{:S(2)}) copy-start(bf16[2048,1]{0,1:T(2,128)(2,1)} %reshape.141) | copy-start | bytes 12292
  97.6 75.7 %collective-permute-start.10 = (f32[128,512]{1,0:T(8,128)}, f32[128,512]{1,0:T(8,128)}, u32[]{:S(2)}, u32[]{:S(2)}) collective-permute-start(f32[128,512]{1,0:T(8,128)} %get-tuple-element.46), channel_id=1, source_target_pairs={{0,32},{32,0},{64,96},{96,64},{1,33},{33,1},{65,97},{97,65},{2,34}... | collective-permute-start | bytes 786440 | tf_op jit(solution)/shard_map/ppermute | solution.py:771
  137.3 12.4 %collective-permute-start.9 = (bf16[256,1024]{1,0:T(8,128)(2,1)S(1)}, bf16[256,1024]{1,0:T(8,128)(2,1)}, u32[]{:S(2)}, u32[]{:S(2)}) collective-permute-start(bf16[256,1024]{1,0:T(8,128)(2,1)S(1)} %dynamic-slice_convert_fusion), channel_id=1, source_target_pairs={{0,64},{64,0},{32,96},{96,32},{1,65},{65,1},{33,97},{97,33},{2,66}... | collective-permute-start | bytes 1572872 | tf_op jit(solution)/shard_map/ppermute | solution.py:753
  149.7 51.4 %all-to-all-start.4 = ((bf16[128,24,512]{2,1,0:T(8,128)(2,1)}), bf16[128,24,512]{2,1,0:T(8,128)(2,1)}, u32[]{:S(2)}, u32[]{:S(2)}) async-start(bf16[128,24,512]{2,1,0:T(8,128)(2,1)} %bitcast.54), calls=%async_computation.4 | async-start | bytes 6291456 | tf_op jit(solution)/shard_map/all_to_all | solution.py:758
  167.6 3.6 %collective-permute-start.11 = (bf16[256,512]{1,0:T(8,128)(2,1)}, bf16[256,512]{1,0:T(8,128)(2,1)}, u32[]{:S(2)}, u32[]{:S(2)}) collective-permute-start(bf16[256,512]{1,0:T(8,128)(2,1)} %dynamic-slice_convert_fusion.1), channel_id=1, source_target_pairs={{0,32},{32,0},{64,96},{96,64},{1,33},{33,1},{65,97},{97,65},{2,34}... | collective-permute-start | bytes 786440 | tf_op jit(solution)/shard_map/ppermute | solution.py:766
  (10 other events, 19.7 us)

commit v7 on v6

--- a/solution.py
+++ b/solution.py
@@ -149,10 +149,9 @@
 
 
 def project_kernel(
-    core, att_hbm, own_hbm, peer_hbm, total_hbm, low_hbm,
-    att, own, peer, total, total_low, att_sem, sems, out_sems,
+    core, att_hbm, own_hbm, peer_hbm, low_hbm, att, own, peer, total_low, att_sem, sems, out_sems,
 ):
-    width = total.shape[1]
+    width = total_low.shape[1]
     step = width // 4
     att_copy = pltpu.make_async_copy(att_hbm, att, att_sem)
     att_copy.start()
@@ -181,13 +180,9 @@
             right, peer[:, cols], preferred_element_type=F32
         )
         total_low[:, cols] = part.astype(BF)
-        total[:, cols] = part
-        for j, (source, target) in enumerate(((total_low, low_hbm), (total, total_hbm))):
-            store = pltpu.make_async_copy(
-                source.at[:, cols], target.at[:, cols], out_sems.at[j, i]
-            )
-            store.start()
-            stores.append(store)
+        store = pltpu.make_async_copy(total_low.at[:, cols], low_hbm.at[:, cols], out_sems.at[i])
+        store.start()
+        stores.append(store)
     for store in stores:
         store.wait()
 
@@ -198,21 +193,17 @@
     hbm = pl.BlockSpec(memory_space=pltpu.HBM)
     return pl.pallas_call(
         project_kernel,
-        out_shape=(
-            jax.ShapeDtypeStruct((rows, width), F32),
-            jax.ShapeDtypeStruct((rows, width), BF),
-        ),
+        out_shape=jax.ShapeDtypeStruct((rows, width), BF),
         in_specs=[pl.BlockSpec(memory_space=pltpu.SMEM), hbm, hbm, hbm],
-        out_specs=(hbm, hbm),
+        out_specs=hbm,
         scratch_shapes=[
             pltpu.VMEM(att.shape, BF),
             pltpu.VMEM((depth, width), BF),
             pltpu.VMEM((depth, width), BF),
-            pltpu.VMEM((rows, width), F32),
             pltpu.VMEM((rows, width), BF),
             pltpu.SemaphoreType.DMA,
             pltpu.SemaphoreType.DMA((2, 4)),
-            pltpu.SemaphoreType.DMA((2, 4)),
+            pltpu.SemaphoreType.DMA((4,)),
         ],
         compiler_params=pltpu.CompilerParams(vmem_limit_bytes=58 << 20),
         cost_estimate=pl.CostEstimate(
@@ -224,7 +215,7 @@
 
 def norm_kernel(
     core, hidden_hbm, near_hbm, far_hbm, gain_hbm, resid_hbm, normed_hbm,
-    hidden, near, far, gain, normed, sems, out_sems,
+    hidden, near, far, gain, resid, normed, sems, out_sems,
 ):
     rows = near.shape[0]
     parts = 2
@@ -252,11 +243,13 @@
         here = pl.ds(i * block, block)
         for copy in copies[i]:
             copy.wait()
-        value = hidden[here, :].astype(F32) + (near[here, :] + far[here, :].astype(F32))
+        value = hidden[here, :].astype(F32) + (
+            near[here, :].astype(F32) + far[here, :].astype(F32)
+        )
         mean_square = jnp.mean(value * value, axis=-1, keepdims=True)
         normed[here, :] = (value * lax.rsqrt(mean_square + 1e-06) * gain[...]).astype(BF)
-        near[here, :] = value
-        for j, (source, target) in enumerate(((normed, normed_hbm), (near, resid_hbm))):
+        resid[here, :] = value
+        for j, (source, target) in enumerate(((normed, normed_hbm), (resid, resid_hbm))):
             store = pltpu.make_async_copy(source.at[here], target.at[here], out_sems.at[j, i])
             store.start()
             stores.append(store)
@@ -277,9 +270,10 @@
         out_specs=(hbm, hbm),
         scratch_shapes=[
             pltpu.VMEM((rows, width), BF),
-            pltpu.VMEM((rows, width), F32),
+            pltpu.VMEM((rows, width), BF),
             pltpu.VMEM((rows, width), BF),
             pltpu.VMEM((1, width), F32),
+            pltpu.VMEM((rows, width), F32),
             pltpu.VMEM((rows, width), BF),
             pltpu.SemaphoreType.DMA((4, 2)),
             pltpu.SemaphoreType.DMA((2, 2)),
@@ -426,9 +420,9 @@
         for copy in copies:
             copy.wait()
 
-    def halves(n, m):
+    def halves(n, start, count):
         lo, hi = bounds[n]
-        here = pl.ds(m * block, block)
+        here = pl.ds(start * block, count * block)
         left = x[here, :]
         g = lax.dot_general(left, gate[lo:hi, :], contract, preferred_element_type=F32)
         u = lax.dot_general(left, up[lo:hi, :], contract, preferred_element_type=F32)
@@ -439,32 +433,25 @@
     begin(x_copies[1:])
     finish([x_copies[0]] + chunks[0])
     begin(chunks[1])
-    halves(0, 0)
+    halves(0, 0, 1)
     finish(x_copies[1:])
     begin(chunks[2])
-    for m in range(1, parts):
-        halves(0, m)
+    halves(0, 1, parts - 1)
     finish(chunks[1])
     begin(down_copies)
-    for m in range(parts):
-        halves(1, m)
+    halves(1, 0, parts)
     finish(chunks[2])
-    for m in range(parts):
-        halves(2, m)
+    halves(2, 0, parts)
     finish(down_copies)
     stores = []
     for i in range(groups):
-        for m in range(parts):
-            here = pl.ds(m * block, block)
-            result = jnp.dot(
-                act[here, :], down[:, i * width : (i + 1) * width], preferred_element_type=F32
-            )
-            out[i, here, :] = result.astype(BF)
-            store = pltpu.make_async_copy(
-                out.at[i, here], out_hbm.at[i, here], out_sems.at[m, i]
-            )
-            store.start()
-            stores.append(store)
+        result = jnp.dot(
+            act[...], down[:, i * width : (i + 1) * width], preferred_element_type=F32
+        )
+        out[i] = result.astype(BF)
+        store = pltpu.make_async_copy(out.at[i], out_hbm.at[i], out_sems.at[i])
+        store.start()
+        stores.append(store)
     for store in stores:
         store.wait()
 
@@ -489,7 +476,7 @@
             pltpu.SemaphoreType.DMA((3,)),
             pltpu.SemaphoreType.DMA((pl.cdiv(2 * hidden, 256), 2, 2)),
             pltpu.SemaphoreType.DMA((2,)),
-            pltpu.SemaphoreType.DMA((3, groups)),
+            pltpu.SemaphoreType.DMA((groups,)),
         ],
         compiler_params=pltpu.CompilerParams(vmem_limit_bytes=60 << 20),
         cost_estimate=pl.CostEstimate(
@@ -709,14 +696,14 @@
     select = select.reshape(EXPERTS * slots_core, tok_rows)
     core_ref = core.reshape(1)
     gathered, select, pieces = lax.optimization_barrier((gathered, select, pieces))
-    projected, projected_low = project(core_ref, gathered, out_proj, out_peer)
+    projected_low = project(core_ref, gathered, out_proj, out_peer)
     projected_far = lax.ppermute(projected_low, "head", CROSS)
     pieces, _ = lax.optimization_barrier((pieces, projected_low))
     landed = lax.all_to_all(pieces, BOTH, split_axis=0, concat_axis=0, tiled=True)
-    projected_far, landed = lax.optimization_barrier((projected_far, landed))
     resid, normed_own = add_and_norm(
-        core_ref, hidden_in, projected, projected_far, norm_gain[None, :]
-    )
+        core_ref, hidden_in, projected_low, projected_far, norm_gain[None, :]
+    )
+    normed_own, landed = lax.optimization_barrier((normed_own, landed))
     normed_peer = lax.ppermute(normed_own, "head", INTRA)
 
     outgoing = gather_rows(select, normed_own, normed_peer)

time: 206 us -> 203 us (0.985)
  blocking collectives: 23.6 us -> 0 us
  starting transfers between devices: 34.2 us -> 46.1 us
  waiting for transfers between devices: 64.8 us -> 73 us
    all_to_all x1 -> x0, blocking collectives: 23.6 us -> none  [per_device(): lax.all_to_all(pieces, BOTH, split_axis=0, concat_axis=0, tiled=True)]
    all_to_all x0 -> x1, starting transfers between devices: none -> 10.1 us  [per_device(): lax.all_to_all(pieces, BOTH, split_axis=0, concat_axis=0, tiled=True)]
    all_to_all x0 -> x1, waiting for transfers between devices: none -> 7.39 us  [per_device(): lax.all_to_all(pieces, BOTH, split_axis=0, concat_axis=0, tiled=True)]
    ppermute x1, waiting for transfers between devices: 0.01 us -> 3.7 us  [per_device(): projected_far = lax.ppermute(projected_low, 'head', CROSS)]
    all_to_all x1, waiting for transfers between devices: 23.1 us -> 20.6 us  [per_device(): lax.all_to_all(outgoing.reshape(tok_count, slots_core, model_width), 'tok...]
    unnamed x44 -> x40, local copies, waits for them, and re-layouts: 6.76 us -> 5.96 us
  transfers between devices with their start and end apart: 16 -> 17, of which waited for: 9 -> 10; matrix products, arithmetic and copies ran while one was open for 21% -> 22% of each run, Pallas kernels for 8% -> 10%
where the time goes in v7:
time: 203 us; the launch traced here: 202 us
  waiting for transfers between devices  73 us (36%)
  starting transfers between devices  46.1 us (23%)
  Pallas kernels  32.7 us (16%)
  local copies, waits for them, and re-layouts  25 us (12%)
  matrix products  15.2 us (7%)
  other arithmetic  8.23 us (4%)
    all_to_all x1, waiting for transfers between devices, per_device(): lax.all_to_all(partial, BOTH, split_axis=0, concat_axis=0, tiled=True)  27.9 us
    all_to_all x1, waiting for transfers between devices, per_device(): lax.all_to_all(outgoing.reshape(tok_count, slots_core, model_width), 'tok...  20.6 us
    pallas_call x1, Pallas kernels, experts(): pl.pallas_call(expert_kernel, out_shape=jax.ShapeDtypeStruct((groups, row...  11.6 us
    all_to_all x1, starting transfers between devices, per_device(): lax.all_to_all(pieces, BOTH, split_axis=0, concat_axis=0, tiled=True)  10.1 us
    all_to_all x1, starting transfers between devices, per_device(): lax.all_to_all(partial, BOTH, split_axis=0, concat_axis=0, tiled=True)  9.9 us
    all_to_all x1, waiting for transfers between devices, per_device(): lax.all_to_all(pieces, BOTH, split_axis=0, concat_axis=0, tiled=True)  7.39 us
    squeeze x4, local copies, waits for them, and re-layouts, place_pages(): landed[h]  6.46 us
    all_to_all x1, starting transfers between devices, per_device(): lax.all_to_all(outgoing.reshape(tok_count, slots_core, model_width), 'tok...  5.96 us
  transfers between devices with their start and end apart: 17, of which 10 were waited for; matrix products, arithmetic and copies ran while one was open for 22% of the time, Pallas kernels for 10%

profile of v7, /device:TPU:0, one launch (start us, length us, event | category | flops | bytes accessed | tf_op | source)
XLA Modules:
  0.0 201.5 jit_solution(8849153313105375923)
XLA Ops:
  0.7 2.1 %pack_heads.1 = bf16[4,256,256]{2,1,0:T(8,128)(2,1)} custom-call(bf16[256,512]{1,0:T(8,128)(2,1)} %keys.1, bf16[256,512]{1,0:T(8,128)(2,1)} %values.1), custom_call_target="tpu_custom_call" | custom-call | bytes 1048576 | tf_op jit(solution)/shard_map/pack_heads/pallas_call | solution.py:36
  2.8 4.5 %all-to-all-start = ((bf16[4,256,256]{2,1,0:T(8,128)(2,1)}), bf16[4,256,256]{2,1,0:T(8,128)(2,1)}, u32[]{:S(2)}, u32[]{:S(2)}) async-start(bf16[4,256,256]{2,1,0:T(8,128)(2,1)} %pack_heads.1), calls=%async_computation | async-start | bytes 1048576 | tf_op jit(solution)/shard_map/all_to_all | solution.py:631
  12.2 4.7 %all-to-all-done.own_hbm = bf16[4,256,256]{2,1,0:T(8,128)(2,1)} async-done(((bf16[4,256,256]{2,1,0:T(8,128)(2,1)}), bf16[4,256,256]{2,1,0:T(8,128)(2,1)}, u32[]{:S(2)}, u32[]{:S(2)}) %all-to-all-start) | async-done | bytes 524320 | tf_op jit(solution)/shard_map/all_to_all | solution.py:631
  16.9 5.8 %collective-permute-start.3 = (bf16[4,256,256]{2,1,0:T(8,128)(2,1)}, bf16[4,256,256]{2,1,0:T(8,128)(2,1)S(1)}, u32[]{:S(2)}, u32[]{:S(2)}) collective-permute-start(bf16[4,256,256]{2,1,0:T(8,128)(2,1)} %all-to-all-done.own_hbm), channel_id=1, source_target_pairs={{0,4},{1,5},{2,6},{3,7},{4,8},{5,9},{6,10},{7,11},{8,12},{9,13},{1... | collective-permute-start | bytes 1572872 | tf_op jit(solution)/shard_map/ppermute | solution.py:659
  28.0 2.7 %collective-permute-done.1 = bf16[256,128]{1,0:T(8,128)(2,1)S(1)} collective-permute-done((bf16[256,128]{1,0:T(8,128)(2,1)S(1)}, bf16[256,128]{1,0:T(8,128)(2,1)S(1)}, u32[]{:S(2)}, u32[]{:S(2)}) %collective-permute-start.1) | collective-permute-done | bytes 65568 | tf_op jit(solution)/shard_map/ppermute | solution.py:646
  33.5 4.7 %row_attention.1 = bf16[2,4,128,128]{3,2,1,0:T(8,128)(2,1)} custom-call(s32[1]{0:T(128)} %bitcast.1.place, s32[1,2048]{1,0:T(1,128)} %bitcast.60, bf16[4,256,128]{2,1,0:T(8,128)(2,1)} %pad_maximum_fusion.1.query_hbm, bf16[4,256,256]{2,1,0:T(8,128)(2,1)} %all-to-all-done.own_hbm, bf16[4,256,256]{2,1,0:T(8,128)(2,1)} %copy-done.15), custom_call_target="tpu_custom_call" | custom-call | flops 671088640 | bytes 3145728 | tf_op jit(solution)/shard_map/row_attention/pallas_call | solution.py:130
  38.2 4.1 %all-to-all-start.1 = ((bf16[8,128,128]{2,1,0:T(8,128)(2,1)}), bf16[8,128,128]{2,1,0:T(8,128)(2,1)}, u32[]{:S(2)}, u32[]{:S(2)}) async-start(bf16[8,128,128]{2,1,0:T(8,128)(2,1)} %bitcast.55), calls=%async_computation.1 | async-start | bytes 524288 | tf_op jit(solution)/shard_map/all_to_all | solution.py:675
  46.8 2.4 %all-to-all-done.1 = bf16[8,128,128]{2,1,0:T(8,128)(2,1)} async-done(((bf16[8,128,128]{2,1,0:T(8,128)(2,1)}), bf16[8,128,128]{2,1,0:T(8,128)(2,1)}, u32[]{:S(2)}, u32[]{:S(2)}) %all-to-all-start.1) | async-done | bytes 262176 | tf_op jit(solution)/shard_map/all_to_all | solution.py:675
  49.2 4.1 %project.1.near_hbm = bf16[128,2048]{1,0:T(8,128)(2,1)} custom-call(s32[1]{0:T(128)} %bitcast.core, bf16[2,4,128,128]{3,2,1,0:T(8,128)(2,1)} %bitcast.8.att_hbm, bf16[512,2048]{1,0:T(8,128)(2,1)} %own_hbm.1, bf16[512,2048]{1,0:T(8,128)(2,1)} %collective-permute-done.4.peer_hbm), custom_call_target="tpu_custom_call" | custom-call | flops 536870912 | bytes 6291456 | tf_op jit(solution)/shard_map/project/pallas_call | solution.py:194
  54.4 10.1 %all-to-all-start.2 = ((bf16[128,2,1024]{2,1,0:T(2,128)(2,1)}), bf16[128,2,1024]{2,1,0:T(2,128)(2,1)S(1)}, u32[]{:S(2)}, u32[]{:S(2)}) async-start(bf16[128,2,1024]{2,1,0:T(2,128)(2,1)} %reshape.135), calls=%async_computation.2 | async-start | bytes 1048576 | tf_op jit(solution)/shard_map/all_to_all | solution.py:702
  64.5 3.7 %collective-permute-done.5.far_hbm = bf16[128,2048]{1,0:T(8,128)(2,1)} collective-permute-done((bf16[128,2048]{1,0:T(8,128)(2,1)}, bf16[128,2048]{1,0:T(8,128)(2,1)}, u32[]{:S(2)}, u32[]{:S(2)}) %collective-permute-start.5) | collective-permute-done | bytes 524320 | tf_op jit(solution)/shard_map/ppermute | solution.py:700
  68.2 2.6 %add_and_norm.1 = (f32[128,2048]{1,0:T(8,128)}, bf16[128,2048]{1,0:T(8,128)(2,1)}) custom-call(s32[1]{0:T(128)} %bitcast.core, bf16[256,2048]{1,0:T(8,128)(2,1)} %hidden_hbm.1, bf16[128,2048]{1,0:T(8,128)(2,1)} %project.1.near_hbm, bf16[128,2048]{1,0:T(8,128)(2,1)} %collective-permute-done.5.far_hbm, f32[1,2048]{1,0:T(1,128)} %bitcast.59), custom_call_target="tpu_custom_call" | custom-call | flops 2097152 | bytes 4194304 | tf_op jit(solution)/shard_map/add_and_norm/pallas_call | solution.py:263
  70.8 7.4 %all-to-all-done.2 = bf16[128,2,1024]{2,1,0:T(2,128)(2,1)S(1)} async-done(((bf16[128,2,1024]{2,1,0:T(2,128)(2,1)}), bf16[128,2,1024]{2,1,0:T(2,128)(2,1)S(1)}, u32[]{:S(2)}, u32[]{:S(2)}) %all-to-all-start.2) | async-done | bytes 524320 | tf_op jit(solution)/shard_map/all_to_all | solution.py:702
  78.2 2.1 %collective-permute-done.6.peer_hbm = bf16[128,2048]{1,0:T(8,128)(2,1)S(1)} collective-permute-done((bf16[128,2048]{1,0:T(8,128)(2,1)}, bf16[128,2048]{1,0:T(8,128)(2,1)S(1)}, u32[]{:S(2)}, u32[]{:S(2)}) %collective-permute-start.6) | collective-permute-done | bytes 524320 | tf_op jit(solution)/shard_map/ppermute | solution.py:707
  81.1 3.5 %gather_rows.1 = bf16[768,2048]{1,0:T(8,128)(2,1)} custom-call(bf16[768,256]{1,0:T(8,128)(2,1)} %fusion.3.select_hbm, bf16[128,2048]{1,0:T(8,128)(2,1)} %get-tuple-element.31.own_hbm, bf16[128,2048]{1,0:T(8,128)(2,1)} %copy-done.7), custom_call_target="tpu_custom_call" | custom-call | flops 805306368 | bytes 5242880 | tf_op jit(solution)/shard_map/gather_rows/pallas_call | solution.py:320
  84.6 6.0 %all-to-all-start.3 = ((bf16[32,24,2048]{2,1,0:T(8,128)(2,1)}), bf16[32,24,2048]{2,1,0:T(8,128)(2,1)}, u32[]{:S(2)}, u32[]{:S(2)}) async-start(bf16[32,24,2048]{2,1,0:T(8,128)(2,1)} %bitcast.53), calls=%async_computation.3 | async-start | bytes 6291456 | tf_op jit(solution)/shard_map/all_to_all | solution.py:718
  100.7 1.9 constant_dynamic-slice_fusion
  106.2 4.4 %fusion.1 = f32[256,2,704]{0,2,1:T(8,128)S(1)} fusion(bf16[2048,2,704]{0,2,1:T(8,128)(2,1)} %param.24, bf16[128,2048]{1,0:T(8,128)(2,1)S(1)} %copy-done.8, bf16[128,2048]{1,0:T(8,128)(2,1)S(1)} %copy-done.6, pred[]{:T(512)S(6)} %eq.102), kind=kOutput, calls=%fused_computation.10 | convolution fusion | flops 1481113600 | bytes 8257537 | tf_op jit(solution)/shard_map/td,dgf->tgf/dot_general | solution.py:725
  112.9 20.6 %all-to-all-done.3 = bf16[32,24,2048]{2,1,0:T(8,128)(2,1)} async-done(((bf16[32,24,2048]{2,1,0:T(8,128)(2,1)}), bf16[32,24,2048]{2,1,0:T(8,128)(2,1)}, u32[]{:S(2)}, u32[]{:S(2)}) %all-to-all-start.3) | async-done | bytes 3145760 | tf_op jit(solution)/shard_map/all_to_all | solution.py:718
  134.7 11.6 %experts.1 = bf16[4,768,512]{2,1,0:T(8,128)(2,1)} custom-call(bf16[768,2048]{1,0:T(8,128)(2,1)} %bitcast.18.x_hbm, bf16[2,352,2048]{2,1,0:T(8,128)(2,1)} %bitcast.63, bf16[2,352,2048]{2,1,0:T(8,128)(2,1)} %collective-permute-done.7.both_peer, bf16[352,2048]{1,0:T(8,128)(2,1)} %bitcast.65, bf16[352,2048]{1,0:T(8,128)(2,1)} %collective-permute-done.8.down_peer), custom_call_target="tpu_custom_call" | custom-call | flops 6643777536 | bytes 15728640 | tf_op jit(solution)/shard_map/experts/pallas_call | solution.py:464
  146.4 9.9 %all-to-all-start.4 = ((bf16[128,24,512]{2,1,0:T(8,128)(2,1)}), bf16[128,24,512]{2,1,0:T(8,128)(2,1)}, u32[]{:S(2)}, u32[]{:S(2)}) async-start(bf16[128,24,512]{2,1,0:T(8,128)(2,1)} %bitcast.54), calls=%async_computation.4 | async-start | bytes 6291456 | tf_op jit(solution)/shard_map/all_to_all | solution.py:745
  167.8 2.0 %convert_add_fusion.1.shared_hbm = f32[256,512]{1,0:T(8,128)} fusion(bf16[256,512]{1,0:T(8,128)(2,1)} %collective-permute-done.11, f32[256,1024]{1,0:T(8,128)} %copy-done.3, s32[]{:T(128)S(6)} %select_n.197), kind=kLoop, calls=%fused_computation.21 | loop fusion | flops 262144 | bytes 1310724 | tf_op jit(solution)/shard_map/add | solution.py:753
  169.9 27.9 %all-to-all-done.4 = bf16[128,24,512]{2,1,0:T(8,128)(2,1)} async-done(((bf16[128,24,512]{2,1,0:T(8,128)(2,1)}), bf16[128,24,512]{2,1,0:T(8,128)(2,1)}, u32[]{:S(2)}, u32[]{:S(2)}) %all-to-all-start.4) | async-done | bytes 3145760 | tf_op jit(solution)/shard_map/all_to_all | solution.py:745
  197.8 3.5 %combine.1 = bf16[256,512]{1,0:T(8,128)(2,1)} custom-call(s32[1]{0:T(128)} %bitcast.core, bf16[256,1536]{1,0:T(8,128)(2,1)} %copy-done.1, bf16[2,1536,512]{2,1,0:T(8,128)(2,1)} %bitcast.24.back_hbm, f32[128,512]{1,0:T(8,128)} %get-tuple-element.43.mine_hbm, f32[128,512]{1,0:T(8,128)} %collective-permute-done.10.peers_hbm, ...), custom_call_target="tpu_custom_call" | custom-call | flops 1610612736 | bytes 7340032 | tf_op jit(solution)/shard_map/combine/pallas_call | solution.py:538
  (108 shorter events, 48.0 us)
Async XLA Ops:
  0.6 110.0 %copy-start = (bf16[704,2048]{1,0:T(8,128)(2,1)S(1)}, bf16[704,2048]{1,0:T(8,128)(2,1)}, u32[]{:S(2)}) copy-start(bf16[704,2048]{1,0:T(8,128)(2,1)} %param.25) | copy-start | bytes 8650756
  0.6 9.6 %copy-start.4 = (bf16[256,512]{1,0:T(8,128)(2,1)S(1)}, bf16[256,512]{1,0:T(8,128)(2,1)}, u32[]{:S(2)}) copy-start(bf16[256,512]{1,0:T(8,128)(2,1)} %values.1) | copy-start | bytes 786436
  0.7 10.6 %copy-start.5 = (bf16[256,512]{1,0:T(8,128)(2,1)S(1)}, bf16[256,512]{1,0:T(8,128)(2,1)}, u32[]{:S(2)}) copy-start(bf16[256,512]{1,0:T(8,128)(2,1)} %keys.1) | copy-start | bytes 786436
  0.7 7.0 %copy-start.12 = (f32[256,4]{0,1:T(4,128)S(1)}, f32[256,4]{0,1:T(4,128)}, u32[]{:S(2)}) copy-start(f32[256,4]{0,1:T(4,128)} %param.28) | copy-start | bytes 12292
  0.7 7.0 %copy-start.13 = (s32[256,4]{0,1:T(4,128)S(1)}, s32[256,4]{0,1:T(4,128)}, u32[]{:S(2)}) copy-start(s32[256,4]{0,1:T(4,128)} %param.27) | copy-start | bytes 12292
  2.8 14.1 %all-to-all-start = ((bf16[4,256,256]{2,1,0:T(8,128)(2,1)}), bf16[4,256,256]{2,1,0:T(8,128)(2,1)}, u32[]{:S(2)}, u32[]{:S(2)}) async-start(bf16[4,256,256]{2,1,0:T(8,128)(2,1)} %pack_heads.1), calls=%async_computation | async-start | bytes 1048576 | tf_op jit(solution)/shard_map/all_to_all | solution.py:631
  7.3 41.9 %collective-permute-start.4 = (bf16[512,2048]{1,0:T(8,128)(2,1)}, bf16[512,2048]{1,0:T(8,128)(2,1)}, u32[]{:S(2)}, u32[]{:S(2)}) collective-permute-start(bf16[512,2048]{1,0:T(8,128)(2,1)} %own_hbm.1), channel_id=1, source_target_pairs={{0,32},{32,0},{64,96},{96,64},{1,33},{33,1},{65,97},{97,65},{2,34}... | collective-permute-start | bytes 6291464 | tf_op jit(solution)/shard_map/ppermute | solution.py:625
  16.9 15.8 %collective-permute-start.3 = (bf16[4,256,256]{2,1,0:T(8,128)(2,1)}, bf16[4,256,256]{2,1,0:T(8,128)(2,1)S(1)}, u32[]{:S(2)}, u32[]{:S(2)}) collective-permute-start(bf16[4,256,256]{2,1,0:T(8,128)(2,1)} %all-to-all-done.own_hbm), channel_id=1, source_target_pairs={{0,4},{1,5},{2,6},{3,7},{4,8},{5,9},{6,10},{7,11},{8,12},{9,13},{1... | collective-permute-start | bytes 1572872 | tf_op jit(solution)/shard_map/ppermute | solution.py:659
  23.7 4.3 %collective-permute-start.2 = (bf16[256,128]{1,0:T(8,128)(2,1)S(1)}, bf16[256,128]{1,0:T(8,128)(2,1)S(1)}, u32[]{:S(2)}, u32[]{:S(2)}) collective-permute-start(bf16[256,128]{1,0:T(8,128)(2,1)S(1)} %get-tuple-element.49), channel_id=1, source_target_pairs={{0,3},{1,0},{2,1},{3,2},{4,7},{5,4},{6,5},{7,6},{8,11},{9,8},{10,9... | collective-permute-start | bytes 196616 | tf_op jit(solution)/shard_map/ppermute | solution.py:646
  24.9 5.8 %collective-permute-start.1 = (bf16[256,128]{1,0:T(8,128)(2,1)S(1)}, bf16[256,128]{1,0:T(8,128)(2,1)S(1)}, u32[]{:S(2)}, u32[]{:S(2)}) collective-permute-start(bf16[256,128]{1,0:T(8,128)(2,1)S(1)} %get-tuple-element.50), channel_id=1, source_target_pairs={{0,2},{1,3},{2,0},{3,1},{4,6},{5,7},{6,4},{7,5},{8,10},{9,11},{10,... | collective-permute-start | bytes 196616 | tf_op jit(solution)/shard_map/ppermute | solution.py:646
  26.4 5.5 %collective-permute-start = (bf16[256,128]{1,0:T(8,128)(2,1)S(1)}, bf16[256,128]{1,0:T(8,128)(2,1)S(1)}, u32[]{:S(2)}, u32[]{:S(2)}) collective-permute-start(bf16[256,128]{1,0:T(8,128)(2,1)S(1)} %get-tuple-element.51), channel_id=1, source_target_pairs={{0,1},{1,2},{2,3},{3,0},{4,5},{5,6},{6,7},{7,4},{8,9},{9,10},{10,1... | collective-permute-start | bytes 196616 | tf_op jit(solution)/shard_map/ppermute | solution.py:646
  38.2 11.0 %all-to-all-start.1 = ((bf16[8,128,128]{2,1,0:T(8,128)(2,1)}), bf16[8,128,128]{2,1,0:T(8,128)(2,1)}, u32[]{:S(2)}, u32[]{:S(2)}) async-start(bf16[8,128,128]{2,1,0:T(8,128)(2,1)} %bitcast.55), calls=%async_computation.1 | async-start | bytes 524288 | tf_op jit(solution)/shard_map/all_to_all | solution.py:675
  53.3 14.9 %collective-permute-start.5 = (bf16[128,2048]{1,0:T(8,128)(2,1)}, bf16[128,2048]{1,0:T(8,128)(2,1)}, u32[]{:S(2)}, u32[]{:S(2)}) collective-permute-start(bf16[128,2048]{1,0:T(8,128)(2,1)} %project.1.near_hbm), channel_id=1, source_target_pairs={{0,64},{64,0},{32,96},{96,32},{1,65},{65,1},{33,97},{97,33},{2,66}... | collective-permute-start | bytes 1572872 | tf_op jit(solution)/shard_map/ppermute | solution.py:700
  54.4 23.8 %all-to-all-start.2 = ((bf16[128,2,1024]{2,1,0:T(2,128)(2,1)}), bf16[128,2,1024]{2,1,0:T(2,128)(2,1)S(1)}, u32[]{:S(2)}, u32[]{:S(2)}) async-start(bf16[128,2,1024]{2,1,0:T(2,128)(2,1)} %reshape.135), calls=%async_computation.2 | async-start | bytes 1048576 | tf_op jit(solution)/shard_map/all_to_all | solution.py:702
  78.2 2.1 %collective-permute-start.6 = (bf16[128,2048]{1,0:T(8,128)(2,1)}, bf16[128,2048]{1,0:T(8,128)(2,1)S(1)}, u32[]{:S(2)}, u32[]{:S(2)}) collective-permute-start(bf16[128,2048]{1,0:T(8,128)(2,1)} %get-tuple-element.31.own_hbm), channel_id=1, source_target_pairs={{0,32},{32,0},{64,96},{96,64},{1,33},{33,1},{65,97},{97,65},{2,34}... | collective-permute-start | bytes 1572872 | tf_op jit(solution)/shard_map/ppermute | solution.py:707
  84.6 48.8 %all-to-all-start.3 = ((bf16[32,24,2048]{2,1,0:T(8,128)(2,1)}), bf16[32,24,2048]{2,1,0:T(8,128)(2,1)}, u32[]{:S(2)}, u32[]{:S(2)}) async-start(bf16[32,24,2048]{2,1,0:T(8,128)(2,1)} %bitcast.53), calls=%async_computation.3 | async-start | bytes 6291456 | tf_op jit(solution)/shard_map/all_to_all | solution.py:718
  90.6 44.1 %collective-permute-start.7 = (bf16[2,352,2048]{2,1,0:T(8,128)(2,1)}, bf16[2,352,2048]{2,1,0:T(8,128)(2,1)}, u32[]{:S(2)}, u32[]{:S(2)}) collective-permute-start(bf16[2,352,2048]{2,1,0:T(8,128)(2,1)} %bitcast.62), channel_id=1, source_target_pairs={{0,32},{32,0},{64,96},{96,64},{1,33},{33,1},{65,97},{97,65},{2,34}... | collective-permute-start | bytes 8650760 | tf_op jit(solution)/shard_map/ppermute | solution.py:626
  90.7 44.0 %collective-permute-start.8 = (bf16[352,2048]{1,0:T(8,128)(2,1)}, bf16[352,2048]{1,0:T(8,128)(2,1)}, u32[]{:S(2)}, u32[]{:S(2)}) collective-permute-start(bf16[352,2048]{1,0:T(8,128)(2,1)} %bitcast.64), channel_id=1, source_target_pairs={{0,32},{32,0},{64,96},{96,64},{1,33},{33,1},{65,97},{97,65},{2,34}... | collective-permute-start | bytes 4325384 | tf_op jit(solution)/shard_map/ppermute | solution.py:627
  92.5 11.9 %copy-start.10 = (bf16[2048,1]{0,1:T(2,128)(2,1)S(1)}, bf16[2048,1]{0,1:T(2,128)(2,1)}, u32[]{:S(2)}) copy-start(bf16[2048,1]{0,1:T(2,128)(2,1)} %reshape.141) | copy-start | bytes 12292
  94.3 10.1 %copy-start.6 = (bf16[128,2048]{1,0:T(8,128)(2,1)S(1)}, bf16[128,2048]{1,0:T(8,128)(2,1)}, u32[]{:S(2)}) copy-start(bf16[128,2048]{1,0:T(8,128)(2,1)} %get-tuple-element.31.own_hbm) | copy-start | bytes 1572868
  102.6 67.3 %collective-permute-start.10 = (f32[128,512]{1,0:T(8,128)}, f32[128,512]{1,0:T(8,128)}, u32[]{:S(2)}, u32[]{:S(2)}) collective-permute-start(f32[128,512]{1,0:T(8,128)} %get-tuple-element.42), channel_id=1, source_target_pairs={{0,32},{32,0},{64,96},{96,64},{1,33},{33,1},{65,97},{97,65},{2,34}... | collective-permute-start | bytes 786440 | tf_op jit(solution)/shard_map/ppermute | solution.py:758
  133.5 12.9 %collective-permute-start.9 = (bf16[256,1024]{1,0:T(8,128)(2,1)S(1)}, bf16[256,1024]{1,0:T(8,128)(2,1)}, u32[]{:S(2)}, u32[]{:S(2)}) collective-permute-start(bf16[256,1024]{1,0:T(8,128)(2,1)S(1)} %dynamic-slice_convert_fusion), channel_id=1, source_target_pairs={{0,64},{64,0},{32,96},{96,32},{1,65},{65,1},{33,97},{97,33},{2,66}... | collective-permute-start | bytes 1572872 | tf_op jit(solution)/shard_map/ppermute | solution.py:740
  146.4 51.5 %all-to-all-start.4 = ((bf16[128,24,512]{2,1,0:T(8,128)(2,1)}), bf16[128,24,512]{2,1,0:T(8,128)(2,1)}, u32[]{:S(2)}, u32[]{:S(2)}) async-start(bf16[128,24,512]{2,1,0:T(8,128)(2,1)} %bitcast.54), calls=%async_computation.4 | async-start | bytes 6291456 | tf_op jit(solution)/shard_map/all_to_all | solution.py:745
  164.3 3.6 %collective-permute-start.11 = (bf16[256,512]{1,0:T(8,128)(2,1)}, bf16[256,512]{1,0:T(8,128)(2,1)}, u32[]{:S(2)}, u32[]{:S(2)}) collective-permute-start(bf16[256,512]{1,0:T(8,128)(2,1)} %dynamic-slice_convert_fusion.1), channel_id=1, source_target_pairs={{0,32},{32,0},{64,96},{96,64},{1,33},{33,1},{65,97},{97,65},{2,34}... | collective-permute-start | bytes 786440 | tf_op jit(solution)/shard_map/ppermute | solution.py:753
  (9 other events, 24.4 us)

commit v8 on v7

--- a/solution.py
+++ b/solution.py
@@ -61,7 +61,7 @@
     ]
     for copy in copies:
         copy.start()
-    for copy in copies:
+    for copy in copies[:2] + copies[3:]:
         copy.wait()
     stores = []
     scale = 1.0 / math.sqrt(HD)
@@ -75,13 +75,6 @@
         row_ids = ids_row[0:1, pl.ds(span + y * block, block)]
         query_ids = jnp.sum(jnp.where(same, row_ids, 0), axis=1, keepdims=True)
         pieces = []
-        for b in range(y, ROW):
-            key = past[b, :, 0:HD]
-            key_ids = ids_row[0:1, pl.ds(b * block, block)]
-            score = lax.dot_general(
-                query, key, (((1,), (1,)), ((), ())), preferred_element_type=F32
-            )
-            pieces.append(jnp.where(query_ids == key_ids, score, -1e30))
         for b in range(y + 1):
             key = own[b, :, 0:HD]
             key_ids = ids_row[0:1, pl.ds(span + b * block, block)]
@@ -92,6 +85,15 @@
             if b == y:
                 allowed = allowed & causal
             pieces.append(jnp.where(allowed, score, -1e30))
+        if y == 0:
+            copies[2].wait()
+        for b in range(y, ROW):
+            key = past[b, :, 0:HD]
+            key_ids = ids_row[0:1, pl.ds(b * block, block)]
+            score = lax.dot_general(
+                query, key, (((1,), (1,)), ((), ())), preferred_element_type=F32
+            )
+            pieces.append(jnp.where(query_ids == key_ids, score, -1e30))
         top = pieces[0].max(-1, keepdims=True)
         for piece in pieces[1:]:
             top = jnp.maximum(top, piece.max(-1, keepdims=True))
@@ -102,13 +104,13 @@
         inverse = 1.0 / total
         mixed = jnp.zeros((block, HD), F32)
         index = 0
+        for b in range(y + 1):
+            prob = weights[index].astype(BF)
+            mixed += jnp.dot(prob, own[b, :, HD : 2 * HD], preferred_element_type=F32)
+            index += 1
         for b in range(y, ROW):
             prob = weights[index].astype(BF)
             mixed += jnp.dot(prob, past[b, :, HD : 2 * HD], preferred_element_type=F32)
-            index += 1
-        for b in range(y + 1):
-            prob = weights[index].astype(BF)
-            mixed += jnp.dot(prob, own[b, :, HD : 2 * HD], preferred_element_type=F32)
             index += 1
         mixed = mixed * inverse
         half = block // 2
@@ -287,13 +289,15 @@
 
 
 def gather_kernel(
-    select_hbm, own_hbm, peer_hbm, out_hbm, select, rows, out, sems, out_sems
+    core, select_hbm, own_hbm, peer_hbm, out_hbm, both_hbm, select, rows, out, sems, out_sems, both_sems
 ):
     half = rows.shape[0] // 2
-    total, block = out.shape[0], out.shape[0] // 3
+    total = out.shape[0]
+    block = total // out_sems.shape[0]
+    own, peer = pl.ds(0, half), pl.ds(half, half)
     copies = [
-        pltpu.make_async_copy(own_hbm, rows.at[pl.ds(0, half)], sems.at[0]),
-        pltpu.make_async_copy(peer_hbm, rows.at[pl.ds(half, half)], sems.at[1]),
+        pltpu.make_async_copy(own_hbm, rows.at[own], sems.at[0]),
+        pltpu.make_async_copy(peer_hbm, rows.at[peer], sems.at[1]),
         pltpu.make_async_copy(select_hbm, select, sems.at[2]),
     ]
     for copy in copies:
@@ -309,32 +313,41 @@
         store = pltpu.make_async_copy(out.at[here], out_hbm.at[here], out_sems.at[i])
         store.start()
         stores.append(store)
+    for j, (source, place) in enumerate(((own, core[0]), (peer, 1 - core[0]))):
+        target = pl.ds(pl.multiple_of(place * half, half), half)
+        store = pltpu.make_async_copy(rows.at[source], both_hbm.at[target], both_sems.at[j])
+        store.start()
+        stores.append(store)
     for store in stores:
         store.wait()
 
 
-def gather_rows(select, own, peer):
+def gather_rows(core, select, own, peer):
     slots, rows = select.shape
     width = own.shape[1]
     hbm = pl.BlockSpec(memory_space=pltpu.HBM)
     return pl.pallas_call(
         gather_kernel,
-        out_shape=jax.ShapeDtypeStruct((slots, width), BF),
-        in_specs=[hbm, hbm, hbm],
-        out_specs=hbm,
+        out_shape=(
+            jax.ShapeDtypeStruct((slots, width), BF),
+            jax.ShapeDtypeStruct((rows, width), BF),
+        ),
+        in_specs=[pl.BlockSpec(memory_space=pltpu.SMEM), hbm, hbm, hbm],
+        out_specs=(hbm, hbm),
         scratch_shapes=[
             pltpu.VMEM((slots, rows), BF),
             pltpu.VMEM((rows, width), BF),
             pltpu.VMEM((slots, width), BF),
             pltpu.SemaphoreType.DMA((3,)),
-            pltpu.SemaphoreType.DMA((3,)),
+            pltpu.SemaphoreType.DMA((6,)),
+            pltpu.SemaphoreType.DMA((2,)),
         ],
         compiler_params=pltpu.CompilerParams(vmem_limit_bytes=58 << 20),
         cost_estimate=pl.CostEstimate(
-            flops=2 * slots * rows * width, bytes_accessed=5 << 20, transcendentals=0
+            flops=2 * slots * rows * width, bytes_accessed=7 << 20, transcendentals=0
         ),
         name="gather_rows",
-    )(select, own, peer)
+    )(core, select, own, peer)
 
 
 def slot_weight_kernel(rank, weight, high):
@@ -659,27 +672,6 @@
     past = lax.ppermute(
         own, "tok", [(s, s + ROW) for s in range(tok_count - ROW)]
     )
-    attended = attention(
-        place_in_row.reshape(1), ids_row, jnp.stack(query_parts, 0), own, past
-    )
-
-    core_groups = [
-        [
-            (chip * CORES + c) * tok_count + r * ROW + y
-            for c in range(CORES)
-            for y in range(ROW)
-        ]
-        for chip in range(CHIPS)
-        for r in range(rows_of_blocks)
-    ]
-    gathered = lax.all_to_all(
-        attended.reshape(CORES * ROW, half, HD),
-        BOTH,
-        split_axis=0,
-        concat_axis=0,
-        tiled=True,
-        axis_index_groups=core_groups,
-    ).reshape(CORES, ROW, half, HD)
     expert_ids = jnp.arange(EXPERTS, dtype=jnp.int32)
     named = routes[:, :, None] == expert_ids[None, None, :]
     onehot = jnp.sum(named.astype(F32), 1)
@@ -694,8 +686,30 @@
     place = jnp.arange(slots_core, dtype=jnp.int32) * CORES
     select = (rank_rel[:, None, :] == (place + core)[None, :, None]).astype(BF)
     select = select.reshape(EXPERTS * slots_core, tok_rows)
+    past, select = lax.optimization_barrier((past, select))
+    attended = attention(
+        place_in_row.reshape(1), ids_row, jnp.stack(query_parts, 0), own, past
+    )
+
+    core_groups = [
+        [
+            (chip * CORES + c) * tok_count + r * ROW + y
+            for c in range(CORES)
+            for y in range(ROW)
+        ]
+        for chip in range(CHIPS)
+        for r in range(rows_of_blocks)
+    ]
+    gathered = lax.all_to_all(
+        attended.reshape(CORES * ROW, half, HD),
+        BOTH,
+        split_axis=0,
+        concat_axis=0,
+        tiled=True,
+        axis_index_groups=core_groups,
+    ).reshape(CORES, ROW, half, HD)
     core_ref = core.reshape(1)
-    gathered, select, pieces = lax.optimization_barrier((gathered, select, pieces))
+    gathered, pieces = lax.optimization_barrier((gathered, pieces))
     projected_low = project(core_ref, gathered, out_proj, out_peer)
     projected_far = lax.ppermute(projected_low, "head", CROSS)
     pieces, _ = lax.optimization_barrier((pieces, projected_low))
@@ -706,15 +720,9 @@
     normed_own, landed = lax.optimization_barrier((normed_own, landed))
     normed_peer = lax.ppermute(normed_own, "head", INTRA)
 
-    outgoing = gather_rows(select, normed_own, normed_peer)
+    outgoing, normed_abs = gather_rows(core_ref, select, normed_own, normed_peer)
     rank, weight_of, _ = lax.optimization_barrier((rank, weight_of, outgoing))
     high = slot_weights(rank, weight_of, CORES * EXPERTS * slots_core)
-    late_own, late_peer, _ = lax.optimization_barrier((normed_own, normed_peer, outgoing))
-    normed_abs = jnp.where(
-        core == 0,
-        jnp.concatenate([late_own, late_peer], 0),
-        jnp.concatenate([late_peer, late_own], 0),
-    )
     arrived = lax.all_to_all(
         outgoing.reshape(tok_count, slots_core, model_width),
         "tok",

time: 203 us -> 204 us (level)
  matrix products: 15.2 us -> 12.9 us
  other arithmetic: 8.23 us -> 10.4 us
    all_to_all x1, waiting for transfers between devices: 4.67 us -> 2.26 us  [per_device(): lax.all_to_all(packed, 'tok', split_axis=0, concat_axis=0, tiled=True, ax...]
    all_to_all x1, waiting for transfers between devices: 2.37 us -> 4.61 us  [per_device(): lax.all_to_all(attended.reshape(CORES * ROW, half, HD), BOTH, split_axis=...]
    unnamed x40 -> x28, local copies, waits for them, and re-layouts: 5.96 us -> 5.85 us
where the time goes in v8:
time: 204 us; the launch traced here: 203 us
  waiting for transfers between devices  74 us (36%)
  starting transfers between devices  46 us (23%)
  Pallas kernels  33 us (16%)
  local copies, waits for them, and re-layouts  25.2 us (12%)
  matrix products  12.9 us (6%)
  other arithmetic  10.4 us (5%)
    all_to_all x1, waiting for transfers between devices, per_device(): lax.all_to_all(partial, BOTH, split_axis=0, concat_axis=0, tiled=True)  27.8 us
    all_to_all x1, waiting for transfers between devices, per_device(): lax.all_to_all(outgoing.reshape(tok_count, slots_core, model_width), 'tok...  21.9 us
    pallas_call x1, Pallas kernels, experts(): pl.pallas_call(expert_kernel, out_shape=jax.ShapeDtypeStruct((groups, row...  11.6 us
    all_to_all x1, starting transfers between devices, per_device(): lax.all_to_all(pieces, BOTH, split_axis=0, concat_axis=0, tiled=True)  9.92 us
    all_to_all x1, starting transfers between devices, per_device(): lax.all_to_all(partial, BOTH, split_axis=0, concat_axis=0, tiled=True)  9.9 us
    all_to_all x1, waiting for transfers between devices, per_device(): lax.all_to_all(pieces, BOTH, split_axis=0, concat_axis=0, tiled=True)  6.71 us
    all_to_all x1, starting transfers between devices, per_device(): lax.all_to_all(outgoing.reshape(tok_count, slots_core, model_width), 'tok...  5.95 us
    unnamed x28, local copies, waits for them, and re-layouts  5.85 us
  transfers between devices with their start and end apart: 17, of which 10 were waited for; matrix products, arithmetic and copies ran while one was open for 22% of the time, Pallas kernels for 10%

profile of v8, /device:TPU:0, one launch (start us, length us, event | category | flops | bytes accessed | tf_op | source)
XLA Modules:
  0.0 202.6 jit_solution(10400827927048438000)
XLA Ops:
  0.7 2.1 %pack_heads.1 = bf16[4,256,256]{2,1,0:T(8,128)(2,1)} custom-call(bf16[256,512]{1,0:T(8,128)(2,1)} %keys.1, bf16[256,512]{1,0:T(8,128)(2,1)} %values.1), custom_call_target="tpu_custom_call" | custom-call | bytes 1048576 | tf_op jit(solution)/shard_map/pack_heads/pallas_call | solution.py:36
  2.7 4.5 %all-to-all-start = ((bf16[4,256,256]{2,1,0:T(8,128)(2,1)}), bf16[4,256,256]{2,1,0:T(8,128)(2,1)}, u32[]{:S(2)}, u32[]{:S(2)}) async-start(bf16[4,256,256]{2,1,0:T(8,128)(2,1)} %pack_heads.1), calls=%async_computation | async-start | bytes 1048576 | tf_op jit(solution)/shard_map/all_to_all | solution.py:644
  14.6 2.3 %all-to-all-done.own_hbm = bf16[4,256,256]{2,1,0:T(8,128)(2,1)} async-done(((bf16[4,256,256]{2,1,0:T(8,128)(2,1)}), bf16[4,256,256]{2,1,0:T(8,128)(2,1)}, u32[]{:S(2)}, u32[]{:S(2)}) %all-to-all-start) | async-done | bytes 524320 | tf_op jit(solution)/shard_map/all_to_all | solution.py:644
  16.9 5.8 %collective-permute-start = (bf16[4,256,256]{2,1,0:T(8,128)(2,1)}, bf16[4,256,256]{2,1,0:T(8,128)(2,1)S(1)}, u32[]{:S(2)}, u32[]{:S(2)}) collective-permute-start(bf16[4,256,256]{2,1,0:T(8,128)(2,1)} %all-to-all-done.own_hbm), channel_id=1, source_target_pairs={{0,4},{1,5},{2,6},{3,7},{4,8},{5,9},{6,10},{7,11},{8,12},{9,13},{1... | collective-permute-start | bytes 1572872 | tf_op jit(solution)/shard_map/ppermute | solution.py:672
  29.3 2.5 %collective-permute-done.2 = bf16[256,128]{1,0:T(8,128)(2,1)S(1)} collective-permute-done((bf16[256,128]{1,0:T(8,128)(2,1)S(1)}, bf16[256,128]{1,0:T(8,128)(2,1)S(1)}, u32[]{:S(2)}, u32[]{:S(2)}) %collective-permute-start.2) | collective-permute-done | bytes 65568 | tf_op jit(solution)/shard_map/ppermute | solution.py:659
  34.4 4.7 %row_attention.1 = bf16[2,4,128,128]{3,2,1,0:T(8,128)(2,1)} custom-call(s32[1]{0:T(128)} %bitcast.3.place, s32[1,2048]{1,0:T(1,128)} %bitcast.61, bf16[4,256,128]{2,1,0:T(8,128)(2,1)} %pad_maximum_fusion.1.query_hbm, bf16[4,256,256]{2,1,0:T(8,128)(2,1)} %all-to-all-done.own_hbm, bf16[4,256,256]{2,1,0:T(8,128)(2,1)} %copy-done.8), custom_call_target="tpu_custom_call" | custom-call | flops 671088640 | bytes 3145728 | tf_op jit(solution)/shard_map/row_attention/pallas_call | solution.py:132
  39.1 4.1 %all-to-all-start.1 = ((bf16[8,128,128]{2,1,0:T(8,128)(2,1)}), bf16[8,128,128]{2,1,0:T(8,128)(2,1)}, u32[]{:S(2)}, u32[]{:S(2)}) async-start(bf16[8,128,128]{2,1,0:T(8,128)(2,1)} %bitcast.56), calls=%async_computation.1 | async-start | bytes 524288 | tf_op jit(solution)/shard_map/all_to_all | solution.py:703
  45.5 4.6 %all-to-all-done.1 = bf16[8,128,128]{2,1,0:T(8,128)(2,1)} async-done(((bf16[8,128,128]{2,1,0:T(8,128)(2,1)}), bf16[8,128,128]{2,1,0:T(8,128)(2,1)}, u32[]{:S(2)}, u32[]{:S(2)}) %all-to-all-start.1) | async-done | bytes 262176 | tf_op jit(solution)/shard_map/all_to_all | solution.py:703
  50.1 4.1 %project.1.near_hbm = bf16[128,2048]{1,0:T(8,128)(2,1)} custom-call(s32[1]{0:T(128)} %bitcast.core, bf16[2,4,128,128]{3,2,1,0:T(8,128)(2,1)} %bitcast.10.att_hbm, bf16[512,2048]{1,0:T(8,128)(2,1)} %own_hbm.1, bf16[512,2048]{1,0:T(8,128)(2,1)} %collective-permute-done.4.peer_hbm), custom_call_target="tpu_custom_call" | custom-call | flops 536870912 | bytes 6291456 | tf_op jit(solution)/shard_map/project/pallas_call | solution.py:196
  55.3 9.9 %all-to-all-start.2 = ((bf16[128,2,1024]{2,1,0:T(2,128)(2,1)}), bf16[128,2,1024]{2,1,0:T(2,128)(2,1)S(1)}, u32[]{:S(2)}, u32[]{:S(2)}) async-start(bf16[128,2,1024]{2,1,0:T(2,128)(2,1)} %reshape.135), calls=%async_computation.2 | async-start | bytes 1048576 | tf_op jit(solution)/shard_map/all_to_all | solution.py:716
  65.2 4.4 %collective-permute-done.5.far_hbm = bf16[128,2048]{1,0:T(8,128)(2,1)} collective-permute-done((bf16[128,2048]{1,0:T(8,128)(2,1)}, bf16[128,2048]{1,0:T(8,128)(2,1)}, u32[]{:S(2)}, u32[]{:S(2)}) %collective-permute-start.5) | collective-permute-done | bytes 524320 | tf_op jit(solution)/shard_map/ppermute | solution.py:714
  69.6 2.6 %add_and_norm.1 = (f32[128,2048]{1,0:T(8,128)}, bf16[128,2048]{1,0:T(8,128)(2,1)}) custom-call(s32[1]{0:T(128)} %bitcast.core, bf16[256,2048]{1,0:T(8,128)(2,1)} %hidden_hbm.1, bf16[128,2048]{1,0:T(8,128)(2,1)} %project.1.near_hbm, bf16[128,2048]{1,0:T(8,128)(2,1)} %collective-permute-done.5.far_hbm, f32[1,2048]{1,0:T(1,128)} %bitcast.60), custom_call_target="tpu_custom_call" | custom-call | flops 2097152 | bytes 4194304 | tf_op jit(solution)/shard_map/add_and_norm/pallas_call | solution.py:265
  72.2 6.7 %all-to-all-done.2 = bf16[128,2,1024]{2,1,0:T(2,128)(2,1)S(1)} async-done(((bf16[128,2,1024]{2,1,0:T(2,128)(2,1)}), bf16[128,2,1024]{2,1,0:T(2,128)(2,1)S(1)}, u32[]{:S(2)}, u32[]{:S(2)}) %all-to-all-start.2) | async-done | bytes 524320 | tf_op jit(solution)/shard_map/all_to_all | solution.py:716
  78.9 2.1 %collective-permute-done.6.peer_hbm = bf16[128,2048]{1,0:T(8,128)(2,1)S(1)} collective-permute-done((bf16[128,2048]{1,0:T(8,128)(2,1)}, bf16[128,2048]{1,0:T(8,128)(2,1)S(1)}, u32[]{:S(2)}, u32[]{:S(2)}) %collective-permute-start.6) | collective-permute-done | bytes 524320 | tf_op jit(solution)/shard_map/ppermute | solution.py:721
  81.8 3.8 %gather_rows.1 = (bf16[768,2048]{1,0:T(8,128)(2,1)}, bf16[256,2048]{1,0:T(8,128)(2,1)}) custom-call(s32[1]{0:T(128)} %bitcast.core, bf16[768,256]{1,0:T(8,128)(2,1)} %fusion.3.select_hbm, bf16[128,2048]{1,0:T(8,128)(2,1)} %get-tuple-element.30.own_hbm, bf16[128,2048]{1,0:T(8,128)(2,1)} %copy-done.9), custom_call_target="tpu_custom_call" | custom-call | flops 805306368 | bytes 7340032 | tf_op jit(solution)/shard_map/gather_rows/pallas_call | solution.py:329
  85.7 5.9 %all-to-all-start.3 = ((bf16[32,24,2048]{2,1,0:T(8,128)(2,1)}), bf16[32,24,2048]{2,1,0:T(8,128)(2,1)}, u32[]{:S(2)}, u32[]{:S(2)}) async-start(bf16[32,24,2048]{2,1,0:T(8,128)(2,1)} %bitcast.54), calls=%async_computation.3 | async-start | bytes 6291456 | tf_op jit(solution)/shard_map/all_to_all | solution.py:726
  101.1 1.9 constant_dynamic-slice_fusion
  105.5 4.7 %fusion.1 = f32[256,2,704]{0,2,1:T(8,128)S(1)} fusion(bf16[2048,2,704]{0,2,1:T(8,128)(2,1)} %param.24, bf16[256,2048]{1,0:T(8,128)(2,1)} %get-tuple-element.34), kind=kOutput, calls=%fused_computation.9 | convolution fusion | flops 1476395008 | bytes 8257536 | tf_op jit(solution)/shard_map/td,dgf->tgf/dot_general | solution.py:733
  112.5 21.9 %all-to-all-done.3 = bf16[32,24,2048]{2,1,0:T(8,128)(2,1)} async-done(((bf16[32,24,2048]{2,1,0:T(8,128)(2,1)}), bf16[32,24,2048]{2,1,0:T(8,128)(2,1)}, u32[]{:S(2)}, u32[]{:S(2)}) %all-to-all-start.3) | async-done | bytes 3145760 | tf_op jit(solution)/shard_map/all_to_all | solution.py:726
  135.8 11.6 %experts.1 = bf16[4,768,512]{2,1,0:T(8,128)(2,1)} custom-call(bf16[768,2048]{1,0:T(8,128)(2,1)} %bitcast.18.x_hbm, bf16[2,352,2048]{2,1,0:T(8,128)(2,1)} %bitcast.64, bf16[2,352,2048]{2,1,0:T(8,128)(2,1)} %collective-permute-done.7.both_peer, bf16[352,2048]{1,0:T(8,128)(2,1)} %bitcast.66, bf16[352,2048]{1,0:T(8,128)(2,1)} %collective-permute-done.8.down_peer), custom_call_target="tpu_custom_call" | custom-call | flops 6643777536 | bytes 15728640 | tf_op jit(solution)/shard_map/experts/pallas_call | solution.py:477
  147.4 9.9 %all-to-all-start.4 = ((bf16[128,24,512]{2,1,0:T(8,128)(2,1)}), bf16[128,24,512]{2,1,0:T(8,128)(2,1)}, u32[]{:S(2)}, u32[]{:S(2)}) async-start(bf16[128,24,512]{2,1,0:T(8,128)(2,1)} %bitcast.55), calls=%async_computation.4 | async-start | bytes 6291456 | tf_op jit(solution)/shard_map/all_to_all | solution.py:753
  169.1 2.0 %convert_add_fusion.1.shared_hbm = f32[256,512]{1,0:T(8,128)} fusion(bf16[256,512]{1,0:T(8,128)(2,1)} %collective-permute-done.11, f32[256,1024]{1,0:T(8,128)} %copy-done.2, s32[]{:T(128)S(6)} %select_n.187), kind=kLoop, calls=%fused_computation.20 | loop fusion | flops 262144 | bytes 1310724 | tf_op jit(solution)/shard_map/add | solution.py:761
  171.1 27.8 %all-to-all-done.4 = bf16[128,24,512]{2,1,0:T(8,128)(2,1)} async-done(((bf16[128,24,512]{2,1,0:T(8,128)(2,1)}), bf16[128,24,512]{2,1,0:T(8,128)(2,1)}, u32[]{:S(2)}, u32[]{:S(2)}) %all-to-all-start.4) | async-done | bytes 3145760 | tf_op jit(solution)/shard_map/all_to_all | solution.py:753
  198.9 3.5 %combine.1 = bf16[256,512]{1,0:T(8,128)(2,1)} custom-call(s32[1]{0:T(128)} %bitcast.core, bf16[256,1536]{1,0:T(8,128)(2,1)} %copy-done.1, bf16[2,1536,512]{2,1,0:T(8,128)(2,1)} %bitcast.24.back_hbm, f32[128,512]{1,0:T(8,128)} %get-tuple-element.45.mine_hbm, f32[128,512]{1,0:T(8,128)} %collective-permute-done.10.peers_hbm, ...), custom_call_target="tpu_custom_call" | custom-call | flops 1610612736 | bytes 7340032 | tf_op jit(solution)/shard_map/combine/pallas_call | solution.py:551
  (96 shorter events, 47.8 us)
Async XLA Ops:
  0.6 109.6 %copy-start = (bf16[704,2048]{1,0:T(8,128)(2,1)S(1)}, bf16[704,2048]{1,0:T(8,128)(2,1)}, u32[]{:S(2)}) copy-start(bf16[704,2048]{1,0:T(8,128)(2,1)} %param.25) | copy-start | bytes 8650756
  0.6 22.0 %copy-start.3 = (bf16[256,512]{1,0:T(8,128)(2,1)S(1)}, bf16[256,512]{1,0:T(8,128)(2,1)}, u32[]{:S(2)}) copy-start(bf16[256,512]{1,0:T(8,128)(2,1)} %values.1) | copy-start | bytes 786436
  2.7 14.1 %all-to-all-start = ((bf16[4,256,256]{2,1,0:T(8,128)(2,1)}), bf16[4,256,256]{2,1,0:T(8,128)(2,1)}, u32[]{:S(2)}, u32[]{:S(2)}) async-start(bf16[4,256,256]{2,1,0:T(8,128)(2,1)} %pack_heads.1), calls=%async_computation | async-start | bytes 1048576 | tf_op jit(solution)/shard_map/all_to_all | solution.py:644
  7.3 42.8 %collective-permute-start.4 = (bf16[512,2048]{1,0:T(8,128)(2,1)}, bf16[512,2048]{1,0:T(8,128)(2,1)}, u32[]{:S(2)}, u32[]{:S(2)}) collective-permute-start(bf16[512,2048]{1,0:T(8,128)(2,1)} %own_hbm.1), channel_id=1, source_target_pairs={{0,32},{32,0},{64,96},{96,64},{1,33},{33,1},{65,97},{97,65},{2,34}... | collective-permute-start | bytes 6291464 | tf_op jit(solution)/shard_map/ppermute | solution.py:638
  10.6 32.5 %copy-start.4 = (bf16[256,512]{1,0:T(8,128)(2,1)S(1)}, bf16[256,512]{1,0:T(8,128)(2,1)}, u32[]{:S(2)}) copy-start(bf16[256,512]{1,0:T(8,128)(2,1)} %keys.1) | copy-start | bytes 786436
  16.9 16.7 %collective-permute-start = (bf16[4,256,256]{2,1,0:T(8,128)(2,1)}, bf16[4,256,256]{2,1,0:T(8,128)(2,1)S(1)}, u32[]{:S(2)}, u32[]{:S(2)}) collective-permute-start(bf16[4,256,256]{2,1,0:T(8,128)(2,1)} %all-to-all-done.own_hbm), channel_id=1, source_target_pairs={{0,4},{1,5},{2,6},{3,7},{4,8},{5,9},{6,10},{7,11},{8,12},{9,13},{1... | collective-permute-start | bytes 1572872 | tf_op jit(solution)/shard_map/ppermute | solution.py:672
  24.6 4.7 %collective-permute-start.3 = (bf16[256,128]{1,0:T(8,128)(2,1)S(1)}, bf16[256,128]{1,0:T(8,128)(2,1)S(1)}, u32[]{:S(2)}, u32[]{:S(2)}) collective-permute-start(bf16[256,128]{1,0:T(8,128)(2,1)S(1)} %get-tuple-element.51), channel_id=1, source_target_pairs={{0,3},{1,0},{2,1},{3,2},{4,7},{5,4},{6,5},{7,6},{8,11},{9,8},{10,9... | collective-permute-start | bytes 196616 | tf_op jit(solution)/shard_map/ppermute | solution.py:659
  25.9 6.0 %collective-permute-start.2 = (bf16[256,128]{1,0:T(8,128)(2,1)S(1)}, bf16[256,128]{1,0:T(8,128)(2,1)S(1)}, u32[]{:S(2)}, u32[]{:S(2)}) collective-permute-start(bf16[256,128]{1,0:T(8,128)(2,1)S(1)} %get-tuple-element.52), channel_id=1, source_target_pairs={{0,2},{1,3},{2,0},{3,1},{4,6},{5,7},{6,4},{7,5},{8,10},{9,11},{10,... | collective-permute-start | bytes 196616 | tf_op jit(solution)/shard_map/ppermute | solution.py:659
  27.3 5.5 %collective-permute-start.1 = (bf16[256,128]{1,0:T(8,128)(2,1)S(1)}, bf16[256,128]{1,0:T(8,128)(2,1)S(1)}, u32[]{:S(2)}, u32[]{:S(2)}) collective-permute-start(bf16[256,128]{1,0:T(8,128)(2,1)S(1)} %get-tuple-element.53), channel_id=1, source_target_pairs={{0,1},{1,2},{2,3},{3,0},{4,5},{5,6},{6,7},{7,4},{8,9},{9,10},{10,1... | collective-permute-start | bytes 196616 | tf_op jit(solution)/shard_map/ppermute | solution.py:659
  39.1 11.0 %all-to-all-start.1 = ((bf16[8,128,128]{2,1,0:T(8,128)(2,1)}), bf16[8,128,128]{2,1,0:T(8,128)(2,1)}, u32[]{:S(2)}, u32[]{:S(2)}) async-start(bf16[8,128,128]{2,1,0:T(8,128)(2,1)} %bitcast.56), calls=%async_computation.1 | async-start | bytes 524288 | tf_op jit(solution)/shard_map/all_to_all | solution.py:703
  54.2 15.4 %collective-permute-start.5 = (bf16[128,2048]{1,0:T(8,128)(2,1)}, bf16[128,2048]{1,0:T(8,128)(2,1)}, u32[]{:S(2)}, u32[]{:S(2)}) collective-permute-start(bf16[128,2048]{1,0:T(8,128)(2,1)} %project.1.near_hbm), channel_id=1, source_target_pairs={{0,64},{64,0},{32,96},{96,32},{1,65},{65,1},{33,97},{97,33},{2,66}... | collective-permute-start | bytes 1572872 | tf_op jit(solution)/shard_map/ppermute | solution.py:714
  55.3 23.6 %all-to-all-start.2 = ((bf16[128,2,1024]{2,1,0:T(2,128)(2,1)}), bf16[128,2,1024]{2,1,0:T(2,128)(2,1)S(1)}, u32[]{:S(2)}, u32[]{:S(2)}) async-start(bf16[128,2,1024]{2,1,0:T(2,128)(2,1)} %reshape.135), calls=%async_computation.2 | async-start | bytes 1048576 | tf_op jit(solution)/shard_map/all_to_all | solution.py:716
  78.9 2.1 %collective-permute-start.6 = (bf16[128,2048]{1,0:T(8,128)(2,1)}, bf16[128,2048]{1,0:T(8,128)(2,1)S(1)}, u32[]{:S(2)}, u32[]{:S(2)}) collective-permute-start(bf16[128,2048]{1,0:T(8,128)(2,1)} %get-tuple-element.30.own_hbm), channel_id=1, source_target_pairs={{0,32},{32,0},{64,96},{96,64},{1,33},{33,1},{65,97},{97,65},{2,34}... | collective-permute-start | bytes 1572872 | tf_op jit(solution)/shard_map/ppermute | solution.py:721
  85.7 6.6 %copy-start.6 = (bf16[2048]{0:T(1024)(128)(2,1)S(1)}, bf16[2048]{0:T(1024)(128)(2,1)}, u32[]{:S(2)}) copy-start(bf16[2048]{0:T(1024)(128)(2,1)} %param.26) | copy-start | bytes 12292
  85.7 7.2 %copy-start.7 = (s32[32]{0:T(128)S(1)}, s32[32]{0:T(128)}, u32[]{:S(2)}) copy-start(s32[32]{0:T(128)} %get-tuple-element.56) | copy-start | bytes 388
  85.7 48.8 %all-to-all-start.3 = ((bf16[32,24,2048]{2,1,0:T(8,128)(2,1)}), bf16[32,24,2048]{2,1,0:T(8,128)(2,1)}, u32[]{:S(2)}, u32[]{:S(2)}) async-start(bf16[32,24,2048]{2,1,0:T(8,128)(2,1)} %bitcast.54), calls=%async_computation.3 | async-start | bytes 6291456 | tf_op jit(solution)/shard_map/all_to_all | solution.py:726
  91.6 44.1 %collective-permute-start.7 = (bf16[2,352,2048]{2,1,0:T(8,128)(2,1)}, bf16[2,352,2048]{2,1,0:T(8,128)(2,1)}, u32[]{:S(2)}, u32[]{:S(2)}) collective-permute-start(bf16[2,352,2048]{2,1,0:T(8,128)(2,1)} %bitcast.63), channel_id=1, source_target_pairs={{0,32},{32,0},{64,96},{96,64},{1,33},{33,1},{65,97},{97,65},{2,34}... | collective-permute-start | bytes 8650760 | tf_op jit(solution)/shard_map/ppermute | solution.py:639
  91.7 44.0 %collective-permute-start.8 = (bf16[352,2048]{1,0:T(8,128)(2,1)}, bf16[352,2048]{1,0:T(8,128)(2,1)}, u32[]{:S(2)}, u32[]{:S(2)}) collective-permute-start(bf16[352,2048]{1,0:T(8,128)(2,1)} %bitcast.65), channel_id=1, source_target_pairs={{0,32},{32,0},{64,96},{96,64},{1,33},{33,1},{65,97},{97,65},{2,34}... | collective-permute-start | bytes 4325384 | tf_op jit(solution)/shard_map/ppermute | solution.py:640
  93.5 10.3 %copy-start.5 = (bf16[2048,1]{0,1:T(2,128)(2,1)S(1)}, bf16[2048,1]{0,1:T(2,128)(2,1)}, u32[]{:S(2)}) copy-start(bf16[2048,1]{0,1:T(2,128)(2,1)} %reshape.141) | copy-start | bytes 12292
  103.0 68.1 %collective-permute-start.10 = (f32[128,512]{1,0:T(8,128)}, f32[128,512]{1,0:T(8,128)}, u32[]{:S(2)}, u32[]{:S(2)}) collective-permute-start(f32[128,512]{1,0:T(8,128)} %get-tuple-element.44), channel_id=1, source_target_pairs={{0,32},{32,0},{64,96},{96,64},{1,33},{33,1},{65,97},{97,65},{2,34}... | collective-permute-start | bytes 786440 | tf_op jit(solution)/shard_map/ppermute | solution.py:766
  134.5 12.9 %collective-permute-start.9 = (bf16[256,1024]{1,0:T(8,128)(2,1)S(1)}, bf16[256,1024]{1,0:T(8,128)(2,1)}, u32[]{:S(2)}, u32[]{:S(2)}) collective-permute-start(bf16[256,1024]{1,0:T(8,128)(2,1)S(1)} %dynamic-slice_convert_fusion), channel_id=1, source_target_pairs={{0,64},{64,0},{32,96},{96,32},{1,65},{65,1},{33,97},{97,33},{2,66}... | collective-permute-start | bytes 1572872 | tf_op jit(solution)/shard_map/ppermute | solution.py:748
  147.4 51.5 %all-to-all-start.4 = ((bf16[128,24,512]{2,1,0:T(8,128)(2,1)}), bf16[128,24,512]{2,1,0:T(8,128)(2,1)}, u32[]{:S(2)}, u32[]{:S(2)}) async-start(bf16[128,24,512]{2,1,0:T(8,128)(2,1)} %bitcast.55), calls=%async_computation.4 | async-start | bytes 6291456 | tf_op jit(solution)/shard_map/all_to_all | solution.py:753
  163.8 1.0 copy-start.2
  165.5 3.6 %collective-permute-start.11 = (bf16[256,512]{1,0:T(8,128)(2,1)}, bf16[256,512]{1,0:T(8,128)(2,1)}, u32[]{:S(2)}, u32[]{:S(2)}) collective-permute-start(bf16[256,512]{1,0:T(8,128)(2,1)} %dynamic-slice_convert_fusion.1), channel_id=1, source_target_pairs={{0,32},{32,0},{64,96},{96,64},{1,33},{33,1},{65,97},{97,65},{2,34}... | collective-permute-start | bytes 786440 | tf_op jit(solution)/shard_map/ppermute | solution.py:761
  (3 other events, 2.5 us)

commit v9 on v7

--- a/solution.py
+++ b/solution.py
@@ -22,26 +22,27 @@
 CROSS = [(0, 2), (2, 0), (1, 3), (3, 1)]
 
 
-def pack_kernel(keys, values, out):
-    for i in range(out.shape[0]):
-        here = pl.ds(i * HD, HD)
-        out[i, :, 0:HD] = keys[:, here]
-        out[i, :, HD : 2 * HD] = values[:, here]
-
-
-def pack_heads(keys, values):
+def pack_kernel(place, keys, values, *outs):
+    for step, out in enumerate(outs):
+        head = lax.rem(place[0] + step, ROW)
+        here = pl.ds(pl.multiple_of(head * HD, HD), HD)
+        out[:, 0:HD] = keys[:, here]
+        out[:, HD : 2 * HD] = values[:, here]
+
+
+def pack_heads(place, keys, values):
     rows, width = keys.shape
     vmem = pl.BlockSpec(memory_space=pltpu.VMEM)
     heads = width // HD
     return pl.pallas_call(
         pack_kernel,
-        out_shape=jax.ShapeDtypeStruct((heads, rows, 2 * HD), BF),
-        in_specs=[vmem, vmem],
-        out_specs=vmem,
+        out_shape=(jax.ShapeDtypeStruct((rows, 2 * HD), BF),) * heads,
+        in_specs=[pl.BlockSpec(memory_space=pltpu.SMEM), vmem, vmem],
+        out_specs=(vmem,) * heads,
         compiler_params=pltpu.CompilerParams(vmem_limit_bytes=60 << 20),
         cost_estimate=pl.CostEstimate(flops=0, bytes_accessed=1 << 20, transcendentals=0),
         name="pack_heads",
-    )(keys, values)
+    )(place, keys, values)
 
 
 def attention_kernel(
@@ -64,6 +65,10 @@
     for copy in copies:
         copy.wait()
     stores = []
+
+    def slot(b):
+        return lax.rem(place[0] + (ROW - b), ROW)
+
     scale = 1.0 / math.sqrt(HD)
     span = ROW * block
     row_pos = lax.broadcasted_iota(jnp.int32, (block, block), 0)
@@ -76,14 +81,14 @@
         query_ids = jnp.sum(jnp.where(same, row_ids, 0), axis=1, keepdims=True)
         pieces = []
         for b in range(y, ROW):
-            key = past[b, :, 0:HD]
+            key = past[slot(b), :, 0:HD]
             key_ids = ids_row[0:1, pl.ds(b * block, block)]
             score = lax.dot_general(
                 query, key, (((1,), (1,)), ((), ())), preferred_element_type=F32
             )
             pieces.append(jnp.where(query_ids == key_ids, score, -1e30))
         for b in range(y + 1):
-            key = own[b, :, 0:HD]
+            key = own[slot(b), :, 0:HD]
             key_ids = ids_row[0:1, pl.ds(span + b * block, block)]
             score = lax.dot_general(
                 query, key, (((1,), (1,)), ((), ())), preferred_element_type=F32
@@ -104,11 +109,11 @@
         index = 0
         for b in range(y, ROW):
             prob = weights[index].astype(BF)
-            mixed += jnp.dot(prob, past[b, :, HD : 2 * HD], preferred_element_type=F32)
+            mixed += jnp.dot(prob, past[slot(b), :, HD : 2 * HD], preferred_element_type=F32)
             index += 1
         for b in range(y + 1):
             prob = weights[index].astype(BF)
-            mixed += jnp.dot(prob, own[b, :, HD : 2 * HD], preferred_element_type=F32)
+            mixed += jnp.dot(prob, own[slot(b), :, HD : 2 * HD], preferred_element_type=F32)
             index += 1
         mixed = mixed * inverse
         half = block // 2
@@ -626,11 +631,21 @@
     gate_up_peer = lax.ppermute(gate_up_own, "head", INTRA)
     down_peer = lax.ppermute(down_own, "head", INTRA)
 
-    packed = pack_heads(keys, values)
-    row_groups = [[r * ROW + y for y in range(ROW)] for r in range(rows_of_blocks)]
-    own = lax.all_to_all(
-        packed, "tok", split_axis=0, concat_axis=0, tiled=True, axis_index_groups=row_groups
-    )
+    place_in_row = tok_index % ROW
+    own = []
+    for step, part in enumerate(pack_heads(place_in_row.reshape(1), keys, values)):
+        if step:
+            part = lax.ppermute(
+                part,
+                "tok",
+                [
+                    (r * ROW + y, r * ROW + (y + step) % ROW)
+                    for r in range(rows_of_blocks)
+                    for y in range(ROW)
+                ],
+            )
+        own.append(part)
+    own = jnp.stack(own, 0)
     span = ROW * tok_rows
     base = (tok_index // ROW) * span
     padded_ids = jnp.concatenate([jnp.full((span,), -1, jnp.int32), request_ids], 0)

time: 203 us -> 204 us (level)
    ppermute x3 -> x6, starting transfers between devices: 2.7 us -> 8.72 us  [per_device(): lax.ppermute(part, 'tok', [(r * ROW + y, r * ROW + (y + step) % ROW) for...]
    all_to_all x1 -> x0, waiting for transfers between devices: 4.67 us -> none  [per_device(): lax.all_to_all(packed, 'tok', split_axis=0, concat_axis=0, tiled=True, ax...]
    all_to_all x1 -> x0, starting transfers between devices: 4.55 us -> none  [per_device(): lax.all_to_all(packed, 'tok', split_axis=0, concat_axis=0, tiled=True, ax...]
    ppermute x1, waiting for transfers between devices: 0.04 us -> 2.67 us  [per_device(): lax.ppermute(own, 'tok', [(s, s + ROW) for s in range(tok_count - ROW)])]
    ppermute x3 -> x6, waiting for transfers between devices: 4.19 us -> 4.88 us  [per_device(): lax.ppermute(part, 'tok', [(r * ROW + y, r * ROW + (y + step) % ROW) for...]
    unnamed x40 -> x34, local copies, waits for them, and re-layouts: 5.96 us -> 5.96 us
  transfers between devices with their start and end apart: 17 -> 19, of which waited for: 10 -> 10; matrix products, arithmetic and copies ran while one was open for 22% -> 23% of each run, Pallas kernels for 10% -> 10%
where the time goes in v9:
time: 204 us; the launch traced here: 203 us
  waiting for transfers between devices  71.4 us (35%)
  starting transfers between devices  47.8 us (23%)
  Pallas kernels  32.8 us (16%)
  local copies, waits for them, and re-layouts  23.5 us (12%)
  matrix products  16.2 us (8%)
  other arithmetic  10.1 us (5%)
    all_to_all x1, waiting for transfers between devices, per_device(): lax.all_to_all(partial, BOTH, split_axis=0, concat_axis=0, tiled=True)  27.9 us
    all_to_all x1, waiting for transfers between devices, per_device(): lax.all_to_all(outgoing.reshape(tok_count, slots_core, model_width), 'tok...  20.4 us
    pallas_call x1, Pallas kernels, experts(): pl.pallas_call(expert_kernel, out_shape=jax.ShapeDtypeStruct((groups, row...  11.6 us
    all_to_all x1, starting transfers between devices, per_device(): lax.all_to_all(pieces, BOTH, split_axis=0, concat_axis=0, tiled=True)  10.2 us
    all_to_all x1, starting transfers between devices, per_device(): lax.all_to_all(partial, BOTH, split_axis=0, concat_axis=0, tiled=True)  9.89 us
    ppermute x6, starting transfers between devices, per_device(): lax.ppermute(part, 'tok', [(r * ROW + y, r * ROW + (y + step) % ROW) for...  8.72 us
    all_to_all x1, waiting for transfers between devices, per_device(): lax.all_to_all(pieces, BOTH, split_axis=0, concat_axis=0, tiled=True)  7.63 us
    squeeze x4, local copies, waits for them, and re-layouts, place_pages(): landed[h]  6.48 us
  transfers between devices with their start and end apart: 19, of which 10 were waited for; matrix products, arithmetic and copies ran while one was open for 23% of the time, Pallas kernels for 10%

profile of v9, /device:TPU:0, one launch (start us, length us, event | category | flops | bytes accessed | tf_op | source)
XLA Modules:
  0.0 203.2 jit_solution(3001931927990978046)
XLA Ops:
  0.7 2.1 %pack_heads.1 = (bf16[256,256]{1,0:T(8,128)(2,1)}, bf16[256,256]{1,0:T(8,128)(2,1)}, bf16[256,256]{1,0:T(8,128)(2,1)}, bf16[256,256]{1,0:T(8,128)(2,1)}) custom-call(s32[1]{0:T(128)} %bitcast.1.place, bf16[256,512]{1,0:T(8,128)(2,1)} %keys.1, bf16[256,512]{1,0:T(8,128)(2,1)} %values.1), custom_call_target="tpu_custom_call" | custom-call | bytes 1048576 | tf_op jit(solution)/shard_map/pack_heads/pallas_call | solution.py:37
  4.4 2.9 %collective-permute-start.1 = (bf16[256,256]{1,0:T(8,128)(2,1)}, bf16[256,256]{1,0:T(8,128)(2,1)}, u32[]{:S(2)}, u32[]{:S(2)}) collective-permute-start(bf16[256,256]{1,0:T(8,128)(2,1)} %get-tuple-element.27), channel_id=1, source_target_pairs={{0,2},{1,3},{2,0},{3,1},{4,6},{5,7},{6,4},{7,5},{8,10},{9,11},{10,... | collective-permute-start | bytes 393224 | tf_op jit(solution)/shard_map/ppermute | solution.py:638
  16.5 5.8 %collective-permute-start.6 = (bf16[4,256,256]{2,1,0:T(8,128)(2,1)S(1)}, bf16[4,256,256]{2,1,0:T(8,128)(2,1)S(1)}, u32[]{:S(2)}, u32[]{:S(2)}) collective-permute-start(bf16[4,256,256]{2,1,0:T(8,128)(2,1)S(1)} %pad_maximum_fusion.own_hbm), channel_id=1, source_target_pairs={{0,4},{1,5},{2,6},{3,7},{4,8},{5,9},{6,10},{7,11},{8,12},{9,13},{1... | collective-permute-start | bytes 1572872 | tf_op jit(solution)/shard_map/ppermute | solution.py:674
  22.9 2.3 %collective-permute-start.4 = (bf16[256,128]{1,0:T(8,128)(2,1)S(1)}, bf16[256,128]{1,0:T(8,128)(2,1)S(1)}, u32[]{:S(2)}, u32[]{:S(2)}) collective-permute-start(bf16[256,128]{1,0:T(8,128)(2,1)S(1)} %get-tuple-element.58), channel_id=1, source_target_pairs={{0,2},{1,3},{2,0},{3,1},{4,6},{5,7},{6,4},{7,5},{8,10},{9,11},{10,... | collective-permute-start | bytes 196616 | tf_op jit(solution)/shard_map/ppermute | solution.py:661
  28.7 2.0 collective-permute-done.3
  31.4 2.7 %collective-permute-done.6.past_hbm = bf16[4,256,256]{2,1,0:T(8,128)(2,1)S(1)} collective-permute-done((bf16[4,256,256]{2,1,0:T(8,128)(2,1)S(1)}, bf16[4,256,256]{2,1,0:T(8,128)(2,1)S(1)}, u32[]{:S(2)}, u32[]{:S(2)}) %collective-permute-start.6) | collective-permute-done | bytes 524320 | tf_op jit(solution)/shard_map/ppermute | solution.py:674
  34.9 4.8 %row_attention.1 = bf16[2,4,128,128]{3,2,1,0:T(8,128)(2,1)} custom-call(s32[1]{0:T(128)} %bitcast.1.place, s32[1,2048]{1,0:T(1,128)} %bitcast.65, bf16[4,256,128]{2,1,0:T(8,128)(2,1)} %pad_maximum_fusion.2.query_hbm, bf16[4,256,256]{2,1,0:T(8,128)(2,1)} %copy-done.7, bf16[4,256,256]{2,1,0:T(8,128)(2,1)} %copy-done.12), custom_call_target="tpu_custom_call" | custom-call | flops 671088640 | bytes 3145728 | tf_op jit(solution)/shard_map/row_attention/pallas_call | solution.py:135
  39.7 4.1 %all-to-all-start = ((bf16[8,128,128]{2,1,0:T(8,128)(2,1)}), bf16[8,128,128]{2,1,0:T(8,128)(2,1)}, u32[]{:S(2)}, u32[]{:S(2)}) async-start(bf16[8,128,128]{2,1,0:T(8,128)(2,1)} %bitcast.59), calls=%async_computation | async-start | bytes 524288 | tf_op jit(solution)/shard_map/all_to_all | solution.py:690
  48.4 2.4 %all-to-all-done = bf16[8,128,128]{2,1,0:T(8,128)(2,1)} async-done(((bf16[8,128,128]{2,1,0:T(8,128)(2,1)}), bf16[8,128,128]{2,1,0:T(8,128)(2,1)}, u32[]{:S(2)}, u32[]{:S(2)}) %all-to-all-start) | async-done | bytes 262176 | tf_op jit(solution)/shard_map/all_to_all | solution.py:690
  50.7 4.1 %project.1.near_hbm = bf16[128,2048]{1,0:T(8,128)(2,1)} custom-call(s32[1]{0:T(128)} %bitcast.core, bf16[2,4,128,128]{3,2,1,0:T(8,128)(2,1)} %bitcast.12.att_hbm, bf16[512,2048]{1,0:T(8,128)(2,1)} %own_hbm.1, bf16[512,2048]{1,0:T(8,128)(2,1)} %collective-permute-done.7.peer_hbm), custom_call_target="tpu_custom_call" | custom-call | flops 536870912 | bytes 6291456 | tf_op jit(solution)/shard_map/project/pallas_call | solution.py:199
  55.9 10.2 %all-to-all-start.1 = ((bf16[128,2,1024]{2,1,0:T(2,128)(2,1)}), bf16[128,2,1024]{2,1,0:T(2,128)(2,1)S(1)}, u32[]{:S(2)}, u32[]{:S(2)}) async-start(bf16[128,2,1024]{2,1,0:T(2,128)(2,1)} %reshape.136), calls=%async_computation.1 | async-start | bytes 1048576 | tf_op jit(solution)/shard_map/all_to_all | solution.py:717
  66.1 3.5 %collective-permute-done.8.far_hbm = bf16[128,2048]{1,0:T(8,128)(2,1)} collective-permute-done((bf16[128,2048]{1,0:T(8,128)(2,1)}, bf16[128,2048]{1,0:T(8,128)(2,1)}, u32[]{:S(2)}, u32[]{:S(2)}) %collective-permute-start.8) | collective-permute-done | bytes 524320 | tf_op jit(solution)/shard_map/ppermute | solution.py:715
  69.6 2.6 %add_and_norm.1 = (f32[128,2048]{1,0:T(8,128)}, bf16[128,2048]{1,0:T(8,128)(2,1)}) custom-call(s32[1]{0:T(128)} %bitcast.core, bf16[256,2048]{1,0:T(8,128)(2,1)} %hidden_hbm.1, bf16[128,2048]{1,0:T(8,128)(2,1)} %project.1.near_hbm, bf16[128,2048]{1,0:T(8,128)(2,1)} %collective-permute-done.8.far_hbm, f32[1,2048]{1,0:T(1,128)} %bitcast.64), custom_call_target="tpu_custom_call" | custom-call | flops 2097152 | bytes 4194304 | tf_op jit(solution)/shard_map/add_and_norm/pallas_call | solution.py:268
  72.2 7.6 %all-to-all-done.1 = bf16[128,2,1024]{2,1,0:T(2,128)(2,1)S(1)} async-done(((bf16[128,2,1024]{2,1,0:T(2,128)(2,1)}), bf16[128,2,1024]{2,1,0:T(2,128)(2,1)S(1)}, u32[]{:S(2)}, u32[]{:S(2)}) %all-to-all-start.1) | async-done | bytes 524320 | tf_op jit(solution)/shard_map/all_to_all | solution.py:717
  79.9 2.1 %collective-permute-done.9.peer_hbm = bf16[128,2048]{1,0:T(8,128)(2,1)S(1)} collective-permute-done((bf16[128,2048]{1,0:T(8,128)(2,1)}, bf16[128,2048]{1,0:T(8,128)(2,1)S(1)}, u32[]{:S(2)}, u32[]{:S(2)}) %collective-permute-start.9) | collective-permute-done | bytes 524320 | tf_op jit(solution)/shard_map/ppermute | solution.py:722
  82.8 3.5 %gather_rows.1 = bf16[768,2048]{1,0:T(8,128)(2,1)} custom-call(bf16[768,256]{1,0:T(8,128)(2,1)} %fusion.3.select_hbm, bf16[128,2048]{1,0:T(8,128)(2,1)} %get-tuple-element.39.own_hbm, bf16[128,2048]{1,0:T(8,128)(2,1)} %copy-done.5), custom_call_target="tpu_custom_call" | custom-call | flops 805306368 | bytes 5242880 | tf_op jit(solution)/shard_map/gather_rows/pallas_call | solution.py:325
  86.3 5.9 %all-to-all-start.2 = ((bf16[32,24,2048]{2,1,0:T(8,128)(2,1)}), bf16[32,24,2048]{2,1,0:T(8,128)(2,1)}, u32[]{:S(2)}, u32[]{:S(2)}) async-start(bf16[32,24,2048]{2,1,0:T(8,128)(2,1)} %bitcast.57), calls=%async_computation.2 | async-start | bytes 6291456 | tf_op jit(solution)/shard_map/all_to_all | solution.py:733
  108.0 4.4 %fusion.1 = f32[256,2,704]{0,2,1:T(8,128)S(1)} fusion(bf16[2048,2,704]{0,2,1:T(8,128)(2,1)} %param.24, bf16[128,2048]{1,0:T(8,128)(2,1)S(1)} %copy-done.6, bf16[128,2048]{1,0:T(8,128)(2,1)S(1)} %copy-done.4, pred[]{:T(512)S(6)} %eq.103), kind=kOutput, calls=%fused_computation.10 | convolution fusion | flops 1481113600 | bytes 8257537 | tf_op jit(solution)/shard_map/td,dgf->tgf/dot_general | solution.py:740
  114.7 20.4 %all-to-all-done.2 = bf16[32,24,2048]{2,1,0:T(8,128)(2,1)} async-done(((bf16[32,24,2048]{2,1,0:T(8,128)(2,1)}), bf16[32,24,2048]{2,1,0:T(8,128)(2,1)}, u32[]{:S(2)}, u32[]{:S(2)}) %all-to-all-start.2) | async-done | bytes 3145760 | tf_op jit(solution)/shard_map/all_to_all | solution.py:733
  136.4 11.6 %experts.1 = bf16[4,768,512]{2,1,0:T(8,128)(2,1)} custom-call(bf16[768,2048]{1,0:T(8,128)(2,1)} %bitcast.22.x_hbm, bf16[2,352,2048]{2,1,0:T(8,128)(2,1)} %bitcast.68, bf16[2,352,2048]{2,1,0:T(8,128)(2,1)} %collective-permute-done.10.both_peer, bf16[352,2048]{1,0:T(8,128)(2,1)} %bitcast.70, bf16[352,2048]{1,0:T(8,128)(2,1)} %collective-permute-done.11.down_peer), custom_call_target="tpu_custom_call" | custom-call | flops 6643777536 | bytes 15728640 | tf_op jit(solution)/shard_map/experts/pallas_call | solution.py:469
  148.0 9.9 %all-to-all-start.3 = ((bf16[128,24,512]{2,1,0:T(8,128)(2,1)}), bf16[128,24,512]{2,1,0:T(8,128)(2,1)}, u32[]{:S(2)}, u32[]{:S(2)}) async-start(bf16[128,24,512]{2,1,0:T(8,128)(2,1)} %bitcast.58), calls=%async_computation.3 | async-start | bytes 6291456 | tf_op jit(solution)/shard_map/all_to_all | solution.py:760
  169.5 2.1 %convert_add_fusion.1.shared_hbm = f32[256,512]{1,0:T(8,128)} fusion(bf16[256,512]{1,0:T(8,128)(2,1)} %collective-permute-done.14, f32[256,1024]{1,0:T(8,128)} %copy-done.3, s32[]{:T(128)S(6)} %select_n.199), kind=kLoop, calls=%fused_computation.22 | loop fusion | flops 262144 | bytes 1310724 | tf_op jit(solution)/shard_map/add | solution.py:768
  171.6 27.9 %all-to-all-done.3 = bf16[128,24,512]{2,1,0:T(8,128)(2,1)} async-done(((bf16[128,24,512]{2,1,0:T(8,128)(2,1)}), bf16[128,24,512]{2,1,0:T(8,128)(2,1)}, u32[]{:S(2)}, u32[]{:S(2)}) %all-to-all-start.3) | async-done | bytes 3145760 | tf_op jit(solution)/shard_map/all_to_all | solution.py:760
  199.5 3.5 %combine.1 = bf16[256,512]{1,0:T(8,128)(2,1)} custom-call(s32[1]{0:T(128)} %bitcast.core, bf16[256,1536]{1,0:T(8,128)(2,1)} %copy-done.1, bf16[2,1536,512]{2,1,0:T(8,128)(2,1)} %bitcast.28.back_hbm, f32[128,512]{1,0:T(8,128)} %get-tuple-element.51.mine_hbm, f32[128,512]{1,0:T(8,128)} %collective-permute-done.13.peers_hbm, ...), custom_call_target="tpu_custom_call" | custom-call | flops 1610612736 | bytes 7340032 | tf_op jit(solution)/shard_map/combine/pallas_call | solution.py:543
  (107 shorter events, 53.6 us)
Async XLA Ops:
  0.6 111.8 %copy-start = (bf16[704,2048]{1,0:T(8,128)(2,1)S(1)}, bf16[704,2048]{1,0:T(8,128)(2,1)}, u32[]{:S(2)}) copy-start(bf16[704,2048]{1,0:T(8,128)(2,1)} %param.25) | copy-start | bytes 8650756
  0.6 21.7 %copy-start.8 = (bf16[256,512]{1,0:T(8,128)(2,1)S(1)}, bf16[256,512]{1,0:T(8,128)(2,1)}, u32[]{:S(2)}) copy-start(bf16[256,512]{1,0:T(8,128)(2,1)} %param.16) | copy-start | bytes 786436
  2.7 22.5 %copy-start.9 = (s32[8192]{0:T(1024)S(1)}, s32[8192]{0:T(1024)}, u32[]{:S(2)}) copy-start(s32[8192]{0:T(1024)} %param.19) | copy-start | bytes 98308
  2.7 12.5 %collective-permute-start = (bf16[256,256]{1,0:T(8,128)(2,1)}, bf16[256,256]{1,0:T(8,128)(2,1)}, u32[]{:S(2)}, u32[]{:S(2)}) collective-permute-start(bf16[256,256]{1,0:T(8,128)(2,1)} %get-tuple-element.26), channel_id=1, source_target_pairs={{0,1},{1,2},{2,3},{3,0},{4,5},{5,6},{6,7},{7,4},{8,9},{9,10},{10,1... | collective-permute-start | bytes 393224 | tf_op jit(solution)/shard_map/ppermute | solution.py:638
  4.4 10.9 %collective-permute-start.1 = (bf16[256,256]{1,0:T(8,128)(2,1)}, bf16[256,256]{1,0:T(8,128)(2,1)}, u32[]{:S(2)}, u32[]{:S(2)}) collective-permute-start(bf16[256,256]{1,0:T(8,128)(2,1)} %get-tuple-element.27), channel_id=1, source_target_pairs={{0,2},{1,3},{2,0},{3,1},{4,6},{5,7},{6,4},{7,5},{8,10},{9,11},{10,... | collective-permute-start | bytes 393224 | tf_op jit(solution)/shard_map/ppermute | solution.py:638
  7.3 8.0 %collective-permute-start.2 = (bf16[256,256]{1,0:T(8,128)(2,1)}, bf16[256,256]{1,0:T(8,128)(2,1)}, u32[]{:S(2)}, u32[]{:S(2)}) collective-permute-start(bf16[256,256]{1,0:T(8,128)(2,1)} %get-tuple-element.28), channel_id=1, source_target_pairs={{0,3},{1,0},{2,1},{3,2},{4,7},{5,4},{6,5},{7,6},{8,11},{9,8},{10,9... | collective-permute-start | bytes 393224 | tf_op jit(solution)/shard_map/ppermute | solution.py:638
  8.7 42.1 %collective-permute-start.7 = (bf16[512,2048]{1,0:T(8,128)(2,1)}, bf16[512,2048]{1,0:T(8,128)(2,1)}, u32[]{:S(2)}, u32[]{:S(2)}) collective-permute-start(bf16[512,2048]{1,0:T(8,128)(2,1)} %own_hbm.1), channel_id=1, source_target_pairs={{0,32},{32,0},{64,96},{96,64},{1,33},{33,1},{65,97},{97,65},{2,34}... | collective-permute-start | bytes 6291464 | tf_op jit(solution)/shard_map/ppermute | solution.py:630
  16.5 17.6 %copy-start.7 = (bf16[4,256,256]{2,1,0:T(8,128)(2,1)}, bf16[4,256,256]{2,1,0:T(8,128)(2,1)S(1)}, u32[]{:S(2)}) copy-start(bf16[4,256,256]{2,1,0:T(8,128)(2,1)S(1)} %pad_maximum_fusion.own_hbm) | copy-start | bytes 1572868
  16.5 17.6 %collective-permute-start.6 = (bf16[4,256,256]{2,1,0:T(8,128)(2,1)S(1)}, bf16[4,256,256]{2,1,0:T(8,128)(2,1)S(1)}, u32[]{:S(2)}, u32[]{:S(2)}) collective-permute-start(bf16[4,256,256]{2,1,0:T(8,128)(2,1)S(1)} %pad_maximum_fusion.own_hbm), channel_id=1, source_target_pairs={{0,4},{1,5},{2,6},{3,7},{4,8},{5,9},{6,10},{7,11},{8,12},{9,13},{1... | collective-permute-start | bytes 1572872 | tf_op jit(solution)/shard_map/ppermute | solution.py:674
  22.4 5.0 %collective-permute-start.5 = (bf16[256,128]{1,0:T(8,128)(2,1)S(1)}, bf16[256,128]{1,0:T(8,128)(2,1)S(1)}, u32[]{:S(2)}, u32[]{:S(2)}) collective-permute-start(bf16[256,128]{1,0:T(8,128)(2,1)S(1)} %get-tuple-element.57), channel_id=1, source_target_pairs={{0,3},{1,0},{2,1},{3,2},{4,7},{5,4},{6,5},{7,6},{8,11},{9,8},{10,9... | collective-permute-start | bytes 196616 | tf_op jit(solution)/shard_map/ppermute | solution.py:661
  22.9 5.8 %collective-permute-start.4 = (bf16[256,128]{1,0:T(8,128)(2,1)S(1)}, bf16[256,128]{1,0:T(8,128)(2,1)S(1)}, u32[]{:S(2)}, u32[]{:S(2)}) collective-permute-start(bf16[256,128]{1,0:T(8,128)(2,1)S(1)} %get-tuple-element.58), channel_id=1, source_target_pairs={{0,2},{1,3},{2,0},{3,1},{4,6},{5,7},{6,4},{7,5},{8,10},{9,11},{10,... | collective-permute-start | bytes 196616 | tf_op jit(solution)/shard_map/ppermute | solution.py:661
  25.2 5.5 %collective-permute-start.3 = (bf16[256,128]{1,0:T(8,128)(2,1)S(1)}, bf16[256,128]{1,0:T(8,128)(2,1)S(1)}, u32[]{:S(2)}, u32[]{:S(2)}) collective-permute-start(bf16[256,128]{1,0:T(8,128)(2,1)S(1)} %get-tuple-element.59), channel_id=1, source_target_pairs={{0,1},{1,2},{2,3},{3,0},{4,5},{5,6},{6,7},{7,4},{8,9},{9,10},{10,1... | collective-permute-start | bytes 196616 | tf_op jit(solution)/shard_map/ppermute | solution.py:661
  39.7 11.0 %all-to-all-start = ((bf16[8,128,128]{2,1,0:T(8,128)(2,1)}), bf16[8,128,128]{2,1,0:T(8,128)(2,1)}, u32[]{:S(2)}, u32[]{:S(2)}) async-start(bf16[8,128,128]{2,1,0:T(8,128)(2,1)} %bitcast.59), calls=%async_computation | async-start | bytes 524288 | tf_op jit(solution)/shard_map/all_to_all | solution.py:690
  54.9 14.8 %collective-permute-start.8 = (bf16[128,2048]{1,0:T(8,128)(2,1)}, bf16[128,2048]{1,0:T(8,128)(2,1)}, u32[]{:S(2)}, u32[]{:S(2)}) collective-permute-start(bf16[128,2048]{1,0:T(8,128)(2,1)} %project.1.near_hbm), channel_id=1, source_target_pairs={{0,64},{64,0},{32,96},{96,32},{1,65},{65,1},{33,97},{97,33},{2,66}... | collective-permute-start | bytes 1572872 | tf_op jit(solution)/shard_map/ppermute | solution.py:715
  55.9 23.9 %all-to-all-start.1 = ((bf16[128,2,1024]{2,1,0:T(2,128)(2,1)}), bf16[128,2,1024]{2,1,0:T(2,128)(2,1)S(1)}, u32[]{:S(2)}, u32[]{:S(2)}) async-start(bf16[128,2,1024]{2,1,0:T(2,128)(2,1)} %reshape.136), calls=%async_computation.1 | async-start | bytes 1048576 | tf_op jit(solution)/shard_map/all_to_all | solution.py:717
  79.9 2.1 %collective-permute-start.9 = (bf16[128,2048]{1,0:T(8,128)(2,1)}, bf16[128,2048]{1,0:T(8,128)(2,1)S(1)}, u32[]{:S(2)}, u32[]{:S(2)}) collective-permute-start(bf16[128,2048]{1,0:T(8,128)(2,1)} %get-tuple-element.39.own_hbm), channel_id=1, source_target_pairs={{0,32},{32,0},{64,96},{96,64},{1,33},{33,1},{65,97},{97,65},{2,34}... | collective-permute-start | bytes 1572872 | tf_op jit(solution)/shard_map/ppermute | solution.py:722
  86.3 48.8 %all-to-all-start.2 = ((bf16[32,24,2048]{2,1,0:T(8,128)(2,1)}), bf16[32,24,2048]{2,1,0:T(8,128)(2,1)}, u32[]{:S(2)}, u32[]{:S(2)}) async-start(bf16[32,24,2048]{2,1,0:T(8,128)(2,1)} %bitcast.57), calls=%async_computation.2 | async-start | bytes 6291456 | tf_op jit(solution)/shard_map/all_to_all | solution.py:733
  92.2 44.1 %collective-permute-start.10 = (bf16[2,352,2048]{2,1,0:T(8,128)(2,1)}, bf16[2,352,2048]{2,1,0:T(8,128)(2,1)}, u32[]{:S(2)}, u32[]{:S(2)}) collective-permute-start(bf16[2,352,2048]{2,1,0:T(8,128)(2,1)} %bitcast.67), channel_id=1, source_target_pairs={{0,32},{32,0},{64,96},{96,64},{1,33},{33,1},{65,97},{97,65},{2,34}... | collective-permute-start | bytes 8650760 | tf_op jit(solution)/shard_map/ppermute | solution.py:631
  92.3 44.0 %collective-permute-start.11 = (bf16[352,2048]{1,0:T(8,128)(2,1)}, bf16[352,2048]{1,0:T(8,128)(2,1)}, u32[]{:S(2)}, u32[]{:S(2)}) collective-permute-start(bf16[352,2048]{1,0:T(8,128)(2,1)} %bitcast.69), channel_id=1, source_target_pairs={{0,32},{32,0},{64,96},{96,64},{1,33},{33,1},{65,97},{97,65},{2,34}... | collective-permute-start | bytes 4325384 | tf_op jit(solution)/shard_map/ppermute | solution.py:632
  94.1 12.1 %copy-start.10 = (bf16[2048,1]{0,1:T(2,128)(2,1)S(1)}, bf16[2048,1]{0,1:T(2,128)(2,1)}, u32[]{:S(2)}) copy-start(bf16[2048,1]{0,1:T(2,128)(2,1)} %reshape.142) | copy-start | bytes 12292
  104.3 67.3 %collective-permute-start.13 = (f32[128,512]{1,0:T(8,128)}, f32[128,512]{1,0:T(8,128)}, u32[]{:S(2)}, u32[]{:S(2)}) collective-permute-start(f32[128,512]{1,0:T(8,128)} %get-tuple-element.50), channel_id=1, source_target_pairs={{0,32},{32,0},{64,96},{96,64},{1,33},{33,1},{65,97},{97,65},{2,34}... | collective-permute-start | bytes 786440 | tf_op jit(solution)/shard_map/ppermute | solution.py:773
  135.1 12.9 %collective-permute-start.12 = (bf16[256,1024]{1,0:T(8,128)(2,1)S(1)}, bf16[256,1024]{1,0:T(8,128)(2,1)}, u32[]{:S(2)}, u32[]{:S(2)}) collective-permute-start(bf16[256,1024]{1,0:T(8,128)(2,1)S(1)} %dynamic-slice_convert_fusion), channel_id=1, source_target_pairs={{0,64},{64,0},{32,96},{96,32},{1,65},{65,1},{33,97},{97,33},{2,66}... | collective-permute-start | bytes 1572872 | tf_op jit(solution)/shard_map/ppermute | solution.py:755
  148.0 51.5 %all-to-all-start.3 = ((bf16[128,24,512]{2,1,0:T(8,128)(2,1)}), bf16[128,24,512]{2,1,0:T(8,128)(2,1)}, u32[]{:S(2)}, u32[]{:S(2)}) async-start(bf16[128,24,512]{2,1,0:T(8,128)(2,1)} %bitcast.58), calls=%async_computation.3 | async-start | bytes 6291456 | tf_op jit(solution)/shard_map/all_to_all | solution.py:760
  165.9 3.6 %collective-permute-start.14 = (bf16[256,512]{1,0:T(8,128)(2,1)}, bf16[256,512]{1,0:T(8,128)(2,1)}, u32[]{:S(2)}, u32[]{:S(2)}) collective-permute-start(bf16[256,512]{1,0:T(8,128)(2,1)} %dynamic-slice_convert_fusion.1), channel_id=1, source_target_pairs={{0,32},{32,0},{64,96},{96,64},{1,33},{33,1},{65,97},{97,65},{2,34}... | collective-permute-start | bytes 786440 | tf_op jit(solution)/shard_map/ppermute | solution.py:768
  (8 other events, 27.3 us)

commit v10 on v9

--- a/solution.py
+++ b/solution.py
@@ -651,7 +651,7 @@
     padded_ids = jnp.concatenate([jnp.full((span,), -1, jnp.int32), request_ids], 0)
     window_ids = lax.dynamic_slice_in_dim(padded_ids, base, 2 * span, 0)
     ids_row = window_ids[None, :]
-    queries, own = lax.optimization_barrier((queries, own))
+    queries, own, page_keys, page_values = lax.optimization_barrier((queries, own, keys, values))
     place_in_row = tok_index % ROW
     query_parts = []
     for step in range(ROW):
@@ -670,7 +670,7 @@
         query_parts.append(part)
     slots_all = page_slots.reshape(tok_count, tok_rows // PAGE)
     owner_all = slots_all // (tok_rows // PAGE)
-    pieces = page_pieces(keys, values, owner_all, tok_count, head_count, tok_index)
+    pieces = page_pieces(page_keys, page_values, owner_all, tok_count, head_count, tok_index)
     past = lax.ppermute(
         own, "tok", [(s, s + ROW) for s in range(tok_count - ROW)]
     )

time: 204 us -> 202 us (level)
  matrix products: 16.2 us -> 13.6 us
    all_to_all x1, waiting for transfers between devices: 7.63 us -> 3.96 us  [per_device(): lax.all_to_all(pieces, BOTH, split_axis=0, concat_axis=0, tiled=True)]
    ppermute x1, waiting for transfers between devices: 3.48 us -> 7.14 us  [per_device(): projected_far = lax.ppermute(projected_low, 'head', CROSS)]
    ppermute x1, waiting for transfers between devices: 2.67 us -> 0.01 us  [per_device(): lax.ppermute(own, 'tok', [(s, s + ROW) for s in range(tok_count - ROW)])]
    dot_general x2, matrix products: 3.87 us -> 1.27 us  [page_pieces(): jnp.dot(pick, part, preferred_element_type=F32).astype(BF)]
    all_to_all x1, waiting for transfers between devices: 2.36 us -> 4.59 us  [per_device(): lax.all_to_all(attended.reshape(CORES * ROW, half, HD), BOTH, split_axis=...]
    unnamed x34 -> x32, local copies, waits for them, and re-layouts: 5.96 us -> 5.17 us
  transfers between devices with their start and end apart: 19 -> 19, of which waited for: 10 -> 9; matrix products, arithmetic and copies ran while one was open for 23% -> 22% of each run, Pallas kernels for 10% -> 10%
where the time goes in v10:
time: 202 us; the launch traced here: 201 us
  waiting for transfers between devices  70.4 us (35%)
  starting transfers between devices  49 us (24%)
  Pallas kernels  32.8 us (16%)
  local copies, waits for them, and re-layouts  23.6 us (12%)
  matrix products  13.6 us (7%)
  other arithmetic  10.6 us (5%)
    all_to_all x1, waiting for transfers between devices, per_device(): lax.all_to_all(partial, BOTH, split_axis=0, concat_axis=0, tiled=True)  27.9 us
    all_to_all x1, waiting for transfers between devices, per_device(): lax.all_to_all(outgoing.reshape(tok_count, slots_core, model_width), 'tok...  20.4 us
    pallas_call x1, Pallas kernels, experts(): pl.pallas_call(expert_kernel, out_shape=jax.ShapeDtypeStruct((groups, row...  11.6 us
    ppermute x6, starting transfers between devices, per_device(): lax.ppermute(part, 'tok', [(r * ROW + y, r * ROW + (y + step) % ROW) for...  9.97 us
    all_to_all x1, starting transfers between devices, per_device(): lax.all_to_all(partial, BOTH, split_axis=0, concat_axis=0, tiled=True)  9.89 us
    all_to_all x1, starting transfers between devices, per_device(): lax.all_to_all(pieces, BOTH, split_axis=0, concat_axis=0, tiled=True)  9.24 us
    ppermute x1, waiting for transfers between devices, per_device(): projected_far = lax.ppermute(projected_low, 'head', CROSS)  7.14 us
    ppermute x1, starting transfers between devices, per_device(): lax.ppermute(own, 'tok', [(s, s + ROW) for s in range(tok_count - ROW)])  6.59 us
  transfers between devices with their start and end apart: 19, of which 9 were waited for; matrix products, arithmetic and copies ran while one was open for 22% of the time, Pallas kernels for 10%

profile of v10, /device:TPU:0, one launch (start us, length us, event | category | flops | bytes accessed | tf_op | source)
XLA Modules:
  0.0 201.2 jit_solution(6261915333278023152)
XLA Ops:
  0.7 2.1 %pack_heads.1 = (bf16[256,256]{1,0:T(8,128)(2,1)}, bf16[256,256]{1,0:T(8,128)(2,1)}, bf16[256,256]{1,0:T(8,128)(2,1)}, bf16[256,256]{1,0:T(8,128)(2,1)}) custom-call(s32[1]{0:T(128)} %bitcast.1.place, bf16[256,512]{1,0:T(8,128)(2,1)} %keys.1, bf16[256,512]{1,0:T(8,128)(2,1)} %values.1), custom_call_target="tpu_custom_call" | custom-call | bytes 1048576 | tf_op jit(solution)/shard_map/pack_heads/pallas_call | solution.py:37
  4.4 2.9 %collective-permute-start.1 = (bf16[256,256]{1,0:T(8,128)(2,1)}, bf16[256,256]{1,0:T(8,128)(2,1)}, u32[]{:S(2)}, u32[]{:S(2)}) collective-permute-start(bf16[256,256]{1,0:T(8,128)(2,1)} %get-tuple-element.29), channel_id=1, source_target_pairs={{0,2},{1,3},{2,0},{3,1},{4,6},{5,7},{6,4},{7,5},{8,10},{9,11},{10,... | collective-permute-start | bytes 393224 | tf_op jit(solution)/shard_map/ppermute | solution.py:638
  13.6 2.0 pad_maximum_fusion.own_hbm
  15.6 6.6 %collective-permute-start.6 = (bf16[4,256,256]{2,1,0:T(8,128)(2,1)}, bf16[4,256,256]{2,1,0:T(8,128)(2,1)}, u32[]{:S(2)}, u32[]{:S(2)}) collective-permute-start(bf16[4,256,256]{2,1,0:T(8,128)(2,1)} %pad_maximum_fusion.own_hbm), channel_id=1, source_target_pairs={{0,4},{1,5},{2,6},{3,7},{4,8},{5,9},{6,10},{7,11},{8,12},{9,13},{1... | collective-permute-start | bytes 1572872 | tf_op jit(solution)/shard_map/ppermute | solution.py:674
  24.4 2.1 %collective-permute-start.5 = (bf16[256,128]{1,0:T(8,128)(2,1)S(1)}, bf16[256,128]{1,0:T(8,128)(2,1)S(1)}, u32[]{:S(2)}, u32[]{:S(2)}) collective-permute-start(bf16[256,128]{1,0:T(8,128)(2,1)S(1)} %get-tuple-element.61), channel_id=1, source_target_pairs={{0,3},{1,0},{2,1},{3,2},{4,7},{5,4},{6,5},{7,6},{8,11},{9,8},{10,9... | collective-permute-start | bytes 196616 | tf_op jit(solution)/shard_map/ppermute | solution.py:661
  29.5 2.8 %collective-permute-done.4 = bf16[256,128]{1,0:T(8,128)(2,1)S(1)} collective-permute-done((bf16[256,128]{1,0:T(8,128)(2,1)S(1)}, bf16[256,128]{1,0:T(8,128)(2,1)S(1)}, u32[]{:S(2)}, u32[]{:S(2)}) %collective-permute-start.4) | collective-permute-done | bytes 65568 | tf_op jit(solution)/shard_map/ppermute | solution.py:661
  33.9 4.8 %row_attention.1 = bf16[2,4,128,128]{3,2,1,0:T(8,128)(2,1)} custom-call(s32[1]{0:T(128)} %bitcast.1.place, s32[1,2048]{1,0:T(1,128)} %bitcast.65, bf16[4,256,128]{2,1,0:T(8,128)(2,1)} %pad_maximum_fusion.2.query_hbm, bf16[4,256,256]{2,1,0:T(8,128)(2,1)} %pad_maximum_fusion.own_hbm, bf16[4,256,256]{2,1,0:T(8,128)(2,1)} %collective-permute-done.6.past_hbm), custom_call_target="tpu_custom_call" | custom-call | flops 671088640 | bytes 3145728 | tf_op jit(solution)/shard_map/row_attention/pallas_call | solution.py:135
  38.7 4.1 %all-to-all-start = ((bf16[8,128,128]{2,1,0:T(8,128)(2,1)}), bf16[8,128,128]{2,1,0:T(8,128)(2,1)}, u32[]{:S(2)}, u32[]{:S(2)}) async-start(bf16[8,128,128]{2,1,0:T(8,128)(2,1)} %bitcast.59), calls=%async_computation | async-start | bytes 524288 | tf_op jit(solution)/shard_map/all_to_all | solution.py:690
  45.1 4.6 %all-to-all-done = bf16[8,128,128]{2,1,0:T(8,128)(2,1)} async-done(((bf16[8,128,128]{2,1,0:T(8,128)(2,1)}), bf16[8,128,128]{2,1,0:T(8,128)(2,1)}, u32[]{:S(2)}, u32[]{:S(2)}) %all-to-all-start) | async-done | bytes 262176 | tf_op jit(solution)/shard_map/all_to_all | solution.py:690
  49.7 4.1 %project.1.near_hbm = bf16[128,2048]{1,0:T(8,128)(2,1)} custom-call(s32[1]{0:T(128)} %bitcast.core, bf16[2,4,128,128]{3,2,1,0:T(8,128)(2,1)} %bitcast.12.att_hbm, bf16[512,2048]{1,0:T(8,128)(2,1)} %own_hbm.1, bf16[512,2048]{1,0:T(8,128)(2,1)} %collective-permute-done.7.peer_hbm), custom_call_target="tpu_custom_call" | custom-call | flops 536870912 | bytes 6291456 | tf_op jit(solution)/shard_map/project/pallas_call | solution.py:199
  54.9 9.2 %all-to-all-start.1 = ((bf16[128,2,1024]{2,1,0:T(2,128)(2,1)}), bf16[128,2,1024]{2,1,0:T(2,128)(2,1)S(1)}, u32[]{:S(2)}, u32[]{:S(2)}) async-start(bf16[128,2,1024]{2,1,0:T(2,128)(2,1)} %reshape.136), calls=%async_computation.1 | async-start | bytes 1048576 | tf_op jit(solution)/shard_map/all_to_all | solution.py:717
  64.2 7.1 %collective-permute-done.8.far_hbm = bf16[128,2048]{1,0:T(8,128)(2,1)} collective-permute-done((bf16[128,2048]{1,0:T(8,128)(2,1)}, bf16[128,2048]{1,0:T(8,128)(2,1)}, u32[]{:S(2)}, u32[]{:S(2)}) %collective-permute-start.8) | collective-permute-done | bytes 524320 | tf_op jit(solution)/shard_map/ppermute | solution.py:715
  71.3 2.6 %add_and_norm.1 = (f32[128,2048]{1,0:T(8,128)}, bf16[128,2048]{1,0:T(8,128)(2,1)}) custom-call(s32[1]{0:T(128)} %bitcast.core, bf16[256,2048]{1,0:T(8,128)(2,1)} %hidden_hbm.1, bf16[128,2048]{1,0:T(8,128)(2,1)} %project.1.near_hbm, bf16[128,2048]{1,0:T(8,128)(2,1)} %collective-permute-done.8.far_hbm, f32[1,2048]{1,0:T(1,128)} %bitcast.64), custom_call_target="tpu_custom_call" | custom-call | flops 2097152 | bytes 4194304 | tf_op jit(solution)/shard_map/add_and_norm/pallas_call | solution.py:268
  73.9 4.0 %all-to-all-done.1 = bf16[128,2,1024]{2,1,0:T(2,128)(2,1)S(1)} async-done(((bf16[128,2,1024]{2,1,0:T(2,128)(2,1)}), bf16[128,2,1024]{2,1,0:T(2,128)(2,1)S(1)}, u32[]{:S(2)}, u32[]{:S(2)}) %all-to-all-start.1) | async-done | bytes 524320 | tf_op jit(solution)/shard_map/all_to_all | solution.py:717
  77.9 2.1 %collective-permute-done.9.peer_hbm = bf16[128,2048]{1,0:T(8,128)(2,1)S(1)} collective-permute-done((bf16[128,2048]{1,0:T(8,128)(2,1)}, bf16[128,2048]{1,0:T(8,128)(2,1)S(1)}, u32[]{:S(2)}, u32[]{:S(2)}) %collective-permute-start.9) | collective-permute-done | bytes 524320 | tf_op jit(solution)/shard_map/ppermute | solution.py:722
  80.8 3.5 %gather_rows.1 = bf16[768,2048]{1,0:T(8,128)(2,1)} custom-call(bf16[768,256]{1,0:T(8,128)(2,1)} %fusion.3.select_hbm, bf16[128,2048]{1,0:T(8,128)(2,1)} %get-tuple-element.43.own_hbm, bf16[128,2048]{1,0:T(8,128)(2,1)} %copy-done.7), custom_call_target="tpu_custom_call" | custom-call | flops 805306368 | bytes 5242880 | tf_op jit(solution)/shard_map/gather_rows/pallas_call | solution.py:325
  84.3 6.0 %all-to-all-start.2 = ((bf16[32,24,2048]{2,1,0:T(8,128)(2,1)}), bf16[32,24,2048]{2,1,0:T(8,128)(2,1)}, u32[]{:S(2)}, u32[]{:S(2)}) async-start(bf16[32,24,2048]{2,1,0:T(8,128)(2,1)} %bitcast.57), calls=%async_computation.2 | async-start | bytes 6291456 | tf_op jit(solution)/shard_map/all_to_all | solution.py:733
  106.1 4.4 %fusion.1 = f32[256,2,704]{0,2,1:T(8,128)S(1)} fusion(bf16[2048,2,704]{0,2,1:T(8,128)(2,1)} %param.24, bf16[128,2048]{1,0:T(8,128)(2,1)S(1)} %copy-done.8, bf16[128,2048]{1,0:T(8,128)(2,1)S(1)} %copy-done.6, pred[]{:T(512)S(6)} %eq.103), kind=kOutput, calls=%fused_computation.10 | convolution fusion | flops 1481113600 | bytes 8257537 | tf_op jit(solution)/shard_map/td,dgf->tgf/dot_general | solution.py:740
  112.7 20.4 %all-to-all-done.2 = bf16[32,24,2048]{2,1,0:T(8,128)(2,1)} async-done(((bf16[32,24,2048]{2,1,0:T(8,128)(2,1)}), bf16[32,24,2048]{2,1,0:T(8,128)(2,1)}, u32[]{:S(2)}, u32[]{:S(2)}) %all-to-all-start.2) | async-done | bytes 3145760 | tf_op jit(solution)/shard_map/all_to_all | solution.py:733
  134.4 11.6 %experts.1 = bf16[4,768,512]{2,1,0:T(8,128)(2,1)} custom-call(bf16[768,2048]{1,0:T(8,128)(2,1)} %bitcast.22.x_hbm, bf16[2,352,2048]{2,1,0:T(8,128)(2,1)} %bitcast.68, bf16[2,352,2048]{2,1,0:T(8,128)(2,1)} %collective-permute-done.10.both_peer, bf16[352,2048]{1,0:T(8,128)(2,1)} %bitcast.70, bf16[352,2048]{1,0:T(8,128)(2,1)} %collective-permute-done.11.down_peer), custom_call_target="tpu_custom_call" | custom-call | flops 6643777536 | bytes 15728640 | tf_op jit(solution)/shard_map/experts/pallas_call | solution.py:469
  146.0 9.9 %all-to-all-start.3 = ((bf16[128,24,512]{2,1,0:T(8,128)(2,1)}), bf16[128,24,512]{2,1,0:T(8,128)(2,1)}, u32[]{:S(2)}, u32[]{:S(2)}) async-start(bf16[128,24,512]{2,1,0:T(8,128)(2,1)} %bitcast.58), calls=%async_computation.3 | async-start | bytes 6291456 | tf_op jit(solution)/shard_map/all_to_all | solution.py:760
  167.5 2.0 %convert_add_fusion.1.shared_hbm = f32[256,512]{1,0:T(8,128)} fusion(bf16[256,512]{1,0:T(8,128)(2,1)} %collective-permute-done.14, f32[256,1024]{1,0:T(8,128)} %copy-done.3, s32[]{:T(128)S(6)} %select_n.199), kind=kLoop, calls=%fused_computation.22 | loop fusion | flops 262144 | bytes 1310724 | tf_op jit(solution)/shard_map/add | solution.py:768
  169.6 27.9 %all-to-all-done.3 = bf16[128,24,512]{2,1,0:T(8,128)(2,1)} async-done(((bf16[128,24,512]{2,1,0:T(8,128)(2,1)}), bf16[128,24,512]{2,1,0:T(8,128)(2,1)}, u32[]{:S(2)}, u32[]{:S(2)}) %all-to-all-start.3) | async-done | bytes 3145760 | tf_op jit(solution)/shard_map/all_to_all | solution.py:760
  197.5 3.5 %combine.1 = bf16[256,512]{1,0:T(8,128)(2,1)} custom-call(s32[1]{0:T(128)} %bitcast.core, bf16[256,1536]{1,0:T(8,128)(2,1)} %copy-done.1, bf16[2,1536,512]{2,1,0:T(8,128)(2,1)} %bitcast.28.back_hbm, f32[128,512]{1,0:T(8,128)} %get-tuple-element.55.mine_hbm, f32[128,512]{1,0:T(8,128)} %collective-permute-done.13.peers_hbm, ...), custom_call_target="tpu_custom_call" | custom-call | flops 1610612736 | bytes 7340032 | tf_op jit(solution)/shard_map/combine/pallas_call | solution.py:543
  (105 shorter events, 49.7 us)
Async XLA Ops:
  0.6 109.9 %copy-start = (bf16[704,2048]{1,0:T(8,128)(2,1)S(1)}, bf16[704,2048]{1,0:T(8,128)(2,1)}, u32[]{:S(2)}) copy-start(bf16[704,2048]{1,0:T(8,128)(2,1)} %param.25) | copy-start | bytes 8650756
  0.7 27.8 %copy-start.4 = (bf16[256,512]{1,0:T(8,128)(2,1)S(1)}, bf16[256,512]{1,0:T(8,128)(2,1)}, u32[]{:S(2)}) copy-start(bf16[256,512]{1,0:T(8,128)(2,1)} %keys.1) | copy-start | bytes 786436
  2.7 10.3 %collective-permute-start = (bf16[256,256]{1,0:T(8,128)(2,1)}, bf16[256,256]{1,0:T(8,128)(2,1)}, u32[]{:S(2)}, u32[]{:S(2)}) collective-permute-start(bf16[256,256]{1,0:T(8,128)(2,1)} %get-tuple-element.28), channel_id=1, source_target_pairs={{0,1},{1,2},{2,3},{3,0},{4,5},{5,6},{6,7},{7,4},{8,9},{9,10},{10,1... | collective-permute-start | bytes 393224 | tf_op jit(solution)/shard_map/ppermute | solution.py:638
  4.4 9.2 %collective-permute-start.1 = (bf16[256,256]{1,0:T(8,128)(2,1)}, bf16[256,256]{1,0:T(8,128)(2,1)}, u32[]{:S(2)}, u32[]{:S(2)}) collective-permute-start(bf16[256,256]{1,0:T(8,128)(2,1)} %get-tuple-element.29), channel_id=1, source_target_pairs={{0,2},{1,3},{2,0},{3,1},{4,6},{5,7},{6,4},{7,5},{8,10},{9,11},{10,... | collective-permute-start | bytes 393224 | tf_op jit(solution)/shard_map/ppermute | solution.py:638
  7.3 6.3 %collective-permute-start.2 = (bf16[256,256]{1,0:T(8,128)(2,1)}, bf16[256,256]{1,0:T(8,128)(2,1)}, u32[]{:S(2)}, u32[]{:S(2)}) collective-permute-start(bf16[256,256]{1,0:T(8,128)(2,1)} %get-tuple-element.30), channel_id=1, source_target_pairs={{0,3},{1,0},{2,1},{3,2},{4,7},{5,4},{6,5},{7,6},{8,11},{9,8},{10,9... | collective-permute-start | bytes 393224 | tf_op jit(solution)/shard_map/ppermute | solution.py:638
  8.6 41.1 %collective-permute-start.7 = (bf16[512,2048]{1,0:T(8,128)(2,1)}, bf16[512,2048]{1,0:T(8,128)(2,1)}, u32[]{:S(2)}, u32[]{:S(2)}) collective-permute-start(bf16[512,2048]{1,0:T(8,128)(2,1)} %own_hbm.1), channel_id=1, source_target_pairs={{0,32},{32,0},{64,96},{96,64},{1,33},{33,1},{65,97},{97,65},{2,34}... | collective-permute-start | bytes 6291464 | tf_op jit(solution)/shard_map/ppermute | solution.py:630
  15.6 18.3 %collective-permute-start.6 = (bf16[4,256,256]{2,1,0:T(8,128)(2,1)}, bf16[4,256,256]{2,1,0:T(8,128)(2,1)}, u32[]{:S(2)}, u32[]{:S(2)}) collective-permute-start(bf16[4,256,256]{2,1,0:T(8,128)(2,1)} %pad_maximum_fusion.own_hbm), channel_id=1, source_target_pairs={{0,4},{1,5},{2,6},{3,7},{4,8},{5,9},{6,10},{7,11},{8,12},{9,13},{1... | collective-permute-start | bytes 1572872 | tf_op jit(solution)/shard_map/ppermute | solution.py:674
  24.4 18.4 %copy-start.5 = (bf16[256,512]{1,0:T(8,128)(2,1)S(1)}, bf16[256,512]{1,0:T(8,128)(2,1)}, u32[]{:S(2)}) copy-start(bf16[256,512]{1,0:T(8,128)(2,1)} %values.1) | copy-start | bytes 786436
  24.4 5.1 %collective-permute-start.5 = (bf16[256,128]{1,0:T(8,128)(2,1)S(1)}, bf16[256,128]{1,0:T(8,128)(2,1)S(1)}, u32[]{:S(2)}, u32[]{:S(2)}) collective-permute-start(bf16[256,128]{1,0:T(8,128)(2,1)S(1)} %get-tuple-element.61), channel_id=1, source_target_pairs={{0,3},{1,0},{2,1},{3,2},{4,7},{5,4},{6,5},{7,6},{8,11},{9,8},{10,9... | collective-permute-start | bytes 196616 | tf_op jit(solution)/shard_map/ppermute | solution.py:661
  26.6 5.8 %collective-permute-start.4 = (bf16[256,128]{1,0:T(8,128)(2,1)S(1)}, bf16[256,128]{1,0:T(8,128)(2,1)S(1)}, u32[]{:S(2)}, u32[]{:S(2)}) collective-permute-start(bf16[256,128]{1,0:T(8,128)(2,1)S(1)} %get-tuple-element.62), channel_id=1, source_target_pairs={{0,2},{1,3},{2,0},{3,1},{4,6},{5,7},{6,4},{7,5},{8,10},{9,11},{10,... | collective-permute-start | bytes 196616 | tf_op jit(solution)/shard_map/ppermute | solution.py:661
  27.7 5.5 %collective-permute-start.3 = (bf16[256,128]{1,0:T(8,128)(2,1)S(1)}, bf16[256,128]{1,0:T(8,128)(2,1)S(1)}, u32[]{:S(2)}, u32[]{:S(2)}) collective-permute-start(bf16[256,128]{1,0:T(8,128)(2,1)S(1)} %get-tuple-element.63), channel_id=1, source_target_pairs={{0,1},{1,2},{2,3},{3,0},{4,5},{5,6},{6,7},{7,4},{8,9},{9,10},{10,1... | collective-permute-start | bytes 196616 | tf_op jit(solution)/shard_map/ppermute | solution.py:661
  38.7 11.0 %all-to-all-start = ((bf16[8,128,128]{2,1,0:T(8,128)(2,1)}), bf16[8,128,128]{2,1,0:T(8,128)(2,1)}, u32[]{:S(2)}, u32[]{:S(2)}) async-start(bf16[8,128,128]{2,1,0:T(8,128)(2,1)} %bitcast.59), calls=%async_computation | async-start | bytes 524288 | tf_op jit(solution)/shard_map/all_to_all | solution.py:690
  53.8 17.5 %collective-permute-start.8 = (bf16[128,2048]{1,0:T(8,128)(2,1)}, bf16[128,2048]{1,0:T(8,128)(2,1)}, u32[]{:S(2)}, u32[]{:S(2)}) collective-permute-start(bf16[128,2048]{1,0:T(8,128)(2,1)} %project.1.near_hbm), channel_id=1, source_target_pairs={{0,64},{64,0},{32,96},{96,32},{1,65},{65,1},{33,97},{97,33},{2,66}... | collective-permute-start | bytes 1572872 | tf_op jit(solution)/shard_map/ppermute | solution.py:715
  54.9 23.0 %all-to-all-start.1 = ((bf16[128,2,1024]{2,1,0:T(2,128)(2,1)}), bf16[128,2,1024]{2,1,0:T(2,128)(2,1)S(1)}, u32[]{:S(2)}, u32[]{:S(2)}) async-start(bf16[128,2,1024]{2,1,0:T(2,128)(2,1)} %reshape.136), calls=%async_computation.1 | async-start | bytes 1048576 | tf_op jit(solution)/shard_map/all_to_all | solution.py:717
  77.9 2.1 %collective-permute-start.9 = (bf16[128,2048]{1,0:T(8,128)(2,1)}, bf16[128,2048]{1,0:T(8,128)(2,1)S(1)}, u32[]{:S(2)}, u32[]{:S(2)}) collective-permute-start(bf16[128,2048]{1,0:T(8,128)(2,1)} %get-tuple-element.43.own_hbm), channel_id=1, source_target_pairs={{0,32},{32,0},{64,96},{96,64},{1,33},{33,1},{65,97},{97,65},{2,34}... | collective-permute-start | bytes 1572872 | tf_op jit(solution)/shard_map/ppermute | solution.py:722
  84.3 48.8 %all-to-all-start.2 = ((bf16[32,24,2048]{2,1,0:T(8,128)(2,1)}), bf16[32,24,2048]{2,1,0:T(8,128)(2,1)}, u32[]{:S(2)}, u32[]{:S(2)}) async-start(bf16[32,24,2048]{2,1,0:T(8,128)(2,1)} %bitcast.57), calls=%async_computation.2 | async-start | bytes 6291456 | tf_op jit(solution)/shard_map/all_to_all | solution.py:733
  90.3 44.1 %collective-permute-start.10 = (bf16[2,352,2048]{2,1,0:T(8,128)(2,1)}, bf16[2,352,2048]{2,1,0:T(8,128)(2,1)}, u32[]{:S(2)}, u32[]{:S(2)}) collective-permute-start(bf16[2,352,2048]{2,1,0:T(8,128)(2,1)} %bitcast.67), channel_id=1, source_target_pairs={{0,32},{32,0},{64,96},{96,64},{1,33},{33,1},{65,97},{97,65},{2,34}... | collective-permute-start | bytes 8650760 | tf_op jit(solution)/shard_map/ppermute | solution.py:631
  90.4 44.0 %collective-permute-start.11 = (bf16[352,2048]{1,0:T(8,128)(2,1)}, bf16[352,2048]{1,0:T(8,128)(2,1)}, u32[]{:S(2)}, u32[]{:S(2)}) collective-permute-start(bf16[352,2048]{1,0:T(8,128)(2,1)} %bitcast.69), channel_id=1, source_target_pairs={{0,32},{32,0},{64,96},{96,64},{1,33},{33,1},{65,97},{97,65},{2,34}... | collective-permute-start | bytes 4325384 | tf_op jit(solution)/shard_map/ppermute | solution.py:632
  92.2 12.1 %copy-start.9 = (bf16[2048,1]{0,1:T(2,128)(2,1)S(1)}, bf16[2048,1]{0,1:T(2,128)(2,1)}, u32[]{:S(2)}) copy-start(bf16[2048,1]{0,1:T(2,128)(2,1)} %reshape.142) | copy-start | bytes 12292
  94.0 10.3 %copy-start.6 = (bf16[128,2048]{1,0:T(8,128)(2,1)S(1)}, bf16[128,2048]{1,0:T(8,128)(2,1)}, u32[]{:S(2)}) copy-start(bf16[128,2048]{1,0:T(8,128)(2,1)} %get-tuple-element.43.own_hbm) | copy-start | bytes 1572868
  102.3 67.3 %collective-permute-start.13 = (f32[128,512]{1,0:T(8,128)}, f32[128,512]{1,0:T(8,128)}, u32[]{:S(2)}, u32[]{:S(2)}) collective-permute-start(f32[128,512]{1,0:T(8,128)} %get-tuple-element.54), channel_id=1, source_target_pairs={{0,32},{32,0},{64,96},{96,64},{1,33},{33,1},{65,97},{97,65},{2,34}... | collective-permute-start | bytes 786440 | tf_op jit(solution)/shard_map/ppermute | solution.py:773
  133.1 12.9 %collective-permute-start.12 = (bf16[256,1024]{1,0:T(8,128)(2,1)S(1)}, bf16[256,1024]{1,0:T(8,128)(2,1)}, u32[]{:S(2)}, u32[]{:S(2)}) collective-permute-start(bf16[256,1024]{1,0:T(8,128)(2,1)S(1)} %dynamic-slice_convert_fusion), channel_id=1, source_target_pairs={{0,64},{64,0},{32,96},{96,32},{1,65},{65,1},{33,97},{97,33},{2,66}... | collective-permute-start | bytes 1572872 | tf_op jit(solution)/shard_map/ppermute | solution.py:755
  146.0 51.4 %all-to-all-start.3 = ((bf16[128,24,512]{2,1,0:T(8,128)(2,1)}), bf16[128,24,512]{2,1,0:T(8,128)(2,1)}, u32[]{:S(2)}, u32[]{:S(2)}) async-start(bf16[128,24,512]{2,1,0:T(8,128)(2,1)} %bitcast.58), calls=%async_computation.3 | async-start | bytes 6291456 | tf_op jit(solution)/shard_map/all_to_all | solution.py:760
  163.9 3.6 %collective-permute-start.14 = (bf16[256,512]{1,0:T(8,128)(2,1)}, bf16[256,512]{1,0:T(8,128)(2,1)}, u32[]{:S(2)}, u32[]{:S(2)}) collective-permute-start(bf16[256,512]{1,0:T(8,128)(2,1)} %dynamic-slice_convert_fusion.1), channel_id=1, source_target_pairs={{0,32},{32,0},{64,96},{96,64},{1,33},{33,1},{65,97},{97,65},{2,34}... | collective-permute-start | bytes 786440 | tf_op jit(solution)/shard_map/ppermute | solution.py:768
  (7 other events, 23.3 us)

commit v11 on v10

--- a/solution.py
+++ b/solution.py
@@ -295,7 +295,7 @@
     select_hbm, own_hbm, peer_hbm, out_hbm, select, rows, out, sems, out_sems
 ):
     half = rows.shape[0] // 2
-    total, block = out.shape[0], out.shape[0] // 3
+    total, block = out.shape[0], out.shape[0] // 6
     copies = [
         pltpu.make_async_copy(own_hbm, rows.at[pl.ds(0, half)], sems.at[0]),
         pltpu.make_async_copy(peer_hbm, rows.at[pl.ds(half, half)], sems.at[1]),
@@ -332,7 +332,7 @@
             pltpu.VMEM((rows, width), BF),
             pltpu.VMEM((slots, width), BF),
             pltpu.SemaphoreType.DMA((3,)),
-            pltpu.SemaphoreType.DMA((3,)),
+            pltpu.SemaphoreType.DMA((6,)),
         ],
         compiler_params=pltpu.CompilerParams(vmem_limit_bytes=58 << 20),
         cost_estimate=pl.CostEstimate(

time: 202 us -> 202 us (level)
  no operation moved by 1% of the time
where the time goes in v11:
time: 202 us; the launch traced here: 201 us
  waiting for transfers between devices  70.4 us (35%)
  starting transfers between devices  49 us (24%)
  Pallas kernels  32.7 us (16%)
  local copies, waits for them, and re-layouts  23.6 us (12%)
  matrix products  13.6 us (7%)
  other arithmetic  10.6 us (5%)
    all_to_all x1, waiting for transfers between devices, per_device(): lax.all_to_all(partial, BOTH, split_axis=0, concat_axis=0, tiled=True)  27.9 us
    all_to_all x1, waiting for transfers between devices, per_device(): lax.all_to_all(outgoing.reshape(tok_count, slots_core, model_width), 'tok...  20.3 us
    pallas_call x1, Pallas kernels, experts(): pl.pallas_call(expert_kernel, out_shape=jax.ShapeDtypeStruct((groups, row...  11.6 us
    ppermute x6, starting transfers between devices, per_device(): lax.ppermute(part, 'tok', [(r * ROW + y, r * ROW + (y + step) % ROW) for...  9.97 us
    all_to_all x1, starting transfers between devices, per_device(): lax.all_to_all(partial, BOTH, split_axis=0, concat_axis=0, tiled=True)  9.91 us
    all_to_all x1, starting transfers between devices, per_device(): lax.all_to_all(pieces, BOTH, split_axis=0, concat_axis=0, tiled=True)  9.24 us
    ppermute x1, waiting for transfers between devices, per_device(): projected_far = lax.ppermute(projected_low, 'head', CROSS)  7.14 us
    ppermute x1, starting transfers between devices, per_device(): lax.ppermute(own, 'tok', [(s, s + ROW) for s in range(tok_count - ROW)])  6.59 us
  transfers between devices with their start and end apart: 19, of which 9 were waited for; matrix products, arithmetic and copies ran while one was open for 22% of the time, Pallas kernels for 10%

profile of v11, /device:TPU:0, one launch (start us, length us, event | category | flops | bytes accessed | tf_op | source)
XLA Modules:
  0.0 201.1 jit_solution(15914350855636123873)
XLA Ops:
  0.7 2.1 %pack_heads.1 = (bf16[256,256]{1,0:T(8,128)(2,1)}, bf16[256,256]{1,0:T(8,128)(2,1)}, bf16[256,256]{1,0:T(8,128)(2,1)}, bf16[256,256]{1,0:T(8,128)(2,1)}) custom-call(s32[1]{0:T(128)} %bitcast.1.place, bf16[256,512]{1,0:T(8,128)(2,1)} %keys.1, bf16[256,512]{1,0:T(8,128)(2,1)} %values.1), custom_call_target="tpu_custom_call" | custom-call | bytes 1048576 | tf_op jit(solution)/shard_map/pack_heads/pallas_call | solution.py:37
  4.4 2.9 %collective-permute-start.1 = (bf16[256,256]{1,0:T(8,128)(2,1)}, bf16[256,256]{1,0:T(8,128)(2,1)}, u32[]{:S(2)}, u32[]{:S(2)}) collective-permute-start(bf16[256,256]{1,0:T(8,128)(2,1)} %get-tuple-element.29), channel_id=1, source_target_pairs={{0,2},{1,3},{2,0},{3,1},{4,6},{5,7},{6,4},{7,5},{8,10},{9,11},{10,... | collective-permute-start | bytes 393224 | tf_op jit(solution)/shard_map/ppermute | solution.py:638
  13.6 2.0 pad_maximum_fusion.own_hbm
  15.6 6.6 %collective-permute-start.6 = (bf16[4,256,256]{2,1,0:T(8,128)(2,1)}, bf16[4,256,256]{2,1,0:T(8,128)(2,1)}, u32[]{:S(2)}, u32[]{:S(2)}) collective-permute-start(bf16[4,256,256]{2,1,0:T(8,128)(2,1)} %pad_maximum_fusion.own_hbm), channel_id=1, source_target_pairs={{0,4},{1,5},{2,6},{3,7},{4,8},{5,9},{6,10},{7,11},{8,12},{9,13},{1... | collective-permute-start | bytes 1572872 | tf_op jit(solution)/shard_map/ppermute | solution.py:674
  24.4 2.1 %collective-permute-start.5 = (bf16[256,128]{1,0:T(8,128)(2,1)S(1)}, bf16[256,128]{1,0:T(8,128)(2,1)S(1)}, u32[]{:S(2)}, u32[]{:S(2)}) collective-permute-start(bf16[256,128]{1,0:T(8,128)(2,1)S(1)} %get-tuple-element.61), channel_id=1, source_target_pairs={{0,3},{1,0},{2,1},{3,2},{4,7},{5,4},{6,5},{7,6},{8,11},{9,8},{10,9... | collective-permute-start | bytes 196616 | tf_op jit(solution)/shard_map/ppermute | solution.py:661
  29.5 2.8 %collective-permute-done.4 = bf16[256,128]{1,0:T(8,128)(2,1)S(1)} collective-permute-done((bf16[256,128]{1,0:T(8,128)(2,1)S(1)}, bf16[256,128]{1,0:T(8,128)(2,1)S(1)}, u32[]{:S(2)}, u32[]{:S(2)}) %collective-permute-start.4) | collective-permute-done | bytes 65568 | tf_op jit(solution)/shard_map/ppermute | solution.py:661
  33.9 4.8 %row_attention.1 = bf16[2,4,128,128]{3,2,1,0:T(8,128)(2,1)} custom-call(s32[1]{0:T(128)} %bitcast.1.place, s32[1,2048]{1,0:T(1,128)} %bitcast.65, bf16[4,256,128]{2,1,0:T(8,128)(2,1)} %pad_maximum_fusion.2.query_hbm, bf16[4,256,256]{2,1,0:T(8,128)(2,1)} %pad_maximum_fusion.own_hbm, bf16[4,256,256]{2,1,0:T(8,128)(2,1)} %collective-permute-done.6.past_hbm), custom_call_target="tpu_custom_call" | custom-call | flops 671088640 | bytes 3145728 | tf_op jit(solution)/shard_map/row_attention/pallas_call | solution.py:135
  38.7 4.1 %all-to-all-start = ((bf16[8,128,128]{2,1,0:T(8,128)(2,1)}), bf16[8,128,128]{2,1,0:T(8,128)(2,1)}, u32[]{:S(2)}, u32[]{:S(2)}) async-start(bf16[8,128,128]{2,1,0:T(8,128)(2,1)} %bitcast.59), calls=%async_computation | async-start | bytes 524288 | tf_op jit(solution)/shard_map/all_to_all | solution.py:690
  45.1 4.6 %all-to-all-done = bf16[8,128,128]{2,1,0:T(8,128)(2,1)} async-done(((bf16[8,128,128]{2,1,0:T(8,128)(2,1)}), bf16[8,128,128]{2,1,0:T(8,128)(2,1)}, u32[]{:S(2)}, u32[]{:S(2)}) %all-to-all-start) | async-done | bytes 262176 | tf_op jit(solution)/shard_map/all_to_all | solution.py:690
  49.7 4.1 %project.1.near_hbm = bf16[128,2048]{1,0:T(8,128)(2,1)} custom-call(s32[1]{0:T(128)} %bitcast.core, bf16[2,4,128,128]{3,2,1,0:T(8,128)(2,1)} %bitcast.12.att_hbm, bf16[512,2048]{1,0:T(8,128)(2,1)} %own_hbm.1, bf16[512,2048]{1,0:T(8,128)(2,1)} %collective-permute-done.7.peer_hbm), custom_call_target="tpu_custom_call" | custom-call | flops 536870912 | bytes 6291456 | tf_op jit(solution)/shard_map/project/pallas_call | solution.py:199
  54.9 9.2 %all-to-all-start.1 = ((bf16[128,2,1024]{2,1,0:T(2,128)(2,1)}), bf16[128,2,1024]{2,1,0:T(2,128)(2,1)S(1)}, u32[]{:S(2)}, u32[]{:S(2)}) async-start(bf16[128,2,1024]{2,1,0:T(2,128)(2,1)} %reshape.136), calls=%async_computation.1 | async-start | bytes 1048576 | tf_op jit(solution)/shard_map/all_to_all | solution.py:717
  64.2 7.1 %collective-permute-done.8.far_hbm = bf16[128,2048]{1,0:T(8,128)(2,1)} collective-permute-done((bf16[128,2048]{1,0:T(8,128)(2,1)}, bf16[128,2048]{1,0:T(8,128)(2,1)}, u32[]{:S(2)}, u32[]{:S(2)}) %collective-permute-start.8) | collective-permute-done | bytes 524320 | tf_op jit(solution)/shard_map/ppermute | solution.py:715
  71.3 2.6 %add_and_norm.1 = (f32[128,2048]{1,0:T(8,128)}, bf16[128,2048]{1,0:T(8,128)(2,1)}) custom-call(s32[1]{0:T(128)} %bitcast.core, bf16[256,2048]{1,0:T(8,128)(2,1)} %hidden_hbm.1, bf16[128,2048]{1,0:T(8,128)(2,1)} %project.1.near_hbm, bf16[128,2048]{1,0:T(8,128)(2,1)} %collective-permute-done.8.far_hbm, f32[1,2048]{1,0:T(1,128)} %bitcast.64), custom_call_target="tpu_custom_call" | custom-call | flops 2097152 | bytes 4194304 | tf_op jit(solution)/shard_map/add_and_norm/pallas_call | solution.py:268
  73.9 4.0 %all-to-all-done.1 = bf16[128,2,1024]{2,1,0:T(2,128)(2,1)S(1)} async-done(((bf16[128,2,1024]{2,1,0:T(2,128)(2,1)}), bf16[128,2,1024]{2,1,0:T(2,128)(2,1)S(1)}, u32[]{:S(2)}, u32[]{:S(2)}) %all-to-all-start.1) | async-done | bytes 524320 | tf_op jit(solution)/shard_map/all_to_all | solution.py:717
  77.9 2.1 %collective-permute-done.9.peer_hbm = bf16[128,2048]{1,0:T(8,128)(2,1)S(1)} collective-permute-done((bf16[128,2048]{1,0:T(8,128)(2,1)}, bf16[128,2048]{1,0:T(8,128)(2,1)S(1)}, u32[]{:S(2)}, u32[]{:S(2)}) %collective-permute-start.9) | collective-permute-done | bytes 524320 | tf_op jit(solution)/shard_map/ppermute | solution.py:722
  80.8 3.4 %gather_rows.1 = bf16[768,2048]{1,0:T(8,128)(2,1)} custom-call(bf16[768,256]{1,0:T(8,128)(2,1)} %fusion.3.select_hbm, bf16[128,2048]{1,0:T(8,128)(2,1)} %get-tuple-element.43.own_hbm, bf16[128,2048]{1,0:T(8,128)(2,1)} %copy-done.7), custom_call_target="tpu_custom_call" | custom-call | flops 805306368 | bytes 5242880 | tf_op jit(solution)/shard_map/gather_rows/pallas_call | solution.py:325
  84.2 6.0 %all-to-all-start.2 = ((bf16[32,24,2048]{2,1,0:T(8,128)(2,1)}), bf16[32,24,2048]{2,1,0:T(8,128)(2,1)}, u32[]{:S(2)}, u32[]{:S(2)}) async-start(bf16[32,24,2048]{2,1,0:T(8,128)(2,1)} %bitcast.57), calls=%async_computation.2 | async-start | bytes 6291456 | tf_op jit(solution)/shard_map/all_to_all | solution.py:733
  106.0 4.4 %fusion.1 = f32[256,2,704]{0,2,1:T(8,128)S(1)} fusion(bf16[2048,2,704]{0,2,1:T(8,128)(2,1)} %param.24, bf16[128,2048]{1,0:T(8,128)(2,1)S(1)} %copy-done.8, bf16[128,2048]{1,0:T(8,128)(2,1)S(1)} %copy-done.6, pred[]{:T(512)S(6)} %eq.103), kind=kOutput, calls=%fused_computation.10 | convolution fusion | flops 1481113600 | bytes 8257537 | tf_op jit(solution)/shard_map/td,dgf->tgf/dot_general | solution.py:740
  112.6 20.3 %all-to-all-done.2 = bf16[32,24,2048]{2,1,0:T(8,128)(2,1)} async-done(((bf16[32,24,2048]{2,1,0:T(8,128)(2,1)}), bf16[32,24,2048]{2,1,0:T(8,128)(2,1)}, u32[]{:S(2)}, u32[]{:S(2)}) %all-to-all-start.2) | async-done | bytes 3145760 | tf_op jit(solution)/shard_map/all_to_all | solution.py:733
  134.3 11.6 %experts.1 = bf16[4,768,512]{2,1,0:T(8,128)(2,1)} custom-call(bf16[768,2048]{1,0:T(8,128)(2,1)} %bitcast.22.x_hbm, bf16[2,352,2048]{2,1,0:T(8,128)(2,1)} %bitcast.68, bf16[2,352,2048]{2,1,0:T(8,128)(2,1)} %collective-permute-done.10.both_peer, bf16[352,2048]{1,0:T(8,128)(2,1)} %bitcast.70, bf16[352,2048]{1,0:T(8,128)(2,1)} %collective-permute-done.11.down_peer), custom_call_target="tpu_custom_call" | custom-call | flops 6643777536 | bytes 15728640 | tf_op jit(solution)/shard_map/experts/pallas_call | solution.py:469
  145.9 9.9 %all-to-all-start.3 = ((bf16[128,24,512]{2,1,0:T(8,128)(2,1)}), bf16[128,24,512]{2,1,0:T(8,128)(2,1)}, u32[]{:S(2)}, u32[]{:S(2)}) async-start(bf16[128,24,512]{2,1,0:T(8,128)(2,1)} %bitcast.58), calls=%async_computation.3 | async-start | bytes 6291456 | tf_op jit(solution)/shard_map/all_to_all | solution.py:760
  167.4 2.0 %convert_add_fusion.1.shared_hbm = f32[256,512]{1,0:T(8,128)} fusion(bf16[256,512]{1,0:T(8,128)(2,1)} %collective-permute-done.14, f32[256,1024]{1,0:T(8,128)} %copy-done.3, s32[]{:T(128)S(6)} %select_n.199), kind=kLoop, calls=%fused_computation.22 | loop fusion | flops 262144 | bytes 1310724 | tf_op jit(solution)/shard_map/add | solution.py:768
  169.5 27.9 %all-to-all-done.3 = bf16[128,24,512]{2,1,0:T(8,128)(2,1)} async-done(((bf16[128,24,512]{2,1,0:T(8,128)(2,1)}), bf16[128,24,512]{2,1,0:T(8,128)(2,1)}, u32[]{:S(2)}, u32[]{:S(2)}) %all-to-all-start.3) | async-done | bytes 3145760 | tf_op jit(solution)/shard_map/all_to_all | solution.py:760
  197.4 3.5 %combine.1 = bf16[256,512]{1,0:T(8,128)(2,1)} custom-call(s32[1]{0:T(128)} %bitcast.core, bf16[256,1536]{1,0:T(8,128)(2,1)} %copy-done.1, bf16[2,1536,512]{2,1,0:T(8,128)(2,1)} %bitcast.28.back_hbm, f32[128,512]{1,0:T(8,128)} %get-tuple-element.55.mine_hbm, f32[128,512]{1,0:T(8,128)} %collective-permute-done.13.peers_hbm, ...), custom_call_target="tpu_custom_call" | custom-call | flops 1610612736 | bytes 7340032 | tf_op jit(solution)/shard_map/combine/pallas_call | solution.py:543
  (105 shorter events, 49.7 us)
Async XLA Ops:
  0.6 109.8 %copy-start = (bf16[704,2048]{1,0:T(8,128)(2,1)S(1)}, bf16[704,2048]{1,0:T(8,128)(2,1)}, u32[]{:S(2)}) copy-start(bf16[704,2048]{1,0:T(8,128)(2,1)} %param.25) | copy-start | bytes 8650756
  0.7 27.8 %copy-start.4 = (bf16[256,512]{1,0:T(8,128)(2,1)S(1)}, bf16[256,512]{1,0:T(8,128)(2,1)}, u32[]{:S(2)}) copy-start(bf16[256,512]{1,0:T(8,128)(2,1)} %keys.1) | copy-start | bytes 786436
  2.7 10.3 %collective-permute-start = (bf16[256,256]{1,0:T(8,128)(2,1)}, bf16[256,256]{1,0:T(8,128)(2,1)}, u32[]{:S(2)}, u32[]{:S(2)}) collective-permute-start(bf16[256,256]{1,0:T(8,128)(2,1)} %get-tuple-element.28), channel_id=1, source_target_pairs={{0,1},{1,2},{2,3},{3,0},{4,5},{5,6},{6,7},{7,4},{8,9},{9,10},{10,1... | collective-permute-start | bytes 393224 | tf_op jit(solution)/shard_map/ppermute | solution.py:638
  4.4 9.2 %collective-permute-start.1 = (bf16[256,256]{1,0:T(8,128)(2,1)}, bf16[256,256]{1,0:T(8,128)(2,1)}, u32[]{:S(2)}, u32[]{:S(2)}) collective-permute-start(bf16[256,256]{1,0:T(8,128)(2,1)} %get-tuple-element.29), channel_id=1, source_target_pairs={{0,2},{1,3},{2,0},{3,1},{4,6},{5,7},{6,4},{7,5},{8,10},{9,11},{10,... | collective-permute-start | bytes 393224 | tf_op jit(solution)/shard_map/ppermute | solution.py:638
  7.3 6.3 %collective-permute-start.2 = (bf16[256,256]{1,0:T(8,128)(2,1)}, bf16[256,256]{1,0:T(8,128)(2,1)}, u32[]{:S(2)}, u32[]{:S(2)}) collective-permute-start(bf16[256,256]{1,0:T(8,128)(2,1)} %get-tuple-element.30), channel_id=1, source_target_pairs={{0,3},{1,0},{2,1},{3,2},{4,7},{5,4},{6,5},{7,6},{8,11},{9,8},{10,9... | collective-permute-start | bytes 393224 | tf_op jit(solution)/shard_map/ppermute | solution.py:638
  8.6 41.1 %collective-permute-start.7 = (bf16[512,2048]{1,0:T(8,128)(2,1)}, bf16[512,2048]{1,0:T(8,128)(2,1)}, u32[]{:S(2)}, u32[]{:S(2)}) collective-permute-start(bf16[512,2048]{1,0:T(8,128)(2,1)} %own_hbm.1), channel_id=1, source_target_pairs={{0,32},{32,0},{64,96},{96,64},{1,33},{33,1},{65,97},{97,65},{2,34}... | collective-permute-start | bytes 6291464 | tf_op jit(solution)/shard_map/ppermute | solution.py:630
  15.6 18.3 %collective-permute-start.6 = (bf16[4,256,256]{2,1,0:T(8,128)(2,1)}, bf16[4,256,256]{2,1,0:T(8,128)(2,1)}, u32[]{:S(2)}, u32[]{:S(2)}) collective-permute-start(bf16[4,256,256]{2,1,0:T(8,128)(2,1)} %pad_maximum_fusion.own_hbm), channel_id=1, source_target_pairs={{0,4},{1,5},{2,6},{3,7},{4,8},{5,9},{6,10},{7,11},{8,12},{9,13},{1... | collective-permute-start | bytes 1572872 | tf_op jit(solution)/shard_map/ppermute | solution.py:674
  24.4 18.4 %copy-start.5 = (bf16[256,512]{1,0:T(8,128)(2,1)S(1)}, bf16[256,512]{1,0:T(8,128)(2,1)}, u32[]{:S(2)}) copy-start(bf16[256,512]{1,0:T(8,128)(2,1)} %values.1) | copy-start | bytes 786436
  24.4 5.1 %collective-permute-start.5 = (bf16[256,128]{1,0:T(8,128)(2,1)S(1)}, bf16[256,128]{1,0:T(8,128)(2,1)S(1)}, u32[]{:S(2)}, u32[]{:S(2)}) collective-permute-start(bf16[256,128]{1,0:T(8,128)(2,1)S(1)} %get-tuple-element.61), channel_id=1, source_target_pairs={{0,3},{1,0},{2,1},{3,2},{4,7},{5,4},{6,5},{7,6},{8,11},{9,8},{10,9... | collective-permute-start | bytes 196616 | tf_op jit(solution)/shard_map/ppermute | solution.py:661
  26.6 5.8 %collective-permute-start.4 = (bf16[256,128]{1,0:T(8,128)(2,1)S(1)}, bf16[256,128]{1,0:T(8,128)(2,1)S(1)}, u32[]{:S(2)}, u32[]{:S(2)}) collective-permute-start(bf16[256,128]{1,0:T(8,128)(2,1)S(1)} %get-tuple-element.62), channel_id=1, source_target_pairs={{0,2},{1,3},{2,0},{3,1},{4,6},{5,7},{6,4},{7,5},{8,10},{9,11},{10,... | collective-permute-start | bytes 196616 | tf_op jit(solution)/shard_map/ppermute | solution.py:661
  27.7 5.5 %collective-permute-start.3 = (bf16[256,128]{1,0:T(8,128)(2,1)S(1)}, bf16[256,128]{1,0:T(8,128)(2,1)S(1)}, u32[]{:S(2)}, u32[]{:S(2)}) collective-permute-start(bf16[256,128]{1,0:T(8,128)(2,1)S(1)} %get-tuple-element.63), channel_id=1, source_target_pairs={{0,1},{1,2},{2,3},{3,0},{4,5},{5,6},{6,7},{7,4},{8,9},{9,10},{10,1... | collective-permute-start | bytes 196616 | tf_op jit(solution)/shard_map/ppermute | solution.py:661
  38.7 11.0 %all-to-all-start = ((bf16[8,128,128]{2,1,0:T(8,128)(2,1)}), bf16[8,128,128]{2,1,0:T(8,128)(2,1)}, u32[]{:S(2)}, u32[]{:S(2)}) async-start(bf16[8,128,128]{2,1,0:T(8,128)(2,1)} %bitcast.59), calls=%async_computation | async-start | bytes 524288 | tf_op jit(solution)/shard_map/all_to_all | solution.py:690
  53.8 17.5 %collective-permute-start.8 = (bf16[128,2048]{1,0:T(8,128)(2,1)}, bf16[128,2048]{1,0:T(8,128)(2,1)}, u32[]{:S(2)}, u32[]{:S(2)}) collective-permute-start(bf16[128,2048]{1,0:T(8,128)(2,1)} %project.1.near_hbm), channel_id=1, source_target_pairs={{0,64},{64,0},{32,96},{96,32},{1,65},{65,1},{33,97},{97,33},{2,66}... | collective-permute-start | bytes 1572872 | tf_op jit(solution)/shard_map/ppermute | solution.py:715
  54.9 23.0 %all-to-all-start.1 = ((bf16[128,2,1024]{2,1,0:T(2,128)(2,1)}), bf16[128,2,1024]{2,1,0:T(2,128)(2,1)S(1)}, u32[]{:S(2)}, u32[]{:S(2)}) async-start(bf16[128,2,1024]{2,1,0:T(2,128)(2,1)} %reshape.136), calls=%async_computation.1 | async-start | bytes 1048576 | tf_op jit(solution)/shard_map/all_to_all | solution.py:717
  77.9 2.1 %collective-permute-start.9 = (bf16[128,2048]{1,0:T(8,128)(2,1)}, bf16[128,2048]{1,0:T(8,128)(2,1)S(1)}, u32[]{:S(2)}, u32[]{:S(2)}) collective-permute-start(bf16[128,2048]{1,0:T(8,128)(2,1)} %get-tuple-element.43.own_hbm), channel_id=1, source_target_pairs={{0,32},{32,0},{64,96},{96,64},{1,33},{33,1},{65,97},{97,65},{2,34}... | collective-permute-start | bytes 1572872 | tf_op jit(solution)/shard_map/ppermute | solution.py:722
  84.2 48.8 %all-to-all-start.2 = ((bf16[32,24,2048]{2,1,0:T(8,128)(2,1)}), bf16[32,24,2048]{2,1,0:T(8,128)(2,1)}, u32[]{:S(2)}, u32[]{:S(2)}) async-start(bf16[32,24,2048]{2,1,0:T(8,128)(2,1)} %bitcast.57), calls=%async_computation.2 | async-start | bytes 6291456 | tf_op jit(solution)/shard_map/all_to_all | solution.py:733
  90.2 44.1 %collective-permute-start.10 = (bf16[2,352,2048]{2,1,0:T(8,128)(2,1)}, bf16[2,352,2048]{2,1,0:T(8,128)(2,1)}, u32[]{:S(2)}, u32[]{:S(2)}) collective-permute-start(bf16[2,352,2048]{2,1,0:T(8,128)(2,1)} %bitcast.67), channel_id=1, source_target_pairs={{0,32},{32,0},{64,96},{96,64},{1,33},{33,1},{65,97},{97,65},{2,34}... | collective-permute-start | bytes 8650760 | tf_op jit(solution)/shard_map/ppermute | solution.py:631
  90.3 44.0 %collective-permute-start.11 = (bf16[352,2048]{1,0:T(8,128)(2,1)}, bf16[352,2048]{1,0:T(8,128)(2,1)}, u32[]{:S(2)}, u32[]{:S(2)}) collective-permute-start(bf16[352,2048]{1,0:T(8,128)(2,1)} %bitcast.69), channel_id=1, source_target_pairs={{0,32},{32,0},{64,96},{96,64},{1,33},{33,1},{65,97},{97,65},{2,34}... | collective-permute-start | bytes 4325384 | tf_op jit(solution)/shard_map/ppermute | solution.py:632
  92.1 12.1 %copy-start.9 = (bf16[2048,1]{0,1:T(2,128)(2,1)S(1)}, bf16[2048,1]{0,1:T(2,128)(2,1)}, u32[]{:S(2)}) copy-start(bf16[2048,1]{0,1:T(2,128)(2,1)} %reshape.142) | copy-start | bytes 12292
  93.9 10.3 %copy-start.6 = (bf16[128,2048]{1,0:T(8,128)(2,1)S(1)}, bf16[128,2048]{1,0:T(8,128)(2,1)}, u32[]{:S(2)}) copy-start(bf16[128,2048]{1,0:T(8,128)(2,1)} %get-tuple-element.43.own_hbm) | copy-start | bytes 1572868
  102.2 67.3 %collective-permute-start.13 = (f32[128,512]{1,0:T(8,128)}, f32[128,512]{1,0:T(8,128)}, u32[]{:S(2)}, u32[]{:S(2)}) collective-permute-start(f32[128,512]{1,0:T(8,128)} %get-tuple-element.54), channel_id=1, source_target_pairs={{0,32},{32,0},{64,96},{96,64},{1,33},{33,1},{65,97},{97,65},{2,34}... | collective-permute-start | bytes 786440 | tf_op jit(solution)/shard_map/ppermute | solution.py:773
  133.0 12.9 %collective-permute-start.12 = (bf16[256,1024]{1,0:T(8,128)(2,1)S(1)}, bf16[256,1024]{1,0:T(8,128)(2,1)}, u32[]{:S(2)}, u32[]{:S(2)}) collective-permute-start(bf16[256,1024]{1,0:T(8,128)(2,1)S(1)} %dynamic-slice_convert_fusion), channel_id=1, source_target_pairs={{0,64},{64,0},{32,96},{96,32},{1,65},{65,1},{33,97},{97,33},{2,66}... | collective-permute-start | bytes 1572872 | tf_op jit(solution)/shard_map/ppermute | solution.py:755
  145.9 51.5 %all-to-all-start.3 = ((bf16[128,24,512]{2,1,0:T(8,128)(2,1)}), bf16[128,24,512]{2,1,0:T(8,128)(2,1)}, u32[]{:S(2)}, u32[]{:S(2)}) async-start(bf16[128,24,512]{2,1,0:T(8,128)(2,1)} %bitcast.58), calls=%async_computation.3 | async-start | bytes 6291456 | tf_op jit(solution)/shard_map/all_to_all | solution.py:760
  163.9 3.6 %collective-permute-start.14 = (bf16[256,512]{1,0:T(8,128)(2,1)}, bf16[256,512]{1,0:T(8,128)(2,1)}, u32[]{:S(2)}, u32[]{:S(2)}) collective-permute-start(bf16[256,512]{1,0:T(8,128)(2,1)} %dynamic-slice_convert_fusion.1), channel_id=1, source_target_pairs={{0,32},{32,0},{64,96},{96,64},{1,33},{33,1},{65,97},{97,65},{2,34}... | collective-permute-start | bytes 786440 | tf_op jit(solution)/shard_map/ppermute | solution.py:768
  (7 other events, 23.3 us)
